TPU v7x, 32 devices: a whole 2x2x4 slice. The times are simulated.
32 devices in a mesh: rows: 4 (over y, x), cols: 8 (over z, core).
Axes of the slice: x: 2, y: 2, z: 4, core: 2. Of those that a mesh axis runs over, the one named last changes fastest.
Arguments:
- images: bfloat16 [2, 64, 256, 1024], P(None, None, 'rows', 'cols'), may hold values from -6 to 6
- first_weight: bfloat16 [9, 64, 64], replicated, may hold values from -0.25 to 0.25
- second_weight: bfloat16 [9, 64, 64], replicated, may hold values from -0.25 to 0.25
- search_ranges: int32 [2, 32, 8], P(None, 'rows', 'cols'), may hold values from 0 to 16, as said below
Outputs:
- matched: bfloat16 [64, 256, 1024], P(None, 'rows', 'cols')
- disparity: float32 [256, 1024], P('rows', 'cols')
Inputs may be any that keep to these rules, and one draw needn't show every extreme that they name: search_ranges[0] is 0 to 1 and search_ranges[1] is 1 to 16; some block has search_ranges[0] = 1 together with search_ranges[1] = 16.
All inputs are finite; a program needn't handle non-finite values.
Results may differ from a plain program's by a relative error of at most 0.008.
Values may be sent and summed in bfloat16 or wider, within the bound.
No kernel may reach another device: no remote copies, remote signals or barrier semaphores. Data moves between devices by JAX's collectives and lax.ppermute only.
A program may use at most 128 MiB of HBM per device.

v0:
```python
import jax
import jax.numpy as jnp
from jax import lax
from jax.sharding import PartitionSpec as P

RG = 8
FIRST_DILATION = 2
SECOND_DILATION = 4
HOPS = 18


sharpness_divisor = 10.0
epsilon = 1e-05


def with_halo(block, sides, width):
    for axis, dim in sides:
        count = lax.axis_size(axis)
        forward = [(i, i + 1) for i in range(count - 1)]
        backward = [(target, source) for source, target in forward]
        low = lax.ppermute(
            lax.slice_in_dim(block, block.shape[dim] - width, None, axis=dim), axis, forward
        )
        high = lax.ppermute(lax.slice_in_dim(block, 0, width, axis=dim), axis, backward)
        block = jnp.concatenate([low, block, high], axis=dim)
    return block


def convolution_layer(images, weights, dilation):
    padded = with_halo(images, (("rows", 2), ("cols", 3)), dilation)
    height = images.shape[2]
    full_width = images.shape[3]
    summed = jnp.zeros((images.shape[0], weights.shape[1], height, full_width), jnp.float32)
    for row_tap in range(3):
        for horizontal_offset in range(3):
            window = padded[
                :,
                :,
                row_tap * dilation : row_tap * dilation + height,
                horizontal_offset * dilation : horizontal_offset * dilation + full_width,
            ]
            summed = summed + jnp.einsum(
                "oc,nchw->nohw",
                weights[3 * row_tap + horizontal_offset],
                window,
                preferred_element_type=jnp.float32,
            )
    return summed


def normalize(feature_maps):
    widened = feature_maps.astype(jnp.float32)
    return (
        widened * lax.rsqrt(jnp.mean(widened * widened, axis=1, keepdims=True) + epsilon)
    ).astype(jnp.bfloat16)


def hop_terms(source_descriptors, key_feats, hop_index, low_edge, high_edge):
    plane_total = source_descriptors.shape[0]
    segment = source_descriptors.shape[2]
    pairing_similarity = jnp.einsum(
        "cri,crm->rim", source_descriptors, key_feats, preferred_element_type=jnp.float32
    ) * (sharpness_divisor / plane_total)
    offsets = (
        hop_index * segment
        + lax.broadcasted_iota(jnp.int32, (segment, segment), 0)
        - lax.broadcasted_iota(jnp.int32, (segment, segment), 1)
    )
    inside = (offsets[None] >= low_edge[:, None, None]) & (offsets[None] < high_edge[:, None, None])
    rounded = jnp.where(inside, jnp.exp(pairing_similarity), 0.0).astype(jnp.bfloat16)
    norm_sum = jnp.sum(rounded, axis=-1, dtype=jnp.float32)
    shift_sum = jnp.sum(rounded * offsets.astype(jnp.float32)[None], axis=-1)
    feature_sum = jnp.einsum("rim,crm->cri", rounded, key_feats, preferred_element_type=jnp.float32)
    return (norm_sum, shift_sum, feature_sum)


def per_device(images, first_weight, second_weight, search_ranges):
    inner_activations = jax.nn.silu(convolution_layer(images, first_weight, FIRST_DILATION)).astype(
        jnp.bfloat16
    )
    feature_maps = (
        images.astype(jnp.float32)
        + convolution_layer(inner_activations, second_weight, SECOND_DILATION)
    ).astype(jnp.bfloat16)
    unit_feats = normalize(feature_maps)
    plane_total = unit_feats.shape[1]
    count_rows = unit_feats.shape[2]
    segment = unit_feats.shape[3]
    peer_count = lax.axis_size("cols")
    column = lax.axis_index("cols")
    band_rows = count_rows // peer_count
    full_width = segment * peer_count
    whole_rows = lax.all_to_all(unit_feats, "cols", split_axis=2, concat_axis=3, tiled=True)
    gathered = lax.all_gather(search_ranges, "cols", axis=2, tiled=True)
    spread_rows = jnp.repeat(gathered, RG, axis=1)
    own_ranges = lax.dynamic_slice_in_dim(spread_rows, column * band_rows, band_rows, 1).reshape(
        2, band_rows * peer_count
    )
    low_edge = segment * own_ranges[0]
    high_edge = segment * (own_ranges[0] + own_ranges[1])
    source_descriptors = whole_rows[0].reshape(plane_total, band_rows * peer_count, segment)
    padded = jnp.pad(whole_rows[1], ((0, 0), (0, 0), ((HOPS - 1) * segment, 0)))

    def accumulate(hop_index, carried):
        norm_sum, shift_sum, feature_sum = carried
        key_feats = lax.dynamic_slice_in_dim(
            padded, (HOPS - 1 - hop_index) * segment, full_width, 2
        )
        key_feats = key_feats.reshape(plane_total, band_rows * peer_count, segment)
        new_terms = hop_terms(source_descriptors, key_feats, hop_index, low_edge, high_edge)
        return (norm_sum + new_terms[0], shift_sum + new_terms[1], feature_sum + new_terms[2])

    zero_rows = jnp.zeros((band_rows * peer_count, segment), jnp.float32)
    zero_feats = jnp.zeros((plane_total, band_rows * peer_count, segment), jnp.float32)
    norm_sum, shift_sum, feature_sum = lax.fori_loop(
        0, HOPS, accumulate, (zero_rows, zero_rows, zero_feats)
    )
    matched_rows = (
        (feature_sum / norm_sum[None])
        .astype(jnp.bfloat16)
        .reshape(plane_total, band_rows, full_width)
    )
    disparity_rows = (shift_sum / norm_sum / segment).reshape(band_rows, full_width)
    matched = lax.all_to_all(matched_rows, "cols", split_axis=2, concat_axis=1, tiled=True)
    disparity = lax.all_to_all(disparity_rows, "cols", split_axis=1, concat_axis=0, tiled=True)
    return (matched, disparity)


def solution(mesh):
    placed = (P(None, None, "rows", "cols"), P(), P(), P(None, "rows", "cols"))
    return jax.shard_map(
        per_device,
        mesh=mesh,
        in_specs=placed,
        out_specs=(P(None, "rows", "cols"), P("rows", "cols")),
        check_vma=False,
    )
```

profile of v0, /device:TPU:4, one launch (start us, length us, event | category | flops | bytes accessed | tf_op | source)
XLA Modules:
  0.0 488.2 jit_solution(17448177616877431964)
XLA Ops:
  3.8 3.4 collective-permute-start
  7.2 3.3 collective-permute-start.1
  10.6 3.7 fusion.64
  15.7 3.2 fusion.101
  19.0 3.7 copy.72
  24.0 3.7 copy.69
  27.7 3.2 collective-permute-start.2
  30.9 4.3 fusion.44
  37.8 4.8 copy.70
  42.7 4.9 fusion.19
  50.7 4.6 copy.73
  55.2 5.3 %fusion.16 = f32[2,64,128,64]{2,3,1,0:T(8,128)} fusion(bf16[2,64,68,128]{3,1,2,0:T(8,128)(2,1)S(1)} %constant_dynamic-update-slice_fusion, bf16[2,64,68,2]{3,1,2,0:T(8,128)(2,1)} %copy.73, bf16[9,64,64]{2,1,0:T(8,128)(2,1)S(1)} %copy-done.13), kind=kOutput, calls=%fused_computation.40 | convolution fusion | flops 138412032 | bytes 6473728 | tf_op jit(solution)/shard_map/oc,nchw->nohw/dot_general | solution.py:42
  60.5 3.5 fusion.13
  64.0 3.2 fusion.46
  67.2 12.5 %fusion.11 = bf16[2,64,64,128]{3,1,2,0:T(8,128)(2,1)S(1)} fusion(f32[2,64,128,64]{2,3,1,0:T(8,128)} %fusion.44, f32[2,64,128,64]{2,3,1,0:T(8,128)} %fusion.46, f32[2,64,128,64]{2,3,1,0:T(8,128)} %fusion.13, f32[2,64,128,64]{2,3,1,0:T(8,128)} %fusion.64, f32[2,64,128,64]{2,3,1,0:T(8,128)} %fusion.19, f32[2,64,128,64]{2,3,1,0:T(8,128)} %fusion.16, ...), kind=kOutput, calls=%fused_computation.35 | convolution fusion | flops 152043520 | bytes 40124416 | tf_op jit(solution)/shard_map/oc,nchw->nohw/dot_general | solution.py:42
  82.2 16.4 %collective-permute-start.5 = (bf16[2,64,4,128]{3,1,2,0:T(8,128)(2,1)S(1)}, bf16[2,64,4,128]{3,1,2,0:T(8,128)(2,1)S(1)}, u32[]{:S(2)}, u32[]{:S(2)}) collective-permute-start(bf16[2,64,4,128]{3,1,2,0:T(8,128)(2,1)S(1)} %get-tuple-element.205), channel_id=1, source_target_pairs={{8,0},{16,8},{24,16},{9,1},{17,9},{25,17},{10,2},{18,10},{26,18},{... | collective-permute-start | bytes 393224 | tf_op jit(solution)/shard_map/ppermute | solution.py:24
  101.7 3.3 fusion.100
  105.0 4.2 copy.76
  111.7 4.0 copy.78
  122.4 4.7 copy.77
  127.2 4.8 copy.79
  132.0 5.9 %pad_maximum_fusion = (bf16[2,64,72,132]{3,1,2,0:T(8,128)(2,1)S(1)}, bf16[2,64,72,132]{3,1,2,0:T(8,128)(2,1)S(1)}) fusion(bf16[2,64,72,4]{3,1,2,0:T(8,128)(2,1)} %copy.79, bf16[2,64,4,128]{3,1,2,0:T(8,128)(2,1)S(1)} %collective-permute-done.5, bf16[2,64,64,128]{3,1,2,0:T(8,128)(2,1)S(1)} %copy-done.1, bf16[2,64,4,128]{3,1,2,0:T(8,128)(2,1)S(1)} %collective-permute-done.4, ...), kind=kLoop, calls=%fused_computation.25 | loop fusion | flops 19464192 | bytes 7372800 | tf_op jit(solution)/shard_map/concatenate | solution.py:25
  153.8 15.0 %fusion.5 = (f32[2,64,128]{2,1,0:T(8,128)S(1)}, bf16[2,64,64,128]{3,1,2,0:T(8,128)(2,1)}) fusion(bf16[2,64,72,132]{3,1,2,0:T(8,128)(2,1)} %copy-done.9, bf16[9,64,64]{2,1,0:T(8,128)(2,1)S(1)} %copy-done.14, f32[2,64,128,64]{2,3,1,0:T(8,128)} %fusion.28, f32[2,64,128,64]{2,3,1,0:T(8,128)} %fusion.30, f32[2,64,128,64]{2,3,1,0:T(8,128)} %fusion.32, ...), kind=kOutput, calls=%fused_computation.26 | convolution fusion | flops 148881408 | bytes 39927808 | tf_op jit(solution)/shard_map/oc,nchw->nohw/dot_general | solution.py:42
  172.7 6.6 %all-to-all-start = ((bf16[2,64,64,128]{3,1,0,2:T(8,128)(2,1)}), bf16[2,64,64,128]{3,1,0,2:T(8,128)(2,1)S(1)}, u32[]{:S(2)}, u32[]{:S(2)}) async-start(bf16[2,64,64,128]{3,1,0,2:T(8,128)(2,1)} %copy.80), calls=%async_computation | async-start | bytes 4194304 | tf_op jit(solution)/shard_map/all_to_all | solution.py:93
  179.4 41.5 %all_gather.3 = s32[2,8,8]{1,0,2:T(2,128)S(1)} all-gather(s32[2,8,1]{1,0,2:T(2,128)S(1)} %bitcast.188), channel_id=1, replica_groups=mesh['rows'=4,'cols'=8] {'cols'}, dimensions={2}, use_global_device_ids=true | all-gather | bytes 576 | tf_op jit(solution)/shard_map/all_gather | solution.py:94
  221.1 7.3 %all-to-all-done = bf16[2,64,64,128]{3,1,0,2:T(8,128)(2,1)S(1)} async-done(((bf16[2,64,64,128]{3,1,0,2:T(8,128)(2,1)}), bf16[2,64,64,128]{3,1,0,2:T(8,128)(2,1)S(1)}, u32[]{:S(2)}, u32[]{:S(2)}) %all-to-all-start) | async-done | bytes 2097184 | tf_op jit(solution)/shard_map/all_to_all | solution.py:93
  232.2 204.3 %while.18 = (s32[]{:T(128)}, f32[64,128]{1,0:T(8,128)S(1)}, f32[64,128]{1,0:T(8,128)S(1)}, f32[64,64,128]{2,0,1:T(8,128)}, s32[64]{0:T(128)S(1)}, /*index=5*/s32...) while((s32[]{:T(128)}, f32[64,128]{1,0:T(8,128)S(1)}, ...), condition=%wide.region_4.5_spmd.clone, body=%wide.region_1.4_spmd.clone.sunk | while | flops 280019072 | bytes 33031948 | solution.py:115
  234.1 5.1 %fusion.117 = (f32[64,128]{1,0:T(8,128)S(1)}, f32[64,128]{1,0:T(8,128)S(1)}, bf16[64,128,128]{1,2,0:T(8,128)(2,1)}) fusion(f32[128,128]{0,1:T(8,128)S(1)} %get-tuple-element.268, bf16[64,64,128]{2,0,1:T(8,128)(2,1)} %get-tuple-element.308, bf16[64,64,128]{2,1,0:T(8,128)(2,1)S(1)} %reshape.96, s32[64]{0:T(128)S(1)} %get-tuple-element.306, ...), kind=kOutput, calls=%fused_computation.2.clone.1 | convolution fusion | flops 144687104 | bytes 4391424 | tf_op jit(solution)/shard_map/while/body/eval_jaxpr/cri,crm->rim/dot_general | solution.py:61
  245.4 5.1 %fusion.117 = (f32[64,128]{1,0:T(8,128)S(1)}, f32[64,128]{1,0:T(8,128)S(1)}, bf16[64,128,128]{1,2,0:T(8,128)(2,1)}) fusion(f32[128,128]{0,1:T(8,128)S(1)} %get-tuple-element.268, bf16[64,64,128]{2,0,1:T(8,128)(2,1)} %get-tuple-element.308, bf16[64,64,128]{2,1,0:T(8,128)(2,1)S(1)} %reshape.96, s32[64]{0:T(128)S(1)} %get-tuple-element.306, ...), kind=kOutput, calls=%fused_computation.2.clone.1 | convolution fusion | flops 144687104 | bytes 4391424 | tf_op jit(solution)/shard_map/while/body/eval_jaxpr/cri,crm->rim/dot_general | solution.py:61
  256.8 5.1 %fusion.117 = (f32[64,128]{1,0:T(8,128)S(1)}, f32[64,128]{1,0:T(8,128)S(1)}, bf16[64,128,128]{1,2,0:T(8,128)(2,1)}) fusion(f32[128,128]{0,1:T(8,128)S(1)} %get-tuple-element.268, bf16[64,64,128]{2,0,1:T(8,128)(2,1)} %get-tuple-element.308, bf16[64,64,128]{2,1,0:T(8,128)(2,1)S(1)} %reshape.96, s32[64]{0:T(128)S(1)} %get-tuple-element.306, ...), kind=kOutput, calls=%fused_computation.2.clone.1 | convolution fusion | flops 144687104 | bytes 4391424 | tf_op jit(solution)/shard_map/while/body/eval_jaxpr/cri,crm->rim/dot_general | solution.py:61
  268.1 5.1 %fusion.117 = (f32[64,128]{1,0:T(8,128)S(1)}, f32[64,128]{1,0:T(8,128)S(1)}, bf16[64,128,128]{1,2,0:T(8,128)(2,1)}) fusion(f32[128,128]{0,1:T(8,128)S(1)} %get-tuple-element.268, bf16[64,64,128]{2,0,1:T(8,128)(2,1)} %get-tuple-element.308, bf16[64,64,128]{2,1,0:T(8,128)(2,1)S(1)} %reshape.96, s32[64]{0:T(128)S(1)} %get-tuple-element.306, ...), kind=kOutput, calls=%fused_computation.2.clone.1 | convolution fusion | flops 144687104 | bytes 4391424 | tf_op jit(solution)/shard_map/while/body/eval_jaxpr/cri,crm->rim/dot_general | solution.py:61
  279.5 5.1 %fusion.117 = (f32[64,128]{1,0:T(8,128)S(1)}, f32[64,128]{1,0:T(8,128)S(1)}, bf16[64,128,128]{1,2,0:T(8,128)(2,1)}) fusion(f32[128,128]{0,1:T(8,128)S(1)} %get-tuple-element.268, bf16[64,64,128]{2,0,1:T(8,128)(2,1)} %get-tuple-element.308, bf16[64,64,128]{2,1,0:T(8,128)(2,1)S(1)} %reshape.96, s32[64]{0:T(128)S(1)} %get-tuple-element.306, ...), kind=kOutput, calls=%fused_computation.2.clone.1 | convolution fusion | flops 144687104 | bytes 4391424 | tf_op jit(solution)/shard_map/while/body/eval_jaxpr/cri,crm->rim/dot_general | solution.py:61
  290.8 5.1 %fusion.117 = (f32[64,128]{1,0:T(8,128)S(1)}, f32[64,128]{1,0:T(8,128)S(1)}, bf16[64,128,128]{1,2,0:T(8,128)(2,1)}) fusion(f32[128,128]{0,1:T(8,128)S(1)} %get-tuple-element.268, bf16[64,64,128]{2,0,1:T(8,128)(2,1)} %get-tuple-element.308, bf16[64,64,128]{2,1,0:T(8,128)(2,1)S(1)} %reshape.96, s32[64]{0:T(128)S(1)} %get-tuple-element.306, ...), kind=kOutput, calls=%fused_computation.2.clone.1 | convolution fusion | flops 144687104 | bytes 4391424 | tf_op jit(solution)/shard_map/while/body/eval_jaxpr/cri,crm->rim/dot_general | solution.py:61
  302.2 5.1 %fusion.117 = (f32[64,128]{1,0:T(8,128)S(1)}, f32[64,128]{1,0:T(8,128)S(1)}, bf16[64,128,128]{1,2,0:T(8,128)(2,1)}) fusion(f32[128,128]{0,1:T(8,128)S(1)} %get-tuple-element.268, bf16[64,64,128]{2,0,1:T(8,128)(2,1)} %get-tuple-element.308, bf16[64,64,128]{2,1,0:T(8,128)(2,1)S(1)} %reshape.96, s32[64]{0:T(128)S(1)} %get-tuple-element.306, ...), kind=kOutput, calls=%fused_computation.2.clone.1 | convolution fusion | flops 144687104 | bytes 4391424 | tf_op jit(solution)/shard_map/while/body/eval_jaxpr/cri,crm->rim/dot_general | solution.py:61
  313.5 5.1 %fusion.117 = (f32[64,128]{1,0:T(8,128)S(1)}, f32[64,128]{1,0:T(8,128)S(1)}, bf16[64,128,128]{1,2,0:T(8,128)(2,1)}) fusion(f32[128,128]{0,1:T(8,128)S(1)} %get-tuple-element.268, bf16[64,64,128]{2,0,1:T(8,128)(2,1)} %get-tuple-element.308, bf16[64,64,128]{2,1,0:T(8,128)(2,1)S(1)} %reshape.96, s32[64]{0:T(128)S(1)} %get-tuple-element.306, ...), kind=kOutput, calls=%fused_computation.2.clone.1 | convolution fusion | flops 144687104 | bytes 4391424 | tf_op jit(solution)/shard_map/while/body/eval_jaxpr/cri,crm->rim/dot_general | solution.py:61
  324.9 5.1 %fusion.117 = (f32[64,128]{1,0:T(8,128)S(1)}, f32[64,128]{1,0:T(8,128)S(1)}, bf16[64,128,128]{1,2,0:T(8,128)(2,1)}) fusion(f32[128,128]{0,1:T(8,128)S(1)} %get-tuple-element.268, bf16[64,64,128]{2,0,1:T(8,128)(2,1)} %get-tuple-element.308, bf16[64,64,128]{2,1,0:T(8,128)(2,1)S(1)} %reshape.96, s32[64]{0:T(128)S(1)} %get-tuple-element.306, ...), kind=kOutput, calls=%fused_computation.2.clone.1 | convolution fusion | flops 144687104 | bytes 4391424 | tf_op jit(solution)/shard_map/while/body/eval_jaxpr/cri,crm->rim/dot_general | solution.py:61
  336.2 5.1 %fusion.117 = (f32[64,128]{1,0:T(8,128)S(1)}, f32[64,128]{1,0:T(8,128)S(1)}, bf16[64,128,128]{1,2,0:T(8,128)(2,1)}) fusion(f32[128,128]{0,1:T(8,128)S(1)} %get-tuple-element.268, bf16[64,64,128]{2,0,1:T(8,128)(2,1)} %get-tuple-element.308, bf16[64,64,128]{2,1,0:T(8,128)(2,1)S(1)} %reshape.96, s32[64]{0:T(128)S(1)} %get-tuple-element.306, ...), kind=kOutput, calls=%fused_computation.2.clone.1 | convolution fusion | flops 144687104 | bytes 4391424 | tf_op jit(solution)/shard_map/while/body/eval_jaxpr/cri,crm->rim/dot_general | solution.py:61
  347.6 5.1 %fusion.117 = (f32[64,128]{1,0:T(8,128)S(1)}, f32[64,128]{1,0:T(8,128)S(1)}, bf16[64,128,128]{1,2,0:T(8,128)(2,1)}) fusion(f32[128,128]{0,1:T(8,128)S(1)} %get-tuple-element.268, bf16[64,64,128]{2,0,1:T(8,128)(2,1)} %get-tuple-element.308, bf16[64,64,128]{2,1,0:T(8,128)(2,1)S(1)} %reshape.96, s32[64]{0:T(128)S(1)} %get-tuple-element.306, ...), kind=kOutput, calls=%fused_computation.2.clone.1 | convolution fusion | flops 144687104 | bytes 4391424 | tf_op jit(solution)/shard_map/while/body/eval_jaxpr/cri,crm->rim/dot_general | solution.py:61
  358.9 5.1 %fusion.117 = (f32[64,128]{1,0:T(8,128)S(1)}, f32[64,128]{1,0:T(8,128)S(1)}, bf16[64,128,128]{1,2,0:T(8,128)(2,1)}) fusion(f32[128,128]{0,1:T(8,128)S(1)} %get-tuple-element.268, bf16[64,64,128]{2,0,1:T(8,128)(2,1)} %get-tuple-element.308, bf16[64,64,128]{2,1,0:T(8,128)(2,1)S(1)} %reshape.96, s32[64]{0:T(128)S(1)} %get-tuple-element.306, ...), kind=kOutput, calls=%fused_computation.2.clone.1 | convolution fusion | flops 144687104 | bytes 4391424 | tf_op jit(solution)/shard_map/while/body/eval_jaxpr/cri,crm->rim/dot_general | solution.py:61
  370.3 5.1 %fusion.117 = (f32[64,128]{1,0:T(8,128)S(1)}, f32[64,128]{1,0:T(8,128)S(1)}, bf16[64,128,128]{1,2,0:T(8,128)(2,1)}) fusion(f32[128,128]{0,1:T(8,128)S(1)} %get-tuple-element.268, bf16[64,64,128]{2,0,1:T(8,128)(2,1)} %get-tuple-element.308, bf16[64,64,128]{2,1,0:T(8,128)(2,1)S(1)} %reshape.96, s32[64]{0:T(128)S(1)} %get-tuple-element.306, ...), kind=kOutput, calls=%fused_computation.2.clone.1 | convolution fusion | flops 144687104 | bytes 4391424 | tf_op jit(solution)/shard_map/while/body/eval_jaxpr/cri,crm->rim/dot_general | solution.py:61
  381.6 5.1 %fusion.117 = (f32[64,128]{1,0:T(8,128)S(1)}, f32[64,128]{1,0:T(8,128)S(1)}, bf16[64,128,128]{1,2,0:T(8,128)(2,1)}) fusion(f32[128,128]{0,1:T(8,128)S(1)} %get-tuple-element.268, bf16[64,64,128]{2,0,1:T(8,128)(2,1)} %get-tuple-element.308, bf16[64,64,128]{2,1,0:T(8,128)(2,1)S(1)} %reshape.96, s32[64]{0:T(128)S(1)} %get-tuple-element.306, ...), kind=kOutput, calls=%fused_computation.2.clone.1 | convolution fusion | flops 144687104 | bytes 4391424 | tf_op jit(solution)/shard_map/while/body/eval_jaxpr/cri,crm->rim/dot_general | solution.py:61
  393.0 5.1 %fusion.117 = (f32[64,128]{1,0:T(8,128)S(1)}, f32[64,128]{1,0:T(8,128)S(1)}, bf16[64,128,128]{1,2,0:T(8,128)(2,1)}) fusion(f32[128,128]{0,1:T(8,128)S(1)} %get-tuple-element.268, bf16[64,64,128]{2,0,1:T(8,128)(2,1)} %get-tuple-element.308, bf16[64,64,128]{2,1,0:T(8,128)(2,1)S(1)} %reshape.96, s32[64]{0:T(128)S(1)} %get-tuple-element.306, ...), kind=kOutput, calls=%fused_computation.2.clone.1 | convolution fusion | flops 144687104 | bytes 4391424 | tf_op jit(solution)/shard_map/while/body/eval_jaxpr/cri,crm->rim/dot_general | solution.py:61
  404.3 5.1 %fusion.117 = (f32[64,128]{1,0:T(8,128)S(1)}, f32[64,128]{1,0:T(8,128)S(1)}, bf16[64,128,128]{1,2,0:T(8,128)(2,1)}) fusion(f32[128,128]{0,1:T(8,128)S(1)} %get-tuple-element.268, bf16[64,64,128]{2,0,1:T(8,128)(2,1)} %get-tuple-element.308, bf16[64,64,128]{2,1,0:T(8,128)(2,1)S(1)} %reshape.96, s32[64]{0:T(128)S(1)} %get-tuple-element.306, ...), kind=kOutput, calls=%fused_computation.2.clone.1 | convolution fusion | flops 144687104 | bytes 4391424 | tf_op jit(solution)/shard_map/while/body/eval_jaxpr/cri,crm->rim/dot_general | solution.py:61
  415.7 5.1 %fusion.117 = (f32[64,128]{1,0:T(8,128)S(1)}, f32[64,128]{1,0:T(8,128)S(1)}, bf16[64,128,128]{1,2,0:T(8,128)(2,1)}) fusion(f32[128,128]{0,1:T(8,128)S(1)} %get-tuple-element.268, bf16[64,64,128]{2,0,1:T(8,128)(2,1)} %get-tuple-element.308, bf16[64,64,128]{2,1,0:T(8,128)(2,1)S(1)} %reshape.96, s32[64]{0:T(128)S(1)} %get-tuple-element.306, ...), kind=kOutput, calls=%fused_computation.2.clone.1 | convolution fusion | flops 144687104 | bytes 4391424 | tf_op jit(solution)/shard_map/while/body/eval_jaxpr/cri,crm->rim/dot_general | solution.py:61
  427.0 5.1 %fusion.117 = (f32[64,128]{1,0:T(8,128)S(1)}, f32[64,128]{1,0:T(8,128)S(1)}, bf16[64,128,128]{1,2,0:T(8,128)(2,1)}) fusion(f32[128,128]{0,1:T(8,128)S(1)} %get-tuple-element.268, bf16[64,64,128]{2,0,1:T(8,128)(2,1)} %get-tuple-element.308, bf16[64,64,128]{2,1,0:T(8,128)(2,1)S(1)} %reshape.96, s32[64]{0:T(128)S(1)} %get-tuple-element.306, ...), kind=kOutput, calls=%fused_computation.2.clone.1 | convolution fusion | flops 144687104 | bytes 4391424 | tf_op jit(solution)/shard_map/while/body/eval_jaxpr/cri,crm->rim/dot_general | solution.py:61
  437.2 5.9 %all-to-all-start.2 = ((f32[8,8,128]{2,0,1:T(8,128)}), f32[8,8,128]{2,0,1:T(8,128)S(1)}, u32[]{:S(2)}, u32[]{:S(2)}) async-start(f32[8,8,128]{2,0,1:T(8,128)} %copy.86), calls=%async_computation.2 | async-start | bytes 65536 | tf_op jit(solution)/shard_map/all_to_all | solution.py:125
  451.1 5.1 %all-to-all-start.1 = ((bf16[8,2,32768]{2,1,0:T(2,128)(2,1)}), bf16[8,2,32768]{2,1,0:T(2,128)(2,1)S(1)}, u32[]{:S(2)}, u32[]{:S(2)}) async-start(bf16[8,2,32768]{2,1,0:T(2,128)(2,1)} %reshape.93), calls=%async_computation.1 | async-start | bytes 2097152 | tf_op jit(solution)/shard_map/all_to_all | solution.py:124
  456.2 26.6 %all-to-all-done.1 = bf16[8,2,32768]{2,1,0:T(2,128)(2,1)S(1)} async-done(((bf16[8,2,32768]{2,1,0:T(2,128)(2,1)}), bf16[8,2,32768]{2,1,0:T(2,128)(2,1)S(1)}, u32[]{:S(2)}, u32[]{:S(2)}) %all-to-all-start.1) | async-done | bytes 1048608 | tf_op jit(solution)/shard_map/all_to_all | solution.py:124
  (263 shorter events, 174.6 us)
Async XLA Ops:
  0.6 9.9 %copy-start.7 = (bf16[2,64,64,128]{3,2,1,0:T(8,128)(2,1)S(1)}, bf16[2,64,64,128]{3,2,1,0:T(8,128)(2,1)}, u32[]{:S(2)}) copy-start(bf16[2,64,64,128]{3,2,1,0:T(8,128)(2,1)} %param.6) | copy-start | bytes 6291460
  0.6 9.9 %copy-start.13 = (bf16[9,64,64]{2,1,0:T(8,128)(2,1)S(1)}, bf16[9,64,64]{2,1,0:T(8,128)(2,1)}, u32[]{:S(2)}) copy-start(bf16[9,64,64]{2,1,0:T(8,128)(2,1)} %param.7) | copy-start | bytes 221188
  3.7 12.0 %copy-start.10 = (bf16[2,64,64,128]{3,1,2,0:T(8,128)(2,1)}, bf16[2,64,64,128]{3,1,2,0:T(8,128)(2,1)S(1)}, u32[]{:S(2)}) copy-start(bf16[2,64,64,128]{3,1,2,0:T(8,128)(2,1)S(1)} %copy.65) | copy-start | bytes 6291460
  3.8 10.4 %collective-permute-start = (bf16[2,64,2,128]{3,1,2,0:T(8,128)(2,1)S(1)}, bf16[2,64,2,128]{3,1,2,0:T(8,128)(2,1)S(1)}, u32[]{:S(2)}, u32[]{:S(2)}) collective-permute-start(bf16[2,64,2,128]{3,1,2,0:T(8,128)(2,1)S(1)} %get-tuple-element.206), channel_id=1, source_target_pairs={{0,8},{8,16},{16,24},{1,9},{9,17},{17,25},{2,10},{10,18},{18,26},{... | collective-permute-start | bytes 196616 | tf_op jit(solution)/shard_map/ppermute | solution.py:21
  7.2 8.5 %collective-permute-start.1 = (bf16[2,64,2,128]{3,1,2,0:T(8,128)(2,1)S(1)}, bf16[2,64,2,128]{3,1,2,0:T(8,128)(2,1)S(1)}, u32[]{:S(2)}, u32[]{:S(2)}) collective-permute-start(bf16[2,64,2,128]{3,1,2,0:T(8,128)(2,1)S(1)} %get-tuple-element.207), channel_id=1, source_target_pairs={{8,0},{16,8},{24,16},{9,1},{17,9},{25,17},{10,2},{18,10},{26,18},{... | collective-permute-start | bytes 196616 | tf_op jit(solution)/shard_map/ppermute | solution.py:24
  22.7 28.0 %collective-permute-start.3 = (bf16[2,64,68,2]{2,1,3,0:T(8,128)(2,1)S(1)}, bf16[2,64,68,2]{2,1,3,0:T(8,128)(2,1)S(1)}, u32[]{:S(2)}, u32[]{:S(2)}) collective-permute-start(bf16[2,64,68,2]{2,1,3,0:T(8,128)(2,1)S(1)} %copy.72), channel_id=1, source_target_pairs={{1,0},{2,1},{3,2},{4,3},{5,4},{6,5},{7,6},{9,8},{10,9},{11,10},{12... | collective-permute-start | bytes 104456 | tf_op jit(solution)/shard_map/ppermute | solution.py:24
  27.7 7.5 %copy-start.11 = (bf16[2,64,64,128]{3,1,2,0:T(8,128)(2,1)S(1)}, bf16[2,64,64,128]{3,1,2,0:T(8,128)(2,1)}, u32[]{:S(2)}) copy-start(bf16[2,64,64,128]{3,1,2,0:T(8,128)(2,1)} %copy-done.10) | copy-start | bytes 6291460
  27.7 10.1 %collective-permute-start.2 = (bf16[2,64,68,2]{2,1,3,0:T(8,128)(2,1)S(1)}, bf16[2,64,68,2]{2,1,3,0:T(8,128)(2,1)S(1)}, u32[]{:S(2)}, u32[]{:S(2)}) collective-permute-start(bf16[2,64,68,2]{2,1,3,0:T(8,128)(2,1)S(1)} %copy.69), channel_id=1, source_target_pairs={{0,1},{1,2},{2,3},{3,4},{4,5},{5,6},{6,7},{8,9},{9,10},{10,11},{11... | collective-permute-start | bytes 104456 | tf_op jit(solution)/shard_map/ppermute | solution.py:21
  42.7 4.9 copy-start.5
  55.2 5.3 %copy-start.4 = (bf16[2,64,68,2]{3,1,2,0:T(8,128)(2,1)S(1)}, bf16[2,64,68,2]{3,1,2,0:T(8,128)(2,1)}, u32[]{:S(2)}) copy-start(bf16[2,64,68,2]{3,1,2,0:T(8,128)(2,1)} %copy.73) | copy-start | bytes 104452
  60.5 3.5 copy-start.6
  67.1 31.5 %copy-start.14 = (bf16[9,64,64]{2,1,0:T(8,128)(2,1)S(1)}, bf16[9,64,64]{2,1,0:T(8,128)(2,1)}, u32[]{:S(2)}) copy-start(bf16[9,64,64]{2,1,0:T(8,128)(2,1)} %param.8) | copy-start | bytes 221188
  79.7 22.0 %copy-start = (bf16[2,64,64,128]{3,1,2,0:T(8,128)(2,1)}, bf16[2,64,64,128]{3,1,2,0:T(8,128)(2,1)S(1)}, u32[]{:S(2)}) copy-start(bf16[2,64,64,128]{3,1,2,0:T(8,128)(2,1)S(1)} %fusion.11) | copy-start | bytes 6291460
  79.7 21.6 %collective-permute-start.4 = (bf16[2,64,4,128]{3,1,2,0:T(8,128)(2,1)S(1)}, bf16[2,64,4,128]{3,1,2,0:T(8,128)(2,1)S(1)}, u32[]{:S(2)}, u32[]{:S(2)}) collective-permute-start(bf16[2,64,4,128]{3,1,2,0:T(8,128)(2,1)S(1)} %get-tuple-element.204), channel_id=1, source_target_pairs={{0,8},{8,16},{16,24},{1,9},{9,17},{17,25},{2,10},{10,18},{18,26},{... | collective-permute-start | bytes 393224 | tf_op jit(solution)/shard_map/ppermute | solution.py:21
  82.2 19.1 %collective-permute-start.5 = (bf16[2,64,4,128]{3,1,2,0:T(8,128)(2,1)S(1)}, bf16[2,64,4,128]{3,1,2,0:T(8,128)(2,1)S(1)}, u32[]{:S(2)}, u32[]{:S(2)}) collective-permute-start(bf16[2,64,4,128]{3,1,2,0:T(8,128)(2,1)S(1)} %get-tuple-element.205), channel_id=1, source_target_pairs={{8,0},{16,8},{24,16},{9,1},{17,9},{25,17},{10,2},{18,10},{26,18},{... | collective-permute-start | bytes 393224 | tf_op jit(solution)/shard_map/ppermute | solution.py:24
  105.0 12.1 %copy-start.1 = (bf16[2,64,64,128]{3,1,2,0:T(8,128)(2,1)S(1)}, bf16[2,64,64,128]{3,1,2,0:T(8,128)(2,1)}, u32[]{:S(2)}) copy-start(bf16[2,64,64,128]{3,1,2,0:T(8,128)(2,1)} %copy-done) | copy-start | bytes 6291460
  109.2 13.3 %collective-permute-start.6 = (bf16[2,64,72,4]{2,1,3,0:T(8,128)(2,1)S(1)}, bf16[2,64,72,4]{2,1,3,0:T(8,128)(2,1)S(1)}, u32[]{:S(2)}, u32[]{:S(2)}) collective-permute-start(bf16[2,64,72,4]{2,1,3,0:T(8,128)(2,1)S(1)} %copy.76), channel_id=1, source_target_pairs={{0,1},{1,2},{2,3},{3,4},{4,5},{5,6},{6,7},{8,9},{9,10},{10,11},{11... | collective-permute-start | bytes 221192 | tf_op jit(solution)/shard_map/ppermute | solution.py:21
  115.8 11.4 %collective-permute-start.7 = (bf16[2,64,72,4]{2,1,3,0:T(8,128)(2,1)S(1)}, bf16[2,64,72,4]{2,1,3,0:T(8,128)(2,1)S(1)}, u32[]{:S(2)}, u32[]{:S(2)}) collective-permute-start(bf16[2,64,72,4]{2,1,3,0:T(8,128)(2,1)S(1)} %copy.78), channel_id=1, source_target_pairs={{1,0},{2,1},{3,2},{4,3},{5,4},{6,5},{7,6},{9,8},{10,9},{11,10},{12... | collective-permute-start | bytes 221192 | tf_op jit(solution)/shard_map/ppermute | solution.py:24
  137.9 8.8 %copy-start.9 = (bf16[2,64,72,132]{3,1,2,0:T(8,128)(2,1)}, bf16[2,64,72,132]{3,1,2,0:T(8,128)(2,1)S(1)}, u32[]{:S(2)}) copy-start(bf16[2,64,72,132]{3,1,2,0:T(8,128)(2,1)S(1)} %get-tuple-element.196) | copy-start | bytes 7299076
  149.5 2.8 copy-start.8
  149.5 4.3 copy-start.12
  171.1 8.2 %copy-start.15 = (s32[2,8,1]{1,2,0:T(1,128)S(1)}, s32[2,8,1]{1,2,0:T(1,128)}, u32[]{:S(2)}) copy-start(s32[2,8,1]{1,2,0:T(1,128)} %param.9) | copy-start | bytes 196
  172.7 55.7 %all-to-all-start = ((bf16[2,64,64,128]{3,1,0,2:T(8,128)(2,1)}), bf16[2,64,64,128]{3,1,0,2:T(8,128)(2,1)S(1)}, u32[]{:S(2)}, u32[]{:S(2)}) async-start(bf16[2,64,64,128]{3,1,0,2:T(8,128)(2,1)} %copy.80), calls=%async_computation | async-start | bytes 4194304 | tf_op jit(solution)/shard_map/all_to_all | solution.py:93
  234.0 5.2 %copy-start.2 = (f32[64,64,128]{2,0,1:T(8,128)S(1)}, f32[64,64,128]{2,0,1:T(8,128)}, u32[]{:S(2)}) copy-start(f32[64,64,128]{2,0,1:T(8,128)} %get-tuple-element.291) | copy-start | bytes 6291460 | tf_op jit(solution)/shard_map/while
  242.2 1.3 copy-start.3
  245.4 5.2 %copy-start.2 = (f32[64,64,128]{2,0,1:T(8,128)S(1)}, f32[64,64,128]{2,0,1:T(8,128)}, u32[]{:S(2)}) copy-start(f32[64,64,128]{2,0,1:T(8,128)} %get-tuple-element.291) | copy-start | bytes 6291460 | tf_op jit(solution)/shard_map/while
  253.6 1.3 copy-start.3
  256.7 5.2 %copy-start.2 = (f32[64,64,128]{2,0,1:T(8,128)S(1)}, f32[64,64,128]{2,0,1:T(8,128)}, u32[]{:S(2)}) copy-start(f32[64,64,128]{2,0,1:T(8,128)} %get-tuple-element.291) | copy-start | bytes 6291460 | tf_op jit(solution)/shard_map/while
  264.9 1.3 copy-start.3
  268.1 5.2 %copy-start.2 = (f32[64,64,128]{2,0,1:T(8,128)S(1)}, f32[64,64,128]{2,0,1:T(8,128)}, u32[]{:S(2)}) copy-start(f32[64,64,128]{2,0,1:T(8,128)} %get-tuple-element.291) | copy-start | bytes 6291460 | tf_op jit(solution)/shard_map/while
  276.3 1.3 copy-start.3
  279.4 5.2 %copy-start.2 = (f32[64,64,128]{2,0,1:T(8,128)S(1)}, f32[64,64,128]{2,0,1:T(8,128)}, u32[]{:S(2)}) copy-start(f32[64,64,128]{2,0,1:T(8,128)} %get-tuple-element.291) | copy-start | bytes 6291460 | tf_op jit(solution)/shard_map/while
  287.6 1.3 copy-start.3
  290.8 5.2 %copy-start.2 = (f32[64,64,128]{2,0,1:T(8,128)S(1)}, f32[64,64,128]{2,0,1:T(8,128)}, u32[]{:S(2)}) copy-start(f32[64,64,128]{2,0,1:T(8,128)} %get-tuple-element.291) | copy-start | bytes 6291460 | tf_op jit(solution)/shard_map/while
  302.1 5.2 %copy-start.2 = (f32[64,64,128]{2,0,1:T(8,128)S(1)}, f32[64,64,128]{2,0,1:T(8,128)}, u32[]{:S(2)}) copy-start(f32[64,64,128]{2,0,1:T(8,128)} %get-tuple-element.291) | copy-start | bytes 6291460 | tf_op jit(solution)/shard_map/while
  313.5 5.2 %copy-start.2 = (f32[64,64,128]{2,0,1:T(8,128)S(1)}, f32[64,64,128]{2,0,1:T(8,128)}, u32[]{:S(2)}) copy-start(f32[64,64,128]{2,0,1:T(8,128)} %get-tuple-element.291) | copy-start | bytes 6291460 | tf_op jit(solution)/shard_map/while
  324.9 5.2 %copy-start.2 = (f32[64,64,128]{2,0,1:T(8,128)S(1)}, f32[64,64,128]{2,0,1:T(8,128)}, u32[]{:S(2)}) copy-start(f32[64,64,128]{2,0,1:T(8,128)} %get-tuple-element.291) | copy-start | bytes 6291460 | tf_op jit(solution)/shard_map/while
  336.2 5.2 %copy-start.2 = (f32[64,64,128]{2,0,1:T(8,128)S(1)}, f32[64,64,128]{2,0,1:T(8,128)}, u32[]{:S(2)}) copy-start(f32[64,64,128]{2,0,1:T(8,128)} %get-tuple-element.291) | copy-start | bytes 6291460 | tf_op jit(solution)/shard_map/while
  347.6 5.2 %copy-start.2 = (f32[64,64,128]{2,0,1:T(8,128)S(1)}, f32[64,64,128]{2,0,1:T(8,128)}, u32[]{:S(2)}) copy-start(f32[64,64,128]{2,0,1:T(8,128)} %get-tuple-element.291) | copy-start | bytes 6291460 | tf_op jit(solution)/shard_map/while
  358.9 5.2 %copy-start.2 = (f32[64,64,128]{2,0,1:T(8,128)S(1)}, f32[64,64,128]{2,0,1:T(8,128)}, u32[]{:S(2)}) copy-start(f32[64,64,128]{2,0,1:T(8,128)} %get-tuple-element.291) | copy-start | bytes 6291460 | tf_op jit(solution)/shard_map/while
  370.3 5.2 %copy-start.2 = (f32[64,64,128]{2,0,1:T(8,128)S(1)}, f32[64,64,128]{2,0,1:T(8,128)}, u32[]{:S(2)}) copy-start(f32[64,64,128]{2,0,1:T(8,128)} %get-tuple-element.291) | copy-start | bytes 6291460 | tf_op jit(solution)/shard_map/while
  381.6 5.2 %copy-start.2 = (f32[64,64,128]{2,0,1:T(8,128)S(1)}, f32[64,64,128]{2,0,1:T(8,128)}, u32[]{:S(2)}) copy-start(f32[64,64,128]{2,0,1:T(8,128)} %get-tuple-element.291) | copy-start | bytes 6291460 | tf_op jit(solution)/shard_map/while
  393.0 5.2 %copy-start.2 = (f32[64,64,128]{2,0,1:T(8,128)S(1)}, f32[64,64,128]{2,0,1:T(8,128)}, u32[]{:S(2)}) copy-start(f32[64,64,128]{2,0,1:T(8,128)} %get-tuple-element.291) | copy-start | bytes 6291460 | tf_op jit(solution)/shard_map/while
  404.3 5.2 %copy-start.2 = (f32[64,64,128]{2,0,1:T(8,128)S(1)}, f32[64,64,128]{2,0,1:T(8,128)}, u32[]{:S(2)}) copy-start(f32[64,64,128]{2,0,1:T(8,128)} %get-tuple-element.291) | copy-start | bytes 6291460 | tf_op jit(solution)/shard_map/while
  415.7 5.2 %copy-start.2 = (f32[64,64,128]{2,0,1:T(8,128)S(1)}, f32[64,64,128]{2,0,1:T(8,128)}, u32[]{:S(2)}) copy-start(f32[64,64,128]{2,0,1:T(8,128)} %get-tuple-element.291) | copy-start | bytes 6291460 | tf_op jit(solution)/shard_map/while
  427.0 5.2 %copy-start.2 = (f32[64,64,128]{2,0,1:T(8,128)S(1)}, f32[64,64,128]{2,0,1:T(8,128)}, u32[]{:S(2)}) copy-start(f32[64,64,128]{2,0,1:T(8,128)} %get-tuple-element.291) | copy-start | bytes 6291460 | tf_op jit(solution)/shard_map/while
  437.2 13.9 %all-to-all-start.2 = ((f32[8,8,128]{2,0,1:T(8,128)}), f32[8,8,128]{2,0,1:T(8,128)S(1)}, u32[]{:S(2)}, u32[]{:S(2)}) async-start(f32[8,8,128]{2,0,1:T(8,128)} %copy.86), calls=%async_computation.2 | async-start | bytes 65536 | tf_op jit(solution)/shard_map/all_to_all | solution.py:125
  451.1 31.7 %all-to-all-start.1 = ((bf16[8,2,32768]{2,1,0:T(2,128)(2,1)}), bf16[8,2,32768]{2,1,0:T(2,128)(2,1)S(1)}, u32[]{:S(2)}, u32[]{:S(2)}) async-start(bf16[8,2,32768]{2,1,0:T(2,128)(2,1)} %reshape.93), calls=%async_computation.1 | async-start | bytes 2097152 | tf_op jit(solution)/shard_map/all_to_all | solution.py:124
  (13 other events, 17.4 us)
where the time goes:
time: 497 us; the launch traced here: 488 us
  matrix products  227 us (46%)
  local copies, waits for them, and re-layouts  120 us (24%)
  starting transfers between devices  51.6 us (10%)
  blocking collectives  41.5 us (8%)
  waiting for transfers between devices  33.9 us (7%)
  other arithmetic  11 us (2%)
    dot_general x18, matrix products, hop_terms(): jnp.einsum('cri,crm->rim', source_descriptors, key_feats, preferred_eleme...  92.6 us
    dot_general x18, matrix products, convolution_layer(): jnp.einsum('oc,nchw->nohw', weights[3 * row_tap + horizontal_offset], win...  80.5 us
    dot_general x18, matrix products, hop_terms(): jnp.einsum('rim,crm->cri', rounded, key_feats, preferred_element_type=jnp...  54.3 us
    all_gather x1, blocking collectives, per_device(): gathered = lax.all_gather(search_ranges, 'cols', axis=2, tiled=True)  41.5 us
    all_to_all x1, waiting for transfers between devices, per_device(): lax.all_to_all(matched_rows, 'cols', split_axis=2, concat_axis=1, tiled=T...  26.6 us
    while x72, local copies, waits for them, and re-layouts  23.5 us
    dynamic_slice x18, local copies, waits for them, and re-layouts, accumulate(): lax.dynamic_slice_in_dim(padded, (HOPS - 1 - hop_index) * segment, full_w...  23.3 us
    ppermute x4, starting transfers between devices, with_halo(): lax.ppermute(lax.slice_in_dim(block, 0, width, axis=dim), axis, backward)  22.3 us
  transfers between devices with their start and end apart: 11, of which 2 were waited for; matrix products, arithmetic and copies ran while one was open for 11% of the time, Pallas kernels for 0%

commit v1 on v0

v1 whole, which is shorter than its diff:
```python
import functools

import jax
import jax.numpy as jnp
from jax import lax
from jax.experimental import pallas as pl
from jax.experimental.pallas import tpu as pltpu
from jax.sharding import PartitionSpec as P

RG = 8
FIRST_DILATION = 2
SECOND_DILATION = 4
HOPS = 18
REACH = FIRST_DILATION + SECOND_DILATION
SLOT = 16

sharpness_divisor = 10.0
epsilon = 1e-05
LOG2E = 1.4426950408889634


def lane_iota(shape):
    return lax.broadcasted_iota(jnp.int32, shape, len(shape) - 1)


def pack_kernel(top_ref, mid_ref, bottom_ref, edge_ref, *, groups, spacing):
    channels, segment = mid_ref.shape[1:]
    rows = mid_ref.shape[0]
    slot_of = lane_iota((channels, segment)) // SLOT
    steps = edge_ref.shape[0]
    for q in range(steps):
        packed = jnp.zeros((channels, segment), jnp.float32)
        for g in range(groups):
            row = g * spacing + q
            if row < REACH:
                source = top_ref[row]
            elif row < REACH + rows:
                source = mid_ref[row - REACH]
            else:
                source = bottom_ref[row - REACH - rows]
            shift = (SLOT * g + SLOT // 2) % segment
            packed = jnp.where(slot_of == g, pltpu.roll(source.astype(jnp.float32), shift, 1), packed)
        edge_ref[q] = packed.astype(jnp.bfloat16)


def pack_edges(top, mid, bottom):
    images, rows, channels, segment = mid.shape
    groups = segment // SLOT
    spacing = (rows + 2 * SECOND_DILATION) // groups
    steps = spacing + 2 * FIRST_DILATION
    return pl.pallas_call(
        functools.partial(pack_kernel, groups=groups, spacing=spacing),
        out_shape=jax.ShapeDtypeStruct((images, steps, channels, segment), jnp.bfloat16),
        grid=(images,),
        in_specs=[
            pl.BlockSpec((None, REACH, channels, segment), lambda n: (n, 0, 0, 0)),
            pl.BlockSpec((None, rows, channels, segment), lambda n: (n, 0, 0, 0)),
            pl.BlockSpec((None, REACH, channels, segment), lambda n: (n, 0, 0, 0)),
        ],
        out_specs=pl.BlockSpec((None, steps, channels, segment), lambda n: (n, 0, 0, 0)),
        name="pack_edges",
    )(top, mid, bottom)


def feature_kernel(
    place_ref, top_ref, mid_ref, bottom_ref, own_ref, partner_ref, cross_ref, w1_ref, w2_ref, unit_ref,
    x_ref, edge_ref, p1_ref, p1e_ref, hid_ref, hide_ref, p2_ref, rhs_ref, *, spacing,
):
    rows, channels, segment = mid_ref.shape
    first_row, last_row, first_col, last_col, odd = (place_ref[i] for i in range(5))
    d1, d2 = FIRST_DILATION, SECOND_DILATION
    all_rows = rows + 2 * REACH
    hidden_rows = rows + 2 * d2
    steps = edge_ref.shape[0]
    groups = segment // SLOT
    lanes = lane_iota((channels, segment))
    in_slot = lanes % SLOT
    half = SLOT // 2

    x_ref[0:REACH] = top_ref[...]
    x_ref[REACH : REACH + rows] = mid_ref[...]
    x_ref[REACH + rows :] = bottom_ref[...]

    for q in range(steps):
        own = own_ref[q].astype(jnp.float32)
        partner = partner_ref[q].astype(jnp.float32)
        cross = cross_ref[q].astype(jnp.float32)
        left = jnp.where(odd == 1, partner, cross)
        right = jnp.where(odd == 1, cross, partner)
        shift = half - REACH
        lower = pltpu.roll(jnp.where(in_slot < half, left, own), segment - shift, 1)
        upper = pltpu.roll(jnp.where(in_slot < half, own, right), shift, 1)
        edge_ref[q] = jnp.where(in_slot < half, lower, upper).astype(jnp.bfloat16)

    def shifted(main, edge, slot, amount):
        main = main.astype(jnp.float32)
        edge = edge.astype(jnp.float32)
        low_from = slot * SLOT + REACH - amount
        high_from = slot * SLOT + half + 2
        before = jnp.where(
            lanes < amount,
            pltpu.roll(edge, lax.rem(segment - low_from, segment), 1),
            pltpu.roll(main, amount, 1),
        )
        after = jnp.where(
            lanes >= segment - amount,
            pltpu.roll(edge, lax.rem(2 * segment - amount - high_from, segment), 1),
            pltpu.roll(main, segment - amount, 1),
        )
        return before.astype(jnp.bfloat16), after.astype(jnp.bfloat16)

    def place(slot_index, main, before, after):
        lo = slot_index * segment
        rhs_ref[0:channels, lo : lo + segment] = before
        rhs_ref[channels : 2 * channels, lo : lo + segment] = main
        rhs_ref[2 * channels :, lo : lo + segment] = after

    def slot_and_step(row):
        slot = jnp.minimum(row // spacing, groups - 1)
        return slot, row - slot * spacing

    def conv(source_ref, sides_ref, weight_ref, product_ref, total, amount, width):
        def body(t, _):
            for j in range(width):
                row = t * width + j
                slot, step = slot_and_step(row)
                main = source_ref[row]
                before, after = shifted(main, sides_ref[step], slot, amount)
                place(j, main, before, after)
            product = jnp.dot(
                weight_ref[...], rhs_ref[:, : width * segment], preferred_element_type=jnp.float32
            )
            for j in range(width):
                product_ref[t * width + j] = product[:, j * segment : (j + 1) * segment]
            return 0

        lax.fori_loop(0, total // width, body, 0)

    conv(x_ref, edge_ref, w1_ref, p1_ref, all_rows, d1, 4)

    for q in range(steps):
        main = edge_ref[q]
        wide = main.astype(jnp.float32)
        place(
            0, main, pltpu.roll(wide, d1, 1).astype(jnp.bfloat16),
            pltpu.roll(wide, segment - d1, 1).astype(jnp.bfloat16),
        )
        p1e_ref[q] = jnp.dot(w1_ref[...], rhs_ref[:, :segment], preferred_element_type=jnp.float32)

    def three(product_ref, row, apart):
        return (
            product_ref[row, 0:channels]
            + product_ref[row + apart, channels : 2 * channels]
            + product_ref[row + 2 * apart, 2 * channels :]
        )

    def silu(v):
        return v / (1.0 + jnp.exp(-v))

    def hidden(t, _):
        for j in range(4):
            row = 4 * t + j
            outside = ((row < d2) & (first_row == 1)) | ((row >= d2 + rows) & (last_row == 1))
            value = silu(three(p1_ref, row, d1))
            hid_ref[row] = jnp.where(outside, 0.0, value).astype(jnp.bfloat16)
        return 0

    lax.fori_loop(0, hidden_rows // 4, hidden, 0)

    left_out = (in_slot < REACH) & (first_col == 1)
    right_out = (in_slot >= half + 2) & (last_col == 1)
    for q in range(spacing):
        row = (lanes // SLOT) * spacing + q
        outside = ((row < d2) & (first_row == 1)) | ((row >= d2 + rows) & (last_row == 1)) | left_out | right_out
        value = silu(three(p1e_ref, q, d1))
        hide_ref[q] = jnp.where(outside, 0.0, value).astype(jnp.bfloat16)

    conv(hid_ref, hide_ref, w2_ref, p2_ref, hidden_rows, d2, 4)

    def finish(t, _):
        for j in range(4):
            row = 4 * t + j
            total = x_ref[row + REACH].astype(jnp.float32) + three(p2_ref, row, d2)
            feature = total.astype(jnp.bfloat16).astype(jnp.float32)
            mean = jnp.sum(feature * feature, axis=0, keepdims=True) * (1.0 / channels)
            unit_ref[row] = (feature * lax.rsqrt(mean + epsilon)).astype(jnp.bfloat16)
        return 0

    lax.fori_loop(0, rows // 4, finish, 0)


def unit_features(index, place, top, mid, bottom, own, partner, cross, w1, w2):
    _, rows, channels, segment = mid.shape
    steps = own.shape[1]
    spacing = steps - 2 * FIRST_DILATION
    hidden_rows = rows + 2 * SECOND_DILATION
    all_rows = rows + 2 * REACH

    def image_of(a):
        return pl.BlockSpec((None,) + a.shape[1:], lambda i: (index, 0, 0, 0))

    def whole(a):
        return pl.BlockSpec(a.shape, lambda i: (0,) * a.ndim)

    return pl.pallas_call(
        functools.partial(feature_kernel, spacing=spacing),
        out_shape=jax.ShapeDtypeStruct((rows, channels, segment), jnp.bfloat16),
        grid=(1,),
        in_specs=[pl.BlockSpec(memory_space=pltpu.SMEM)]
        + [image_of(a) for a in (top, mid, bottom, own, partner, cross)]
        + [whole(w1), whole(w2)],
        out_specs=pl.BlockSpec((rows, channels, segment), lambda i: (0, 0, 0)),
        scratch_shapes=[
            pltpu.VMEM((all_rows, channels, segment), jnp.bfloat16),
            pltpu.VMEM((steps, channels, segment), jnp.bfloat16),
            pltpu.VMEM((all_rows, 3 * channels, segment), jnp.float32),
            pltpu.VMEM((steps, 3 * channels, segment), jnp.float32),
            pltpu.VMEM((hidden_rows, channels, segment), jnp.bfloat16),
            pltpu.VMEM((spacing, channels, segment), jnp.bfloat16),
            pltpu.VMEM((hidden_rows, 3 * channels, segment), jnp.float32),
            pltpu.VMEM((3 * channels, 4 * segment), jnp.bfloat16),
        ],
        name=f"unit_features_{index}",
    )(place, top, mid, bottom, own, partner, cross, w1, w2)


def correlate_kernel(
    table_ref, left_ref, even_ref, odd_ref, acc_in_ref, acc_ref, bias_ref, *, step, scale
):
    group = pl.program_id(0)
    rows, channels, segment = left_ref.shape
    block = table_ref[0, 0]
    low = segment * table_ref[1, group]
    high = low + segment * table_ref[2, group]
    base = segment * (block - 2 * (block // 2 - step))
    active = (base + segment - 1 >= low) & (base - 2 * segment + 1 < high) & (block // 2 >= step)
    if step == 0:
        acc_ref[...] = jnp.zeros_like(acc_ref)
    else:
        acc_ref[...] = acc_in_ref[...]

    @pl.when(active)
    def _():
        wide = (segment, 2 * segment)
        offsets = base + lax.broadcasted_iota(jnp.int32, wide, 0) - lax.broadcasted_iota(jnp.int32, wide, 1)
        inside = (offsets >= low) & (offsets < high)
        bias_ref[...] = jnp.where(inside, 0.0, -1e30)
        kind = lax.broadcasted_iota(jnp.int32, (16, 2 * segment), 0)
        column = lax.broadcasted_iota(jnp.int32, (16, 2 * segment), 1)
        extra = jnp.where(kind == 0, 1, jnp.where(kind == 1, column, jnp.where(kind == 2, step, 0)))
        extra = extra.astype(jnp.float32).astype(jnp.bfloat16)
        for r in range(rows):
            keys = jnp.concatenate([even_ref[r], odd_ref[r]], axis=1)
            scores = lax.dot_general(
                left_ref[r], keys, (((0,), (0,)), ((), ())), preferred_element_type=jnp.float32
            )
            weights = jnp.exp2(scores * scale + bias_ref[...]).astype(jnp.bfloat16)
            extended = jnp.concatenate([keys, extra], axis=0)
            acc_ref[r, :, 0 : channels + 16] += lax.dot_general(
                weights, extended, (((1,), (1,)), ((), ())), preferred_element_type=jnp.float32
            )


def correlate(table, left, even, odd, acc, step):
    rows, channels, segment = left.shape
    scale = sharpness_divisor / channels * LOG2E
    acc_spec = pl.BlockSpec((RG, segment, 128), lambda g: (g, 0, 0))
    row_spec = pl.BlockSpec((RG, channels, segment), lambda g: (g, 0, 0))
    first = acc is None
    if first:
        acc = jnp.zeros((8, 128), jnp.float32)
    return pl.pallas_call(
        functools.partial(correlate_kernel, step=step, scale=scale),
        out_shape=jax.ShapeDtypeStruct((rows, segment, 128), jnp.float32),
        grid=(rows // RG,),
        in_specs=[
            pl.BlockSpec(memory_space=pltpu.SMEM),
            row_spec,
            row_spec,
            row_spec,
            pl.BlockSpec((8, 128), lambda g: (0, 0)) if first else acc_spec,
        ],
        out_specs=acc_spec,
        scratch_shapes=[pltpu.VMEM((segment, 2 * segment), jnp.float32)],
        input_output_aliases={} if first else {4: 0},
        name=f"correlate_{step}",
    )(table, left, even, odd, acc)


def finish_kernel(table_ref, acc_ref, matched_ref, disparity_ref, *, channels):
    group = pl.program_id(0)
    rows, segment, _ = acc_ref.shape
    block = table_ref[0, 0]
    low = segment * table_ref[1, group]
    high = low + segment * table_ref[2, group]
    x = block * segment + lax.broadcasted_iota(jnp.int32, (1, segment), 1)
    start = jnp.maximum(low, x + 1)
    beyond = jnp.maximum(high - start, 0)
    beyond_sum = ((start + high - 1) * beyond).astype(jnp.float32) * 0.5
    beyond = beyond.astype(jnp.float32)
    xf = x.astype(jnp.float32)
    chip = (block // 2).astype(jnp.float32)
    for r in range(rows):
        turned = acc_ref[r].T
        near = turned[channels : channels + 1]
        column = turned[channels + 1 : channels + 2]
        steps = turned[channels + 2 : channels + 3]
        norm = near + beyond
        shift = (xf - 2 * segment * chip) * near - column + (2 * segment) * steps + beyond_sum
        matched_ref[r] = (turned[:channels] / norm).astype(jnp.bfloat16)
        disparity_ref[r : r + 1, :] = shift / norm * (1.0 / segment)


def finish(table, acc, channels):
    rows, segment, _ = acc.shape
    return pl.pallas_call(
        functools.partial(finish_kernel, channels=channels),
        out_shape=(
            jax.ShapeDtypeStruct((rows, channels, segment), jnp.bfloat16),
            jax.ShapeDtypeStruct((rows, segment), jnp.float32),
        ),
        grid=(rows // RG,),
        in_specs=[
            pl.BlockSpec(memory_space=pltpu.SMEM),
            pl.BlockSpec((RG, segment, 128), lambda g: (g, 0, 0)),
        ],
        out_specs=(
            pl.BlockSpec((RG, channels, segment), lambda g: (g, 0, 0)),
            pl.BlockSpec((RG, segment), lambda g: (g, 0)),
        ),
        name="finish",
    )(table, acc)


def both_ways(pairs):
    return pairs + [(b, a) for a, b in pairs]


def stacked(weight):
    taps, out_channels, in_channels = weight.shape
    split = weight.reshape(3, 3, out_channels, in_channels).transpose(0, 2, 1, 3)
    return split.reshape(3 * out_channels, 3 * in_channels)


def per_device(images, first_weight, second_weight, search_ranges):
    row_count = lax.axis_size("rows")
    col_count = lax.axis_size("cols")
    row = lax.axis_index("rows")
    col = lax.axis_index("cols")
    rows = images.shape[2]
    segment = images.shape[3]
    channels = images.shape[1]
    odd = col % 2

    mid = images.transpose(0, 2, 1, 3)
    top_rows = mid[:, :REACH]
    bottom_rows = mid[:, rows - REACH :]
    up = [(i, i + 1) for i in range(row_count - 1)]
    top = lax.ppermute(bottom_rows, "rows", up)
    bottom = lax.ppermute(top_rows, "rows", [(b, a) for a, b in up])
    own = pack_edges(top, mid, bottom)
    partner = lax.ppermute(own, "cols", [(i, i ^ 1) for i in range(col_count)])
    cross = lax.ppermute(own, "cols", both_ways([(i, i + 1) for i in range(1, col_count - 1, 2)]))
    place = jnp.stack(
        [row == 0, row == row_count - 1, col == 0, col == col_count - 1, odd == 1]
    ).astype(jnp.int32)
    w1, w2 = stacked(first_weight), stacked(second_weight)
    shared = (place, top, mid, bottom, own, partner, cross, w1, w2)
    right = unit_features(1, *shared)

    groups = rows // RG
    table = jnp.concatenate(
        [jnp.full((1, groups), col, jnp.int32), search_ranges.reshape(2, groups)], axis=0
    )
    chips = col_count // 2
    last = min(chips - 1, (HOPS - 1 + 1) // 2)
    swap = [(i, i ^ 1) for i in range(col_count)]
    hop = [(i, i + 2) for i in range(col_count - 2)]

    def pair(mine):
        theirs = lax.ppermute(mine, "cols", swap)
        return jnp.where(odd == 1, theirs, mine), jnp.where(odd == 1, mine, theirs)

    left = unit_features(0, *shared)
    acc = None
    mine = right
    for step in range(last + 1):
        if step:
            mine = lax.ppermute(mine, "cols", hop)
        even_keys, odd_keys = pair(mine)
        acc = correlate(table, left, even_keys, odd_keys, acc, step)
    matched, disparity = finish(table, acc, channels)
    return matched.transpose(1, 0, 2), disparity


def solution(mesh):
    placed = (P(None, None, "rows", "cols"), P(), P(), P(None, "rows", "cols"))
    return jax.shard_map(
        per_device,
        mesh=mesh,
        in_specs=placed,
        out_specs=(P(None, "rows", "cols"), P("rows", "cols")),
        check_vma=False,
    )
```

time: 497 us -> 210 us (0.42)
  the two profiles are of different devices: /device:TPU:4 before, /device:TPU:27 now
where the time goes in v1:
time: 210 us; the launch traced here: 208 us
  Pallas kernels  84 us (40%)
  waiting for transfers between devices  83.5 us (40%)
  starting transfers between devices  16.3 us (8%)
  other arithmetic  11.8 us (6%)
  local copies, waits for them, and re-layouts  11.3 us (5%)
    ppermute x3, waiting for transfers between devices, per_device(): mine = lax.ppermute(mine, 'cols', hop)  75.9 us
    pallas_call x2, Pallas kernels, unit_features(): pl.pallas_call(functools.partial(feature_kernel, spacing=spacing), out_sh...  38.9 us
    pallas_call x4, Pallas kernels, correlate(): pl.pallas_call(functools.partial(correlate_kernel, step=step, scale=scale...  35.5 us
    select_n x4, other arithmetic, pair(): jnp.where(odd == 1, mine, theirs)  11.3 us
    unnamed x20, local copies, waits for them, and re-layouts  8.13 us
    pallas_call x1, Pallas kernels, finish(): pl.pallas_call(functools.partial(finish_kernel, channels=channels), out_s...  6.59 us
    ppermute x1, waiting for transfers between devices, per_device(): bottom = lax.ppermute(top_rows, 'rows', [(b, a) for a, b in up])  5.17 us
    ppermute x4, starting transfers between devices, pair(): theirs = lax.ppermute(mine, 'cols', swap)  4.88 us
  transfers between devices with their start and end apart: 11, of which 5 were waited for; matrix products, arithmetic and copies ran while one was open for 6% of the time, Pallas kernels for 22%

profile of v1, /device:TPU:27, one launch (start us, length us, event | category | flops | bytes accessed | tf_op | source)
XLA Modules:
  0.0 207.7 jit_solution(8955868217976830027)
XLA Ops:
  0.6 3.0 %copy.20 = bf16[2,64,64,128]{3,1,2,0:T(8,128)(2,1)S(1)} copy(bf16[2,64,64,128]{3,2,1,0:T(8,128)(2,1)} %param.4) | data formatting | bytes 4194304 | tf_op args[0]
  3.7 3.1 %collective-permute-start = (bf16[2,6,64,128]{3,2,1,0:T(8,128)(2,1)S(1)}, bf16[2,6,64,128]{3,2,1,0:T(8,128)(2,1)S(1)}, u32[]{:S(2)}, u32[]{:S(2)}) collective-permute-start(bf16[2,6,64,128]{3,2,1,0:T(8,128)(2,1)S(1)} %get-tuple-element.19), channel_id=1, source_target_pairs={{0,8},{8,16},{16,24},{1,9},{9,17},{17,25},{2,10},{10,18},{18,26},{... | collective-permute-start | bytes 589832 | tf_op jit(solution)/shard_map/ppermute | solution.py:359
  6.8 0.0 copy-start.8
  6.8 2.2 %collective-permute-start.1 = (bf16[2,6,64,128]{3,2,1,0:T(8,128)(2,1)S(1)}, bf16[2,6,64,128]{3,2,1,0:T(8,128)(2,1)S(1)}, u32[]{:S(2)}, u32[]{:S(2)}) collective-permute-start(bf16[2,6,64,128]{3,2,1,0:T(8,128)(2,1)S(1)} %get-tuple-element.18), channel_id=1, source_target_pairs={{8,0},{16,8},{24,16},{9,1},{17,9},{25,17},{10,2},{18,10},{26,18},{... | collective-permute-start | bytes 589832 | tf_op jit(solution)/shard_map/ppermute | solution.py:360
  9.0 2.4 %collective-permute-done.top_ref = bf16[2,6,64,128]{3,2,1,0:T(8,128)(2,1)S(1)} collective-permute-done((bf16[2,6,64,128]{3,2,1,0:T(8,128)(2,1)S(1)}, bf16[2,6,64,128]{3,2,1,0:T(8,128)(2,1)S(1)}, u32[]{:S(2)}, u32[]{:S(2)}) %collective-permute-start) | collective-permute-done | bytes 196640 | tf_op jit(solution)/shard_map/ppermute | solution.py:359
  11.4 5.2 %collective-permute-done.1.bottom_ref = bf16[2,6,64,128]{3,2,1,0:T(8,128)(2,1)S(1)} collective-permute-done((bf16[2,6,64,128]{3,2,1,0:T(8,128)(2,1)S(1)}, bf16[2,6,64,128]{3,2,1,0:T(8,128)(2,1)S(1)}, u32[]{:S(2)}, u32[]{:S(2)}) %collective-permute-start.1) | collective-permute-done | bytes 196640 | tf_op jit(solution)/shard_map/ppermute | solution.py:360
  16.5 0.7 copy-done.3
  17.2 3.0 %pack_edges.1.own_ref = bf16[2,13,64,128]{3,2,1,0:T(8,128)(2,1)} custom-call(bf16[2,6,64,128]{3,2,1,0:T(8,128)(2,1)} %copy-done.2, bf16[2,64,64,128]{3,2,1,0:T(8,128)(2,1)} %bitcast.19, bf16[2,6,64,128]{3,2,1,0:T(8,128)(2,1)} %copy-done.3), custom_call_target="tpu_custom_call" | custom-call | tf_op jit(solution)/shard_map/pack_edges/pallas_call | solution.py:51
  20.2 1.5 collective-permute-start.2
  21.7 0.7 collective-permute-start.3
  22.4 0.1 stack.23
  22.5 0.5 convert_element_type.3.place_ref
  23.1 0.1 copy.22
  23.2 0.8 reshape.21.w1_ref
  24.0 0.1 copy.21
  24.1 0.8 reshape.23.w2_ref
  24.9 0.0 collective-permute-done.2.partner_ref
  24.9 0.0 collective-permute-done.3.cross_ref
  24.9 0.8 copy-done.4
  25.7 0.8 copy-done.5
  26.5 19.4 %unit_features_1.1 = bf16[64,64,128]{2,1,0:T(8,128)(2,1)} custom-call(s32[5]{0:T(128)} %convert_element_type.3.place_ref, bf16[2,6,64,128]{3,2,1,0:T(8,128)(2,1)} %copy-done.2, bf16[2,64,64,128]{3,2,1,0:T(8,128)(2,1)} %bitcast.20, bf16[2,6,64,128]{3,2,1,0:T(8,128)(2,1)} %copy-done.3, bf16[2,13,64,128]{3,2,1,0:T(8,128)(2,1)} %pack_edges.1.own_ref, ...), custom_call_target="tpu_custom_call" | custom-call | tf_op jit(solution)/shard_map/unit_features_1/pallas_call | solution.py:205
  45.9 1.4 collective-permute-start.4
  47.4 28.7 %collective-permute-done.4 = bf16[64,64,128]{2,1,0:T(8,128)(2,1)} collective-permute-done((bf16[64,64,128]{2,1,0:T(8,128)(2,1)}, bf16[64,64,128]{2,1,0:T(8,128)(2,1)}, u32[]{:S(2)}, u32[]{:S(2)}) %collective-permute-start.4) | collective-permute-done | bytes 1048608 | tf_op jit(solution)/shard_map/ppermute | solution.py:389
  76.1 1.3 collective-permute-start.5
  77.4 25.9 %collective-permute-done.5 = bf16[64,64,128]{2,1,0:T(8,128)(2,1)S(1)} collective-permute-done((bf16[64,64,128]{2,1,0:T(8,128)(2,1)}, bf16[64,64,128]{2,1,0:T(8,128)(2,1)S(1)}, u32[]{:S(2)}, u32[]{:S(2)}) %collective-permute-start.5) | collective-permute-done | bytes 1048608 | tf_op jit(solution)/shard_map/ppermute | solution.py:389
  103.3 1.3 collective-permute-start.6
  104.6 1.8 collective-permute-start.10
  106.4 0.1 collective-permute-start.9
  106.4 0.4 collective-permute-start.8
  106.9 21.3 %collective-permute-done.6 = bf16[64,64,128]{2,1,0:T(8,128)(2,1)S(1)} collective-permute-done((bf16[64,64,128]{2,1,0:T(8,128)(2,1)S(1)}, bf16[64,64,128]{2,1,0:T(8,128)(2,1)S(1)}, u32[]{:S(2)}, u32[]{:S(2)}) %collective-permute-start.6) | collective-permute-done | bytes 1048608 | tf_op jit(solution)/shard_map/ppermute | solution.py:389
  128.2 2.6 %collective-permute-start.7 = (bf16[64,64,128]{2,1,0:T(8,128)(2,1)S(1)}, bf16[64,64,128]{2,1,0:T(8,128)(2,1)}, u32[]{:S(2)}, u32[]{:S(2)}) collective-permute-start(bf16[64,64,128]{2,1,0:T(8,128)(2,1)S(1)} %collective-permute-done.6), channel_id=1, source_target_pairs={{0,1},{1,0},{2,3},{3,2},{4,5},{5,4},{6,7},{7,6},{8,9},{9,8},{10,11... | collective-permute-start | bytes 3145736 | tf_op jit(solution)/shard_map/ppermute | solution.py:381
  130.8 0.6 concatenate.3.table_ref
  131.3 19.4 %unit_features_0.1.left_ref = bf16[64,64,128]{2,1,0:T(8,128)(2,1)} custom-call(s32[5]{0:T(128)} %convert_element_type.3.place_ref, bf16[2,6,64,128]{3,2,1,0:T(8,128)(2,1)} %copy-done.2, bf16[2,64,64,128]{3,2,1,0:T(8,128)(2,1)} %bitcast.21, bf16[2,6,64,128]{3,2,1,0:T(8,128)(2,1)} %copy-done.3, bf16[2,13,64,128]{3,2,1,0:T(8,128)(2,1)} %pack_edges.1.own_ref, ...), custom_call_target="tpu_custom_call" | custom-call | tf_op jit(solution)/shard_map/unit_features_0/pallas_call | solution.py:205
  150.8 0.0 collective-permute-done.10
  150.8 2.8 %broadcast_select_fusion = (bf16[64,64,128]{2,1,0:T(8,128)(2,1)}, bf16[64,64,128]{2,1,0:T(8,128)(2,1)}) fusion(bf16[64,64,128]{2,1,0:T(8,128)(2,1)S(1)} %copy-done.1, bf16[64,64,128]{2,1,0:T(8,128)(2,1)} %collective-permute-done.10, pred[]{:T(512)} %eq.29), kind=kLoop, calls=%fused_computation.1 | loop fusion | flops 1048576 | bytes 4194305 | tf_op jit(solution)/shard_map/jit(_where)/select_n | solution.py:382
  153.6 0.6 broadcast_in_dim.4.acc_in_ref
  154.2 8.5 %correlate_0.1.acc_in_ref = f32[64,128,128]{2,1,0:T(8,128)} custom-call(s32[3,8]{1,0:T(4,128)} %concatenate.3.table_ref, bf16[64,64,128]{2,1,0:T(8,128)(2,1)} %unit_features_0.1.left_ref, bf16[64,64,128]{2,1,0:T(8,128)(2,1)} %get-tuple-element.11.even_ref, bf16[64,64,128]{2,1,0:T(8,128)(2,1)} %get-tuple-element.10.odd_ref, f32[8,128]{1,0:T(8,128)} %broadcast_in_dim.4.acc_in_ref), custom_call_target="tpu_custom_call" | custom-call | tf_op jit(solution)/shard_map/correlate_0/pallas_call | solution.py:272
  162.7 0.0 collective-permute-done.9
  162.7 3.1 %broadcast_select_fusion.2 = (bf16[64,64,128]{2,1,0:T(8,128)(2,1)}, bf16[64,64,128]{2,1,0:T(8,128)(2,1)}) fusion(bf16[64,64,128]{2,1,0:T(8,128)(2,1)} %collective-permute-done.4, bf16[64,64,128]{2,1,0:T(8,128)(2,1)} %collective-permute-done.9, pred[]{:T(512)} %eq.29), kind=kLoop, calls=%fused_computation.3 | loop fusion | flops 1048576 | bytes 4194305 | tf_op jit(solution)/shard_map/jit(_where)/select_n | solution.py:382
  165.8 8.8 %correlate_1.1.acc_in_ref = f32[64,128,128]{2,1,0:T(8,128)} custom-call(s32[3,8]{1,0:T(4,128)} %concatenate.3.table_ref, bf16[64,64,128]{2,1,0:T(8,128)(2,1)} %unit_features_0.1.left_ref, bf16[64,64,128]{2,1,0:T(8,128)(2,1)} %get-tuple-element.13.even_ref, bf16[64,64,128]{2,1,0:T(8,128)(2,1)} %get-tuple-element.12.odd_ref, ...), custom_call_target="tpu_custom_call", output_to_operand_aliasing={{}: (4, {})} | custom-call | tf_op jit(solution)/shard_map/correlate_1/pallas_call | solution.py:272
  174.6 0.0 collective-permute-done.8
  174.6 2.7 %broadcast_select_fusion.4 = (bf16[64,64,128]{2,1,0:T(8,128)(2,1)}, bf16[64,64,128]{2,1,0:T(8,128)(2,1)}) fusion(bf16[64,64,128]{2,1,0:T(8,128)(2,1)S(1)} %collective-permute-done.5, bf16[64,64,128]{2,1,0:T(8,128)(2,1)} %collective-permute-done.8, pred[]{:T(512)} %eq.29), kind=kLoop, calls=%fused_computation.5 | loop fusion | flops 1048576 | bytes 4194305 | tf_op jit(solution)/shard_map/jit(_where)/select_n | solution.py:382
  177.4 9.2 %correlate_2.1.acc_in_ref = f32[64,128,128]{2,1,0:T(8,128)} custom-call(s32[3,8]{1,0:T(4,128)} %concatenate.3.table_ref, bf16[64,64,128]{2,1,0:T(8,128)(2,1)} %unit_features_0.1.left_ref, bf16[64,64,128]{2,1,0:T(8,128)(2,1)} %get-tuple-element.15.even_ref, bf16[64,64,128]{2,1,0:T(8,128)(2,1)} %get-tuple-element.14.odd_ref, ...), custom_call_target="tpu_custom_call", output_to_operand_aliasing={{}: (4, {})} | custom-call | tf_op jit(solution)/shard_map/correlate_2/pallas_call | solution.py:272
  186.6 0.0 collective-permute-done.7
  186.6 2.7 %broadcast_select_fusion.6 = (bf16[64,64,128]{2,1,0:T(8,128)(2,1)}, bf16[64,64,128]{2,1,0:T(8,128)(2,1)}) fusion(bf16[64,64,128]{2,1,0:T(8,128)(2,1)S(1)} %collective-permute-done.6, bf16[64,64,128]{2,1,0:T(8,128)(2,1)} %collective-permute-done.7, pred[]{:T(512)} %eq.29), kind=kLoop, calls=%fused_computation.7 | loop fusion | flops 1048576 | bytes 4194305 | tf_op jit(solution)/shard_map/jit(_where)/select_n | solution.py:382
  189.3 9.0 %correlate_3.1.acc_ref = f32[64,128,128]{2,1,0:T(8,128)} custom-call(s32[3,8]{1,0:T(4,128)} %concatenate.3.table_ref, bf16[64,64,128]{2,1,0:T(8,128)(2,1)} %unit_features_0.1.left_ref, bf16[64,64,128]{2,1,0:T(8,128)(2,1)} %get-tuple-element.17.even_ref, bf16[64,64,128]{2,1,0:T(8,128)(2,1)} %get-tuple-element.16.odd_ref, ...), custom_call_target="tpu_custom_call", output_to_operand_aliasing={{}: (4, {})} | custom-call | tf_op jit(solution)/shard_map/correlate_3/pallas_call | solution.py:272
  198.2 6.6 %finish.1 = (bf16[64,64,128]{2,1,0:T(8,128)(2,1)}, f32[64,128]{1,0:T(8,128)}) custom-call(s32[3,8]{1,0:T(4,128)} %concatenate.3.table_ref, f32[64,128,128]{2,1,0:T(8,128)} %correlate_3.1.acc_ref), custom_call_target="tpu_custom_call" | custom-call | tf_op jit(solution)/shard_map/finish/pallas_call | solution.py:316
  204.8 2.9 %copy.16 = bf16[64,64,128]{2,1,0:T(8,128)(2,1)} copy(bf16[64,64,128]{2,0,1:T(8,128)(2,1)} %bitcast.22) | data formatting | bytes 2097152
  (15 shorter events, 0.1 us)
Async XLA Ops:
  0.6 22.4 %copy-start.6 = (bf16[9,64,64]{2,1,0:T(8,128)(2,1)S(1)}, bf16[9,64,64]{2,1,0:T(8,128)(2,1)}, u32[]{:S(2)}) copy-start(bf16[9,64,64]{2,1,0:T(8,128)(2,1)} %param.5) | copy-start | bytes 221188
  0.6 23.4 %copy-start.7 = (bf16[9,64,64]{2,1,0:T(8,128)(2,1)S(1)}, bf16[9,64,64]{2,1,0:T(8,128)(2,1)}, u32[]{:S(2)}) copy-start(bf16[9,64,64]{2,1,0:T(8,128)(2,1)} %param.6) | copy-start | bytes 221188
  3.6 12.9 %copy-start = (bf16[2,64,64,128]{3,1,2,0:T(8,128)(2,1)}, bf16[2,64,64,128]{3,1,2,0:T(8,128)(2,1)S(1)}, u32[]{:S(2)}) copy-start(bf16[2,64,64,128]{3,1,2,0:T(8,128)(2,1)S(1)} %copy.20) | copy-start | bytes 6291460
  3.7 7.7 %collective-permute-start = (bf16[2,6,64,128]{3,2,1,0:T(8,128)(2,1)S(1)}, bf16[2,6,64,128]{3,2,1,0:T(8,128)(2,1)S(1)}, u32[]{:S(2)}, u32[]{:S(2)}) collective-permute-start(bf16[2,6,64,128]{3,2,1,0:T(8,128)(2,1)S(1)} %get-tuple-element.19), channel_id=1, source_target_pairs={{0,8},{8,16},{16,24},{1,9},{9,17},{17,25},{2,10},{10,18},{18,26},{... | collective-permute-start | bytes 589832 | tf_op jit(solution)/shard_map/ppermute | solution.py:359
  6.8 123.9 %copy-start.8 = (s32[2,8,1]{1,2,0:T(1,128)S(1)}, s32[2,8,1]{1,2,0:T(1,128)}, u32[]{:S(2)}) copy-start(s32[2,8,1]{1,2,0:T(1,128)} %param.7) | copy-start | bytes 196
  6.8 9.7 %collective-permute-start.1 = (bf16[2,6,64,128]{3,2,1,0:T(8,128)(2,1)S(1)}, bf16[2,6,64,128]{3,2,1,0:T(8,128)(2,1)S(1)}, u32[]{:S(2)}, u32[]{:S(2)}) collective-permute-start(bf16[2,6,64,128]{3,2,1,0:T(8,128)(2,1)S(1)} %get-tuple-element.18), channel_id=1, source_target_pairs={{8,0},{16,8},{24,16},{9,1},{17,9},{25,17},{10,2},{18,10},{26,18},{... | collective-permute-start | bytes 589832 | tf_op jit(solution)/shard_map/ppermute | solution.py:360
  11.4 5.2 %copy-start.2 = (bf16[2,6,64,128]{3,2,1,0:T(8,128)(2,1)}, bf16[2,6,64,128]{3,2,1,0:T(8,128)(2,1)S(1)}, u32[]{:S(2)}) copy-start(bf16[2,6,64,128]{3,2,1,0:T(8,128)(2,1)S(1)} %collective-permute-done.top_ref) | copy-start | bytes 589828
  16.5 0.7 copy-start.3
  20.2 4.7 %collective-permute-start.2 = (bf16[2,13,64,128]{3,2,1,0:T(8,128)(2,1)}, bf16[2,13,64,128]{3,2,1,0:T(8,128)(2,1)S(1)}, u32[]{:S(2)}, u32[]{:S(2)}) collective-permute-start(bf16[2,13,64,128]{3,2,1,0:T(8,128)(2,1)} %pack_edges.1.own_ref), channel_id=1, source_target_pairs={{0,1},{1,0},{2,3},{3,2},{4,5},{5,4},{6,7},{7,6},{8,9},{9,8},{10,11... | collective-permute-start | bytes 1277960 | tf_op jit(solution)/shard_map/ppermute | solution.py:362
  21.7 3.2 %collective-permute-start.3 = (bf16[2,13,64,128]{3,2,1,0:T(8,128)(2,1)}, bf16[2,13,64,128]{3,2,1,0:T(8,128)(2,1)S(1)}, u32[]{:S(2)}, u32[]{:S(2)}) collective-permute-start(bf16[2,13,64,128]{3,2,1,0:T(8,128)(2,1)} %pack_edges.1.own_ref), channel_id=1, source_target_pairs={{1,2},{3,4},{5,6},{2,1},{4,3},{6,5},{9,10},{11,12},{13,14},{10,9},... | collective-permute-start | bytes 1277960 | tf_op jit(solution)/shard_map/ppermute | solution.py:363
  24.9 0.8 copy-start.4
  25.7 0.8 copy-start.5
  45.9 104.9 %copy-start.1 = (bf16[64,64,128]{2,1,0:T(8,128)(2,1)S(1)}, bf16[64,64,128]{2,1,0:T(8,128)(2,1)}, u32[]{:S(2)}) copy-start(bf16[64,64,128]{2,1,0:T(8,128)(2,1)} %unit_features_1.1) | copy-start | bytes 3145732
  45.9 30.1 %collective-permute-start.4 = (bf16[64,64,128]{2,1,0:T(8,128)(2,1)}, bf16[64,64,128]{2,1,0:T(8,128)(2,1)}, u32[]{:S(2)}, u32[]{:S(2)}) collective-permute-start(bf16[64,64,128]{2,1,0:T(8,128)(2,1)} %unit_features_1.1), channel_id=1, source_target_pairs={{0,2},{1,3},{2,4},{3,5},{4,6},{5,7},{8,10},{9,11},{10,12},{11,13},... | collective-permute-start | bytes 3145736 | tf_op jit(solution)/shard_map/ppermute | solution.py:389
  76.1 27.2 %collective-permute-start.5 = (bf16[64,64,128]{2,1,0:T(8,128)(2,1)}, bf16[64,64,128]{2,1,0:T(8,128)(2,1)S(1)}, u32[]{:S(2)}, u32[]{:S(2)}) collective-permute-start(bf16[64,64,128]{2,1,0:T(8,128)(2,1)} %collective-permute-done.4), channel_id=1, source_target_pairs={{0,2},{1,3},{2,4},{3,5},{4,6},{5,7},{8,10},{9,11},{10,12},{11,13},... | collective-permute-start | bytes 3145736 | tf_op jit(solution)/shard_map/ppermute | solution.py:389
  103.3 24.9 %collective-permute-start.6 = (bf16[64,64,128]{2,1,0:T(8,128)(2,1)S(1)}, bf16[64,64,128]{2,1,0:T(8,128)(2,1)S(1)}, u32[]{:S(2)}, u32[]{:S(2)}) collective-permute-start(bf16[64,64,128]{2,1,0:T(8,128)(2,1)S(1)} %collective-permute-done.5), channel_id=1, source_target_pairs={{0,2},{1,3},{2,4},{3,5},{4,6},{5,7},{8,10},{9,11},{10,12},{11,13},... | collective-permute-start | bytes 3145736 | tf_op jit(solution)/shard_map/ppermute | solution.py:389
  104.6 46.2 %collective-permute-start.10 = (bf16[64,64,128]{2,1,0:T(8,128)(2,1)}, bf16[64,64,128]{2,1,0:T(8,128)(2,1)}, u32[]{:S(2)}, u32[]{:S(2)}) collective-permute-start(bf16[64,64,128]{2,1,0:T(8,128)(2,1)} %unit_features_1.1), channel_id=1, source_target_pairs={{0,1},{1,0},{2,3},{3,2},{4,5},{5,4},{6,7},{7,6},{8,9},{9,8},{10,11... | collective-permute-start | bytes 3145736 | tf_op jit(solution)/shard_map/ppermute | solution.py:381
  106.4 56.4 %collective-permute-start.9 = (bf16[64,64,128]{2,1,0:T(8,128)(2,1)}, bf16[64,64,128]{2,1,0:T(8,128)(2,1)}, u32[]{:S(2)}, u32[]{:S(2)}) collective-permute-start(bf16[64,64,128]{2,1,0:T(8,128)(2,1)} %collective-permute-done.4), channel_id=1, source_target_pairs={{0,1},{1,0},{2,3},{3,2},{4,5},{5,4},{6,7},{7,6},{8,9},{9,8},{10,11... | collective-permute-start | bytes 3145736 | tf_op jit(solution)/shard_map/ppermute | solution.py:381
  106.4 68.2 %collective-permute-start.8 = (bf16[64,64,128]{2,1,0:T(8,128)(2,1)S(1)}, bf16[64,64,128]{2,1,0:T(8,128)(2,1)}, u32[]{:S(2)}, u32[]{:S(2)}) collective-permute-start(bf16[64,64,128]{2,1,0:T(8,128)(2,1)S(1)} %collective-permute-done.5), channel_id=1, source_target_pairs={{0,1},{1,0},{2,3},{3,2},{4,5},{5,4},{6,7},{7,6},{8,9},{9,8},{10,11... | collective-permute-start | bytes 3145736 | tf_op jit(solution)/shard_map/ppermute | solution.py:381
  128.2 58.4 %collective-permute-start.7 = (bf16[64,64,128]{2,1,0:T(8,128)(2,1)S(1)}, bf16[64,64,128]{2,1,0:T(8,128)(2,1)}, u32[]{:S(2)}, u32[]{:S(2)}) collective-permute-start(bf16[64,64,128]{2,1,0:T(8,128)(2,1)S(1)} %collective-permute-done.6), channel_id=1, source_target_pairs={{0,1},{1,0},{2,3},{3,2},{4,5},{5,4},{6,7},{7,6},{8,9},{9,8},{10,11... | collective-permute-start | bytes 3145736 | tf_op jit(solution)/shard_map/ppermute | solution.py:381

commit v2 on v0

v2 whole, which is shorter than its diff:
```python
import functools

import jax
import jax.numpy as jnp
from jax import lax
from jax.experimental import pallas as pl
from jax.experimental.pallas import tpu as pltpu
from jax.sharding import PartitionSpec as P


RG = 8
FIRST_DILATION = 2
SECOND_DILATION = 4
HOPS = 18
REACH = FIRST_DILATION + SECOND_DILATION
SLOT = 16

sharpness_divisor = 10.0
epsilon = 1e-05
VMEM_LIMIT = 64 << 20
LOG2E = 1.4426950408889634


def lane_iota(shape):
    return lax.broadcasted_iota(jnp.int32, shape, len(shape) - 1)


def cost(microseconds):
    return pl.CostEstimate(
        flops=int(microseconds * 1e9), transcendentals=0, bytes_accessed=int(microseconds * 3e6)
    )


def pack_kernel(x_ref, edge_ref, *, groups, spacing, offset):
    channels, segment = x_ref.shape[1:]
    slot_of = lane_iota((channels, segment)) // SLOT
    for q in range(edge_ref.shape[0]):
        packed = None
        for g in range(groups):
            shift = (SLOT * g + SLOT // 2) % segment
            moved = pltpu.roll(x_ref[offset + g * spacing + q], shift, 1)
            packed = moved if packed is None else jnp.where(slot_of == g, moved, packed)
        edge_ref[q] = packed


def edge_steps(rows, segment):
    spacing = (rows + 2 * SECOND_DILATION) // (segment // SLOT)
    return spacing, spacing + 2 * FIRST_DILATION


def pack_edges(x, rows, offset):
    parts, held, channels, segment = x.shape
    spacing, steps = edge_steps(rows, segment)
    return pl.pallas_call(
        functools.partial(pack_kernel, groups=segment // SLOT, spacing=spacing, offset=offset),
        out_shape=jax.ShapeDtypeStruct((parts, steps, channels, segment), jnp.bfloat16),
        grid=(parts,),
        in_specs=[pl.BlockSpec((None, held, channels, segment), lambda n: (n, 0, 0, 0))],
        out_specs=pl.BlockSpec((None, steps, channels, segment), lambda n: (n, 0, 0, 0)),
        compiler_params=pltpu.CompilerParams(vmem_limit_bytes=VMEM_LIMIT),
        cost_estimate=cost(2),
    )(x)


def feature_kernel(
    place_ref, x_ref, own_ref, partner_ref, cross_ref, w1_ref, w2_ref, unit_ref,
    w_ref, edge_ref, side_ref, p1_ref, p1e_ref, hid_ref, hide_ref, p2_ref, rhs0_ref, rhs1_ref,
    *, spacing, offset, ends, mesh_shape,
):
    part = pl.program_id(0)
    rows = unit_ref.shape[0]
    channels, segment = x_ref.shape[1:]
    first_row, last_row = place_ref[0] == 0, place_ref[0] == mesh_shape[0] - 1
    first_col, last_col = place_ref[1] == 0, place_ref[1] == mesh_shape[1] - 1
    odd = place_ref[1] % 2 == 1
    above = first_row & (part == 0) & ends
    below = last_row & (part == pl.num_programs(0) - 1) & ends
    d1, d2 = FIRST_DILATION, SECOND_DILATION
    all_rows = rows + 2 * REACH
    hidden_rows = rows + 2 * d2
    steps = edge_ref.shape[0]
    groups = segment // SLOT
    lanes = lane_iota((channels, segment))
    in_slot = lanes % SLOT
    half = SLOT // 2
    rhs = (rhs0_ref, rhs1_ref)
    width = rhs0_ref.shape[1] // segment

    def stack(taps_ref):
        for a in range(3):
            for b in range(3):
                w_ref[a * channels : (a + 1) * channels, b * channels : (b + 1) * channels] = taps_ref[3 * a + b]

    for q in range(steps):
        own = own_ref[q]
        partner = partner_ref[q]
        cross = cross_ref[q]
        left = jnp.where(odd, partner, cross)
        right = jnp.where(odd, cross, partner)
        shift = half - REACH
        lower = pltpu.roll(jnp.where(in_slot < half, left, own), segment - shift, 1)
        upper = pltpu.roll(jnp.where(in_slot < half, own, right), shift, 1)
        edge_ref[q] = jnp.where(in_slot < half, lower, upper)
        side_ref[q] = pltpu.roll(jnp.where(in_slot < half, left, right), segment - shift, 1)

    def shifted(main, side, slot, amount):
        aligned = pltpu.roll(side, segment - REACH - slot * SLOT, 1)
        before = pltpu.roll(jnp.where(lanes >= segment - amount, aligned, main), amount, 1)
        after = pltpu.roll(jnp.where(lanes < amount, aligned, main), segment - amount, 1)
        return before, after

    def put(target, j, main, before, after):
        lo = j * segment
        target[0:channels, lo : lo + segment] = before
        target[channels : 2 * channels, lo : lo + segment] = main
        target[2 * channels :, lo : lo + segment] = after

    def multiply(source, product_ref, base):
        product = jnp.dot(w_ref[...], source[...], preferred_element_type=jnp.float32)
        for j in range(width):
            product_ref[base + j] = product[:, j * segment : (j + 1) * segment]

    def conv(source_ref, skip, sides_ref, product_ref, total, amount):
        def build(t, target):
            for j in range(width):
                row = jnp.minimum(t * width + j, total - 1)
                slot = jnp.minimum(row // spacing, groups - 1)
                main = source_ref[row + skip]
                put(target, j, main, *shifted(main, sides_ref[row - slot * spacing], slot, amount))

        build(0, rhs0_ref)

        def body(u, _):
            build(2 * u + 1, rhs1_ref)
            multiply(rhs0_ref, product_ref, 2 * u * width)
            build(2 * u + 2, rhs0_ref)
            multiply(rhs1_ref, product_ref, (2 * u + 1) * width)
            return 0

        lax.fori_loop(0, pl.cdiv(total, 2 * width), body, 0)

    stack(w1_ref)
    conv(x_ref, offset, side_ref, p1_ref, all_rows, d1)

    for t in range(pl.cdiv(steps, width)):
        target = rhs[t % 2]
        for j in range(width):
            main = edge_ref[min(t * width + j, steps - 1)]
            put(target, j, main, pltpu.roll(main, d1, 1), pltpu.roll(main, segment - d1, 1))
        multiply(target, p1e_ref, t * width)

    def three(product_ref, row, apart):
        return (
            product_ref[row, 0:channels]
            + product_ref[row + apart, channels : 2 * channels]
            + product_ref[row + 2 * apart, 2 * channels :]
        )

    def silu(v):
        return v / (1.0 + jnp.exp(-v))

    def hidden(t, _):
        for j in range(8):
            row = 8 * t + j
            outside = ((row < d2) & above) | ((row >= d2 + rows) & below)
            value = silu(three(p1_ref, row, d1))
            hid_ref[row] = jnp.where(outside, 0.0, value).astype(jnp.bfloat16)
        return 0

    lax.fori_loop(0, hidden_rows // 8, hidden, 0)

    left_out = (in_slot < REACH) & first_col
    right_out = (in_slot >= half + 2) & last_col
    for q in range(spacing):
        row = (lanes // SLOT) * spacing + q
        outside = ((row < d2) & above) | ((row >= d2 + rows) & below) | left_out | right_out
        value = silu(three(p1e_ref, q, d1))
        value = jnp.where(outside, 0.0, value).astype(jnp.bfloat16)
        gap = half + 2 - REACH
        hide_ref[q] = jnp.where(in_slot < REACH, value, pltpu.roll(value, segment - gap, 1))

    stack(w2_ref)
    conv(hid_ref, 0, hide_ref, p2_ref, hidden_rows, d2)

    def finish(t, _):
        for j in range(8):
            row = 8 * t + j
            total = x_ref[row + offset + REACH].astype(jnp.float32) + three(p2_ref, row, d2)
            feature = total.astype(jnp.bfloat16).astype(jnp.float32)
            mean = jnp.sum(feature * feature, axis=0, keepdims=True) * (1.0 / channels)
            unit_ref[row] = (feature * lax.rsqrt(mean + epsilon)).astype(jnp.bfloat16)
        return 0

    lax.fori_loop(0, rows // 8, finish, 0)


def unit_features(place, x, rows, offset, ends, edges, w1, w2, mesh_shape):
    parts, _, channels, segment = x.shape
    all_rows = rows + 2 * REACH
    hidden_rows = rows + 2 * SECOND_DILATION
    spacing, steps = edge_steps(rows, segment)
    width = 8

    def part_of(a):
        return pl.BlockSpec((None,) + a.shape[1:], lambda i: (i, 0, 0, 0))

    def whole(a):
        return pl.BlockSpec(a.shape, lambda i: (0,) * a.ndim)

    def up_to(n, m):
        return pl.cdiv(n, m) * m

    products = (3 * channels, segment)
    return pl.pallas_call(
        functools.partial(
            feature_kernel, spacing=spacing, offset=offset, ends=ends, mesh_shape=mesh_shape
        ),
        out_shape=jax.ShapeDtypeStruct((parts, rows, channels, segment), jnp.bfloat16),
        grid=(parts,),
        in_specs=[pl.BlockSpec(memory_space=pltpu.SMEM)]
        + [part_of(a) for a in (x, *edges)]
        + [whole(w1), whole(w2)],
        out_specs=pl.BlockSpec((None, rows, channels, segment), lambda i: (i, 0, 0, 0)),
        scratch_shapes=[
            pltpu.VMEM((3 * channels, 3 * channels), jnp.bfloat16),
            pltpu.VMEM((steps, channels, segment), jnp.bfloat16),
            pltpu.VMEM((steps, channels, segment), jnp.bfloat16),
            pltpu.VMEM((up_to(all_rows, 2 * width),) + products, jnp.float32),
            pltpu.VMEM((up_to(steps, width),) + products, jnp.float32),
            pltpu.VMEM((hidden_rows, channels, segment), jnp.bfloat16),
            pltpu.VMEM((spacing, channels, segment), jnp.bfloat16),
            pltpu.VMEM((up_to(hidden_rows, 2 * width),) + products, jnp.float32),
            pltpu.VMEM((3 * channels, width * segment), jnp.bfloat16),
            pltpu.VMEM((3 * channels, width * segment), jnp.bfloat16),
        ],
        compiler_params=pltpu.CompilerParams(vmem_limit_bytes=VMEM_LIMIT),
        cost_estimate=cost(parts * rows * 0.2),
    )(place, x, *edges, w1, w2)


def add_step(place_ref, range_ref, group, step, left_ref, mine_ref, theirs_ref, acc_ref, bias_ref):
    _, channels, segment = left_ref.shape
    block = place_ref[1]
    low = segment * range_ref[0, group]
    high = low + segment * range_ref[1, group]
    odd = block % 2
    base = segment * (block - 2 * (block // 2 - step))
    active = (base + segment - 1 >= low) & (base - 2 * segment + 1 < high) & (block // 2 >= step)
    scale = sharpness_divisor / channels * LOG2E

    def key_column(shape):
        column = lane_iota(shape)
        own = column < segment
        return column % segment + segment * jnp.where(own, odd, 1 - odd)

    @pl.when(active)
    def _():
        wide = (segment, 2 * segment)
        offsets = base + lax.broadcasted_iota(jnp.int32, wide, 0) - key_column(wide)
        inside = (offsets >= low) & (offsets < high)
        bias_ref[...] = jnp.where(inside, 0.0, -1e30)
        kind = lax.broadcasted_iota(jnp.int32, (16, 2 * segment), 0)
        column = key_column((16, 2 * segment))
        extra = jnp.where(kind == 0, 1, jnp.where(kind == 1, column, jnp.where(kind == 2, step, 0)))
        extra = extra.astype(jnp.float32).astype(jnp.bfloat16)
        for r in range(left_ref.shape[0]):
            keys = jnp.concatenate([mine_ref[r], theirs_ref[r]], axis=1)
            scores = lax.dot_general(
                left_ref[r], keys, (((0,), (0,)), ((), ())), preferred_element_type=jnp.float32
            )
            weights = jnp.exp2(scores * scale + bias_ref[...]).astype(jnp.bfloat16)
            extended = jnp.concatenate([keys, extra], axis=0)
            acc_ref[r, :, 0 : channels + 16] += lax.dot_general(
                weights, extended, (((1,), (1,)), ((), ())), preferred_element_type=jnp.float32
            )


def group_of(i, inner, groups):
    return i + 1 if inner else i * (groups - 1)


def gather_kernel(place_ref, range_ref, left_ref, *refs, inner, groups):
    keys, (acc_ref, bias_ref) = refs[:-2], refs[-2:]
    group = group_of(pl.program_id(0), inner, groups)
    acc_ref[...] = jnp.zeros_like(acc_ref)
    for step in range(len(keys) // 2):
        add_step(
            place_ref, range_ref, group, step, left_ref, keys[2 * step], keys[2 * step + 1],
            acc_ref, bias_ref,
        )


def finish_kernel(
    place_ref, range_ref, left_ref, mine_ref, theirs_ref, acc_in_ref, *refs, inner, groups, step
):
    matched_ref, disparity_ref, acc_ref, bias_ref, rows_ref = refs[-5:]
    group = group_of(pl.program_id(0), inner, groups)
    rows, channels, segment = left_ref.shape
    acc_ref[...] = acc_in_ref[...]
    add_step(
        place_ref, range_ref, group, step, left_ref, mine_ref, theirs_ref, acc_ref, bias_ref
    )
    block = place_ref[1]
    low = segment * range_ref[0, group]
    high = low + segment * range_ref[1, group]
    x = block * segment + lane_iota((1, segment))
    from_chip = (x - 2 * segment * (block // 2)).astype(jnp.float32)
    start = jnp.maximum(low, x + 1)
    beyond = jnp.maximum(high - start, 0)
    beyond_sum = ((start + high - 1) * beyond).astype(jnp.float32) * 0.5
    beyond = beyond.astype(jnp.float32)
    for r in range(rows):
        turned = acc_ref[r].T
        near = turned[channels : channels + 1]
        column = turned[channels + 1 : channels + 2]
        passed = turned[channels + 2 : channels + 3]
        inverse = 1.0 / (near + beyond)
        shift = from_chip * near - column + (2 * segment) * passed + beyond_sum
        rows_ref[r] = turned[:channels] * inverse
        disparity_ref[r : r + 1, :] = shift * inverse * (1.0 / segment)
    matched_ref[...] = jnp.swapaxes(rows_ref[...].astype(jnp.bfloat16), 0, 1)


def correlate(place, ranges, left, keys, inner):
    rows, channels, segment = left.shape
    groups = rows // RG
    own_groups = keys[0][0].shape[0] // RG
    block = (RG, channels, segment)
    smem = pl.BlockSpec(memory_space=pltpu.SMEM)
    return pl.pallas_call(
        functools.partial(gather_kernel, inner=inner, groups=groups),
        out_shape=jax.ShapeDtypeStruct((own_groups * RG, segment, 128), jnp.float32),
        grid=(own_groups,),
        in_specs=[smem, smem, pl.BlockSpec(block, lambda i: (group_of(i, inner, groups), 0, 0))]
        + [pl.BlockSpec(block, lambda i: (i, 0, 0))] * (2 * len(keys)),
        out_specs=pl.BlockSpec((RG, segment, 128), lambda i: (i, 0, 0)),
        scratch_shapes=[pltpu.VMEM((segment, 2 * segment), jnp.float32)],
        compiler_params=pltpu.CompilerParams(vmem_limit_bytes=VMEM_LIMIT),
        cost_estimate=cost(1.5 * own_groups),
    )(place, ranges, left, *[a for pair in keys for a in pair])


def finish(place, ranges, left, pair, acc, outs, inner, step):
    rows, channels, segment = left.shape
    groups = rows // RG
    own_groups = acc.shape[0] // RG
    block = (RG, channels, segment)
    smem = pl.BlockSpec(memory_space=pltpu.SMEM)

    def group(i):
        return group_of(i, inner, groups)

    given = () if outs is None else tuple(outs)
    return pl.pallas_call(
        functools.partial(finish_kernel, inner=inner, groups=groups, step=step),
        out_shape=(
            jax.ShapeDtypeStruct((channels, rows, segment), jnp.bfloat16),
            jax.ShapeDtypeStruct((rows, segment), jnp.float32),
        ),
        grid=(own_groups,),
        in_specs=[
            smem,
            smem,
            pl.BlockSpec(block, lambda i: (group(i), 0, 0)),
            pl.BlockSpec(block, lambda i: (i, 0, 0)),
            pl.BlockSpec(block, lambda i: (i, 0, 0)),
            pl.BlockSpec((RG, segment, 128), lambda i: (i, 0, 0)),
        ]
        + [pl.BlockSpec(memory_space=pl.ANY)] * len(given),
        out_specs=(
            pl.BlockSpec((channels, RG, segment), lambda i: (0, group(i), 0)),
            pl.BlockSpec((RG, segment), lambda i: (group(i), 0)),
        ),
        scratch_shapes=[
            pltpu.VMEM((RG, segment, 128), jnp.float32),
            pltpu.VMEM((segment, 2 * segment), jnp.float32),
            pltpu.VMEM((RG, channels, segment), jnp.float32),
        ],
        input_output_aliases={6: 0, 7: 1} if given else {},
        compiler_params=pltpu.CompilerParams(vmem_limit_bytes=VMEM_LIMIT),
        cost_estimate=cost(own_groups),
    )(place, ranges, left, *pair, acc, *given)


def both_ways(pairs):
    return pairs + [(b, a) for a, b in pairs]


def program(images, first_weight, second_weight, search_ranges):
    row_count = lax.axis_size("rows")
    col_count = lax.axis_size("cols")
    col = lax.axis_index("cols")
    channels, rows, segment = images.shape[1:]
    place = jnp.stack([lax.axis_index("rows"), col]).astype(jnp.int32)
    ranges = search_ranges.reshape(2, rows // RG)

    swap = [(i, i ^ 1) for i in range(col_count)]
    across = both_ways([(i, i + 1) for i in range(1, col_count - 1, 2)])
    hop = [(i, (i + 2) % col_count) for i in range(col_count)]
    down = [(i, i + 1) for i in range(row_count - 1)]
    up = [(b, a) for a, b in down]

    def exchanged(x, count, offset):
        own = pack_edges(x, count, offset)
        cross = lax.ppermute(own, "cols", across)
        partner = lax.ppermute(own, "cols", swap)
        return own, partner, cross

    def features(x, count, offset, ends, edges):
        return unit_features(
            place, x, count, offset, ends, edges, first_weight, second_weight,
            (row_count, col_count),
        )

    inner = rows - 2 * RG
    right_rows = images[1].transpose(1, 0, 2)
    edges_a = exchanged(right_rows[None], inner, RG - REACH)

    later, edges_a = lax.optimization_barrier((images, edges_a[0])), edges_a
    later = later[0]
    top = lax.ppermute(later[:, :, rows - REACH :].transpose(0, 2, 1, 3), "rows", down)
    bottom = lax.ppermute(later[:, :, :REACH].transpose(0, 2, 1, 3), "rows", up)
    right_a = features(right_rows[None], inner, RG - REACH, False, edges_a)[0]

    top, bottom, _ = lax.optimization_barrier((top, bottom, right_a[:1, :8]))
    outer = jnp.stack(
        [
            jnp.concatenate([top[1], right_rows[: RG + REACH]]),
            jnp.concatenate([right_rows[rows - RG - REACH :], bottom[1]]),
        ]
    )
    edges_b = exchanged(outer, RG, 0)
    right_b = features(outer, RG, 0, True, edges_b).reshape(2 * RG, channels, segment)

    left_rows = jnp.concatenate([top[0], later[0].transpose(1, 0, 2), bottom[0]])[None]
    edges_l = exchanged(left_rows, rows, 0)
    left = features(left_rows, rows, 0, True, edges_l)[0]

    steps = min(col_count // 2 - 1, HOPS // 2)

    def pair(mine):
        return mine, lax.ppermute(mine, "cols", swap)

    def chain(mine):
        pairs = [pair(mine)]
        for _ in range(1, steps + 1):
            mine = lax.ppermute(mine, "cols", hop)
            pairs.append(pair(mine))
        return pairs

    keys_a, keys_b = chain(right_a), chain(right_b)
    acc_a = correlate(place, ranges, left, keys_a[:-1], True)
    acc_b = correlate(place, ranges, left, keys_b[:-1], False)
    outs = finish(place, ranges, left, keys_a[-1], acc_a, None, True, steps)
    return finish(place, ranges, left, keys_b[-1], acc_b, outs, False, steps)


def solution(mesh):
    placed = (P(None, None, "rows", "cols"), P(), P(), P(None, "rows", "cols"))
    return jax.shard_map(
        program,
        mesh=mesh,
        in_specs=placed,
        out_specs=(P(None, "rows", "cols"), P("rows", "cols")),
        check_vma=False,
    )
```

time: 497 us -> 151 us (0.30)
  the two profiles are of different devices: /device:TPU:4 before, /device:TPU:29 now
where the time goes in v2:
time: 151 us; the launch traced here: 150 us
  Pallas kernels  65.4 us (43%)
  starting transfers between devices  46.7 us (31%)
  waiting for transfers between devices  20.3 us (13%)
  local copies, waits for them, and re-layouts  12.9 us (9%)
  other arithmetic  3.72 us (2%)
    pallas_call x3, Pallas kernels, unit_features(): pl.pallas_call(functools.partial(feature_kernel, spacing=spacing, offset=...  31.5 us
    ppermute x6, starting transfers between devices, chain(): mine = lax.ppermute(mine, 'cols', hop)  25.2 us
    ppermute x6, waiting for transfers between devices, chain(): mine = lax.ppermute(mine, 'cols', hop)  19.9 us
    pallas_call x2, Pallas kernels, correlate(): pl.pallas_call(functools.partial(gather_kernel, inner=inner, groups=group...  16.4 us
    ppermute x8, starting transfers between devices, pair(): return (mine, lax.ppermute(mine, 'cols', swap))  10.6 us
    pallas_call x2, Pallas kernels, finish(): pl.pallas_call(functools.partial(finish_kernel, inner=inner, groups=group...  10.5 us
    pallas_call x3, Pallas kernels, pack_edges(): pl.pallas_call(functools.partial(pack_kernel, groups=segment // SLOT, spa...  6.97 us
    ppermute x3, starting transfers between devices, exchanged(): cross = lax.ppermute(own, 'cols', across)  4 us
  transfers between devices with their start and end apart: 22, of which 4 were waited for; matrix products, arithmetic and copies ran while one was open for 8% of the time, Pallas kernels for 40%

profile of v2, /device:TPU:29, one launch (start us, length us, event | category | flops | bytes accessed | tf_op | source)
XLA Modules:
  0.0 149.7 jit_solution(12289785874134044034)
XLA Ops:
  0.6 0.0 slice-start
  0.6 1.2 slice-done
  1.9 1.6 %copy.15 = bf16[1,64,64,128]{3,1,2,0:T(8,128)(2,1)} copy(bf16[1,64,64,128]{3,2,1,0:T(8,128)(2,1)S(1)} %slice-done) | data formatting | bytes 2097152
  3.5 2.3 %shard_map.59.own_ref = bf16[1,11,64,128]{3,2,1,0:T(8,128)(2,1)} custom-call(bf16[1,64,64,128]{3,2,1,0:T(8,128)(2,1)} %bitcast.36), custom_call_target="tpu_custom_call" | custom-call | flops 2000000000 | bytes 6000000 | tf_op jit(solution)/shard_map/pallas_call | solution.py:54
  5.8 0.7 collective-permute-start.13
  6.5 1.3 collective-permute-start.14
  7.8 2.9 %copy.9 = bf16[2,64,64,128]{3,1,2,0:T(8,128)(2,1)S(1)} copy(bf16[2,64,64,128]{3,2,1,0:T(8,128)(2,1)} %param.4) | data formatting | bytes 4194304 | tf_op jit(solution)/shard_map/optimization_barrier | solution.py:419
  10.8 1.3 copy-done
  12.1 0.8 slice_bitcast_fusion.1
  12.9 3.1 %collective-permute-start = (bf16[2,6,64,128]{3,2,1,0:T(8,128)(2,1)}, bf16[2,6,64,128]{3,2,1,0:T(8,128)(2,1)}, u32[]{:S(2)}, u32[]{:S(2)}) collective-permute-start(bf16[2,6,64,128]{3,2,1,0:T(8,128)(2,1)} %get-tuple-element.13), channel_id=1, source_target_pairs={{0,8},{8,16},{16,24},{1,9},{9,17},{17,25},{2,10},{10,18},{18,26},{... | collective-permute-start | bytes 589832 | tf_op jit(solution)/shard_map/ppermute | solution.py:421
  16.0 3.1 %collective-permute-start.1 = (bf16[2,6,64,128]{3,2,1,0:T(8,128)(2,1)}, bf16[2,6,64,128]{3,2,1,0:T(8,128)(2,1)}, u32[]{:S(2)}, u32[]{:S(2)}) collective-permute-start(bf16[2,6,64,128]{3,2,1,0:T(8,128)(2,1)} %get-tuple-element.12), channel_id=1, source_target_pairs={{8,0},{16,8},{24,16},{9,1},{17,9},{25,17},{10,2},{18,10},{26,18},{... | collective-permute-start | bytes 589832 | tf_op jit(solution)/shard_map/ppermute | solution.py:422
  19.1 0.6 pad_add_fusion.place_ref
  19.7 1.9 %fusion = (bf16[14,64,128]{2,1,0:T(8,128)(2,1)}, bf16[14,64,128]{2,1,0:T(8,128)(2,1)}) fusion(bf16[64,64,128]{2,1,0:T(8,128)(2,1)} %bitcast.37), kind=kLoop, calls=%fused_computation.14 | loop fusion | bytes 917504 | tf_op jit(solution)/shard_map/slice | solution.py:428
  21.6 0.0 collective-permute-done.13.partner_ref
  21.6 10.4 %shard_map.65 = bf16[1,48,64,128]{3,2,1,0:T(8,128)(2,1)} custom-call(s32[2]{0:T(128)} %pad_add_fusion.place_ref, bf16[1,64,64,128]{3,2,1,0:T(8,128)(2,1)} %bitcast.38, bf16[1,11,64,128]{3,2,1,0:T(8,128)(2,1)} %shard_map.59.own_ref, bf16[1,11,64,128]{3,2,1,0:T(8,128)(2,1)} %collective-permute-done.13.partner_ref, ...), custom_call_target="tpu_custom_call" | custom-call | flops 9600000000 | bytes 28800000 | tf_op jit(solution)/shard_map/pallas_call | solution.py:214
  32.0 1.7 %collective-permute-start.15 = (bf16[48,64,128]{2,1,0:T(8,128)(2,1)}, bf16[48,64,128]{2,1,0:T(8,128)(2,1)}, u32[]{:S(2)}, u32[]{:S(2)}) collective-permute-start(bf16[48,64,128]{2,1,0:T(8,128)(2,1)} %bitcast.39), channel_id=1, source_target_pairs={{0,2},{1,3},{2,4},{3,5},{4,6},{5,7},{6,0},{7,1},{8,10},{9,11},{10,... | collective-permute-start | bytes 2359304 | tf_op jit(solution)/shard_map/ppermute | solution.py:447
  33.7 1.7 %slice_bitcast_fusion.3 = (bf16[6,64,128]{2,1,0:T(8,128)(2,1)S(1)}, bf16[6,64,128]{2,1,0:T(8,128)(2,1)}, bf16[6,64,128]{2,1,0:T(8,128)(2,1)}, bf16[6,64,128]{2,1,0:T(8,128)(2,1)S(1)}) fusion(bf16[2,6,64,128]{3,2,1,0:T(8,128)(2,1)} %collective-permute-done.1, bf16[2,6,64,128]{3,2,1,0:T(8,128)(2,1)} %collective-permute-done), kind=kLoop, calls=%fused_computation.9 | loop fusion | bytes 786432 | tf_op jit(solution)/shard_map/squeeze | solution.py:429
  35.4 1.0 maximum_bitcast_fusion.1
  36.5 0.9 pad_maximum_fusion.x_ref
  37.3 2.2 %shard_map.62.own_ref = bf16[2,6,64,128]{3,2,1,0:T(8,128)(2,1)} custom-call(bf16[2,20,64,128]{3,2,1,0:T(8,128)(2,1)} %pad_maximum_fusion.x_ref), custom_call_target="tpu_custom_call" | custom-call | flops 2000000000 | bytes 6000000 | tf_op jit(solution)/shard_map/pallas_call | solution.py:54
  39.5 0.1 collective-permute-start.4
  39.6 1.3 collective-permute-start.5
  40.9 0.4 collective-permute-done.4.partner_ref
  41.3 8.5 %shard_map.63 = bf16[2,8,64,128]{3,2,1,0:T(8,128)(2,1)} custom-call(s32[2]{0:T(128)} %pad_add_fusion.place_ref, bf16[2,20,64,128]{3,2,1,0:T(8,128)(2,1)} %pad_maximum_fusion.x_ref, bf16[2,6,64,128]{3,2,1,0:T(8,128)(2,1)} %shard_map.62.own_ref, bf16[2,6,64,128]{3,2,1,0:T(8,128)(2,1)} %collective-permute-done.4.partner_ref, ...), custom_call_target="tpu_custom_call" | custom-call | flops 3200000000 | bytes 9600000 | tf_op jit(solution)/shard_map/pallas_call | solution.py:214
  49.8 15.9 %collective-permute-start.6 = (bf16[16,64,128]{2,1,0:T(8,128)(2,1)}, bf16[16,64,128]{2,1,0:T(8,128)(2,1)}, u32[]{:S(2)}, u32[]{:S(2)}) collective-permute-start(bf16[16,64,128]{2,1,0:T(8,128)(2,1)} %bitcast.42), channel_id=1, source_target_pairs={{0,2},{1,3},{2,4},{3,5},{4,6},{5,7},{6,0},{7,1},{8,10},{9,11},{10,... | collective-permute-start | bytes 786440 | tf_op jit(solution)/shard_map/ppermute | solution.py:447
  65.7 0.3 collective-permute-start.16
  66.0 1.3 slice_bitcast_fusion
  67.4 1.2 maximum_bitcast_fusion.x_ref
  68.6 3.6 %collective-permute-done.6.refs_2_ = bf16[16,64,128]{2,1,0:T(8,128)(2,1)} collective-permute-done((bf16[16,64,128]{2,1,0:T(8,128)(2,1)}, bf16[16,64,128]{2,1,0:T(8,128)(2,1)}, u32[]{:S(2)}, u32[]{:S(2)}) %collective-permute-start.6) | collective-permute-done | bytes 262176 | tf_op jit(solution)/shard_map/ppermute | solution.py:447
  72.2 4.0 %collective-permute-start.7 = (bf16[16,64,128]{2,1,0:T(8,128)(2,1)}, bf16[16,64,128]{2,1,0:T(8,128)(2,1)}, u32[]{:S(2)}, u32[]{:S(2)}) collective-permute-start(bf16[16,64,128]{2,1,0:T(8,128)(2,1)} %collective-permute-done.6.refs_2_), channel_id=1, source_target_pairs={{0,2},{1,3},{2,4},{3,5},{4,6},{5,7},{6,0},{7,1},{8,10},{9,11},{10,... | collective-permute-start | bytes 786440 | tf_op jit(solution)/shard_map/ppermute | solution.py:447
  76.2 2.5 %shard_map.60.own_ref = bf16[1,13,64,128]{3,2,1,0:T(8,128)(2,1)} custom-call(bf16[1,76,64,128]{3,2,1,0:T(8,128)(2,1)} %maximum_bitcast_fusion.x_ref), custom_call_target="tpu_custom_call" | custom-call | flops 2000000000 | bytes 6000000 | tf_op jit(solution)/shard_map/pallas_call | solution.py:54
  78.7 0.5 collective-permute-start.10
  79.2 13.7 %collective-permute-done.7.refs_4_ = bf16[16,64,128]{2,1,0:T(8,128)(2,1)} collective-permute-done((bf16[16,64,128]{2,1,0:T(8,128)(2,1)}, bf16[16,64,128]{2,1,0:T(8,128)(2,1)}, u32[]{:S(2)}, u32[]{:S(2)}) %collective-permute-start.7) | collective-permute-done | bytes 262176 | tf_op jit(solution)/shard_map/ppermute | solution.py:447
  92.9 1.4 collective-permute-start.12
  94.3 1.3 collective-permute-start.3
  95.7 6.2 %collective-permute-start.19 = (bf16[48,64,128]{2,1,0:T(8,128)(2,1)}, bf16[48,64,128]{2,1,0:T(8,128)(2,1)}, u32[]{:S(2)}, u32[]{:S(2)}) collective-permute-start(bf16[48,64,128]{2,1,0:T(8,128)(2,1)} %bitcast.40), channel_id=1, source_target_pairs={{0,1},{1,0},{2,3},{3,2},{4,5},{5,4},{6,7},{7,6},{8,9},{9,8},{10,11... | collective-permute-start | bytes 2359304 | tf_op jit(solution)/shard_map/ppermute | solution.py:442
  101.9 1.8 %collective-permute-start.8 = (bf16[16,64,128]{2,1,0:T(8,128)(2,1)}, bf16[16,64,128]{2,1,0:T(8,128)(2,1)}, u32[]{:S(2)}, u32[]{:S(2)}) collective-permute-start(bf16[16,64,128]{2,1,0:T(8,128)(2,1)} %collective-permute-done.7.refs_4_), channel_id=1, source_target_pairs={{0,2},{1,3},{2,4},{3,5},{4,6},{5,7},{6,0},{7,1},{8,10},{9,11},{10,... | collective-permute-start | bytes 786440 | tf_op jit(solution)/shard_map/ppermute | solution.py:447
  103.7 0.8 collective-permute-start.20
  104.5 0.1 collective-permute-start.21
  104.6 1.5 %collective-permute-start.17 = (bf16[48,64,128]{2,1,0:T(8,128)(2,1)}, bf16[48,64,128]{2,1,0:T(8,128)(2,1)}, u32[]{:S(2)}, u32[]{:S(2)}) collective-permute-start(bf16[48,64,128]{2,1,0:T(8,128)(2,1)} %collective-permute-done.16.refs_4_), channel_id=1, source_target_pairs={{0,2},{1,3},{2,4},{3,5},{4,6},{5,7},{6,0},{7,1},{8,10},{9,11},{10,... | collective-permute-start | bytes 2359304 | tf_op jit(solution)/shard_map/ppermute | solution.py:447
  106.1 12.6 %shard_map.61 = bf16[1,64,64,128]{3,2,1,0:T(8,128)(2,1)} custom-call(s32[2]{0:T(128)} %pad_add_fusion.place_ref, bf16[1,76,64,128]{3,2,1,0:T(8,128)(2,1)} %maximum_bitcast_fusion.x_ref, bf16[1,13,64,128]{3,2,1,0:T(8,128)(2,1)} %shard_map.60.own_ref, bf16[1,13,64,128]{3,2,1,0:T(8,128)(2,1)} %collective-permute-done.2.partner_ref, ...), custom_call_target="tpu_custom_call" | custom-call | flops 12800000000 | bytes 38400000 | tf_op jit(solution)/shard_map/pallas_call | solution.py:214
  118.7 0.6 collective-permute-start.9
  119.2 5.0 %shard_map.64.acc_in_ref = f32[16,128,128]{2,1,0:T(8,128)} custom-call(s32[2]{0:T(128)} %pad_add_fusion.place_ref, s32[2,8]{1,0:T(2,128)} %bitcast.45, bf16[64,64,128]{2,1,0:T(8,128)(2,1)} %bitcast.49, bf16[16,64,128]{2,1,0:T(8,128)(2,1)} %bitcast.44, bf16[16,64,128]{2,1,0:T(8,128)(2,1)} %collective-permute-done.10.refs_1_, ...), custom_call_target="tpu_custom_call" | custom-call | flops 3000000000 | bytes 9000000 | tf_op jit(solution)/shard_map/pallas_call | solution.py:330
  124.3 2.6 %collective-permute-done.17.mine_ref = bf16[48,64,128]{2,1,0:T(8,128)(2,1)} collective-permute-done((bf16[48,64,128]{2,1,0:T(8,128)(2,1)}, bf16[48,64,128]{2,1,0:T(8,128)(2,1)}, u32[]{:S(2)}, u32[]{:S(2)}) %collective-permute-start.17) | collective-permute-done | bytes 786464 | tf_op jit(solution)/shard_map/ppermute | solution.py:447
  126.8 1.0 collective-permute-start.18
  127.8 11.4 %shard_map.66.acc_in_ref = f32[48,128,128]{2,1,0:T(8,128)} custom-call(s32[2]{0:T(128)} %pad_add_fusion.place_ref, s32[2,8]{1,0:T(2,128)} %bitcast.46, bf16[64,64,128]{2,1,0:T(8,128)(2,1)} %bitcast.50, bf16[48,64,128]{2,1,0:T(8,128)(2,1)} %bitcast.41, bf16[48,64,128]{2,1,0:T(8,128)(2,1)} %collective-permute-done.19.refs_1_, ...), custom_call_target="tpu_custom_call" | custom-call | flops 8999999488 | bytes 27000000 | tf_op jit(solution)/shard_map/pallas_call | solution.py:330
  139.2 7.5 %shard_map.67 = (bf16[64,64,128]{2,1,0:T(8,128)(2,1)}, f32[64,128]{1,0:T(8,128)}) custom-call(s32[2]{0:T(128)} %pad_add_fusion.place_ref, s32[2,8]{1,0:T(2,128)} %bitcast.47, bf16[64,64,128]{2,1,0:T(8,128)(2,1)} %bitcast.51, bf16[48,64,128]{2,1,0:T(8,128)(2,1)} %collective-permute-done.17.mine_ref, bf16[48,64,128]{2,1,0:T(8,128)(2,1)} %collective-permute-done.18.theirs_ref, ...), custom_call_target="tpu_custom_call" | custom-call | flops 6000000000 | bytes 18000000 | tf_op jit(solution)/shard_map/pallas_call | solution.py:354
  146.7 3.0 %shard_map.68 = (bf16[64,64,128]{2,1,0:T(8,128)(2,1)}, f32[64,128]{1,0:T(8,128)}) custom-call(s32[2]{0:T(128)} %pad_add_fusion.place_ref, s32[2,8]{1,0:T(2,128)} %bitcast.48, bf16[64,64,128]{2,1,0:T(8,128)(2,1)} %bitcast.52, bf16[16,64,128]{2,1,0:T(8,128)(2,1)} %collective-permute-done.8.mine_ref, ...), custom_call_target="tpu_custom_call", output_to_operand_aliasing={{0}: (6, {}), {1}: (7, {})} | custom-call | flops 2000000000 | bytes 6000000 | tf_op jit(solution)/shard_map/pallas_call | solution.py:354
  (27 shorter events, 0.1 us)
Async XLA Ops:
  0.6 1.2 slice-start
  5.8 15.8 %collective-permute-start.13 = (bf16[1,11,64,128]{3,2,1,0:T(8,128)(2,1)}, bf16[1,11,64,128]{3,2,1,0:T(8,128)(2,1)}, u32[]{:S(2)}, u32[]{:S(2)}) collective-permute-start(bf16[1,11,64,128]{3,2,1,0:T(8,128)(2,1)} %shard_map.59.own_ref), channel_id=1, source_target_pairs={{0,1},{1,0},{2,3},{3,2},{4,5},{5,4},{6,7},{7,6},{8,9},{9,8},{10,11... | collective-permute-start | bytes 540680 | tf_op jit(solution)/shard_map/ppermute | solution.py:406
  6.5 15.1 %collective-permute-start.14 = (bf16[1,11,64,128]{3,2,1,0:T(8,128)(2,1)}, bf16[1,11,64,128]{3,2,1,0:T(8,128)(2,1)}, u32[]{:S(2)}, u32[]{:S(2)}) collective-permute-start(bf16[1,11,64,128]{3,2,1,0:T(8,128)(2,1)} %shard_map.59.own_ref), channel_id=1, source_target_pairs={{1,2},{3,4},{5,6},{2,1},{4,3},{6,5},{9,10},{11,12},{13,14},{10,9},... | collective-permute-start | bytes 540680 | tf_op jit(solution)/shard_map/ppermute | solution.py:405
  10.8 1.3 copy-start
  12.9 20.8 %collective-permute-start = (bf16[2,6,64,128]{3,2,1,0:T(8,128)(2,1)}, bf16[2,6,64,128]{3,2,1,0:T(8,128)(2,1)}, u32[]{:S(2)}, u32[]{:S(2)}) collective-permute-start(bf16[2,6,64,128]{3,2,1,0:T(8,128)(2,1)} %get-tuple-element.13), channel_id=1, source_target_pairs={{0,8},{8,16},{16,24},{1,9},{9,17},{17,25},{2,10},{10,18},{18,26},{... | collective-permute-start | bytes 589832 | tf_op jit(solution)/shard_map/ppermute | solution.py:421
  16.0 17.7 %collective-permute-start.1 = (bf16[2,6,64,128]{3,2,1,0:T(8,128)(2,1)}, bf16[2,6,64,128]{3,2,1,0:T(8,128)(2,1)}, u32[]{:S(2)}, u32[]{:S(2)}) collective-permute-start(bf16[2,6,64,128]{3,2,1,0:T(8,128)(2,1)} %get-tuple-element.12), channel_id=1, source_target_pairs={{8,0},{16,8},{24,16},{9,1},{17,9},{25,17},{10,2},{18,10},{26,18},{... | collective-permute-start | bytes 589832 | tf_op jit(solution)/shard_map/ppermute | solution.py:422
  32.0 4.4 %copy-start.1 = (bf16[14,64,128]{2,1,0:T(8,128)(2,1)S(1)}, bf16[14,64,128]{2,1,0:T(8,128)(2,1)}, u32[]{:S(2)}) copy-start(bf16[14,64,128]{2,1,0:T(8,128)(2,1)} %get-tuple-element.15) | copy-start | bytes 688132
  32.0 33.8 %collective-permute-start.15 = (bf16[48,64,128]{2,1,0:T(8,128)(2,1)}, bf16[48,64,128]{2,1,0:T(8,128)(2,1)}, u32[]{:S(2)}, u32[]{:S(2)}) collective-permute-start(bf16[48,64,128]{2,1,0:T(8,128)(2,1)} %bitcast.39), channel_id=1, source_target_pairs={{0,2},{1,3},{2,4},{3,5},{4,6},{5,7},{6,0},{7,1},{8,10},{9,11},{10,... | collective-permute-start | bytes 2359304 | tf_op jit(solution)/shard_map/ppermute | solution.py:447
  39.5 1.8 %collective-permute-start.4 = (bf16[2,6,64,128]{3,2,1,0:T(8,128)(2,1)}, bf16[2,6,64,128]{3,2,1,0:T(8,128)(2,1)}, u32[]{:S(2)}, u32[]{:S(2)}) collective-permute-start(bf16[2,6,64,128]{3,2,1,0:T(8,128)(2,1)} %shard_map.62.own_ref), channel_id=1, source_target_pairs={{0,1},{1,0},{2,3},{3,2},{4,5},{5,4},{6,7},{7,6},{8,9},{9,8},{10,11... | collective-permute-start | bytes 589832 | tf_op jit(solution)/shard_map/ppermute | solution.py:406
  39.6 1.7 %collective-permute-start.5 = (bf16[2,6,64,128]{3,2,1,0:T(8,128)(2,1)}, bf16[2,6,64,128]{3,2,1,0:T(8,128)(2,1)}, u32[]{:S(2)}, u32[]{:S(2)}) collective-permute-start(bf16[2,6,64,128]{3,2,1,0:T(8,128)(2,1)} %shard_map.62.own_ref), channel_id=1, source_target_pairs={{1,2},{3,4},{5,6},{2,1},{4,3},{6,5},{9,10},{11,12},{13,14},{10,9},... | collective-permute-start | bytes 589832 | tf_op jit(solution)/shard_map/ppermute | solution.py:405
  49.8 17.5 %copy-start.2 = (bf16[6,64,128]{2,1,0:T(8,128)(2,1)S(1)}, bf16[6,64,128]{2,1,0:T(8,128)(2,1)}, u32[]{:S(2)}) copy-start(bf16[6,64,128]{2,1,0:T(8,128)(2,1)} %get-tuple-element.21) | copy-start | bytes 294916
  49.8 17.5 %copy-start.3 = (bf16[6,64,128]{2,1,0:T(8,128)(2,1)S(1)}, bf16[6,64,128]{2,1,0:T(8,128)(2,1)}, u32[]{:S(2)}) copy-start(bf16[6,64,128]{2,1,0:T(8,128)(2,1)} %get-tuple-element.22) | copy-start | bytes 294916
  49.8 22.4 %collective-permute-start.6 = (bf16[16,64,128]{2,1,0:T(8,128)(2,1)}, bf16[16,64,128]{2,1,0:T(8,128)(2,1)}, u32[]{:S(2)}, u32[]{:S(2)}) collective-permute-start(bf16[16,64,128]{2,1,0:T(8,128)(2,1)} %bitcast.42), channel_id=1, source_target_pairs={{0,2},{1,3},{2,4},{3,5},{4,6},{5,7},{6,0},{7,1},{8,10},{9,11},{10,... | collective-permute-start | bytes 786440 | tf_op jit(solution)/shard_map/ppermute | solution.py:447
  65.7 38.7 %collective-permute-start.16 = (bf16[48,64,128]{2,1,0:T(8,128)(2,1)}, bf16[48,64,128]{2,1,0:T(8,128)(2,1)}, u32[]{:S(2)}, u32[]{:S(2)}) collective-permute-start(bf16[48,64,128]{2,1,0:T(8,128)(2,1)} %collective-permute-done.15.refs_2_), channel_id=1, source_target_pairs={{0,2},{1,3},{2,4},{3,5},{4,6},{5,7},{6,0},{7,1},{8,10},{9,11},{10,... | collective-permute-start | bytes 2359304 | tf_op jit(solution)/shard_map/ppermute | solution.py:447
  72.2 20.7 %collective-permute-start.7 = (bf16[16,64,128]{2,1,0:T(8,128)(2,1)}, bf16[16,64,128]{2,1,0:T(8,128)(2,1)}, u32[]{:S(2)}, u32[]{:S(2)}) collective-permute-start(bf16[16,64,128]{2,1,0:T(8,128)(2,1)} %collective-permute-done.6.refs_2_), channel_id=1, source_target_pairs={{0,2},{1,3},{2,4},{3,5},{4,6},{5,7},{6,0},{7,1},{8,10},{9,11},{10,... | collective-permute-start | bytes 786440 | tf_op jit(solution)/shard_map/ppermute | solution.py:447
  78.7 15.7 %collective-permute-start.2 = (bf16[1,13,64,128]{3,2,1,0:T(8,128)(2,1)}, bf16[1,13,64,128]{3,2,1,0:T(8,128)(2,1)}, u32[]{:S(2)}, u32[]{:S(2)}) collective-permute-start(bf16[1,13,64,128]{3,2,1,0:T(8,128)(2,1)} %shard_map.60.own_ref), channel_id=1, source_target_pairs={{0,1},{1,0},{2,3},{3,2},{4,5},{5,4},{6,7},{7,6},{8,9},{9,8},{10,11... | collective-permute-start | bytes 638984 | tf_op jit(solution)/shard_map/ppermute | solution.py:406
  78.7 23.3 %collective-permute-start.10 = (bf16[16,64,128]{2,1,0:T(8,128)(2,1)}, bf16[16,64,128]{2,1,0:T(8,128)(2,1)}, u32[]{:S(2)}, u32[]{:S(2)}) collective-permute-start(bf16[16,64,128]{2,1,0:T(8,128)(2,1)} %bitcast.43), channel_id=1, source_target_pairs={{0,1},{1,0},{2,3},{3,2},{4,5},{5,4},{6,7},{7,6},{8,9},{9,8},{10,11... | collective-permute-start | bytes 786440 | tf_op jit(solution)/shard_map/ppermute | solution.py:442
  79.2 24.5 %collective-permute-start.11 = (bf16[16,64,128]{2,1,0:T(8,128)(2,1)}, bf16[16,64,128]{2,1,0:T(8,128)(2,1)}, u32[]{:S(2)}, u32[]{:S(2)}) collective-permute-start(bf16[16,64,128]{2,1,0:T(8,128)(2,1)} %collective-permute-done.6.refs_2_), channel_id=1, source_target_pairs={{0,1},{1,0},{2,3},{3,2},{4,5},{5,4},{6,7},{7,6},{8,9},{9,8},{10,11... | collective-permute-start | bytes 786440 | tf_op jit(solution)/shard_map/ppermute | solution.py:442
  92.9 11.7 %collective-permute-start.12 = (bf16[16,64,128]{2,1,0:T(8,128)(2,1)}, bf16[16,64,128]{2,1,0:T(8,128)(2,1)}, u32[]{:S(2)}, u32[]{:S(2)}) collective-permute-start(bf16[16,64,128]{2,1,0:T(8,128)(2,1)} %collective-permute-done.7.refs_4_), channel_id=1, source_target_pairs={{0,1},{1,0},{2,3},{3,2},{4,5},{5,4},{6,7},{7,6},{8,9},{9,8},{10,11... | collective-permute-start | bytes 786440 | tf_op jit(solution)/shard_map/ppermute | solution.py:442
  94.3 1.3 collective-permute-start.3
  95.7 32.1 %collective-permute-start.19 = (bf16[48,64,128]{2,1,0:T(8,128)(2,1)}, bf16[48,64,128]{2,1,0:T(8,128)(2,1)}, u32[]{:S(2)}, u32[]{:S(2)}) collective-permute-start(bf16[48,64,128]{2,1,0:T(8,128)(2,1)} %bitcast.40), channel_id=1, source_target_pairs={{0,1},{1,0},{2,3},{3,2},{4,5},{5,4},{6,7},{7,6},{8,9},{9,8},{10,11... | collective-permute-start | bytes 2359304 | tf_op jit(solution)/shard_map/ppermute | solution.py:442
  101.9 16.8 %collective-permute-start.8 = (bf16[16,64,128]{2,1,0:T(8,128)(2,1)}, bf16[16,64,128]{2,1,0:T(8,128)(2,1)}, u32[]{:S(2)}, u32[]{:S(2)}) collective-permute-start(bf16[16,64,128]{2,1,0:T(8,128)(2,1)} %collective-permute-done.7.refs_4_), channel_id=1, source_target_pairs={{0,2},{1,3},{2,4},{3,5},{4,6},{5,7},{6,0},{7,1},{8,10},{9,11},{10,... | collective-permute-start | bytes 786440 | tf_op jit(solution)/shard_map/ppermute | solution.py:447
  103.7 24.1 %collective-permute-start.20 = (bf16[48,64,128]{2,1,0:T(8,128)(2,1)}, bf16[48,64,128]{2,1,0:T(8,128)(2,1)}, u32[]{:S(2)}, u32[]{:S(2)}) collective-permute-start(bf16[48,64,128]{2,1,0:T(8,128)(2,1)} %collective-permute-done.15.refs_2_), channel_id=1, source_target_pairs={{0,1},{1,0},{2,3},{3,2},{4,5},{5,4},{6,7},{7,6},{8,9},{9,8},{10,11... | collective-permute-start | bytes 2359304 | tf_op jit(solution)/shard_map/ppermute | solution.py:442
  104.5 23.3 %collective-permute-start.21 = (bf16[48,64,128]{2,1,0:T(8,128)(2,1)}, bf16[48,64,128]{2,1,0:T(8,128)(2,1)}, u32[]{:S(2)}, u32[]{:S(2)}) collective-permute-start(bf16[48,64,128]{2,1,0:T(8,128)(2,1)} %collective-permute-done.16.refs_4_), channel_id=1, source_target_pairs={{0,1},{1,0},{2,3},{3,2},{4,5},{5,4},{6,7},{7,6},{8,9},{9,8},{10,11... | collective-permute-start | bytes 2359304 | tf_op jit(solution)/shard_map/ppermute | solution.py:442
  104.6 22.3 %collective-permute-start.17 = (bf16[48,64,128]{2,1,0:T(8,128)(2,1)}, bf16[48,64,128]{2,1,0:T(8,128)(2,1)}, u32[]{:S(2)}, u32[]{:S(2)}) collective-permute-start(bf16[48,64,128]{2,1,0:T(8,128)(2,1)} %collective-permute-done.16.refs_4_), channel_id=1, source_target_pairs={{0,2},{1,3},{2,4},{3,5},{4,6},{5,7},{6,0},{7,1},{8,10},{9,11},{10,... | collective-permute-start | bytes 2359304 | tf_op jit(solution)/shard_map/ppermute | solution.py:447
  118.7 28.0 %collective-permute-start.9 = (bf16[16,64,128]{2,1,0:T(8,128)(2,1)}, bf16[16,64,128]{2,1,0:T(8,128)(2,1)}, u32[]{:S(2)}, u32[]{:S(2)}) collective-permute-start(bf16[16,64,128]{2,1,0:T(8,128)(2,1)} %collective-permute-done.8.mine_ref), channel_id=1, source_target_pairs={{0,1},{1,0},{2,3},{3,2},{4,5},{5,4},{6,7},{7,6},{8,9},{9,8},{10,11... | collective-permute-start | bytes 786440 | tf_op jit(solution)/shard_map/ppermute | solution.py:442
  126.8 12.4 %collective-permute-start.18 = (bf16[48,64,128]{2,1,0:T(8,128)(2,1)}, bf16[48,64,128]{2,1,0:T(8,128)(2,1)}, u32[]{:S(2)}, u32[]{:S(2)}) collective-permute-start(bf16[48,64,128]{2,1,0:T(8,128)(2,1)} %collective-permute-done.17.mine_ref), channel_id=1, source_target_pairs={{0,1},{1,0},{2,3},{3,2},{4,5},{5,4},{6,7},{7,6},{8,9},{9,8},{10,11... | collective-permute-start | bytes 2359304 | tf_op jit(solution)/shard_map/ppermute | solution.py:442

commit v3 on v2

--- a/solution.py
+++ b/solution.py
@@ -31,16 +31,59 @@
     )
 
 
-def pack_kernel(x_ref, edge_ref, *, groups, spacing, offset):
+def cost(microseconds):
+    return pl.CostEstimate(
+        flops=int(microseconds * 1e9), transcendentals=0, bytes_accessed=int(microseconds * 3e6)
+    )
+
+
+def rows_kernel(place_ref, image_ref, above_ref, below_ref, x_ref, *, last_row):
+    rows = image_ref.shape[1]
+    held = above_ref.shape[1]
+    inside_above = (place_ref[0] > 0).astype(jnp.float32)
+    inside_below = (place_ref[0] < last_row).astype(jnp.float32)
+
+    def turned(piece, keep):
+        piece = jnp.swapaxes(piece, 0, 1)
+        return (piece.astype(jnp.float32) * keep).astype(jnp.bfloat16)
+
+    x_ref[0:REACH] = turned(above_ref[...], inside_above)[held - REACH :]
+    for start in range(0, rows, 16):
+        x_ref[REACH + start : REACH + start + 16] = jnp.swapaxes(image_ref[:, start : start + 16], 0, 1)
+    x_ref[REACH + rows :] = turned(below_ref[...], inside_below)[:REACH]
+
+
+def with_rows(place, images, above, below, row_count):
+    count, channels, rows, segment = images.shape
+    held = above.shape[2]
+
+    def image_of(extent):
+        return pl.BlockSpec((None, channels, extent, segment), lambda n: (n, 0, 0, 0))
+
+    all_rows = rows + 2 * REACH
+    return pl.pallas_call(
+        functools.partial(rows_kernel, last_row=row_count - 1),
+        out_shape=jax.ShapeDtypeStruct((count, all_rows, channels, segment), jnp.bfloat16),
+        grid=(count,),
+        in_specs=[pl.BlockSpec(memory_space=pltpu.SMEM), image_of(rows), image_of(held), image_of(held)],
+        out_specs=pl.BlockSpec((None, all_rows, channels, segment), lambda n: (n, 0, 0, 0)),
+        compiler_params=pltpu.CompilerParams(vmem_limit_bytes=VMEM_LIMIT),
+        cost_estimate=cost(3),
+        name="with_rows",
+    )(place, images, above, below)
+
+
+def pack_into(x_ref, edge_ref, base, rows, first):
     channels, segment = x_ref.shape[1:]
     slot_of = lane_iota((channels, segment)) // SLOT
-    for q in range(edge_ref.shape[0]):
+    spacing, steps = edge_steps(rows, segment)
+    for q in range(steps):
         packed = None
-        for g in range(groups):
+        for g in range(segment // SLOT):
             shift = (SLOT * g + SLOT // 2) % segment
-            moved = pltpu.roll(x_ref[offset + g * spacing + q], shift, 1)
+            moved = pltpu.roll(x_ref[first + g * spacing + q], shift, 1)
             packed = moved if packed is None else jnp.where(slot_of == g, moved, packed)
-        edge_ref[q] = packed
+        edge_ref[base + q] = packed
 
 
 def edge_steps(rows, segment):
@@ -48,26 +91,39 @@
     return spacing, spacing + 2 * FIRST_DILATION
 
 
-def pack_edges(x, rows, offset):
-    parts, held, channels, segment = x.shape
-    spacing, steps = edge_steps(rows, segment)
+def pack_kernel(*refs, chunks):
+    edge_ref = refs[-1]
+    base = 0
+    for index, rows, first in chunks:
+        pack_into(refs[index], edge_ref, base, rows, first)
+        base += edge_steps(rows, edge_ref.shape[2])[1]
+
+
+def pack_edges(sources, chunks):
+    channels, segment = sources[0][0].shape[2:]
+    total = sum(edge_steps(rows, segment)[1] for _, rows, _ in chunks)
+
+    def image_of(a, n):
+        return pl.BlockSpec((None,) + a.shape[1:], lambda i: (n, 0, 0, 0))
+
     return pl.pallas_call(
-        functools.partial(pack_kernel, groups=segment // SLOT, spacing=spacing, offset=offset),
-        out_shape=jax.ShapeDtypeStruct((parts, steps, channels, segment), jnp.bfloat16),
-        grid=(parts,),
-        in_specs=[pl.BlockSpec((None, held, channels, segment), lambda n: (n, 0, 0, 0))],
-        out_specs=pl.BlockSpec((None, steps, channels, segment), lambda n: (n, 0, 0, 0)),
+        functools.partial(pack_kernel, chunks=chunks),
+        out_shape=jax.ShapeDtypeStruct((total, channels, segment), jnp.bfloat16),
+        grid=(1,),
+        in_specs=[image_of(a, n) for a, n in sources],
+        out_specs=pl.BlockSpec((total, channels, segment), lambda i: (0, 0, 0)),
         compiler_params=pltpu.CompilerParams(vmem_limit_bytes=VMEM_LIMIT),
         cost_estimate=cost(2),
-    )(x)
+    )(*[a for a, _ in sources])
 
 
 def feature_kernel(
     place_ref, x_ref, own_ref, partner_ref, cross_ref, w1_ref, w2_ref, unit_ref,
     w_ref, edge_ref, side_ref, p1_ref, p1e_ref, hid_ref, hide_ref, p2_ref, rhs0_ref, rhs1_ref,
-    *, spacing, offset, ends, mesh_shape,
+    *, spacing, offset, apart, ends, mesh_shape,
 ):
     part = pl.program_id(0)
+    offset = offset + part * apart
     rows = unit_ref.shape[0]
     channels, segment = x_ref.shape[1:]
     first_row, last_row = place_ref[0] == 0, place_ref[0] == mesh_shape[0] - 1
@@ -194,16 +250,13 @@
     lax.fori_loop(0, rows // 8, finish, 0)
 
 
-def unit_features(place, x, rows, offset, ends, edges, w1, w2, mesh_shape):
-    parts, _, channels, segment = x.shape
+def unit_features(place, x, index, parts, rows, offset, apart, ends, edges, edge_block, w1, w2, mesh_shape):
+    _, held, channels, segment = x.shape
     all_rows = rows + 2 * REACH
     hidden_rows = rows + 2 * SECOND_DILATION
     spacing, steps = edge_steps(rows, segment)
     width = 8
 
-    def part_of(a):
-        return pl.BlockSpec((None,) + a.shape[1:], lambda i: (i, 0, 0, 0))
-
     def whole(a):
         return pl.BlockSpec(a.shape, lambda i: (0,) * a.ndim)
 
@@ -213,14 +266,17 @@
     products = (3 * channels, segment)
     return pl.pallas_call(
         functools.partial(
-            feature_kernel, spacing=spacing, offset=offset, ends=ends, mesh_shape=mesh_shape
+            feature_kernel, spacing=spacing, offset=offset, apart=apart, ends=ends, mesh_shape=mesh_shape
         ),
-        out_shape=jax.ShapeDtypeStruct((parts, rows, channels, segment), jnp.bfloat16),
+        out_shape=jax.ShapeDtypeStruct((parts * rows, channels, segment), jnp.bfloat16),
         grid=(parts,),
-        in_specs=[pl.BlockSpec(memory_space=pltpu.SMEM)]
-        + [part_of(a) for a in (x, *edges)]
+        in_specs=[
+            pl.BlockSpec(memory_space=pltpu.SMEM),
+            pl.BlockSpec((None, held, channels, segment), lambda i: (index, 0, 0, 0)),
+        ]
+        + [pl.BlockSpec((pl.Element(steps), pl.Element(channels), pl.Element(segment)), lambda i: (edge_block + i * steps, 0, 0)) for _ in edges]
         + [whole(w1), whole(w2)],
-        out_specs=pl.BlockSpec((None, rows, channels, segment), lambda i: (i, 0, 0, 0)),
+        out_specs=pl.BlockSpec((rows, channels, segment), lambda i: (i, 0, 0)),
         scratch_shapes=[
             pltpu.VMEM((3 * channels, 3 * channels), jnp.bfloat16),
             pltpu.VMEM((steps, channels, segment), jnp.bfloat16),
@@ -390,51 +446,41 @@
     row_count = lax.axis_size("rows")
     col_count = lax.axis_size("cols")
     col = lax.axis_index("cols")
-    channels, rows, segment = images.shape[1:]
+    _, rows, segment = images.shape[1:]
     place = jnp.stack([lax.axis_index("rows"), col]).astype(jnp.int32)
     ranges = search_ranges.reshape(2, rows // RG)
 
     swap = [(i, i ^ 1) for i in range(col_count)]
     across = both_ways([(i, i + 1) for i in range(1, col_count - 1, 2)])
     hop = [(i, (i + 2) % col_count) for i in range(col_count)]
-    down = [(i, i + 1) for i in range(row_count - 1)]
+    down = [(i, (i + 1) % row_count) for i in range(row_count)]
     up = [(b, a) for a, b in down]
 
-    def exchanged(x, count, offset):
-        own = pack_edges(x, count, offset)
+    def exchanged(sources, chunks):
+        own = pack_edges(sources, chunks)
         cross = lax.ppermute(own, "cols", across)
         partner = lax.ppermute(own, "cols", swap)
         return own, partner, cross
 
-    def features(x, count, offset, ends, edges):
+    def features(x, index, parts, count, offset, apart, ends, edges, edge_block):
         return unit_features(
-            place, x, count, offset, ends, edges, first_weight, second_weight,
-            (row_count, col_count),
+            place, x, index, parts, count, offset, apart, ends, edges, edge_block,
+            first_weight, second_weight, (row_count, col_count),
         )
 
+    above = lax.ppermute(images[:, :, rows - RG :], "rows", down)
+    below = lax.ppermute(images[:, :, :RG], "rows", up)
+
     inner = rows - 2 * RG
-    right_rows = images[1].transpose(1, 0, 2)
-    edges_a = exchanged(right_rows[None], inner, RG - REACH)
-
-    later, edges_a = lax.optimization_barrier((images, edges_a[0])), edges_a
-    later = later[0]
-    top = lax.ppermute(later[:, :, rows - REACH :].transpose(0, 2, 1, 3), "rows", down)
-    bottom = lax.ppermute(later[:, :, :REACH].transpose(0, 2, 1, 3), "rows", up)
-    right_a = features(right_rows[None], inner, RG - REACH, False, edges_a)[0]
-
-    top, bottom, _ = lax.optimization_barrier((top, bottom, right_a[:1, :8]))
-    outer = jnp.stack(
-        [
-            jnp.concatenate([top[1], right_rows[: RG + REACH]]),
-            jnp.concatenate([right_rows[rows - RG - REACH :], bottom[1]]),
-        ]
-    )
-    edges_b = exchanged(outer, RG, 0)
-    right_b = features(outer, RG, 0, True, edges_b).reshape(2 * RG, channels, segment)
-
-    left_rows = jnp.concatenate([top[0], later[0].transpose(1, 0, 2), bottom[0]])[None]
-    edges_l = exchanged(left_rows, rows, 0)
-    left = features(left_rows, rows, 0, True, edges_l)[0]
+    right_rows = images[1].transpose(1, 0, 2)[None]
+    edges_a = exchanged([(right_rows, 0)], ((0, inner, RG - REACH),))
+    x = with_rows(place, images, above, below, row_count)
+    chunks = ((0, RG, 0), (0, RG, rows - RG), (1, rows, 0))
+    edges_r = exchanged([(x, 1), (x, 0)], chunks)
+
+    right_a = features(right_rows, 0, 1, inner, RG - REACH, 0, False, edges_a, 0)
+    right_b = features(x, 1, 2, RG, 0, rows - RG, True, edges_r, 0)
+    left = features(x, 0, 1, rows, 0, 0, True, edges_r, 2 * edge_steps(RG, segment)[1])
 
     steps = min(col_count // 2 - 1, HOPS // 2)
 

time: 151 us -> 137 us (0.907)
  the two profiles are of different devices: /device:TPU:29 before, /device:TPU:30 now
where the time goes in v3:
time: 137 us; the launch traced here: 136 us
  Pallas kernels  67.5 us (49%)
  waiting for transfers between devices  42 us (31%)
  starting transfers between devices  20.2 us (15%)
  local copies, waits for them, and re-layouts  5.38 us (4%)
    pallas_call x3, Pallas kernels, unit_features(): pl.pallas_call(functools.partial(feature_kernel, spacing=spacing, offset=...  31.9 us
    ppermute x6, waiting for transfers between devices, chain(): mine = lax.ppermute(mine, 'cols', hop)  28.5 us
    pallas_call x2, Pallas kernels, correlate(): pl.pallas_call(functools.partial(gather_kernel, inner=inner, groups=group...  15.3 us
    ppermute x2, waiting for transfers between devices, exchanged(): cross = lax.ppermute(own, 'cols', across)  13.4 us
    pallas_call x2, Pallas kernels, finish(): pl.pallas_call(functools.partial(finish_kernel, inner=inner, groups=group...  11.1 us
    ppermute x6, starting transfers between devices, chain(): mine = lax.ppermute(mine, 'cols', hop)  9.26 us
    pallas_call x2, Pallas kernels, pack_edges(): pl.pallas_call(functools.partial(pack_kernel, chunks=chunks), out_shape=j...  5.66 us
    ppermute x8, starting transfers between devices, pair(): return (mine, lax.ppermute(mine, 'cols', swap))  4.02 us
  transfers between devices with their start and end apart: 20, of which 4 were waited for; matrix products, arithmetic and copies ran while one was open for 2% of the time, Pallas kernels for 45%

profile of v3, /device:TPU:30, one launch (start us, length us, event | category | flops | bytes accessed | tf_op | source)
XLA Modules:
  0.0 136.3 jit_solution(14067447132229643697)
XLA Ops:
  0.6 0.0 slice-start
  0.6 1.2 slice-done
  1.9 1.6 %copy.11 = bf16[1,64,64,128]{3,1,2,0:T(8,128)(2,1)} copy(bf16[1,64,64,128]{3,2,1,0:T(8,128)(2,1)S(1)} %slice-done) | data formatting | bytes 2097152
  3.5 2.3 %shard_map.63.own_ref = bf16[11,64,128]{2,1,0:T(8,128)(2,1)} custom-call(bf16[1,64,64,128]{3,2,1,0:T(8,128)(2,1)} %bitcast.10), custom_call_target="tpu_custom_call" | custom-call | flops 2000000000 | bytes 6000000 | tf_op jit(solution)/shard_map/pallas_call | solution.py:109
  5.8 1.9 %collective-permute-start.12 = (bf16[11,64,128]{2,1,0:T(8,128)(2,1)}, bf16[11,64,128]{2,1,0:T(8,128)(2,1)}, u32[]{:S(2)}, u32[]{:S(2)}) collective-permute-start(bf16[11,64,128]{2,1,0:T(8,128)(2,1)} %shard_map.63.own_ref), channel_id=1, source_target_pairs={{1,2},{3,4},{5,6},{2,1},{4,3},{6,5},{9,10},{11,12},{13,14},{10,9},... | collective-permute-start | bytes 540680 | tf_op jit(solution)/shard_map/ppermute | solution.py:461
  7.8 0.1 collective-permute-start.11
  7.8 1.9 %fusion = (bf16[2,64,8,128]{3,2,1,0:T(8,128)(2,1)}, bf16[2,64,8,128]{3,2,1,0:T(8,128)(2,1)}) fusion(bf16[2,64,64,128]{3,2,1,0:T(8,128)(2,1)} %image_ref.1), kind=kLoop, calls=%fused_computation.2 | loop fusion | bytes 1048576 | tf_op jit(solution)/shard_map/slice | solution.py:472
  9.7 0.5 collective-permute-start.1
  10.2 2.4 %collective-permute-start = (bf16[2,64,8,128]{3,2,1,0:T(8,128)(2,1)}, bf16[2,64,8,128]{3,2,1,0:T(8,128)(2,1)}, u32[]{:S(2)}, u32[]{:S(2)}) collective-permute-start(bf16[2,64,8,128]{3,2,1,0:T(8,128)(2,1)} %get-tuple-element.7), channel_id=1, source_target_pairs={{0,8},{8,16},{16,24},{24,0},{1,9},{9,17},{17,25},{25,1},{2,10},{10... | collective-permute-start | bytes 786440 | tf_op jit(solution)/shard_map/ppermute | solution.py:471
  12.6 0.6 pad_add_fusion.place_ref
  13.2 0.0 collective-permute-done.11.partner_ref
  13.2 10.4 %shard_map.64.refs_0_ = bf16[48,64,128]{2,1,0:T(8,128)(2,1)} custom-call(s32[2]{0:T(128)} %pad_add_fusion.place_ref, bf16[1,64,64,128]{3,2,1,0:T(8,128)(2,1)} %bitcast.11, bf16[11,64,128]{2,1,0:T(8,128)(2,1)} %shard_map.63.own_ref, bf16[11,64,128]{2,1,0:T(8,128)(2,1)} %collective-permute-done.11.partner_ref, ...), custom_call_target="tpu_custom_call" | custom-call | flops 9600000000 | bytes 28800000 | tf_op jit(solution)/shard_map/pallas_call | solution.py:267
  23.6 1.9 %collective-permute-start.13 = (bf16[48,64,128]{2,1,0:T(8,128)(2,1)}, bf16[48,64,128]{2,1,0:T(8,128)(2,1)}, u32[]{:S(2)}, u32[]{:S(2)}) collective-permute-start(bf16[48,64,128]{2,1,0:T(8,128)(2,1)} %shard_map.64.refs_0_), channel_id=1, source_target_pairs={{0,2},{1,3},{2,4},{3,5},{4,6},{5,7},{6,0},{7,1},{8,10},{9,11},{10,... | collective-permute-start | bytes 2359304 | tf_op jit(solution)/shard_map/ppermute | solution.py:493
  25.5 0.0 collective-permute-done.1.below_ref
  25.5 0.0 collective-permute-done.above_ref
  25.5 3.5 %with_rows.1.refs_0_.refs_1_.x_ref = bf16[2,76,64,128]{3,2,1,0:T(8,128)(2,1)} custom-call(s32[2]{0:T(128)} %pad_add_fusion.place_ref, bf16[2,64,64,128]{3,2,1,0:T(8,128)(2,1)} %image_ref.1, bf16[2,64,8,128]{3,2,1,0:T(8,128)(2,1)} %collective-permute-done.above_ref, bf16[2,64,8,128]{3,2,1,0:T(8,128)(2,1)} %collective-permute-done.1.below_ref), custom_call_target="tpu_custom_call" | custom-call | flops 3000000000 | bytes 9000000 | tf_op jit(solution)/shard_map/with_rows/pallas_call | solution.py:64
  29.0 3.3 %shard_map.59.own_ref = bf16[25,64,128]{2,1,0:T(8,128)(2,1)} custom-call(bf16[2,76,64,128]{3,2,1,0:T(8,128)(2,1)} %with_rows.1.refs_0_.refs_1_.x_ref, bf16[2,76,64,128]{3,2,1,0:T(8,128)(2,1)} %with_rows.1.refs_0_.refs_1_.x_ref), custom_call_target="tpu_custom_call" | custom-call | flops 2000000000 | bytes 6000000 | tf_op jit(solution)/shard_map/pallas_call | solution.py:109
  32.3 1.9 %collective-permute-start.3 = (bf16[25,64,128]{2,1,0:T(8,128)(2,1)}, bf16[25,64,128]{2,1,0:T(8,128)(2,1)}, u32[]{:S(2)}, u32[]{:S(2)}) collective-permute-start(bf16[25,64,128]{2,1,0:T(8,128)(2,1)} %shard_map.59.own_ref), channel_id=1, source_target_pairs={{1,2},{3,4},{5,6},{2,1},{4,3},{6,5},{9,10},{11,12},{13,14},{10,9},... | collective-permute-start | bytes 1228808 | tf_op jit(solution)/shard_map/ppermute | solution.py:461
  34.2 0.1 collective-permute-start.2
  34.3 13.4 %collective-permute-done.3.cross_ref = bf16[25,64,128]{2,1,0:T(8,128)(2,1)} collective-permute-done((bf16[25,64,128]{2,1,0:T(8,128)(2,1)}, bf16[25,64,128]{2,1,0:T(8,128)(2,1)}, u32[]{:S(2)}, u32[]{:S(2)}) %collective-permute-start.3) | collective-permute-done | bytes 409632 | tf_op jit(solution)/shard_map/ppermute | solution.py:461
  47.7 0.0 collective-permute-done.2.partner_ref
  47.7 8.9 %shard_map.61.refs_0_ = bf16[16,64,128]{2,1,0:T(8,128)(2,1)} custom-call(s32[2]{0:T(128)} %pad_add_fusion.place_ref, bf16[2,76,64,128]{3,2,1,0:T(8,128)(2,1)} %with_rows.1.refs_0_.refs_1_.x_ref, bf16[25,64,128]{2,1,0:T(8,128)(2,1)} %shard_map.59.own_ref, bf16[25,64,128]{2,1,0:T(8,128)(2,1)} %collective-permute-done.2.partner_ref, ...), custom_call_target="tpu_custom_call" | custom-call | flops 3200000000 | bytes 9600000 | tf_op jit(solution)/shard_map/pallas_call | solution.py:267
  56.6 3.0 %collective-permute-start.14 = (bf16[48,64,128]{2,1,0:T(8,128)(2,1)}, bf16[48,64,128]{2,1,0:T(8,128)(2,1)}, u32[]{:S(2)}, u32[]{:S(2)}) collective-permute-start(bf16[48,64,128]{2,1,0:T(8,128)(2,1)} %collective-permute-done.13.refs_2_), channel_id=1, source_target_pairs={{0,2},{1,3},{2,4},{3,5},{4,6},{5,7},{6,0},{7,1},{8,10},{9,11},{10,... | collective-permute-start | bytes 2359304 | tf_op jit(solution)/shard_map/ppermute | solution.py:493
  59.6 6.4 %collective-permute-done.4.refs_2_ = bf16[16,64,128]{2,1,0:T(8,128)(2,1)S(1)} collective-permute-done((bf16[16,64,128]{2,1,0:T(8,128)(2,1)}, bf16[16,64,128]{2,1,0:T(8,128)(2,1)S(1)}, u32[]{:S(2)}, u32[]{:S(2)}) %collective-permute-start.4) | collective-permute-done | bytes 262176 | tf_op jit(solution)/shard_map/ppermute | solution.py:493
  66.0 0.6 collective-permute-start.5
  66.6 3.2 %collective-permute-start.8 = (bf16[16,64,128]{2,1,0:T(8,128)(2,1)}, bf16[16,64,128]{2,1,0:T(8,128)(2,1)S(1)}, u32[]{:S(2)}, u32[]{:S(2)}) collective-permute-start(bf16[16,64,128]{2,1,0:T(8,128)(2,1)} %shard_map.61.refs_0_), channel_id=1, source_target_pairs={{0,1},{1,0},{2,3},{3,2},{4,5},{5,4},{6,7},{7,6},{8,9},{9,8},{10,11... | collective-permute-start | bytes 786440 | tf_op jit(solution)/shard_map/ppermute | solution.py:488
  69.8 0.0 collective-permute-start.9
  69.8 17.6 %collective-permute-done.5.refs_4_ = bf16[16,64,128]{2,1,0:T(8,128)(2,1)} collective-permute-done((bf16[16,64,128]{2,1,0:T(8,128)(2,1)S(1)}, bf16[16,64,128]{2,1,0:T(8,128)(2,1)}, u32[]{:S(2)}, u32[]{:S(2)}) %collective-permute-start.5) | collective-permute-done | bytes 262176 | tf_op jit(solution)/shard_map/ppermute | solution.py:493
  87.5 0.5 collective-permute-start.17
  88.0 0.0 collective-permute-done.8.refs_1_
  88.0 0.1 collective-permute-start.18
  88.1 0.0 collective-permute-done.9.refs_3_
  88.1 0.6 copy-done.1
  88.7 2.2 %collective-permute-start.6 = (bf16[16,64,128]{2,1,0:T(8,128)(2,1)}, bf16[16,64,128]{2,1,0:T(8,128)(2,1)}, u32[]{:S(2)}, u32[]{:S(2)}) collective-permute-start(bf16[16,64,128]{2,1,0:T(8,128)(2,1)} %collective-permute-done.5.refs_4_), channel_id=1, source_target_pairs={{0,2},{1,3},{2,4},{3,5},{4,6},{5,7},{6,0},{7,1},{8,10},{9,11},{10,... | collective-permute-start | bytes 786440 | tf_op jit(solution)/shard_map/ppermute | solution.py:493
  90.9 0.0 collective-permute-done.14.refs_4_
  90.9 0.2 collective-permute-start.19
  91.2 0.0 collective-permute-done.10.refs_5_
  91.2 1.5 %collective-permute-start.15 = (bf16[48,64,128]{2,1,0:T(8,128)(2,1)}, bf16[48,64,128]{2,1,0:T(8,128)(2,1)}, u32[]{:S(2)}, u32[]{:S(2)}) collective-permute-start(bf16[48,64,128]{2,1,0:T(8,128)(2,1)} %collective-permute-done.14.refs_4_), channel_id=1, source_target_pairs={{0,2},{1,3},{2,4},{3,5},{4,6},{5,7},{6,0},{7,1},{8,10},{9,11},{10,... | collective-permute-start | bytes 2359304 | tf_op jit(solution)/shard_map/ppermute | solution.py:493
  92.7 12.6 %shard_map.60.left_ref = bf16[64,64,128]{2,1,0:T(8,128)(2,1)} custom-call(s32[2]{0:T(128)} %pad_add_fusion.place_ref, bf16[2,76,64,128]{3,2,1,0:T(8,128)(2,1)} %with_rows.1.refs_0_.refs_1_.x_ref, bf16[25,64,128]{2,1,0:T(8,128)(2,1)} %shard_map.59.own_ref, bf16[25,64,128]{2,1,0:T(8,128)(2,1)} %collective-permute-done.2.partner_ref, ...), custom_call_target="tpu_custom_call" | custom-call | flops 12800000000 | bytes 38400000 | tf_op jit(solution)/shard_map/pallas_call | solution.py:267
  105.3 4.5 %shard_map.62.acc_in_ref = f32[16,128,128]{2,1,0:T(8,128)} custom-call(s32[2]{0:T(128)} %pad_add_fusion.place_ref, s32[2,8]{1,0:T(2,128)} %bitcast.12, bf16[64,64,128]{2,1,0:T(8,128)(2,1)} %shard_map.60.left_ref, bf16[16,64,128]{2,1,0:T(8,128)(2,1)} %shard_map.61.refs_0_, bf16[16,64,128]{2,1,0:T(8,128)(2,1)} %copy-done.1, bf16[16,64,128]{2,1,0:T(8,128)(2,1)} %copy-done, ...), custom_call_target="tpu_custom_call" | custom-call | flops 3000000000 | bytes 9000000 | tf_op jit(solution)/shard_map/pallas_call | solution.py:386
  109.8 4.5 %collective-permute-done.15.mine_ref = bf16[48,64,128]{2,1,0:T(8,128)(2,1)} collective-permute-done((bf16[48,64,128]{2,1,0:T(8,128)(2,1)}, bf16[48,64,128]{2,1,0:T(8,128)(2,1)}, u32[]{:S(2)}, u32[]{:S(2)}) %collective-permute-start.15) | collective-permute-done | bytes 786464 | tf_op jit(solution)/shard_map/ppermute | solution.py:493
  114.3 0.0 collective-permute-start.16
  114.3 0.0 collective-permute-done.17.refs_1_
  114.3 0.0 collective-permute-done.18.refs_3_
  114.3 0.0 collective-permute-done.19.refs_5_
  114.4 10.8 %shard_map.65.acc_in_ref = f32[48,128,128]{2,1,0:T(8,128)} custom-call(s32[2]{0:T(128)} %pad_add_fusion.place_ref, s32[2,8]{1,0:T(2,128)} %bitcast.13, bf16[64,64,128]{2,1,0:T(8,128)(2,1)} %shard_map.60.left_ref, bf16[48,64,128]{2,1,0:T(8,128)(2,1)} %shard_map.64.refs_0_, bf16[48,64,128]{2,1,0:T(8,128)(2,1)} %collective-permute-done.17.refs_1_, ...), custom_call_target="tpu_custom_call" | custom-call | flops 8999999488 | bytes 27000000 | tf_op jit(solution)/shard_map/pallas_call | solution.py:386
  125.2 7.5 %shard_map.66 = (bf16[64,64,128]{2,1,0:T(8,128)(2,1)}, f32[64,128]{1,0:T(8,128)}) custom-call(s32[2]{0:T(128)} %pad_add_fusion.place_ref, s32[2,8]{1,0:T(2,128)} %bitcast.14, bf16[64,64,128]{2,1,0:T(8,128)(2,1)} %shard_map.60.left_ref, bf16[48,64,128]{2,1,0:T(8,128)(2,1)} %collective-permute-done.15.mine_ref, ...), custom_call_target="tpu_custom_call" | custom-call | flops 6000000000 | bytes 18000000 | tf_op jit(solution)/shard_map/pallas_call | solution.py:410
  132.7 3.6 %shard_map.67 = (bf16[64,64,128]{2,1,0:T(8,128)(2,1)}, f32[64,128]{1,0:T(8,128)}) custom-call(s32[2]{0:T(128)} %pad_add_fusion.place_ref, s32[2,8]{1,0:T(2,128)} %bitcast.15, bf16[64,64,128]{2,1,0:T(8,128)(2,1)} %shard_map.60.left_ref, bf16[16,64,128]{2,1,0:T(8,128)(2,1)} %collective-permute-done.6.mine_ref, ...), custom_call_target="tpu_custom_call", output_to_operand_aliasing={{0}: (6, {}), {1}: (7, {})} | custom-call | flops 2000000000 | bytes 6000000 | tf_op jit(solution)/shard_map/pallas_call | solution.py:410
  (13 shorter events, 0.0 us)
Async XLA Ops:
  0.6 1.2 slice-start
  5.8 7.4 %collective-permute-start.12 = (bf16[11,64,128]{2,1,0:T(8,128)(2,1)}, bf16[11,64,128]{2,1,0:T(8,128)(2,1)}, u32[]{:S(2)}, u32[]{:S(2)}) collective-permute-start(bf16[11,64,128]{2,1,0:T(8,128)(2,1)} %shard_map.63.own_ref), channel_id=1, source_target_pairs={{1,2},{3,4},{5,6},{2,1},{4,3},{6,5},{9,10},{11,12},{13,14},{10,9},... | collective-permute-start | bytes 540680 | tf_op jit(solution)/shard_map/ppermute | solution.py:461
  7.8 5.5 %collective-permute-start.11 = (bf16[11,64,128]{2,1,0:T(8,128)(2,1)}, bf16[11,64,128]{2,1,0:T(8,128)(2,1)}, u32[]{:S(2)}, u32[]{:S(2)}) collective-permute-start(bf16[11,64,128]{2,1,0:T(8,128)(2,1)} %shard_map.63.own_ref), channel_id=1, source_target_pairs={{0,1},{1,0},{2,3},{3,2},{4,5},{5,4},{6,7},{7,6},{8,9},{9,8},{10,11... | collective-permute-start | bytes 540680 | tf_op jit(solution)/shard_map/ppermute | solution.py:462
  9.7 15.8 %collective-permute-start.1 = (bf16[2,64,8,128]{3,2,1,0:T(8,128)(2,1)}, bf16[2,64,8,128]{3,2,1,0:T(8,128)(2,1)}, u32[]{:S(2)}, u32[]{:S(2)}) collective-permute-start(bf16[2,64,8,128]{3,2,1,0:T(8,128)(2,1)} %get-tuple-element.6), channel_id=1, source_target_pairs={{8,0},{16,8},{24,16},{0,24},{9,1},{17,9},{25,17},{1,25},{10,2},{18... | collective-permute-start | bytes 786440 | tf_op jit(solution)/shard_map/ppermute | solution.py:472
  10.2 15.3 %collective-permute-start = (bf16[2,64,8,128]{3,2,1,0:T(8,128)(2,1)}, bf16[2,64,8,128]{3,2,1,0:T(8,128)(2,1)}, u32[]{:S(2)}, u32[]{:S(2)}) collective-permute-start(bf16[2,64,8,128]{3,2,1,0:T(8,128)(2,1)} %get-tuple-element.7), channel_id=1, source_target_pairs={{0,8},{8,16},{16,24},{24,0},{1,9},{9,17},{17,25},{25,1},{2,10},{10... | collective-permute-start | bytes 786440 | tf_op jit(solution)/shard_map/ppermute | solution.py:471
  23.6 33.0 %collective-permute-start.13 = (bf16[48,64,128]{2,1,0:T(8,128)(2,1)}, bf16[48,64,128]{2,1,0:T(8,128)(2,1)}, u32[]{:S(2)}, u32[]{:S(2)}) collective-permute-start(bf16[48,64,128]{2,1,0:T(8,128)(2,1)} %shard_map.64.refs_0_), channel_id=1, source_target_pairs={{0,2},{1,3},{2,4},{3,5},{4,6},{5,7},{6,0},{7,1},{8,10},{9,11},{10,... | collective-permute-start | bytes 2359304 | tf_op jit(solution)/shard_map/ppermute | solution.py:493
  32.3 15.4 %collective-permute-start.3 = (bf16[25,64,128]{2,1,0:T(8,128)(2,1)}, bf16[25,64,128]{2,1,0:T(8,128)(2,1)}, u32[]{:S(2)}, u32[]{:S(2)}) collective-permute-start(bf16[25,64,128]{2,1,0:T(8,128)(2,1)} %shard_map.59.own_ref), channel_id=1, source_target_pairs={{1,2},{3,4},{5,6},{2,1},{4,3},{6,5},{9,10},{11,12},{13,14},{10,9},... | collective-permute-start | bytes 1228808 | tf_op jit(solution)/shard_map/ppermute | solution.py:461
  34.2 13.5 %collective-permute-start.2 = (bf16[25,64,128]{2,1,0:T(8,128)(2,1)}, bf16[25,64,128]{2,1,0:T(8,128)(2,1)}, u32[]{:S(2)}, u32[]{:S(2)}) collective-permute-start(bf16[25,64,128]{2,1,0:T(8,128)(2,1)} %shard_map.59.own_ref), channel_id=1, source_target_pairs={{0,1},{1,0},{2,3},{3,2},{4,5},{5,4},{6,7},{7,6},{8,9},{9,8},{10,11... | collective-permute-start | bytes 1228808 | tf_op jit(solution)/shard_map/ppermute | solution.py:462
  56.6 9.4 %collective-permute-start.4 = (bf16[16,64,128]{2,1,0:T(8,128)(2,1)}, bf16[16,64,128]{2,1,0:T(8,128)(2,1)S(1)}, u32[]{:S(2)}, u32[]{:S(2)}) collective-permute-start(bf16[16,64,128]{2,1,0:T(8,128)(2,1)} %shard_map.61.refs_0_), channel_id=1, source_target_pairs={{0,2},{1,3},{2,4},{3,5},{4,6},{5,7},{6,0},{7,1},{8,10},{9,11},{10,... | collective-permute-start | bytes 786440 | tf_op jit(solution)/shard_map/ppermute | solution.py:493
  56.6 34.3 %collective-permute-start.14 = (bf16[48,64,128]{2,1,0:T(8,128)(2,1)}, bf16[48,64,128]{2,1,0:T(8,128)(2,1)}, u32[]{:S(2)}, u32[]{:S(2)}) collective-permute-start(bf16[48,64,128]{2,1,0:T(8,128)(2,1)} %collective-permute-done.13.refs_2_), channel_id=1, source_target_pairs={{0,2},{1,3},{2,4},{3,5},{4,6},{5,7},{6,0},{7,1},{8,10},{9,11},{10,... | collective-permute-start | bytes 2359304 | tf_op jit(solution)/shard_map/ppermute | solution.py:493
  66.0 3.8 %copy-start = (bf16[16,64,128]{2,1,0:T(8,128)(2,1)}, bf16[16,64,128]{2,1,0:T(8,128)(2,1)S(1)}, u32[]{:S(2)}) copy-start(bf16[16,64,128]{2,1,0:T(8,128)(2,1)S(1)} %collective-permute-done.4.refs_2_) | copy-start | bytes 786436
  66.0 21.4 %collective-permute-start.5 = (bf16[16,64,128]{2,1,0:T(8,128)(2,1)S(1)}, bf16[16,64,128]{2,1,0:T(8,128)(2,1)}, u32[]{:S(2)}, u32[]{:S(2)}) collective-permute-start(bf16[16,64,128]{2,1,0:T(8,128)(2,1)S(1)} %collective-permute-done.4.refs_2_), channel_id=1, source_target_pairs={{0,2},{1,3},{2,4},{3,5},{4,6},{5,7},{6,0},{7,1},{8,10},{9,11},{10,... | collective-permute-start | bytes 786440 | tf_op jit(solution)/shard_map/ppermute | solution.py:493
  66.6 21.4 %collective-permute-start.8 = (bf16[16,64,128]{2,1,0:T(8,128)(2,1)}, bf16[16,64,128]{2,1,0:T(8,128)(2,1)S(1)}, u32[]{:S(2)}, u32[]{:S(2)}) collective-permute-start(bf16[16,64,128]{2,1,0:T(8,128)(2,1)} %shard_map.61.refs_0_), channel_id=1, source_target_pairs={{0,1},{1,0},{2,3},{3,2},{4,5},{5,4},{6,7},{7,6},{8,9},{9,8},{10,11... | collective-permute-start | bytes 786440 | tf_op jit(solution)/shard_map/ppermute | solution.py:488
  69.8 18.2 %collective-permute-start.9 = (bf16[16,64,128]{2,1,0:T(8,128)(2,1)S(1)}, bf16[16,64,128]{2,1,0:T(8,128)(2,1)S(1)}, u32[]{:S(2)}, u32[]{:S(2)}) collective-permute-start(bf16[16,64,128]{2,1,0:T(8,128)(2,1)S(1)} %collective-permute-done.4.refs_2_), channel_id=1, source_target_pairs={{0,1},{1,0},{2,3},{3,2},{4,5},{5,4},{6,7},{7,6},{8,9},{9,8},{10,11... | collective-permute-start | bytes 786440 | tf_op jit(solution)/shard_map/ppermute | solution.py:488
  87.5 3.7 %collective-permute-start.10 = (bf16[16,64,128]{2,1,0:T(8,128)(2,1)}, bf16[16,64,128]{2,1,0:T(8,128)(2,1)}, u32[]{:S(2)}, u32[]{:S(2)}) collective-permute-start(bf16[16,64,128]{2,1,0:T(8,128)(2,1)} %collective-permute-done.5.refs_4_), channel_id=1, source_target_pairs={{0,1},{1,0},{2,3},{3,2},{4,5},{5,4},{6,7},{7,6},{8,9},{9,8},{10,11... | collective-permute-start | bytes 786440 | tf_op jit(solution)/shard_map/ppermute | solution.py:488
  87.5 26.9 %collective-permute-start.17 = (bf16[48,64,128]{2,1,0:T(8,128)(2,1)}, bf16[48,64,128]{2,1,0:T(8,128)(2,1)}, u32[]{:S(2)}, u32[]{:S(2)}) collective-permute-start(bf16[48,64,128]{2,1,0:T(8,128)(2,1)} %shard_map.64.refs_0_), channel_id=1, source_target_pairs={{0,1},{1,0},{2,3},{3,2},{4,5},{5,4},{6,7},{7,6},{8,9},{9,8},{10,11... | collective-permute-start | bytes 2359304 | tf_op jit(solution)/shard_map/ppermute | solution.py:488
  88.0 0.7 copy-start.1
  88.0 26.4 %collective-permute-start.18 = (bf16[48,64,128]{2,1,0:T(8,128)(2,1)}, bf16[48,64,128]{2,1,0:T(8,128)(2,1)}, u32[]{:S(2)}, u32[]{:S(2)}) collective-permute-start(bf16[48,64,128]{2,1,0:T(8,128)(2,1)} %collective-permute-done.13.refs_2_), channel_id=1, source_target_pairs={{0,1},{1,0},{2,3},{3,2},{4,5},{5,4},{6,7},{7,6},{8,9},{9,8},{10,11... | collective-permute-start | bytes 2359304 | tf_op jit(solution)/shard_map/ppermute | solution.py:488
  88.7 2.3 %copy-start.2 = (bf16[16,64,128]{2,1,0:T(8,128)(2,1)}, bf16[16,64,128]{2,1,0:T(8,128)(2,1)S(1)}, u32[]{:S(2)}) copy-start(bf16[16,64,128]{2,1,0:T(8,128)(2,1)S(1)} %collective-permute-done.9.refs_3_) | copy-start | bytes 786436
  88.7 16.6 %collective-permute-start.6 = (bf16[16,64,128]{2,1,0:T(8,128)(2,1)}, bf16[16,64,128]{2,1,0:T(8,128)(2,1)}, u32[]{:S(2)}, u32[]{:S(2)}) collective-permute-start(bf16[16,64,128]{2,1,0:T(8,128)(2,1)} %collective-permute-done.5.refs_4_), channel_id=1, source_target_pairs={{0,2},{1,3},{2,4},{3,5},{4,6},{5,7},{6,0},{7,1},{8,10},{9,11},{10,... | collective-permute-start | bytes 786440 | tf_op jit(solution)/shard_map/ppermute | solution.py:493
  90.9 23.4 %collective-permute-start.19 = (bf16[48,64,128]{2,1,0:T(8,128)(2,1)}, bf16[48,64,128]{2,1,0:T(8,128)(2,1)}, u32[]{:S(2)}, u32[]{:S(2)}) collective-permute-start(bf16[48,64,128]{2,1,0:T(8,128)(2,1)} %collective-permute-done.14.refs_4_), channel_id=1, source_target_pairs={{0,1},{1,0},{2,3},{3,2},{4,5},{5,4},{6,7},{7,6},{8,9},{9,8},{10,11... | collective-permute-start | bytes 2359304 | tf_op jit(solution)/shard_map/ppermute | solution.py:488
  91.2 23.2 %collective-permute-start.15 = (bf16[48,64,128]{2,1,0:T(8,128)(2,1)}, bf16[48,64,128]{2,1,0:T(8,128)(2,1)}, u32[]{:S(2)}, u32[]{:S(2)}) collective-permute-start(bf16[48,64,128]{2,1,0:T(8,128)(2,1)} %collective-permute-done.14.refs_4_), channel_id=1, source_target_pairs={{0,2},{1,3},{2,4},{3,5},{4,6},{5,7},{6,0},{7,1},{8,10},{9,11},{10,... | collective-permute-start | bytes 2359304 | tf_op jit(solution)/shard_map/ppermute | solution.py:493
  105.3 27.4 %collective-permute-start.7 = (bf16[16,64,128]{2,1,0:T(8,128)(2,1)}, bf16[16,64,128]{2,1,0:T(8,128)(2,1)}, u32[]{:S(2)}, u32[]{:S(2)}) collective-permute-start(bf16[16,64,128]{2,1,0:T(8,128)(2,1)} %collective-permute-done.6.mine_ref), channel_id=1, source_target_pairs={{0,1},{1,0},{2,3},{3,2},{4,5},{5,4},{6,7},{7,6},{8,9},{9,8},{10,11... | collective-permute-start | bytes 786440 | tf_op jit(solution)/shard_map/ppermute | solution.py:488
  114.3 10.9 %collective-permute-start.16 = (bf16[48,64,128]{2,1,0:T(8,128)(2,1)}, bf16[48,64,128]{2,1,0:T(8,128)(2,1)}, u32[]{:S(2)}, u32[]{:S(2)}) collective-permute-start(bf16[48,64,128]{2,1,0:T(8,128)(2,1)} %collective-permute-done.15.mine_ref), channel_id=1, source_target_pairs={{0,1},{1,0},{2,3},{3,2},{4,5},{5,4},{6,7},{7,6},{8,9},{9,8},{10,11... | collective-permute-start | bytes 2359304 | tf_op jit(solution)/shard_map/ppermute | solution.py:488

commit v4 on v3

--- a/solution.py
+++ b/solution.py
@@ -53,23 +53,27 @@
     x_ref[REACH + rows :] = turned(below_ref[...], inside_below)[:REACH]
 
 
-def with_rows(place, images, above, below, row_count):
-    count, channels, rows, segment = images.shape
+def with_rows(place, images, index, above, below, row_count):
+    _, channels, rows, segment = images.shape
     held = above.shape[2]
 
-    def image_of(extent):
-        return pl.BlockSpec((None, channels, extent, segment), lambda n: (n, 0, 0, 0))
+    def image_of(extent, first):
+        return pl.BlockSpec((None, channels, extent, segment), lambda n: (first, 0, 0, 0))
 
     all_rows = rows + 2 * REACH
     return pl.pallas_call(
         functools.partial(rows_kernel, last_row=row_count - 1),
-        out_shape=jax.ShapeDtypeStruct((count, all_rows, channels, segment), jnp.bfloat16),
-        grid=(count,),
-        in_specs=[pl.BlockSpec(memory_space=pltpu.SMEM), image_of(rows), image_of(held), image_of(held)],
-        out_specs=pl.BlockSpec((None, all_rows, channels, segment), lambda n: (n, 0, 0, 0)),
+        out_shape=jax.ShapeDtypeStruct((1, all_rows, channels, segment), jnp.bfloat16),
+        grid=(1,),
+        in_specs=[
+            pl.BlockSpec(memory_space=pltpu.SMEM),
+            image_of(rows, index),
+            image_of(held, 0),
+            image_of(held, 0),
+        ],
+        out_specs=pl.BlockSpec((None, all_rows, channels, segment), lambda n: (0, 0, 0, 0)),
         compiler_params=pltpu.CompilerParams(vmem_limit_bytes=VMEM_LIMIT),
-        cost_estimate=cost(3),
-        name="with_rows",
+        cost_estimate=cost(2),
     )(place, images, above, below)
 
 
@@ -160,9 +164,17 @@
         side_ref[q] = pltpu.roll(jnp.where(in_slot < half, left, right), segment - shift, 1)
 
     def shifted(main, side, slot, amount):
-        aligned = pltpu.roll(side, segment - REACH - slot * SLOT, 1)
-        before = pltpu.roll(jnp.where(lanes >= segment - amount, aligned, main), amount, 1)
-        after = pltpu.roll(jnp.where(lanes < amount, aligned, main), segment - amount, 1)
+        to_start = segment - REACH - slot * SLOT
+        before = jnp.where(
+            lanes < amount,
+            pltpu.roll(side, lax.rem(to_start + amount, segment), 1),
+            pltpu.roll(main, amount, 1),
+        )
+        after = jnp.where(
+            lanes >= segment - amount,
+            pltpu.roll(side, lax.rem(to_start + segment - amount, segment), 1),
+            pltpu.roll(main, segment - amount, 1),
+        )
         return before, after
 
     def put(target, j, main, before, after):
@@ -319,11 +331,19 @@
         column = key_column((16, 2 * segment))
         extra = jnp.where(kind == 0, 1, jnp.where(kind == 1, column, jnp.where(kind == 2, step, 0)))
         extra = extra.astype(jnp.float32).astype(jnp.bfloat16)
-        for r in range(left_ref.shape[0]):
+
+        def score(r):
             keys = jnp.concatenate([mine_ref[r], theirs_ref[r]], axis=1)
-            scores = lax.dot_general(
+            return keys, lax.dot_general(
                 left_ref[r], keys, (((0,), (0,)), ((), ())), preferred_element_type=jnp.float32
             )
+
+        rows = left_ref.shape[0]
+        upcoming = score(0)
+        for r in range(rows):
+            keys, scores = upcoming
+            if r + 1 < rows:
+                upcoming = score(r + 1)
             weights = jnp.exp2(scores * scale + bias_ref[...]).astype(jnp.bfloat16)
             extended = jnp.concatenate([keys, extra], axis=0)
             acc_ref[r, :, 0 : channels + 16] += lax.dot_general(
@@ -347,10 +367,10 @@
 
 
 def finish_kernel(
-    place_ref, range_ref, left_ref, mine_ref, theirs_ref, acc_in_ref, *refs, inner, groups, step
+    place_ref, range_ref, left_ref, mine_ref, theirs_ref, acc_in_ref, *refs, first, inner, groups, step
 ):
     matched_ref, disparity_ref, acc_ref, bias_ref, rows_ref = refs[-5:]
-    group = group_of(pl.program_id(0), inner, groups)
+    group = group_of(first + pl.program_id(0), inner, groups)
     rows, channels, segment = left_ref.shape
     acc_ref[...] = acc_in_ref[...]
     add_step(
@@ -396,19 +416,20 @@
     )(place, ranges, left, *[a for pair in keys for a in pair])
 
 
-def finish(place, ranges, left, pair, acc, outs, inner, step):
+def finish(place, ranges, left, pair, acc, piece, outs, inner, step):
     rows, channels, segment = left.shape
     groups = rows // RG
-    own_groups = acc.shape[0] // RG
+    own_groups = pair[0].shape[0] // RG
+    first = piece * own_groups
     block = (RG, channels, segment)
     smem = pl.BlockSpec(memory_space=pltpu.SMEM)
 
     def group(i):
-        return group_of(i, inner, groups)
+        return group_of(first + i, inner, groups)
 
     given = () if outs is None else tuple(outs)
     return pl.pallas_call(
-        functools.partial(finish_kernel, inner=inner, groups=groups, step=step),
+        functools.partial(finish_kernel, first=first, inner=inner, groups=groups, step=step),
         out_shape=(
             jax.ShapeDtypeStruct((channels, rows, segment), jnp.bfloat16),
             jax.ShapeDtypeStruct((rows, segment), jnp.float32),
@@ -420,7 +441,7 @@
             pl.BlockSpec(block, lambda i: (group(i), 0, 0)),
             pl.BlockSpec(block, lambda i: (i, 0, 0)),
             pl.BlockSpec(block, lambda i: (i, 0, 0)),
-            pl.BlockSpec((RG, segment, 128), lambda i: (i, 0, 0)),
+            pl.BlockSpec((RG, segment, 128), lambda i: (first + i, 0, 0)),
         ]
         + [pl.BlockSpec(memory_space=pl.ANY)] * len(given),
         out_specs=(
@@ -446,7 +467,7 @@
     row_count = lax.axis_size("rows")
     col_count = lax.axis_size("cols")
     col = lax.axis_index("cols")
-    _, rows, segment = images.shape[1:]
+    _, rows, _ = images.shape[1:]
     place = jnp.stack([lax.axis_index("rows"), col]).astype(jnp.int32)
     ranges = search_ranges.reshape(2, rows // RG)
 
@@ -468,37 +489,51 @@
             first_weight, second_weight, (row_count, col_count),
         )
 
-    above = lax.ppermute(images[:, :, rows - RG :], "rows", down)
-    below = lax.ppermute(images[:, :, :RG], "rows", up)
+    def rows_around(images, index):
+        image = images[index : index + 1]
+        above = lax.ppermute(image[:, :, rows - RG :], "rows", down)
+        below = lax.ppermute(image[:, :, :RG], "rows", up)
+        return with_rows(place, images, index, above, below, row_count)
 
     inner = rows - 2 * RG
     right_rows = images[1].transpose(1, 0, 2)[None]
     edges_a = exchanged([(right_rows, 0)], ((0, inner, RG - REACH),))
-    x = with_rows(place, images, above, below, row_count)
-    chunks = ((0, RG, 0), (0, RG, rows - RG), (1, rows, 0))
-    edges_r = exchanged([(x, 1), (x, 0)], chunks)
-
+    right_x = rows_around(images, 1)
+    edges_b = exchanged([(right_x, 0)], ((0, RG, 0), (0, RG, rows - RG)))
     right_a = features(right_rows, 0, 1, inner, RG - REACH, 0, False, edges_a, 0)
-    right_b = features(x, 1, 2, RG, 0, rows - RG, True, edges_r, 0)
-    left = features(x, 0, 1, rows, 0, 0, True, edges_r, 2 * edge_steps(RG, segment)[1])
+    right_b = features(right_x, 0, 2, RG, 0, rows - RG, True, edges_b, 0)
+
+    later, _ = lax.optimization_barrier((images, right_a[:1, :8]))
+    left_x = rows_around(later, 0)
+    edges_l = exchanged([(left_x, 0)], ((0, rows, 0),))
+    left = features(left_x, 0, 1, rows, 0, 0, True, edges_l, 0)
 
     steps = min(col_count // 2 - 1, HOPS // 2)
 
     def pair(mine):
         return mine, lax.ppermute(mine, "cols", swap)
 
-    def chain(mine):
+    def chain(mine, pieces):
         pairs = [pair(mine)]
-        for _ in range(1, steps + 1):
+        for _ in range(1, steps):
             mine = lax.ppermute(mine, "cols", hop)
             pairs.append(pair(mine))
-        return pairs
-
-    keys_a, keys_b = chain(right_a), chain(right_b)
-    acc_a = correlate(place, ranges, left, keys_a[:-1], True)
-    acc_b = correlate(place, ranges, left, keys_b[:-1], False)
-    outs = finish(place, ranges, left, keys_a[-1], acc_a, None, True, steps)
-    return finish(place, ranges, left, keys_b[-1], acc_b, outs, False, steps)
+        last = []
+        for piece in range(pieces):
+            extent = mine.shape[0] // pieces
+            part = lax.slice_in_dim(mine, piece * extent, (piece + 1) * extent)
+            part = lax.ppermute(part, "cols", hop)
+            last.append(pair(part))
+        return pairs, last
+
+    keys_a, last_a = chain(right_a, 2)
+    keys_b, last_b = chain(right_b, 1)
+    acc_a = correlate(place, ranges, left, keys_a, True)
+    acc_b = correlate(place, ranges, left, keys_b, False)
+    outs = None
+    for piece, keys in enumerate(last_a):
+        outs = finish(place, ranges, left, keys, acc_a, piece, outs, True, steps)
+    return finish(place, ranges, left, last_b[0], acc_b, 0, outs, False, steps)
 
 
 def solution(mesh):

time: 137 us -> 132 us (0.964)
  waiting for transfers between devices: 42 us -> 26.7 us
  starting transfers between devices: 20.2 us -> 26 us
  local copies, waits for them, and re-layouts: 5.38 us -> 8.23 us
    ppermute x6 -> x4, waiting for transfers between devices: 28.5 us -> 11 us  [chain(): mine = lax.ppermute(mine, 'cols', hop)]
    ppermute x2 -> x7, waiting for transfers between devices: 0.01 us -> 9.36 us  [the longest x3 6.52 us: chain(): part = lax.ppermute(part, 'cols', hop)]
    ppermute x2 -> x3, waiting for transfers between devices: 13.4 us -> 6.37 us  [exchanged(): cross = lax.ppermute(own, 'cols', across)]
    ppermute x2 -> x7, starting transfers between devices: 2.92 us -> 9.23 us  [the longest x3 5.13 us: chain(): part = lax.ppermute(part, 'cols', hop)]
    ppermute x2 -> x3, starting transfers between devices: 3.82 us -> 8.4 us  [exchanged(): cross = lax.ppermute(own, 'cols', across)]
    pallas_call x3, Pallas kernels: 31.9 us -> 27.5 us  [unit_features(): pl.pallas_call(functools.partial(feature_kernel, spacing=spacing, offset=...]
    ppermute x8 -> x9, starting transfers between devices: 4.02 us -> 1.1 us  [pair(): return (mine, lax.ppermute(mine, 'cols', swap))]
    slice x1 -> x3, local copies, waits for them, and re-layouts: 1.88 us -> 4.7 us  [the longest x2 2.67 us: rows_around(): below = lax.ppermute(image[:, :, :RG], 'rows', up)]
  transfers between devices with their start and end apart: 20 -> 26, of which waited for: 4 -> 7; matrix products, arithmetic and copies ran while one was open for 2% -> 4% of each run, Pallas kernels for 45% -> 41%
where the time goes in v4:
time: 132 us; the launch traced here: 131 us
  Pallas kernels  68.3 us (52%)
  waiting for transfers between devices  26.7 us (20%)
  starting transfers between devices  26 us (20%)
  local copies, waits for them, and re-layouts  8.23 us (6%)
    pallas_call x3, Pallas kernels, unit_features(): pl.pallas_call(functools.partial(feature_kernel, spacing=spacing, offset=...  27.5 us
    pallas_call x2, Pallas kernels, correlate(): pl.pallas_call(functools.partial(gather_kernel, inner=inner, groups=group...  15.2 us
    pallas_call x3, Pallas kernels, finish(): pl.pallas_call(functools.partial(finish_kernel, first=first, inner=inner,...  12.6 us
    ppermute x4, waiting for transfers between devices, chain(): mine = lax.ppermute(mine, 'cols', hop)  11 us
    ppermute x3, starting transfers between devices, exchanged(): cross = lax.ppermute(own, 'cols', across)  8.4 us
    pallas_call x3, Pallas kernels, pack_edges(): pl.pallas_call(functools.partial(pack_kernel, chunks=chunks), out_shape=j...  7.25 us
    ppermute x4, starting transfers between devices, chain(): mine = lax.ppermute(mine, 'cols', hop)  6.79 us
    ppermute x3, waiting for transfers between devices, chain(): part = lax.ppermute(part, 'cols', hop)  6.52 us
  transfers between devices with their start and end apart: 26, of which 7 were waited for; matrix products, arithmetic and copies ran while one was open for 4% of the time, Pallas kernels for 41%

profile of v4, /device:TPU:30, one launch (start us, length us, event | category | flops | bytes accessed | tf_op | source)
XLA Modules:
  0.0 130.7 jit_solution(5251729042983740324)
XLA Ops:
  0.6 0.0 slice-start
  0.6 1.2 slice-done
  1.9 1.6 %copy.13 = bf16[1,64,64,128]{3,1,2,0:T(8,128)(2,1)} copy(bf16[1,64,64,128]{3,2,1,0:T(8,128)(2,1)S(1)} %slice-done) | data formatting | bytes 2097152
  3.5 2.3 %shard_map.66.own_ref = bf16[11,64,128]{2,1,0:T(8,128)(2,1)} custom-call(bf16[1,64,64,128]{3,2,1,0:T(8,128)(2,1)} %bitcast.10), custom_call_target="tpu_custom_call" | custom-call | flops 2000000000 | bytes 6000000 | tf_op jit(solution)/shard_map/pallas_call | solution.py:113
  5.8 0.0 collective-permute-start.15
  5.8 2.5 %collective-permute-start.16 = (bf16[11,64,128]{2,1,0:T(8,128)(2,1)}, bf16[11,64,128]{2,1,0:T(8,128)(2,1)}, u32[]{:S(2)}, u32[]{:S(2)}) collective-permute-start(bf16[11,64,128]{2,1,0:T(8,128)(2,1)} %shard_map.66.own_ref), channel_id=1, source_target_pairs={{1,2},{3,4},{5,6},{2,1},{4,3},{6,5},{9,10},{11,12},{13,14},{10,9},... | collective-permute-start | bytes 540680 | tf_op jit(solution)/shard_map/ppermute | solution.py:482
  8.3 0.6 pad_add_fusion.place_ref
  9.0 0.0 collective-permute-done.15.partner_ref
  9.0 4.0 %collective-permute-done.16.cross_ref = bf16[11,64,128]{2,1,0:T(8,128)(2,1)} collective-permute-done((bf16[11,64,128]{2,1,0:T(8,128)(2,1)}, bf16[11,64,128]{2,1,0:T(8,128)(2,1)}, u32[]{:S(2)}, u32[]{:S(2)}) %collective-permute-start.16) | collective-permute-done | bytes 180256 | tf_op jit(solution)/shard_map/ppermute | solution.py:482
  13.0 9.0 %shard_map.67.refs_0_ = bf16[48,64,128]{2,1,0:T(8,128)(2,1)} custom-call(s32[2]{0:T(128)} %pad_add_fusion.place_ref, bf16[1,64,64,128]{3,2,1,0:T(8,128)(2,1)} %bitcast.11, bf16[11,64,128]{2,1,0:T(8,128)(2,1)} %shard_map.66.own_ref, bf16[11,64,128]{2,1,0:T(8,128)(2,1)} %collective-permute-done.15.partner_ref, ...), custom_call_target="tpu_custom_call" | custom-call | flops 9600000000 | bytes 28800000 | tf_op jit(solution)/shard_map/pallas_call | solution.py:279
  22.0 1.0 fusion
  22.9 0.5 collective-permute-start.4
  23.5 1.5 %collective-permute-start.5 = (bf16[1,64,8,128]{3,2,1,0:T(8,128)(2,1)S(1)}, bf16[1,64,8,128]{3,2,1,0:T(8,128)(2,1)}, u32[]{:S(2)}, u32[]{:S(2)}) collective-permute-start(bf16[1,64,8,128]{3,2,1,0:T(8,128)(2,1)S(1)} %get-tuple-element.10), channel_id=1, source_target_pairs={{8,0},{16,8},{24,16},{0,24},{9,1},{17,9},{25,17},{1,25},{10,2},{18... | collective-permute-start | bytes 393224 | tf_op jit(solution)/shard_map/ppermute | solution.py:495
  25.0 1.7 %fusion.1 = (bf16[1,64,8,128]{3,2,1,0:T(8,128)(2,1)}, bf16[1,64,8,128]{3,2,1,0:T(8,128)(2,1)}) fusion(bf16[2,64,64,128]{3,2,1,0:T(8,128)(2,1)} %image_ref.2), kind=kLoop, calls=%fused_computation.3 | loop fusion | bytes 524288 | tf_op jit(solution)/shard_map/slice | solution.py:495
  26.7 1.4 %collective-permute-start = (bf16[1,64,8,128]{3,2,1,0:T(8,128)(2,1)}, bf16[1,64,8,128]{3,2,1,0:T(8,128)(2,1)}, u32[]{:S(2)}, u32[]{:S(2)}) collective-permute-start(bf16[1,64,8,128]{3,2,1,0:T(8,128)(2,1)} %get-tuple-element.13), channel_id=1, source_target_pairs={{0,8},{8,16},{16,24},{24,0},{1,9},{9,17},{17,25},{25,1},{2,10},{10... | collective-permute-start | bytes 393224 | tf_op jit(solution)/shard_map/ppermute | solution.py:494
  28.1 0.6 collective-permute-start.1
  28.7 0.6 collective-permute-done.4.above_ref
  29.4 0.7 copy-done
  30.0 2.2 %collective-permute-done.5.below_ref = bf16[1,64,8,128]{3,2,1,0:T(8,128)(2,1)} collective-permute-done((bf16[1,64,8,128]{3,2,1,0:T(8,128)(2,1)S(1)}, bf16[1,64,8,128]{3,2,1,0:T(8,128)(2,1)}, u32[]{:S(2)}, u32[]{:S(2)}) %collective-permute-start.5) | collective-permute-done | bytes 131104 | tf_op jit(solution)/shard_map/ppermute | solution.py:495
  32.2 2.9 %shard_map.62.refs_0_.x_ref = bf16[1,76,64,128]{3,2,1,0:T(8,128)(2,1)} custom-call(s32[2]{0:T(128)} %pad_add_fusion.place_ref, bf16[2,64,64,128]{3,2,1,0:T(8,128)(2,1)} %image_ref.2, bf16[1,64,8,128]{3,2,1,0:T(8,128)(2,1)} %copy-done, bf16[1,64,8,128]{3,2,1,0:T(8,128)(2,1)} %collective-permute-done.5.below_ref), custom_call_target="tpu_custom_call" | custom-call | flops 2000000000 | bytes 6000000 | tf_op jit(solution)/shard_map/pallas_call | solution.py:64
  35.1 2.4 %shard_map.63.own_ref = bf16[12,64,128]{2,1,0:T(8,128)(2,1)} custom-call(bf16[1,76,64,128]{3,2,1,0:T(8,128)(2,1)} %shard_map.62.refs_0_.x_ref), custom_call_target="tpu_custom_call" | custom-call | flops 2000000000 | bytes 6000000 | tf_op jit(solution)/shard_map/pallas_call | solution.py:113
  37.5 0.0 collective-permute-start.6
  37.5 4.0 %collective-permute-start.7 = (bf16[12,64,128]{2,1,0:T(8,128)(2,1)}, bf16[12,64,128]{2,1,0:T(8,128)(2,1)}, u32[]{:S(2)}, u32[]{:S(2)}) collective-permute-start(bf16[12,64,128]{2,1,0:T(8,128)(2,1)} %shard_map.63.own_ref), channel_id=1, source_target_pairs={{1,2},{3,4},{5,6},{2,1},{4,3},{6,5},{9,10},{11,12},{13,14},{10,9},... | collective-permute-start | bytes 589832 | tf_op jit(solution)/shard_map/ppermute | solution.py:482
  41.6 2.7 %collective-permute-start.18 = (bf16[48,64,128]{2,1,0:T(8,128)(2,1)}, bf16[48,64,128]{2,1,0:T(8,128)(2,1)}, u32[]{:S(2)}, u32[]{:S(2)}) collective-permute-start(bf16[48,64,128]{2,1,0:T(8,128)(2,1)} %collective-permute-done.17.refs_2_), channel_id=1, source_target_pairs={{0,2},{1,3},{2,4},{3,5},{4,6},{5,7},{6,0},{7,1},{8,10},{9,11},{10,... | collective-permute-start | bytes 2359304 | tf_op jit(solution)/shard_map/ppermute | solution.py:519
  44.2 2.9 %shard_map.59.refs_0_.x_ref = bf16[1,76,64,128]{3,2,1,0:T(8,128)(2,1)} custom-call(s32[2]{0:T(128)} %pad_add_fusion.place_ref, bf16[2,64,64,128]{3,2,1,0:T(8,128)(2,1)} %image_ref.2, bf16[1,64,8,128]{3,2,1,0:T(8,128)(2,1)} %collective-permute-done.above_ref, bf16[1,64,8,128]{3,2,1,0:T(8,128)(2,1)} %collective-permute-done.1.below_ref), custom_call_target="tpu_custom_call" | custom-call | flops 2000000000 | bytes 6000000 | tf_op jit(solution)/shard_map/pallas_call | solution.py:64
  47.1 7.7 %shard_map.64.refs_0_ = bf16[16,64,128]{2,1,0:T(8,128)(2,1)} custom-call(s32[2]{0:T(128)} %pad_add_fusion.place_ref, bf16[1,76,64,128]{3,2,1,0:T(8,128)(2,1)} %shard_map.62.refs_0_.x_ref, bf16[12,64,128]{2,1,0:T(8,128)(2,1)} %shard_map.63.own_ref, bf16[12,64,128]{2,1,0:T(8,128)(2,1)} %collective-permute-done.6.partner_ref, ...), custom_call_target="tpu_custom_call" | custom-call | flops 3200000000 | bytes 9600000 | tf_op jit(solution)/shard_map/pallas_call | solution.py:279
  54.9 0.0 collective-permute-start.8
  54.9 2.5 %shard_map.60.own_ref = bf16[13,64,128]{2,1,0:T(8,128)(2,1)} custom-call(bf16[1,76,64,128]{3,2,1,0:T(8,128)(2,1)} %shard_map.59.refs_0_.x_ref), custom_call_target="tpu_custom_call" | custom-call | flops 2000000000 | bytes 6000000 | tf_op jit(solution)/shard_map/pallas_call | solution.py:113
  57.4 0.5 collective-permute-start.2
  57.9 9.8 %collective-permute-done.8.refs_2_ = bf16[16,64,128]{2,1,0:T(8,128)(2,1)} collective-permute-done((bf16[16,64,128]{2,1,0:T(8,128)(2,1)}, bf16[16,64,128]{2,1,0:T(8,128)(2,1)}, u32[]{:S(2)}, u32[]{:S(2)}) %collective-permute-start.8) | collective-permute-done | bytes 262176 | tf_op jit(solution)/shard_map/ppermute | solution.py:519
  67.7 4.1 %collective-permute-start.9 = (bf16[16,64,128]{2,1,0:T(8,128)(2,1)}, bf16[16,64,128]{2,1,0:T(8,128)(2,1)}, u32[]{:S(2)}, u32[]{:S(2)}) collective-permute-start(bf16[16,64,128]{2,1,0:T(8,128)(2,1)} %collective-permute-done.8.refs_2_), channel_id=1, source_target_pairs={{0,2},{1,3},{2,4},{3,5},{4,6},{5,7},{6,0},{7,1},{8,10},{9,11},{10,... | collective-permute-start | bytes 786440 | tf_op jit(solution)/shard_map/ppermute | solution.py:519
  71.8 0.5 collective-permute-start.13
  72.3 1.9 %collective-permute-start.3 = (bf16[13,64,128]{2,1,0:T(8,128)(2,1)}, bf16[13,64,128]{2,1,0:T(8,128)(2,1)}, u32[]{:S(2)}, u32[]{:S(2)}) collective-permute-start(bf16[13,64,128]{2,1,0:T(8,128)(2,1)} %shard_map.60.own_ref), channel_id=1, source_target_pairs={{1,2},{3,4},{5,6},{2,1},{4,3},{6,5},{9,10},{11,12},{13,14},{10,9},... | collective-permute-start | bytes 638984 | tf_op jit(solution)/shard_map/ppermute | solution.py:482
  74.2 2.0 %fusion.2 = (bf16[24,64,128]{2,1,0:T(8,128)(2,1)}, bf16[24,64,128]{2,1,0:T(8,128)(2,1)}) fusion(bf16[48,64,128]{2,1,0:T(8,128)(2,1)} %collective-permute-done.18.refs_4_), kind=kLoop, calls=%fused_computation.4 | loop fusion | bytes 1572864 | tf_op jit(solution)/shard_map/slice | solution.py:524
  76.3 1.1 collective-permute-done.9.refs_4_
  77.4 2.4 %collective-permute-done.3.cross_ref = bf16[13,64,128]{2,1,0:T(8,128)(2,1)} collective-permute-done((bf16[13,64,128]{2,1,0:T(8,128)(2,1)}, bf16[13,64,128]{2,1,0:T(8,128)(2,1)}, u32[]{:S(2)}, u32[]{:S(2)}) %collective-permute-start.3) | collective-permute-done | bytes 213024 | tf_op jit(solution)/shard_map/ppermute | solution.py:482
  79.8 4.0 %collective-permute-start.24 = (bf16[24,64,128]{2,1,0:T(8,128)(2,1)}, bf16[24,64,128]{2,1,0:T(8,128)(2,1)}, u32[]{:S(2)}, u32[]{:S(2)}) collective-permute-start(bf16[24,64,128]{2,1,0:T(8,128)(2,1)} %get-tuple-element.14), channel_id=1, source_target_pairs={{0,2},{1,3},{2,4},{3,5},{4,6},{5,7},{6,0},{7,1},{8,10},{9,11},{10,... | collective-permute-start | bytes 1179656 | tf_op jit(solution)/shard_map/ppermute | solution.py:525
  83.8 0.5 collective-permute-start.19
  84.3 10.8 %shard_map.61.left_ref = bf16[64,64,128]{2,1,0:T(8,128)(2,1)} custom-call(s32[2]{0:T(128)} %pad_add_fusion.place_ref, bf16[1,76,64,128]{3,2,1,0:T(8,128)(2,1)} %shard_map.59.refs_0_.x_ref, bf16[13,64,128]{2,1,0:T(8,128)(2,1)} %shard_map.60.own_ref, bf16[13,64,128]{2,1,0:T(8,128)(2,1)} %collective-permute-done.2.partner_ref, ...), custom_call_target="tpu_custom_call" | custom-call | flops 12800000000 | bytes 38400000 | tf_op jit(solution)/shard_map/pallas_call | solution.py:279
  95.1 0.6 collective-permute-start.10
  95.7 4.5 %shard_map.65.acc_in_ref = f32[16,128,128]{2,1,0:T(8,128)} custom-call(s32[2]{0:T(128)} %pad_add_fusion.place_ref, s32[2,8]{1,0:T(2,128)} %bitcast.12, bf16[64,64,128]{2,1,0:T(8,128)(2,1)} %shard_map.61.left_ref, bf16[16,64,128]{2,1,0:T(8,128)(2,1)} %shard_map.64.refs_0_, bf16[16,64,128]{2,1,0:T(8,128)(2,1)} %collective-permute-done.12.refs_1_, ...), custom_call_target="tpu_custom_call" | custom-call | flops 3000000000 | bytes 9000000 | tf_op jit(solution)/shard_map/pallas_call | solution.py:406
  100.2 6.5 %collective-permute-done.10.mine_ref = bf16[16,64,128]{2,1,0:T(8,128)(2,1)} collective-permute-done((bf16[16,64,128]{2,1,0:T(8,128)(2,1)}, bf16[16,64,128]{2,1,0:T(8,128)(2,1)}, u32[]{:S(2)}, u32[]{:S(2)}) %collective-permute-start.10) | collective-permute-done | bytes 262176 | tf_op jit(solution)/shard_map/ppermute | solution.py:525
  106.7 0.5 collective-permute-start.25
  107.2 0.1 collective-permute-start.20
  107.3 10.7 %shard_map.68.acc_in_ref = f32[48,128,128]{2,1,0:T(8,128)} custom-call(s32[2]{0:T(128)} %pad_add_fusion.place_ref, s32[2,8]{1,0:T(2,128)} %bitcast.13, bf16[64,64,128]{2,1,0:T(8,128)(2,1)} %shard_map.61.left_ref, bf16[48,64,128]{2,1,0:T(8,128)(2,1)} %shard_map.67.refs_0_, bf16[48,64,128]{2,1,0:T(8,128)(2,1)} %collective-permute-done.21.refs_1_, ...), custom_call_target="tpu_custom_call" | custom-call | flops 8999999488 | bytes 27000000 | tf_op jit(solution)/shard_map/pallas_call | solution.py:406
  118.1 4.8 %shard_map.69 = (bf16[64,64,128]{2,1,0:T(8,128)(2,1)}, f32[64,128]{1,0:T(8,128)}) custom-call(s32[2]{0:T(128)} %pad_add_fusion.place_ref, s32[2,8]{1,0:T(2,128)} %bitcast.14, bf16[64,64,128]{2,1,0:T(8,128)(2,1)} %shard_map.61.left_ref, bf16[24,64,128]{2,1,0:T(8,128)(2,1)} %collective-permute-done.24.mine_ref, ...), custom_call_target="tpu_custom_call" | custom-call | flops 3000000000 | bytes 9000000 | tf_op jit(solution)/shard_map/pallas_call | solution.py:431
  122.9 4.2 %shard_map.70 = (bf16[64,64,128]{2,1,0:T(8,128)(2,1)}, f32[64,128]{1,0:T(8,128)}) custom-call(s32[2]{0:T(128)} %pad_add_fusion.place_ref, s32[2,8]{1,0:T(2,128)} %bitcast.15, bf16[64,64,128]{2,1,0:T(8,128)(2,1)} %shard_map.61.left_ref, bf16[24,64,128]{2,1,0:T(8,128)(2,1)} %collective-permute-done.19.mine_ref, ...), custom_call_target="tpu_custom_call", output_to_operand_aliasing={{0}: (6, {}), {1}: (7, {})} | custom-call | flops 3000000000 | bytes 9000000 | tf_op jit(solution)/shard_map/pallas_call | solution.py:431
  127.1 3.6 %shard_map.71 = (bf16[64,64,128]{2,1,0:T(8,128)(2,1)}, f32[64,128]{1,0:T(8,128)}) custom-call(s32[2]{0:T(128)} %pad_add_fusion.place_ref, s32[2,8]{1,0:T(2,128)} %bitcast.16, bf16[64,64,128]{2,1,0:T(8,128)(2,1)} %shard_map.61.left_ref, bf16[16,64,128]{2,1,0:T(8,128)(2,1)} %collective-permute-done.10.mine_ref, ...), custom_call_target="tpu_custom_call", output_to_operand_aliasing={{0}: (6, {}), {1}: (7, {})} | custom-call | flops 2000000000 | bytes 6000000 | tf_op jit(solution)/shard_map/pallas_call | solution.py:431
  (26 shorter events, 0.1 us)
Async XLA Ops:
  0.6 1.2 slice-start
  5.8 3.1 %collective-permute-start.15 = (bf16[11,64,128]{2,1,0:T(8,128)(2,1)}, bf16[11,64,128]{2,1,0:T(8,128)(2,1)}, u32[]{:S(2)}, u32[]{:S(2)}) collective-permute-start(bf16[11,64,128]{2,1,0:T(8,128)(2,1)} %shard_map.66.own_ref), channel_id=1, source_target_pairs={{0,1},{1,0},{2,3},{3,2},{4,5},{5,4},{6,7},{7,6},{8,9},{9,8},{10,11... | collective-permute-start | bytes 540680 | tf_op jit(solution)/shard_map/ppermute | solution.py:483
  5.8 7.1 %collective-permute-start.16 = (bf16[11,64,128]{2,1,0:T(8,128)(2,1)}, bf16[11,64,128]{2,1,0:T(8,128)(2,1)}, u32[]{:S(2)}, u32[]{:S(2)}) collective-permute-start(bf16[11,64,128]{2,1,0:T(8,128)(2,1)} %shard_map.66.own_ref), channel_id=1, source_target_pairs={{1,2},{3,4},{5,6},{2,1},{4,3},{6,5},{9,10},{11,12},{13,14},{10,9},... | collective-permute-start | bytes 540680 | tf_op jit(solution)/shard_map/ppermute | solution.py:482
  22.0 19.6 %collective-permute-start.17 = (bf16[48,64,128]{2,1,0:T(8,128)(2,1)}, bf16[48,64,128]{2,1,0:T(8,128)(2,1)}, u32[]{:S(2)}, u32[]{:S(2)}) collective-permute-start(bf16[48,64,128]{2,1,0:T(8,128)(2,1)} %shard_map.67.refs_0_), channel_id=1, source_target_pairs={{0,2},{1,3},{2,4},{3,5},{4,6},{5,7},{6,0},{7,1},{8,10},{9,11},{10,... | collective-permute-start | bytes 2359304 | tf_op jit(solution)/shard_map/ppermute | solution.py:519
  22.9 6.4 %collective-permute-start.4 = (bf16[1,64,8,128]{3,2,1,0:T(8,128)(2,1)S(1)}, bf16[1,64,8,128]{3,2,1,0:T(8,128)(2,1)S(1)}, u32[]{:S(2)}, u32[]{:S(2)}) collective-permute-start(bf16[1,64,8,128]{3,2,1,0:T(8,128)(2,1)S(1)} %get-tuple-element.11), channel_id=1, source_target_pairs={{0,8},{8,16},{16,24},{24,0},{1,9},{9,17},{17,25},{25,1},{2,10},{10... | collective-permute-start | bytes 393224 | tf_op jit(solution)/shard_map/ppermute | solution.py:494
  23.5 8.7 %collective-permute-start.5 = (bf16[1,64,8,128]{3,2,1,0:T(8,128)(2,1)S(1)}, bf16[1,64,8,128]{3,2,1,0:T(8,128)(2,1)}, u32[]{:S(2)}, u32[]{:S(2)}) collective-permute-start(bf16[1,64,8,128]{3,2,1,0:T(8,128)(2,1)S(1)} %get-tuple-element.10), channel_id=1, source_target_pairs={{8,0},{16,8},{24,16},{0,24},{9,1},{17,9},{25,17},{1,25},{10,2},{18... | collective-permute-start | bytes 393224 | tf_op jit(solution)/shard_map/ppermute | solution.py:495
  26.7 17.5 %collective-permute-start = (bf16[1,64,8,128]{3,2,1,0:T(8,128)(2,1)}, bf16[1,64,8,128]{3,2,1,0:T(8,128)(2,1)}, u32[]{:S(2)}, u32[]{:S(2)}) collective-permute-start(bf16[1,64,8,128]{3,2,1,0:T(8,128)(2,1)} %get-tuple-element.13), channel_id=1, source_target_pairs={{0,8},{8,16},{16,24},{24,0},{1,9},{9,17},{17,25},{25,1},{2,10},{10... | collective-permute-start | bytes 393224 | tf_op jit(solution)/shard_map/ppermute | solution.py:494
  28.1 16.2 %collective-permute-start.1 = (bf16[1,64,8,128]{3,2,1,0:T(8,128)(2,1)}, bf16[1,64,8,128]{3,2,1,0:T(8,128)(2,1)}, u32[]{:S(2)}, u32[]{:S(2)}) collective-permute-start(bf16[1,64,8,128]{3,2,1,0:T(8,128)(2,1)} %get-tuple-element.12), channel_id=1, source_target_pairs={{8,0},{16,8},{24,16},{0,24},{9,1},{17,9},{25,17},{1,25},{10,2},{18... | collective-permute-start | bytes 393224 | tf_op jit(solution)/shard_map/ppermute | solution.py:495
  29.4 0.7 copy-start
  37.5 9.6 %collective-permute-start.6 = (bf16[12,64,128]{2,1,0:T(8,128)(2,1)}, bf16[12,64,128]{2,1,0:T(8,128)(2,1)}, u32[]{:S(2)}, u32[]{:S(2)}) collective-permute-start(bf16[12,64,128]{2,1,0:T(8,128)(2,1)} %shard_map.63.own_ref), channel_id=1, source_target_pairs={{0,1},{1,0},{2,3},{3,2},{4,5},{5,4},{6,7},{7,6},{8,9},{9,8},{10,11... | collective-permute-start | bytes 589832 | tf_op jit(solution)/shard_map/ppermute | solution.py:483
  37.5 9.6 %collective-permute-start.7 = (bf16[12,64,128]{2,1,0:T(8,128)(2,1)}, bf16[12,64,128]{2,1,0:T(8,128)(2,1)}, u32[]{:S(2)}, u32[]{:S(2)}) collective-permute-start(bf16[12,64,128]{2,1,0:T(8,128)(2,1)} %shard_map.63.own_ref), channel_id=1, source_target_pairs={{1,2},{3,4},{5,6},{2,1},{4,3},{6,5},{9,10},{11,12},{13,14},{10,9},... | collective-permute-start | bytes 589832 | tf_op jit(solution)/shard_map/ppermute | solution.py:482
  41.6 30.7 %collective-permute-start.18 = (bf16[48,64,128]{2,1,0:T(8,128)(2,1)}, bf16[48,64,128]{2,1,0:T(8,128)(2,1)}, u32[]{:S(2)}, u32[]{:S(2)}) collective-permute-start(bf16[48,64,128]{2,1,0:T(8,128)(2,1)} %collective-permute-done.17.refs_2_), channel_id=1, source_target_pairs={{0,2},{1,3},{2,4},{3,5},{4,6},{5,7},{6,0},{7,1},{8,10},{9,11},{10,... | collective-permute-start | bytes 2359304 | tf_op jit(solution)/shard_map/ppermute | solution.py:519
  47.1 37.2 %collective-permute-start.21 = (bf16[48,64,128]{2,1,0:T(8,128)(2,1)}, bf16[48,64,128]{2,1,0:T(8,128)(2,1)}, u32[]{:S(2)}, u32[]{:S(2)}) collective-permute-start(bf16[48,64,128]{2,1,0:T(8,128)(2,1)} %shard_map.67.refs_0_), channel_id=1, source_target_pairs={{0,1},{1,0},{2,3},{3,2},{4,5},{5,4},{6,7},{7,6},{8,9},{9,8},{10,11... | collective-permute-start | bytes 2359304 | tf_op jit(solution)/shard_map/ppermute | solution.py:514
  54.9 12.8 %collective-permute-start.8 = (bf16[16,64,128]{2,1,0:T(8,128)(2,1)}, bf16[16,64,128]{2,1,0:T(8,128)(2,1)}, u32[]{:S(2)}, u32[]{:S(2)}) collective-permute-start(bf16[16,64,128]{2,1,0:T(8,128)(2,1)} %shard_map.64.refs_0_), channel_id=1, source_target_pairs={{0,2},{1,3},{2,4},{3,5},{4,6},{5,7},{6,0},{7,1},{8,10},{9,11},{10,... | collective-permute-start | bytes 786440 | tf_op jit(solution)/shard_map/ppermute | solution.py:519
  57.4 14.4 %collective-permute-start.2 = (bf16[13,64,128]{2,1,0:T(8,128)(2,1)}, bf16[13,64,128]{2,1,0:T(8,128)(2,1)}, u32[]{:S(2)}, u32[]{:S(2)}) collective-permute-start(bf16[13,64,128]{2,1,0:T(8,128)(2,1)} %shard_map.60.own_ref), channel_id=1, source_target_pairs={{0,1},{1,0},{2,3},{3,2},{4,5},{5,4},{6,7},{7,6},{8,9},{9,8},{10,11... | collective-permute-start | bytes 638984 | tf_op jit(solution)/shard_map/ppermute | solution.py:483
  67.7 9.7 %collective-permute-start.9 = (bf16[16,64,128]{2,1,0:T(8,128)(2,1)}, bf16[16,64,128]{2,1,0:T(8,128)(2,1)}, u32[]{:S(2)}, u32[]{:S(2)}) collective-permute-start(bf16[16,64,128]{2,1,0:T(8,128)(2,1)} %collective-permute-done.8.refs_2_), channel_id=1, source_target_pairs={{0,2},{1,3},{2,4},{3,5},{4,6},{5,7},{6,0},{7,1},{8,10},{9,11},{10,... | collective-permute-start | bytes 786440 | tf_op jit(solution)/shard_map/ppermute | solution.py:519
  71.8 8.0 %collective-permute-start.12 = (bf16[16,64,128]{2,1,0:T(8,128)(2,1)}, bf16[16,64,128]{2,1,0:T(8,128)(2,1)}, u32[]{:S(2)}, u32[]{:S(2)}) collective-permute-start(bf16[16,64,128]{2,1,0:T(8,128)(2,1)} %shard_map.64.refs_0_), channel_id=1, source_target_pairs={{0,1},{1,0},{2,3},{3,2},{4,5},{5,4},{6,7},{7,6},{8,9},{9,8},{10,11... | collective-permute-start | bytes 786440 | tf_op jit(solution)/shard_map/ppermute | solution.py:514
  71.8 12.0 %collective-permute-start.13 = (bf16[16,64,128]{2,1,0:T(8,128)(2,1)}, bf16[16,64,128]{2,1,0:T(8,128)(2,1)}, u32[]{:S(2)}, u32[]{:S(2)}) collective-permute-start(bf16[16,64,128]{2,1,0:T(8,128)(2,1)} %collective-permute-done.8.refs_2_), channel_id=1, source_target_pairs={{0,1},{1,0},{2,3},{3,2},{4,5},{5,4},{6,7},{7,6},{8,9},{9,8},{10,11... | collective-permute-start | bytes 786440 | tf_op jit(solution)/shard_map/ppermute | solution.py:514
  72.3 7.5 %collective-permute-start.3 = (bf16[13,64,128]{2,1,0:T(8,128)(2,1)}, bf16[13,64,128]{2,1,0:T(8,128)(2,1)}, u32[]{:S(2)}, u32[]{:S(2)}) collective-permute-start(bf16[13,64,128]{2,1,0:T(8,128)(2,1)} %shard_map.60.own_ref), channel_id=1, source_target_pairs={{1,2},{3,4},{5,6},{2,1},{4,3},{6,5},{9,10},{11,12},{13,14},{10,9},... | collective-permute-start | bytes 638984 | tf_op jit(solution)/shard_map/ppermute | solution.py:482
  77.4 17.7 %collective-permute-start.14 = (bf16[16,64,128]{2,1,0:T(8,128)(2,1)}, bf16[16,64,128]{2,1,0:T(8,128)(2,1)}, u32[]{:S(2)}, u32[]{:S(2)}) collective-permute-start(bf16[16,64,128]{2,1,0:T(8,128)(2,1)} %collective-permute-done.9.refs_4_), channel_id=1, source_target_pairs={{0,1},{1,0},{2,3},{3,2},{4,5},{5,4},{6,7},{7,6},{8,9},{9,8},{10,11... | collective-permute-start | bytes 786440 | tf_op jit(solution)/shard_map/ppermute | solution.py:514
  79.8 27.5 %collective-permute-start.22 = (bf16[48,64,128]{2,1,0:T(8,128)(2,1)}, bf16[48,64,128]{2,1,0:T(8,128)(2,1)}, u32[]{:S(2)}, u32[]{:S(2)}) collective-permute-start(bf16[48,64,128]{2,1,0:T(8,128)(2,1)} %collective-permute-done.17.refs_2_), channel_id=1, source_target_pairs={{0,1},{1,0},{2,3},{3,2},{4,5},{5,4},{6,7},{7,6},{8,9},{9,8},{10,11... | collective-permute-start | bytes 2359304 | tf_op jit(solution)/shard_map/ppermute | solution.py:514
  79.8 26.9 %collective-permute-start.24 = (bf16[24,64,128]{2,1,0:T(8,128)(2,1)}, bf16[24,64,128]{2,1,0:T(8,128)(2,1)}, u32[]{:S(2)}, u32[]{:S(2)}) collective-permute-start(bf16[24,64,128]{2,1,0:T(8,128)(2,1)} %get-tuple-element.14), channel_id=1, source_target_pairs={{0,2},{1,3},{2,4},{3,5},{4,6},{5,7},{6,0},{7,1},{8,10},{9,11},{10,... | collective-permute-start | bytes 1179656 | tf_op jit(solution)/shard_map/ppermute | solution.py:525
  83.8 23.4 %collective-permute-start.19 = (bf16[24,64,128]{2,1,0:T(8,128)(2,1)}, bf16[24,64,128]{2,1,0:T(8,128)(2,1)}, u32[]{:S(2)}, u32[]{:S(2)}) collective-permute-start(bf16[24,64,128]{2,1,0:T(8,128)(2,1)} %get-tuple-element.15), channel_id=1, source_target_pairs={{0,2},{1,3},{2,4},{3,5},{4,6},{5,7},{6,0},{7,1},{8,10},{9,11},{10,... | collective-permute-start | bytes 1179656 | tf_op jit(solution)/shard_map/ppermute | solution.py:525
  84.3 23.0 %collective-permute-start.23 = (bf16[48,64,128]{2,1,0:T(8,128)(2,1)}, bf16[48,64,128]{2,1,0:T(8,128)(2,1)}, u32[]{:S(2)}, u32[]{:S(2)}) collective-permute-start(bf16[48,64,128]{2,1,0:T(8,128)(2,1)} %collective-permute-done.18.refs_4_), channel_id=1, source_target_pairs={{0,1},{1,0},{2,3},{3,2},{4,5},{5,4},{6,7},{7,6},{8,9},{9,8},{10,11... | collective-permute-start | bytes 2359304 | tf_op jit(solution)/shard_map/ppermute | solution.py:514
  95.1 11.6 %collective-permute-start.10 = (bf16[16,64,128]{2,1,0:T(8,128)(2,1)}, bf16[16,64,128]{2,1,0:T(8,128)(2,1)}, u32[]{:S(2)}, u32[]{:S(2)}) collective-permute-start(bf16[16,64,128]{2,1,0:T(8,128)(2,1)} %collective-permute-done.9.refs_4_), channel_id=1, source_target_pairs={{0,2},{1,3},{2,4},{3,5},{4,6},{5,7},{6,0},{7,1},{8,10},{9,11},{10,... | collective-permute-start | bytes 786440 | tf_op jit(solution)/shard_map/ppermute | solution.py:525
  106.7 20.4 %collective-permute-start.11 = (bf16[16,64,128]{2,1,0:T(8,128)(2,1)}, bf16[16,64,128]{2,1,0:T(8,128)(2,1)}, u32[]{:S(2)}, u32[]{:S(2)}) collective-permute-start(bf16[16,64,128]{2,1,0:T(8,128)(2,1)} %collective-permute-done.10.mine_ref), channel_id=1, source_target_pairs={{0,1},{1,0},{2,3},{3,2},{4,5},{5,4},{6,7},{7,6},{8,9},{9,8},{10,11... | collective-permute-start | bytes 786440 | tf_op jit(solution)/shard_map/ppermute | solution.py:514
  106.7 11.3 %collective-permute-start.25 = (bf16[24,64,128]{2,1,0:T(8,128)(2,1)}, bf16[24,64,128]{2,1,0:T(8,128)(2,1)}, u32[]{:S(2)}, u32[]{:S(2)}) collective-permute-start(bf16[24,64,128]{2,1,0:T(8,128)(2,1)} %collective-permute-done.24.mine_ref), channel_id=1, source_target_pairs={{0,1},{1,0},{2,3},{3,2},{4,5},{5,4},{6,7},{7,6},{8,9},{9,8},{10,11... | collective-permute-start | bytes 1179656 | tf_op jit(solution)/shard_map/ppermute | solution.py:514
  107.2 15.6 %collective-permute-start.20 = (bf16[24,64,128]{2,1,0:T(8,128)(2,1)}, bf16[24,64,128]{2,1,0:T(8,128)(2,1)}, u32[]{:S(2)}, u32[]{:S(2)}) collective-permute-start(bf16[24,64,128]{2,1,0:T(8,128)(2,1)} %collective-permute-done.19.mine_ref), channel_id=1, source_target_pairs={{0,1},{1,0},{2,3},{3,2},{4,5},{5,4},{6,7},{7,6},{8,9},{9,8},{10,11... | collective-permute-start | bytes 1179656 | tf_op jit(solution)/shard_map/ppermute | solution.py:514

commit v5 on v4

--- a/solution.py
+++ b/solution.py
@@ -37,57 +37,36 @@
     )
 
 
-def rows_kernel(place_ref, image_ref, above_ref, below_ref, x_ref, *, last_row):
-    rows = image_ref.shape[1]
-    held = above_ref.shape[1]
-    inside_above = (place_ref[0] > 0).astype(jnp.float32)
-    inside_below = (place_ref[0] < last_row).astype(jnp.float32)
-
-    def turned(piece, keep):
-        piece = jnp.swapaxes(piece, 0, 1)
-        return (piece.astype(jnp.float32) * keep).astype(jnp.bfloat16)
-
-    x_ref[0:REACH] = turned(above_ref[...], inside_above)[held - REACH :]
-    for start in range(0, rows, 16):
-        x_ref[REACH + start : REACH + start + 16] = jnp.swapaxes(image_ref[:, start : start + 16], 0, 1)
-    x_ref[REACH + rows :] = turned(below_ref[...], inside_below)[:REACH]
-
-
-def with_rows(place, images, index, above, below, row_count):
+def turn_kernel(image_ref, mid_ref, first_ref, last_ref):
+    piece = jnp.swapaxes(image_ref[...], 0, 1)
+    mid_ref[...] = piece
+
+    @pl.when(pl.program_id(0) == 0)
+    def _():
+        first_ref[...] = piece[:REACH]
+
+    @pl.when(pl.program_id(0) == pl.num_programs(0) - 1)
+    def _():
+        last_ref[...] = piece[piece.shape[0] - REACH :]
+
+
+def turned(images, index):
     _, channels, rows, segment = images.shape
-    held = above.shape[2]
-
-    def image_of(extent, first):
-        return pl.BlockSpec((None, channels, extent, segment), lambda n: (first, 0, 0, 0))
-
-    all_rows = rows + 2 * REACH
+    step = 2 * RG
+    edge = jax.ShapeDtypeStruct((REACH, channels, segment), jnp.bfloat16)
     return pl.pallas_call(
-        functools.partial(rows_kernel, last_row=row_count - 1),
-        out_shape=jax.ShapeDtypeStruct((1, all_rows, channels, segment), jnp.bfloat16),
-        grid=(1,),
-        in_specs=[
-            pl.BlockSpec(memory_space=pltpu.SMEM),
-            image_of(rows, index),
-            image_of(held, 0),
-            image_of(held, 0),
-        ],
-        out_specs=pl.BlockSpec((None, all_rows, channels, segment), lambda n: (0, 0, 0, 0)),
+        turn_kernel,
+        out_shape=(jax.ShapeDtypeStruct((rows, channels, segment), jnp.bfloat16), edge, edge),
+        grid=(rows // step,),
+        in_specs=[pl.BlockSpec((None, channels, step, segment), lambda i: (index, 0, i, 0))],
+        out_specs=(
+            pl.BlockSpec((step, channels, segment), lambda i: (i, 0, 0)),
+            whole(edge),
+            whole(edge),
+        ),
         compiler_params=pltpu.CompilerParams(vmem_limit_bytes=VMEM_LIMIT),
         cost_estimate=cost(2),
-    )(place, images, above, below)
-
-
-def pack_into(x_ref, edge_ref, base, rows, first):
-    channels, segment = x_ref.shape[1:]
-    slot_of = lane_iota((channels, segment)) // SLOT
-    spacing, steps = edge_steps(rows, segment)
-    for q in range(steps):
-        packed = None
-        for g in range(segment // SLOT):
-            shift = (SLOT * g + SLOT // 2) % segment
-            moved = pltpu.roll(x_ref[first + g * spacing + q], shift, 1)
-            packed = moved if packed is None else jnp.where(slot_of == g, moved, packed)
-        edge_ref[base + q] = packed
+    )(images)
 
 
 def edge_steps(rows, segment):
@@ -95,41 +74,63 @@
     return spacing, spacing + 2 * FIRST_DILATION
 
 
-def pack_kernel(*refs, chunks):
-    edge_ref = refs[-1]
+def kept(piece, inside):
+    return jnp.where(inside, piece, jnp.zeros_like(piece))
+
+
+def pack_kernel(place_ref, *refs, chunks, last_row):
+    mid_ref, edge_ref = refs[0], refs[-1]
+    rows, channels, segment = mid_ref.shape
+    slot_of = lane_iota((channels, segment)) // SLOT
+
+    def row_at(row):
+        if row < 0:
+            return kept(refs[1][row + REACH], place_ref[0] > 0)
+        if row >= rows:
+            return kept(refs[2][row - rows], place_ref[0] < last_row)
+        return mid_ref[row]
+
     base = 0
-    for index, rows, first in chunks:
-        pack_into(refs[index], edge_ref, base, rows, first)
-        base += edge_steps(rows, edge_ref.shape[2])[1]
-
-
-def pack_edges(sources, chunks):
-    channels, segment = sources[0][0].shape[2:]
-    total = sum(edge_steps(rows, segment)[1] for _, rows, _ in chunks)
-
-    def image_of(a, n):
-        return pl.BlockSpec((None,) + a.shape[1:], lambda i: (n, 0, 0, 0))
-
+    for count, first in chunks:
+        spacing, steps = edge_steps(count, segment)
+        for q in range(steps):
+            packed = None
+            for g in range(segment // SLOT):
+                shift = (SLOT * g + SLOT // 2) % segment
+                moved = pltpu.roll(row_at(first - REACH + g * spacing + q), shift, 1)
+                packed = moved if packed is None else jnp.where(slot_of == g, moved, packed)
+            edge_ref[base + q] = packed
+        base += steps
+
+
+def whole(a):
+    return pl.BlockSpec(a.shape, lambda i: (0,) * a.ndim)
+
+
+def pack_edges(place, pieces, chunks, row_count):
+    _, channels, segment = pieces[0].shape
+    total = sum(edge_steps(count, segment)[1] for count, _ in chunks)
     return pl.pallas_call(
-        functools.partial(pack_kernel, chunks=chunks),
+        functools.partial(pack_kernel, chunks=chunks, last_row=row_count - 1),
         out_shape=jax.ShapeDtypeStruct((total, channels, segment), jnp.bfloat16),
         grid=(1,),
-        in_specs=[image_of(a, n) for a, n in sources],
+        in_specs=[pl.BlockSpec(memory_space=pltpu.SMEM)] + [whole(a) for a in pieces],
         out_specs=pl.BlockSpec((total, channels, segment), lambda i: (0, 0, 0)),
         compiler_params=pltpu.CompilerParams(vmem_limit_bytes=VMEM_LIMIT),
         cost_estimate=cost(2),
-    )(*[a for a, _ in sources])
-
-
-def feature_kernel(
-    place_ref, x_ref, own_ref, partner_ref, cross_ref, w1_ref, w2_ref, unit_ref,
-    w_ref, edge_ref, side_ref, p1_ref, p1e_ref, hid_ref, hide_ref, p2_ref, rhs0_ref, rhs1_ref,
-    *, spacing, offset, apart, ends, mesh_shape,
-):
+    )(place, *pieces)
+
+
+def feature_kernel(place_ref, *refs, spacing, offset, mesh_shape):
+    (
+        own_ref, partner_ref, cross_ref, w1_ref, w2_ref, unit_ref,
+        w_ref, edge_ref, side_ref, p1_ref, p1e_ref, hid_ref, hide_ref, p2_ref, rhs0_ref, rhs1_ref, x_ref,
+    ) = refs[-17:]
     part = pl.program_id(0)
-    offset = offset + part * apart
+    ends = len(refs) == 20
+    mid_ref = refs[0]
+    held, channels, segment = mid_ref.shape
     rows = unit_ref.shape[0]
-    channels, segment = x_ref.shape[1:]
     first_row, last_row = place_ref[0] == 0, place_ref[0] == mesh_shape[0] - 1
     first_col, last_col = place_ref[1] == 0, place_ref[1] == mesh_shape[1] - 1
     odd = place_ref[1] % 2 == 1
@@ -207,6 +208,28 @@
 
         lax.fori_loop(0, pl.cdiv(total, 2 * width), body, 0)
 
+    if ends:
+        top = kept(refs[1][...], ~first_row)
+        bottom = kept(refs[2][...], ~last_row)
+        if rows == held:
+            x_ref[0:REACH] = top
+            x_ref[REACH : REACH + rows] = mid_ref[...]
+            x_ref[REACH + rows :] = bottom
+        else:
+
+            @pl.when(part == 0)
+            def _():
+                x_ref[0:REACH] = top
+                x_ref[REACH:] = mid_ref[: rows + REACH]
+
+            @pl.when(part == 1)
+            def _():
+                x_ref[: rows + REACH] = mid_ref[held - rows - REACH :]
+                x_ref[rows + REACH :] = bottom
+
+    else:
+        x_ref = mid_ref
+
     stack(w1_ref)
     conv(x_ref, offset, side_ref, p1_ref, all_rows, d1)
 
@@ -262,31 +285,25 @@
     lax.fori_loop(0, rows // 8, finish, 0)
 
 
-def unit_features(place, x, index, parts, rows, offset, apart, ends, edges, edge_block, w1, w2, mesh_shape):
-    _, held, channels, segment = x.shape
+def unit_features(place, pieces, parts, rows, offset, edges, w1, w2, mesh_shape):
+    _, channels, segment = pieces[0].shape
     all_rows = rows + 2 * REACH
     hidden_rows = rows + 2 * SECOND_DILATION
     spacing, steps = edge_steps(rows, segment)
     width = 8
 
-    def whole(a):
-        return pl.BlockSpec(a.shape, lambda i: (0,) * a.ndim)
-
     def up_to(n, m):
         return pl.cdiv(n, m) * m
 
     products = (3 * channels, segment)
+    assembled = all_rows if len(pieces) == 3 else 1
     return pl.pallas_call(
-        functools.partial(
-            feature_kernel, spacing=spacing, offset=offset, apart=apart, ends=ends, mesh_shape=mesh_shape
-        ),
+        functools.partial(feature_kernel, spacing=spacing, offset=offset, mesh_shape=mesh_shape),
         out_shape=jax.ShapeDtypeStruct((parts * rows, channels, segment), jnp.bfloat16),
         grid=(parts,),
-        in_specs=[
-            pl.BlockSpec(memory_space=pltpu.SMEM),
-            pl.BlockSpec((None, held, channels, segment), lambda i: (index, 0, 0, 0)),
-        ]
-        + [pl.BlockSpec((pl.Element(steps), pl.Element(channels), pl.Element(segment)), lambda i: (edge_block + i * steps, 0, 0)) for _ in edges]
+        in_specs=[pl.BlockSpec(memory_space=pltpu.SMEM)]
+        + [whole(a) for a in pieces]
+        + [pl.BlockSpec((steps, channels, segment), lambda i: (i, 0, 0)) for _ in edges]
         + [whole(w1), whole(w2)],
         out_specs=pl.BlockSpec((rows, channels, segment), lambda i: (i, 0, 0)),
         scratch_shapes=[
@@ -300,10 +317,11 @@
             pltpu.VMEM((up_to(hidden_rows, 2 * width),) + products, jnp.float32),
             pltpu.VMEM((3 * channels, width * segment), jnp.bfloat16),
             pltpu.VMEM((3 * channels, width * segment), jnp.bfloat16),
+            pltpu.VMEM((assembled, channels, segment), jnp.bfloat16),
         ],
         compiler_params=pltpu.CompilerParams(vmem_limit_bytes=VMEM_LIMIT),
         cost_estimate=cost(parts * rows * 0.2),
-    )(place, x, *edges, w1, w2)
+    )(place, *pieces, *edges, w1, w2)
 
 
 def add_step(place_ref, range_ref, group, step, left_ref, mine_ref, theirs_ref, acc_ref, bias_ref):
@@ -355,13 +373,13 @@
     return i + 1 if inner else i * (groups - 1)
 
 
-def gather_kernel(place_ref, range_ref, left_ref, *refs, inner, groups):
-    keys, (acc_ref, bias_ref) = refs[:-2], refs[-2:]
+def gather_kernel(place_ref, range_ref, left_ref, *refs, inner, groups, start, count):
+    keys, (acc_ref, bias_ref) = refs[: 2 * count], refs[-2:]
     group = group_of(pl.program_id(0), inner, groups)
-    acc_ref[...] = jnp.zeros_like(acc_ref)
-    for step in range(len(keys) // 2):
+    acc_ref[...] = refs[2 * count][...] if start else jnp.zeros_like(acc_ref)
+    for index in range(count):
         add_step(
-            place_ref, range_ref, group, step, left_ref, keys[2 * step], keys[2 * step + 1],
+            place_ref, range_ref, group, start + index, left_ref, keys[2 * index], keys[2 * index + 1],
             acc_ref, bias_ref,
         )
 
@@ -397,23 +415,27 @@
     matched_ref[...] = jnp.swapaxes(rows_ref[...].astype(jnp.bfloat16), 0, 1)
 
 
-def correlate(place, ranges, left, keys, inner):
+def correlate(place, ranges, left, keys, acc, start, inner):
     rows, channels, segment = left.shape
     groups = rows // RG
     own_groups = keys[0][0].shape[0] // RG
     block = (RG, channels, segment)
     smem = pl.BlockSpec(memory_space=pltpu.SMEM)
+    acc_spec = pl.BlockSpec((RG, segment, 128), lambda i: (i, 0, 0))
+    given = (acc,) if start else ()
     return pl.pallas_call(
-        functools.partial(gather_kernel, inner=inner, groups=groups),
+        functools.partial(gather_kernel, inner=inner, groups=groups, start=start, count=len(keys)),
         out_shape=jax.ShapeDtypeStruct((own_groups * RG, segment, 128), jnp.float32),
         grid=(own_groups,),
         in_specs=[smem, smem, pl.BlockSpec(block, lambda i: (group_of(i, inner, groups), 0, 0))]
-        + [pl.BlockSpec(block, lambda i: (i, 0, 0))] * (2 * len(keys)),
-        out_specs=pl.BlockSpec((RG, segment, 128), lambda i: (i, 0, 0)),
+        + [pl.BlockSpec(block, lambda i: (i, 0, 0))] * (2 * len(keys))
+        + [acc_spec] * len(given),
+        out_specs=acc_spec,
         scratch_shapes=[pltpu.VMEM((segment, 2 * segment), jnp.float32)],
+        input_output_aliases={3 + 2 * len(keys): 0} if given else {},
         compiler_params=pltpu.CompilerParams(vmem_limit_bytes=VMEM_LIMIT),
         cost_estimate=cost(1.5 * own_groups),
-    )(place, ranges, left, *[a for pair in keys for a in pair])
+    )(place, ranges, left, *[a for pair in keys for a in pair], *given)
 
 
 def finish(place, ranges, left, pair, acc, piece, outs, inner, step):
@@ -477,36 +499,34 @@
     down = [(i, (i + 1) % row_count) for i in range(row_count)]
     up = [(b, a) for a, b in down]
 
-    def exchanged(sources, chunks):
-        own = pack_edges(sources, chunks)
+    def exchanged(pieces, chunks):
+        own = pack_edges(place, pieces, chunks, row_count)
         cross = lax.ppermute(own, "cols", across)
         partner = lax.ppermute(own, "cols", swap)
         return own, partner, cross
 
-    def features(x, index, parts, count, offset, apart, ends, edges, edge_block):
+    def features(pieces, parts, count, offset, edges):
         return unit_features(
-            place, x, index, parts, count, offset, apart, ends, edges, edge_block,
-            first_weight, second_weight, (row_count, col_count),
+            place, pieces, parts, count, offset, edges, first_weight, second_weight,
+            (row_count, col_count),
         )
 
-    def rows_around(images, index):
-        image = images[index : index + 1]
-        above = lax.ppermute(image[:, :, rows - RG :], "rows", down)
-        below = lax.ppermute(image[:, :, :RG], "rows", up)
-        return with_rows(place, images, index, above, below, row_count)
+    def rows_of(index):
+        mid, first, last = turned(images, index)
+        above = lax.ppermute(last, "rows", down)
+        below = lax.ppermute(first, "rows", up)
+        return mid, above, below
 
     inner = rows - 2 * RG
-    right_rows = images[1].transpose(1, 0, 2)[None]
-    edges_a = exchanged([(right_rows, 0)], ((0, inner, RG - REACH),))
-    right_x = rows_around(images, 1)
-    edges_b = exchanged([(right_x, 0)], ((0, RG, 0), (0, RG, rows - RG)))
-    right_a = features(right_rows, 0, 1, inner, RG - REACH, 0, False, edges_a, 0)
-    right_b = features(right_x, 0, 2, RG, 0, rows - RG, True, edges_b, 0)
-
-    later, _ = lax.optimization_barrier((images, right_a[:1, :8]))
-    left_x = rows_around(later, 0)
-    edges_l = exchanged([(left_x, 0)], ((0, rows, 0),))
-    left = features(left_x, 0, 1, rows, 0, 0, True, edges_l, 0)
+    right_rows = rows_of(1)
+    edges_a = exchanged(right_rows[:1], ((inner, RG),))
+    edges_b = exchanged(right_rows, ((RG, 0), (RG, rows - RG)))
+    right_a = features(right_rows[:1], 1, inner, RG - REACH, edges_a)
+    right_b = features(right_rows, 2, RG, 0, edges_b)
+
+    left_rows = rows_of(0)
+    edges_l = exchanged(left_rows, ((rows, 0),))
+    left = features(left_rows, 1, rows, 0, edges_l)
 
     steps = min(col_count // 2 - 1, HOPS // 2)
 
@@ -528,8 +548,15 @@
 
     keys_a, last_a = chain(right_a, 2)
     keys_b, last_b = chain(right_b, 1)
-    acc_a = correlate(place, ranges, left, keys_a, True)
-    acc_b = correlate(place, ranges, left, keys_b, False)
+    early = max(steps - 1, 1)
+
+    def totals(keys, inside):
+        acc = correlate(place, ranges, left, keys[:early], None, 0, inside)
+        if early == steps:
+            return acc
+        return correlate(place, ranges, left, keys[early:], acc, early, inside)
+
+    acc_a, acc_b = totals(keys_a, True), totals(keys_b, False)
     outs = None
     for piece, keys in enumerate(last_a):
         outs = finish(place, ranges, left, keys, acc_a, piece, outs, True, steps)

time: 132 us -> 133 us (level)
  the two profiles are of different devices: /device:TPU:30 before, /device:TPU:4 now
where the time goes in v5:
time: 133 us; the launch traced here: 131 us
  Pallas kernels  69.6 us (52%)
  waiting for transfers between devices  33.5 us (25%)
  starting transfers between devices  24.4 us (18%)
  local copies, waits for them, and re-layouts  2.04 us (2%)
    ppermute x3, waiting for transfers between devices, chain(): part = lax.ppermute(part, 'cols', hop)  29.9 us
    pallas_call x3, Pallas kernels, unit_features(): pl.pallas_call(functools.partial(feature_kernel, spacing=spacing, offset=...  27.7 us
    pallas_call x4, Pallas kernels, correlate(): pl.pallas_call(functools.partial(gather_kernel, inner=inner, groups=group...  17.5 us
    pallas_call x3, Pallas kernels, finish(): pl.pallas_call(functools.partial(finish_kernel, first=first, inner=inner,...  9.82 us
    pallas_call x3, Pallas kernels, pack_edges(): pl.pallas_call(functools.partial(pack_kernel, chunks=chunks, last_row=row...  7.31 us
    pallas_call x2, Pallas kernels, turned(): pl.pallas_call(turn_kernel, out_shape=(jax.ShapeDtypeStruct((rows, channe...  7.25 us
    ppermute x4, starting transfers between devices, chain(): mine = lax.ppermute(mine, 'cols', hop)  6.77 us
    ppermute x9, starting transfers between devices, pair(): return (mine, lax.ppermute(mine, 'cols', swap))  4.12 us
  transfers between devices with their start and end apart: 26, of which 4 were waited for; matrix products, arithmetic and copies ran while one was open for 2% of the time, Pallas kernels for 49%

profile of v5, /device:TPU:4, one launch (start us, length us, event | category | flops | bytes accessed | tf_op | source)
XLA Modules:
  0.0 130.9 jit_solution(8178368317213585599)
XLA Ops:
  0.6 3.6 %shard_map.62 = (bf16[64,64,128]{2,1,0:T(8,128)(2,1)}, bf16[6,64,128]{2,1,0:T(8,128)(2,1)}, bf16[6,64,128]{2,1,0:T(8,128)(2,1)}) custom-call(bf16[2,64,64,128]{3,2,1,0:T(8,128)(2,1)} %image_ref.3), custom_call_target="tpu_custom_call" | custom-call | flops 2000000000 | bytes 6000000 | tf_op jit(solution)/shard_map/pallas_call | solution.py:57
  4.3 1.5 %collective-permute-start.4 = (bf16[6,64,128]{2,1,0:T(8,128)(2,1)}, bf16[6,64,128]{2,1,0:T(8,128)(2,1)}, u32[]{:S(2)}, u32[]{:S(2)}) collective-permute-start(bf16[6,64,128]{2,1,0:T(8,128)(2,1)} %get-tuple-element.16), channel_id=1, source_target_pairs={{0,8},{8,16},{16,24},{24,0},{1,9},{9,17},{17,25},{25,1},{2,10},{10... | collective-permute-start | bytes 294920 | tf_op jit(solution)/shard_map/ppermute | solution.py:516
  5.8 1.4 %collective-permute-start.5 = (bf16[6,64,128]{2,1,0:T(8,128)(2,1)}, bf16[6,64,128]{2,1,0:T(8,128)(2,1)}, u32[]{:S(2)}, u32[]{:S(2)}) collective-permute-start(bf16[6,64,128]{2,1,0:T(8,128)(2,1)} %get-tuple-element.17), channel_id=1, source_target_pairs={{8,0},{16,8},{24,16},{0,24},{9,1},{17,9},{25,17},{1,25},{10,2},{18... | collective-permute-start | bytes 294920 | tf_op jit(solution)/shard_map/ppermute | solution.py:517
  7.2 0.7 pad_add_fusion.place_ref
  7.9 2.3 %shard_map.67.refs_1_ = bf16[11,64,128]{2,1,0:T(8,128)(2,1)} custom-call(s32[2]{0:T(128)} %pad_add_fusion.place_ref, bf16[64,64,128]{2,1,0:T(8,128)(2,1)} %get-tuple-element.15.refs_0_), custom_call_target="tpu_custom_call" | custom-call | flops 2000000000 | bytes 6000000 | tf_op jit(solution)/shard_map/pallas_call | solution.py:113
  10.2 0.0 collective-permute-start.15
  10.2 1.3 %collective-permute-start.16 = (bf16[11,64,128]{2,1,0:T(8,128)(2,1)}, bf16[11,64,128]{2,1,0:T(8,128)(2,1)}, u32[]{:S(2)}, u32[]{:S(2)}) collective-permute-start(bf16[11,64,128]{2,1,0:T(8,128)(2,1)} %shard_map.67.refs_1_), channel_id=1, source_target_pairs={{1,2},{3,4},{5,6},{2,1},{4,3},{6,5},{9,10},{11,12},{13,14},{10,9},... | collective-permute-start | bytes 540680 | tf_op jit(solution)/shard_map/ppermute | solution.py:504
  11.5 0.0 collective-permute-done.4.refs_1_
  11.5 0.0 collective-permute-done.5.refs_2_
  11.5 2.5 %shard_map.63.refs_3_ = bf16[12,64,128]{2,1,0:T(8,128)(2,1)} custom-call(s32[2]{0:T(128)} %pad_add_fusion.place_ref, bf16[64,64,128]{2,1,0:T(8,128)(2,1)} %get-tuple-element.15.refs_0_, bf16[6,64,128]{2,1,0:T(8,128)(2,1)} %collective-permute-done.4.refs_1_, bf16[6,64,128]{2,1,0:T(8,128)(2,1)} %collective-permute-done.5.refs_2_), custom_call_target="tpu_custom_call" | custom-call | flops 2000000000 | bytes 6000000 | tf_op jit(solution)/shard_map/pallas_call | solution.py:113
  14.0 2.3 %collective-permute-start.6 = (bf16[12,64,128]{2,1,0:T(8,128)(2,1)}, bf16[12,64,128]{2,1,0:T(8,128)(2,1)}, u32[]{:S(2)}, u32[]{:S(2)}) collective-permute-start(bf16[12,64,128]{2,1,0:T(8,128)(2,1)} %shard_map.63.refs_3_), channel_id=1, source_target_pairs={{0,1},{1,0},{2,3},{3,2},{4,5},{5,4},{6,7},{7,6},{8,9},{9,8},{10,11... | collective-permute-start | bytes 589832 | tf_op jit(solution)/shard_map/ppermute | solution.py:505
  16.3 1.3 %collective-permute-start.7 = (bf16[12,64,128]{2,1,0:T(8,128)(2,1)}, bf16[12,64,128]{2,1,0:T(8,128)(2,1)}, u32[]{:S(2)}, u32[]{:S(2)}) collective-permute-start(bf16[12,64,128]{2,1,0:T(8,128)(2,1)} %shard_map.63.refs_3_), channel_id=1, source_target_pairs={{1,2},{3,4},{5,6},{2,1},{4,3},{6,5},{9,10},{11,12},{13,14},{10,9},... | collective-permute-start | bytes 589832 | tf_op jit(solution)/shard_map/ppermute | solution.py:504
  17.6 0.0 collective-permute-done.15.refs_2_
  17.6 0.0 collective-permute-done.16.refs_3_
  17.6 9.0 %shard_map.68.refs_0_ = bf16[48,64,128]{2,1,0:T(8,128)(2,1)} custom-call(s32[2]{0:T(128)} %pad_add_fusion.place_ref, bf16[64,64,128]{2,1,0:T(8,128)(2,1)} %get-tuple-element.15.refs_0_, bf16[11,64,128]{2,1,0:T(8,128)(2,1)} %shard_map.67.refs_1_, bf16[11,64,128]{2,1,0:T(8,128)(2,1)} %collective-permute-done.15.refs_2_, ...), custom_call_target="tpu_custom_call" | custom-call | flops 9600000000 | bytes 28800000 | tf_op jit(solution)/shard_map/pallas_call | solution.py:300
  26.6 2.2 %collective-permute-start.17 = (bf16[48,64,128]{2,1,0:T(8,128)(2,1)}, bf16[48,64,128]{2,1,0:T(8,128)(2,1)}, u32[]{:S(2)}, u32[]{:S(2)}) collective-permute-start(bf16[48,64,128]{2,1,0:T(8,128)(2,1)} %shard_map.68.refs_0_), channel_id=1, source_target_pairs={{0,2},{1,3},{2,4},{3,5},{4,6},{5,7},{6,0},{7,1},{8,10},{9,11},{10,... | collective-permute-start | bytes 2359304 | tf_op jit(solution)/shard_map/ppermute | solution.py:539
  28.8 3.6 %shard_map.59 = (bf16[64,64,128]{2,1,0:T(8,128)(2,1)}, bf16[6,64,128]{2,1,0:T(8,128)(2,1)}, bf16[6,64,128]{2,1,0:T(8,128)(2,1)}) custom-call(bf16[2,64,64,128]{3,2,1,0:T(8,128)(2,1)} %image_ref.3), custom_call_target="tpu_custom_call" | custom-call | flops 2000000000 | bytes 6000000 | tf_op jit(solution)/shard_map/pallas_call | solution.py:57
  32.4 0.6 collective-permute-start
  33.0 2.3 %collective-permute-start.1 = (bf16[6,64,128]{2,1,0:T(8,128)(2,1)}, bf16[6,64,128]{2,1,0:T(8,128)(2,1)}, u32[]{:S(2)}, u32[]{:S(2)}) collective-permute-start(bf16[6,64,128]{2,1,0:T(8,128)(2,1)} %get-tuple-element.14), channel_id=1, source_target_pairs={{8,0},{16,8},{24,16},{0,24},{9,1},{17,9},{25,17},{1,25},{10,2},{18... | collective-permute-start | bytes 294920 | tf_op jit(solution)/shard_map/ppermute | solution.py:517
  35.4 0.0 collective-permute-done.6.refs_4_
  35.4 0.0 collective-permute-done.7.refs_5_
  35.4 7.9 %shard_map.64.refs_0_ = bf16[16,64,128]{2,1,0:T(8,128)(2,1)} custom-call(s32[2]{0:T(128)} %pad_add_fusion.place_ref, bf16[64,64,128]{2,1,0:T(8,128)(2,1)} %get-tuple-element.15.refs_0_, bf16[6,64,128]{2,1,0:T(8,128)(2,1)} %collective-permute-done.4.refs_1_, bf16[6,64,128]{2,1,0:T(8,128)(2,1)} %collective-permute-done.5.refs_2_, ...), custom_call_target="tpu_custom_call" | custom-call | flops 3200000000 | bytes 9600000 | tf_op jit(solution)/shard_map/pallas_call | solution.py:300
  43.3 1.6 %collective-permute-start.8 = (bf16[16,64,128]{2,1,0:T(8,128)(2,1)}, bf16[16,64,128]{2,1,0:T(8,128)(2,1)}, u32[]{:S(2)}, u32[]{:S(2)}) collective-permute-start(bf16[16,64,128]{2,1,0:T(8,128)(2,1)} %shard_map.64.refs_0_), channel_id=1, source_target_pairs={{0,2},{1,3},{2,4},{3,5},{4,6},{5,7},{6,0},{7,1},{8,10},{9,11},{10,... | collective-permute-start | bytes 786440 | tf_op jit(solution)/shard_map/ppermute | solution.py:539
  44.9 0.0 collective-permute-done.refs_1_
  44.9 2.5 %shard_map.60.refs_3_ = bf16[13,64,128]{2,1,0:T(8,128)(2,1)} custom-call(s32[2]{0:T(128)} %pad_add_fusion.place_ref, bf16[64,64,128]{2,1,0:T(8,128)(2,1)} %get-tuple-element.12.refs_0_, bf16[6,64,128]{2,1,0:T(8,128)(2,1)} %collective-permute-done.refs_1_, bf16[6,64,128]{2,1,0:T(8,128)(2,1)} %collective-permute-done.1.refs_2_), custom_call_target="tpu_custom_call" | custom-call | flops 2000000000 | bytes 6000000 | tf_op jit(solution)/shard_map/pallas_call | solution.py:113
  47.4 1.3 %collective-permute-start.3 = (bf16[13,64,128]{2,1,0:T(8,128)(2,1)}, bf16[13,64,128]{2,1,0:T(8,128)(2,1)}, u32[]{:S(2)}, u32[]{:S(2)}) collective-permute-start(bf16[13,64,128]{2,1,0:T(8,128)(2,1)} %shard_map.60.refs_3_), channel_id=1, source_target_pairs={{1,2},{3,4},{5,6},{2,1},{4,3},{6,5},{9,10},{11,12},{13,14},{10,9},... | collective-permute-start | bytes 638984 | tf_op jit(solution)/shard_map/ppermute | solution.py:504
  48.7 2.3 %collective-permute-start.22 = (bf16[48,64,128]{2,1,0:T(8,128)(2,1)}, bf16[48,64,128]{2,1,0:T(8,128)(2,1)}, u32[]{:S(2)}, u32[]{:S(2)}) collective-permute-start(bf16[48,64,128]{2,1,0:T(8,128)(2,1)} %shard_map.68.refs_0_), channel_id=1, source_target_pairs={{0,1},{1,0},{2,3},{3,2},{4,5},{5,4},{6,7},{7,6},{8,9},{9,8},{10,11... | collective-permute-start | bytes 2359304 | tf_op jit(solution)/shard_map/ppermute | solution.py:534
  51.1 0.1 collective-permute-start.13
  51.1 3.5 %collective-permute-done.8.refs_2_ = bf16[16,64,128]{2,1,0:T(8,128)(2,1)} collective-permute-done((bf16[16,64,128]{2,1,0:T(8,128)(2,1)}, bf16[16,64,128]{2,1,0:T(8,128)(2,1)}, u32[]{:S(2)}, u32[]{:S(2)}) %collective-permute-start.8) | collective-permute-done | bytes 262176 | tf_op jit(solution)/shard_map/ppermute | solution.py:539
  54.7 1.0 collective-permute-start.14
  55.6 1.8 %collective-permute-start.9 = (bf16[16,64,128]{2,1,0:T(8,128)(2,1)}, bf16[16,64,128]{2,1,0:T(8,128)(2,1)}, u32[]{:S(2)}, u32[]{:S(2)}) collective-permute-start(bf16[16,64,128]{2,1,0:T(8,128)(2,1)} %collective-permute-done.8.refs_2_), channel_id=1, source_target_pairs={{0,2},{1,3},{2,4},{3,5},{4,6},{5,7},{6,0},{7,1},{8,10},{9,11},{10,... | collective-permute-start | bytes 786440 | tf_op jit(solution)/shard_map/ppermute | solution.py:539
  57.5 1.1 collective-permute-start.18
  58.6 10.8 %shard_map.61.left_ref = bf16[64,64,128]{2,1,0:T(8,128)(2,1)} custom-call(s32[2]{0:T(128)} %pad_add_fusion.place_ref, bf16[64,64,128]{2,1,0:T(8,128)(2,1)} %get-tuple-element.12.refs_0_, bf16[6,64,128]{2,1,0:T(8,128)(2,1)} %collective-permute-done.refs_1_, bf16[6,64,128]{2,1,0:T(8,128)(2,1)} %collective-permute-done.1.refs_2_, ...), custom_call_target="tpu_custom_call" | custom-call | flops 12800000000 | bytes 38400000 | tf_op jit(solution)/shard_map/pallas_call | solution.py:300
  69.4 0.3 collective-permute-start.10
  69.8 0.2 collective-permute-start.23
  70.0 2.8 %shard_map.65.refs_2_ = f32[16,128,128]{2,1,0:T(8,128)} custom-call(s32[2]{0:T(128)} %pad_add_fusion.place_ref, s32[2,8]{1,0:T(2,128)} %bitcast.3, bf16[64,64,128]{2,1,0:T(8,128)(2,1)} %shard_map.61.left_ref, bf16[16,64,128]{2,1,0:T(8,128)(2,1)} %shard_map.64.refs_0_, bf16[16,64,128]{2,1,0:T(8,128)(2,1)} %collective-permute-done.13.refs_1_, ...), custom_call_target="tpu_custom_call" | custom-call | flops 3000000000 | bytes 9000000 | tf_op jit(solution)/shard_map/pallas_call | solution.py:426
  72.8 15.9 %collective-permute-done.10.mine_ref = bf16[16,64,128]{2,1,0:T(8,128)(2,1)} collective-permute-done((bf16[16,64,128]{2,1,0:T(8,128)(2,1)}, bf16[16,64,128]{2,1,0:T(8,128)(2,1)}, u32[]{:S(2)}, u32[]{:S(2)}) %collective-permute-start.10) | collective-permute-done | bytes 262176 | tf_op jit(solution)/shard_map/ppermute | solution.py:545
  88.7 0.5 collective-permute-start.11
  89.2 2.4 %shard_map.66.acc_in_ref = f32[16,128,128]{2,1,0:T(8,128)} custom-call(s32[2]{0:T(128)} %pad_add_fusion.place_ref, s32[2,8]{1,0:T(2,128)} %bitcast.4, bf16[64,64,128]{2,1,0:T(8,128)(2,1)} %shard_map.61.left_ref, bf16[16,64,128]{2,1,0:T(8,128)(2,1)} %collective-permute-done.9.refs_0_, ...), custom_call_target="tpu_custom_call", output_to_operand_aliasing={{}: (5, {})} | custom-call | flops 3000000000 | bytes 9000000 | tf_op jit(solution)/shard_map/pallas_call | solution.py:426
  91.6 2.0 %fusion = (bf16[24,64,128]{2,1,0:T(8,128)(2,1)}, bf16[24,64,128]{2,1,0:T(8,128)(2,1)}) fusion(bf16[48,64,128]{2,1,0:T(8,128)(2,1)} %collective-permute-done.18.refs_0_), kind=kLoop, calls=%fused_computation.1 | loop fusion | bytes 1572864 | tf_op jit(solution)/shard_map/slice | solution.py:544
  93.7 1.0 collective-permute-start.19
  94.7 6.5 %shard_map.69.refs_2_ = f32[48,128,128]{2,1,0:T(8,128)} custom-call(s32[2]{0:T(128)} %pad_add_fusion.place_ref, s32[2,8]{1,0:T(2,128)} %bitcast.5, bf16[64,64,128]{2,1,0:T(8,128)(2,1)} %shard_map.61.left_ref, bf16[48,64,128]{2,1,0:T(8,128)(2,1)} %shard_map.68.refs_0_, bf16[48,64,128]{2,1,0:T(8,128)(2,1)} %collective-permute-done.22.refs_1_, ...), custom_call_target="tpu_custom_call" | custom-call | flops 8999999488 | bytes 27000000 | tf_op jit(solution)/shard_map/pallas_call | solution.py:426
  101.2 6.5 %collective-permute-done.24.mine_ref = bf16[24,64,128]{2,1,0:T(8,128)(2,1)} collective-permute-done((bf16[24,64,128]{2,1,0:T(8,128)(2,1)}, bf16[24,64,128]{2,1,0:T(8,128)(2,1)}, u32[]{:S(2)}, u32[]{:S(2)}) %collective-permute-start.24) | collective-permute-done | bytes 393248 | tf_op jit(solution)/shard_map/ppermute | solution.py:545
  107.8 7.5 %collective-permute-done.19.mine_ref = bf16[24,64,128]{2,1,0:T(8,128)(2,1)} collective-permute-done((bf16[24,64,128]{2,1,0:T(8,128)(2,1)}, bf16[24,64,128]{2,1,0:T(8,128)(2,1)}, u32[]{:S(2)}, u32[]{:S(2)}) %collective-permute-start.19) | collective-permute-done | bytes 393248 | tf_op jit(solution)/shard_map/ppermute | solution.py:545
  115.3 5.8 %shard_map.70.acc_in_ref = f32[48,128,128]{2,1,0:T(8,128)} custom-call(s32[2]{0:T(128)} %pad_add_fusion.place_ref, s32[2,8]{1,0:T(2,128)} %bitcast.6, bf16[64,64,128]{2,1,0:T(8,128)(2,1)} %shard_map.61.left_ref, bf16[48,64,128]{2,1,0:T(8,128)(2,1)} %collective-permute-done.18.refs_0_, ...), custom_call_target="tpu_custom_call", output_to_operand_aliasing={{}: (5, {})} | custom-call | flops 8999999488 | bytes 27000000 | tf_op jit(solution)/shard_map/pallas_call | solution.py:426
  121.1 3.7 %shard_map.71 = (bf16[64,64,128]{2,1,0:T(8,128)(2,1)}, f32[64,128]{1,0:T(8,128)}) custom-call(s32[2]{0:T(128)} %pad_add_fusion.place_ref, s32[2,8]{1,0:T(2,128)} %bitcast.7, bf16[64,64,128]{2,1,0:T(8,128)(2,1)} %shard_map.61.left_ref, bf16[24,64,128]{2,1,0:T(8,128)(2,1)} %collective-permute-done.24.mine_ref, ...), custom_call_target="tpu_custom_call" | custom-call | flops 3000000000 | bytes 9000000 | tf_op jit(solution)/shard_map/pallas_call | solution.py:453
  124.8 3.7 %shard_map.72 = (bf16[64,64,128]{2,1,0:T(8,128)(2,1)}, f32[64,128]{1,0:T(8,128)}) custom-call(s32[2]{0:T(128)} %pad_add_fusion.place_ref, s32[2,8]{1,0:T(2,128)} %bitcast.8, bf16[64,64,128]{2,1,0:T(8,128)(2,1)} %shard_map.61.left_ref, bf16[24,64,128]{2,1,0:T(8,128)(2,1)} %collective-permute-done.19.mine_ref, ...), custom_call_target="tpu_custom_call", output_to_operand_aliasing={{0}: (6, {}), {1}: (7, {})} | custom-call | flops 3000000000 | bytes 9000000 | tf_op jit(solution)/shard_map/pallas_call | solution.py:453
  128.5 2.5 %shard_map.73 = (bf16[64,64,128]{2,1,0:T(8,128)(2,1)}, f32[64,128]{1,0:T(8,128)}) custom-call(s32[2]{0:T(128)} %pad_add_fusion.place_ref, s32[2,8]{1,0:T(2,128)} %bitcast.9, bf16[64,64,128]{2,1,0:T(8,128)(2,1)} %shard_map.61.left_ref, bf16[16,64,128]{2,1,0:T(8,128)(2,1)} %collective-permute-done.10.mine_ref, ...), custom_call_target="tpu_custom_call", output_to_operand_aliasing={{0}: (6, {}), {1}: (7, {})} | custom-call | flops 2000000000 | bytes 6000000 | tf_op jit(solution)/shard_map/pallas_call | solution.py:453
  (21 shorter events, 0.1 us)
Async XLA Ops:
  4.3 7.3 %collective-permute-start.4 = (bf16[6,64,128]{2,1,0:T(8,128)(2,1)}, bf16[6,64,128]{2,1,0:T(8,128)(2,1)}, u32[]{:S(2)}, u32[]{:S(2)}) collective-permute-start(bf16[6,64,128]{2,1,0:T(8,128)(2,1)} %get-tuple-element.16), channel_id=1, source_target_pairs={{0,8},{8,16},{16,24},{24,0},{1,9},{9,17},{17,25},{25,1},{2,10},{10... | collective-permute-start | bytes 294920 | tf_op jit(solution)/shard_map/ppermute | solution.py:516
  5.8 5.8 %collective-permute-start.5 = (bf16[6,64,128]{2,1,0:T(8,128)(2,1)}, bf16[6,64,128]{2,1,0:T(8,128)(2,1)}, u32[]{:S(2)}, u32[]{:S(2)}) collective-permute-start(bf16[6,64,128]{2,1,0:T(8,128)(2,1)} %get-tuple-element.17), channel_id=1, source_target_pairs={{8,0},{16,8},{24,16},{0,24},{9,1},{17,9},{25,17},{1,25},{10,2},{18... | collective-permute-start | bytes 294920 | tf_op jit(solution)/shard_map/ppermute | solution.py:517
  10.2 7.4 %collective-permute-start.15 = (bf16[11,64,128]{2,1,0:T(8,128)(2,1)}, bf16[11,64,128]{2,1,0:T(8,128)(2,1)}, u32[]{:S(2)}, u32[]{:S(2)}) collective-permute-start(bf16[11,64,128]{2,1,0:T(8,128)(2,1)} %shard_map.67.refs_1_), channel_id=1, source_target_pairs={{0,1},{1,0},{2,3},{3,2},{4,5},{5,4},{6,7},{7,6},{8,9},{9,8},{10,11... | collective-permute-start | bytes 540680 | tf_op jit(solution)/shard_map/ppermute | solution.py:505
  10.2 7.4 %collective-permute-start.16 = (bf16[11,64,128]{2,1,0:T(8,128)(2,1)}, bf16[11,64,128]{2,1,0:T(8,128)(2,1)}, u32[]{:S(2)}, u32[]{:S(2)}) collective-permute-start(bf16[11,64,128]{2,1,0:T(8,128)(2,1)} %shard_map.67.refs_1_), channel_id=1, source_target_pairs={{1,2},{3,4},{5,6},{2,1},{4,3},{6,5},{9,10},{11,12},{13,14},{10,9},... | collective-permute-start | bytes 540680 | tf_op jit(solution)/shard_map/ppermute | solution.py:504
  14.0 21.4 %collective-permute-start.6 = (bf16[12,64,128]{2,1,0:T(8,128)(2,1)}, bf16[12,64,128]{2,1,0:T(8,128)(2,1)}, u32[]{:S(2)}, u32[]{:S(2)}) collective-permute-start(bf16[12,64,128]{2,1,0:T(8,128)(2,1)} %shard_map.63.refs_3_), channel_id=1, source_target_pairs={{0,1},{1,0},{2,3},{3,2},{4,5},{5,4},{6,7},{7,6},{8,9},{9,8},{10,11... | collective-permute-start | bytes 589832 | tf_op jit(solution)/shard_map/ppermute | solution.py:505
  16.3 19.1 %collective-permute-start.7 = (bf16[12,64,128]{2,1,0:T(8,128)(2,1)}, bf16[12,64,128]{2,1,0:T(8,128)(2,1)}, u32[]{:S(2)}, u32[]{:S(2)}) collective-permute-start(bf16[12,64,128]{2,1,0:T(8,128)(2,1)} %shard_map.63.refs_3_), channel_id=1, source_target_pairs={{1,2},{3,4},{5,6},{2,1},{4,3},{6,5},{9,10},{11,12},{13,14},{10,9},... | collective-permute-start | bytes 589832 | tf_op jit(solution)/shard_map/ppermute | solution.py:504
  26.6 30.9 %collective-permute-start.17 = (bf16[48,64,128]{2,1,0:T(8,128)(2,1)}, bf16[48,64,128]{2,1,0:T(8,128)(2,1)}, u32[]{:S(2)}, u32[]{:S(2)}) collective-permute-start(bf16[48,64,128]{2,1,0:T(8,128)(2,1)} %shard_map.68.refs_0_), channel_id=1, source_target_pairs={{0,2},{1,3},{2,4},{3,5},{4,6},{5,7},{6,0},{7,1},{8,10},{9,11},{10,... | collective-permute-start | bytes 2359304 | tf_op jit(solution)/shard_map/ppermute | solution.py:539
  32.4 12.4 %collective-permute-start = (bf16[6,64,128]{2,1,0:T(8,128)(2,1)}, bf16[6,64,128]{2,1,0:T(8,128)(2,1)}, u32[]{:S(2)}, u32[]{:S(2)}) collective-permute-start(bf16[6,64,128]{2,1,0:T(8,128)(2,1)} %get-tuple-element.13), channel_id=1, source_target_pairs={{0,8},{8,16},{16,24},{24,0},{1,9},{9,17},{17,25},{25,1},{2,10},{10... | collective-permute-start | bytes 294920 | tf_op jit(solution)/shard_map/ppermute | solution.py:516
  33.0 11.8 %collective-permute-start.1 = (bf16[6,64,128]{2,1,0:T(8,128)(2,1)}, bf16[6,64,128]{2,1,0:T(8,128)(2,1)}, u32[]{:S(2)}, u32[]{:S(2)}) collective-permute-start(bf16[6,64,128]{2,1,0:T(8,128)(2,1)} %get-tuple-element.14), channel_id=1, source_target_pairs={{8,0},{16,8},{24,16},{0,24},{9,1},{17,9},{25,17},{1,25},{10,2},{18... | collective-permute-start | bytes 294920 | tf_op jit(solution)/shard_map/ppermute | solution.py:517
  43.3 11.4 %collective-permute-start.8 = (bf16[16,64,128]{2,1,0:T(8,128)(2,1)}, bf16[16,64,128]{2,1,0:T(8,128)(2,1)}, u32[]{:S(2)}, u32[]{:S(2)}) collective-permute-start(bf16[16,64,128]{2,1,0:T(8,128)(2,1)} %shard_map.64.refs_0_), channel_id=1, source_target_pairs={{0,2},{1,3},{2,4},{3,5},{4,6},{5,7},{6,0},{7,1},{8,10},{9,11},{10,... | collective-permute-start | bytes 786440 | tf_op jit(solution)/shard_map/ppermute | solution.py:539
  47.4 3.7 %collective-permute-start.2 = (bf16[13,64,128]{2,1,0:T(8,128)(2,1)}, bf16[13,64,128]{2,1,0:T(8,128)(2,1)}, u32[]{:S(2)}, u32[]{:S(2)}) collective-permute-start(bf16[13,64,128]{2,1,0:T(8,128)(2,1)} %shard_map.60.refs_3_), channel_id=1, source_target_pairs={{0,1},{1,0},{2,3},{3,2},{4,5},{5,4},{6,7},{7,6},{8,9},{9,8},{10,11... | collective-permute-start | bytes 638984 | tf_op jit(solution)/shard_map/ppermute | solution.py:505
  47.4 8.3 %collective-permute-start.3 = (bf16[13,64,128]{2,1,0:T(8,128)(2,1)}, bf16[13,64,128]{2,1,0:T(8,128)(2,1)}, u32[]{:S(2)}, u32[]{:S(2)}) collective-permute-start(bf16[13,64,128]{2,1,0:T(8,128)(2,1)} %shard_map.60.refs_3_), channel_id=1, source_target_pairs={{1,2},{3,4},{5,6},{2,1},{4,3},{6,5},{9,10},{11,12},{13,14},{10,9},... | collective-permute-start | bytes 638984 | tf_op jit(solution)/shard_map/ppermute | solution.py:504
  48.7 46.0 %collective-permute-start.22 = (bf16[48,64,128]{2,1,0:T(8,128)(2,1)}, bf16[48,64,128]{2,1,0:T(8,128)(2,1)}, u32[]{:S(2)}, u32[]{:S(2)}) collective-permute-start(bf16[48,64,128]{2,1,0:T(8,128)(2,1)} %shard_map.68.refs_0_), channel_id=1, source_target_pairs={{0,1},{1,0},{2,3},{3,2},{4,5},{5,4},{6,7},{7,6},{8,9},{9,8},{10,11... | collective-permute-start | bytes 2359304 | tf_op jit(solution)/shard_map/ppermute | solution.py:534
  51.1 18.4 %collective-permute-start.13 = (bf16[16,64,128]{2,1,0:T(8,128)(2,1)}, bf16[16,64,128]{2,1,0:T(8,128)(2,1)}, u32[]{:S(2)}, u32[]{:S(2)}) collective-permute-start(bf16[16,64,128]{2,1,0:T(8,128)(2,1)} %shard_map.64.refs_0_), channel_id=1, source_target_pairs={{0,1},{1,0},{2,3},{3,2},{4,5},{5,4},{6,7},{7,6},{8,9},{9,8},{10,11... | collective-permute-start | bytes 786440 | tf_op jit(solution)/shard_map/ppermute | solution.py:534
  54.7 15.1 %collective-permute-start.14 = (bf16[16,64,128]{2,1,0:T(8,128)(2,1)}, bf16[16,64,128]{2,1,0:T(8,128)(2,1)}, u32[]{:S(2)}, u32[]{:S(2)}) collective-permute-start(bf16[16,64,128]{2,1,0:T(8,128)(2,1)} %collective-permute-done.8.refs_2_), channel_id=1, source_target_pairs={{0,1},{1,0},{2,3},{3,2},{4,5},{5,4},{6,7},{7,6},{8,9},{9,8},{10,11... | collective-permute-start | bytes 786440 | tf_op jit(solution)/shard_map/ppermute | solution.py:534
  55.6 13.8 %collective-permute-start.9 = (bf16[16,64,128]{2,1,0:T(8,128)(2,1)}, bf16[16,64,128]{2,1,0:T(8,128)(2,1)}, u32[]{:S(2)}, u32[]{:S(2)}) collective-permute-start(bf16[16,64,128]{2,1,0:T(8,128)(2,1)} %collective-permute-done.8.refs_2_), channel_id=1, source_target_pairs={{0,2},{1,3},{2,4},{3,5},{4,6},{5,7},{6,0},{7,1},{8,10},{9,11},{10,... | collective-permute-start | bytes 786440 | tf_op jit(solution)/shard_map/ppermute | solution.py:539
  57.5 34.2 %collective-permute-start.18 = (bf16[48,64,128]{2,1,0:T(8,128)(2,1)}, bf16[48,64,128]{2,1,0:T(8,128)(2,1)}, u32[]{:S(2)}, u32[]{:S(2)}) collective-permute-start(bf16[48,64,128]{2,1,0:T(8,128)(2,1)} %collective-permute-done.17.refs_2_), channel_id=1, source_target_pairs={{0,2},{1,3},{2,4},{3,5},{4,6},{5,7},{6,0},{7,1},{8,10},{9,11},{10,... | collective-permute-start | bytes 2359304 | tf_op jit(solution)/shard_map/ppermute | solution.py:539
  69.4 19.8 %collective-permute-start.12 = (bf16[16,64,128]{2,1,0:T(8,128)(2,1)}, bf16[16,64,128]{2,1,0:T(8,128)(2,1)}, u32[]{:S(2)}, u32[]{:S(2)}) collective-permute-start(bf16[16,64,128]{2,1,0:T(8,128)(2,1)} %collective-permute-done.9.refs_0_), channel_id=1, source_target_pairs={{0,1},{1,0},{2,3},{3,2},{4,5},{5,4},{6,7},{7,6},{8,9},{9,8},{10,11... | collective-permute-start | bytes 786440 | tf_op jit(solution)/shard_map/ppermute | solution.py:534
  69.4 19.3 %collective-permute-start.10 = (bf16[16,64,128]{2,1,0:T(8,128)(2,1)}, bf16[16,64,128]{2,1,0:T(8,128)(2,1)}, u32[]{:S(2)}, u32[]{:S(2)}) collective-permute-start(bf16[16,64,128]{2,1,0:T(8,128)(2,1)} %collective-permute-done.9.refs_0_), channel_id=1, source_target_pairs={{0,2},{1,3},{2,4},{3,5},{4,6},{5,7},{6,0},{7,1},{8,10},{9,11},{10,... | collective-permute-start | bytes 786440 | tf_op jit(solution)/shard_map/ppermute | solution.py:545
  69.8 25.0 %collective-permute-start.23 = (bf16[48,64,128]{2,1,0:T(8,128)(2,1)}, bf16[48,64,128]{2,1,0:T(8,128)(2,1)}, u32[]{:S(2)}, u32[]{:S(2)}) collective-permute-start(bf16[48,64,128]{2,1,0:T(8,128)(2,1)} %collective-permute-done.17.refs_2_), channel_id=1, source_target_pairs={{0,1},{1,0},{2,3},{3,2},{4,5},{5,4},{6,7},{7,6},{8,9},{9,8},{10,11... | collective-permute-start | bytes 2359304 | tf_op jit(solution)/shard_map/ppermute | solution.py:534
  88.7 39.7 %collective-permute-start.11 = (bf16[16,64,128]{2,1,0:T(8,128)(2,1)}, bf16[16,64,128]{2,1,0:T(8,128)(2,1)}, u32[]{:S(2)}, u32[]{:S(2)}) collective-permute-start(bf16[16,64,128]{2,1,0:T(8,128)(2,1)} %collective-permute-done.10.mine_ref), channel_id=1, source_target_pairs={{0,1},{1,0},{2,3},{3,2},{4,5},{5,4},{6,7},{7,6},{8,9},{9,8},{10,11... | collective-permute-start | bytes 786440 | tf_op jit(solution)/shard_map/ppermute | solution.py:534
  93.7 14.1 %collective-permute-start.24 = (bf16[24,64,128]{2,1,0:T(8,128)(2,1)}, bf16[24,64,128]{2,1,0:T(8,128)(2,1)}, u32[]{:S(2)}, u32[]{:S(2)}) collective-permute-start(bf16[24,64,128]{2,1,0:T(8,128)(2,1)} %get-tuple-element.22), channel_id=1, source_target_pairs={{0,2},{1,3},{2,4},{3,5},{4,6},{5,7},{6,0},{7,1},{8,10},{9,11},{10,... | collective-permute-start | bytes 1179656 | tf_op jit(solution)/shard_map/ppermute | solution.py:545
  93.7 21.6 %collective-permute-start.19 = (bf16[24,64,128]{2,1,0:T(8,128)(2,1)}, bf16[24,64,128]{2,1,0:T(8,128)(2,1)}, u32[]{:S(2)}, u32[]{:S(2)}) collective-permute-start(bf16[24,64,128]{2,1,0:T(8,128)(2,1)} %get-tuple-element.23), channel_id=1, source_target_pairs={{0,2},{1,3},{2,4},{3,5},{4,6},{5,7},{6,0},{7,1},{8,10},{9,11},{10,... | collective-permute-start | bytes 1179656 | tf_op jit(solution)/shard_map/ppermute | solution.py:545
  94.7 20.5 %collective-permute-start.21 = (bf16[48,64,128]{2,1,0:T(8,128)(2,1)}, bf16[48,64,128]{2,1,0:T(8,128)(2,1)}, u32[]{:S(2)}, u32[]{:S(2)}) collective-permute-start(bf16[48,64,128]{2,1,0:T(8,128)(2,1)} %collective-permute-done.18.refs_0_), channel_id=1, source_target_pairs={{0,1},{1,0},{2,3},{3,2},{4,5},{5,4},{6,7},{7,6},{8,9},{9,8},{10,11... | collective-permute-start | bytes 2359304 | tf_op jit(solution)/shard_map/ppermute | solution.py:534
  107.8 13.3 %collective-permute-start.25 = (bf16[24,64,128]{2,1,0:T(8,128)(2,1)}, bf16[24,64,128]{2,1,0:T(8,128)(2,1)}, u32[]{:S(2)}, u32[]{:S(2)}) collective-permute-start(bf16[24,64,128]{2,1,0:T(8,128)(2,1)} %collective-permute-done.24.mine_ref), channel_id=1, source_target_pairs={{0,1},{1,0},{2,3},{3,2},{4,5},{5,4},{6,7},{7,6},{8,9},{9,8},{10,11... | collective-permute-start | bytes 1179656 | tf_op jit(solution)/shard_map/ppermute | solution.py:534
  115.2 9.5 %collective-permute-start.20 = (bf16[24,64,128]{2,1,0:T(8,128)(2,1)}, bf16[24,64,128]{2,1,0:T(8,128)(2,1)}, u32[]{:S(2)}, u32[]{:S(2)}) collective-permute-start(bf16[24,64,128]{2,1,0:T(8,128)(2,1)} %collective-permute-done.19.mine_ref), channel_id=1, source_target_pairs={{0,1},{1,0},{2,3},{3,2},{4,5},{5,4},{6,7},{7,6},{8,9},{9,8},{10,11... | collective-permute-start | bytes 1179656 | tf_op jit(solution)/shard_map/ppermute | solution.py:534

commit v6 on v5

--- a/solution.py
+++ b/solution.py
@@ -37,38 +37,6 @@
     )
 
 
-def turn_kernel(image_ref, mid_ref, first_ref, last_ref):
-    piece = jnp.swapaxes(image_ref[...], 0, 1)
-    mid_ref[...] = piece
-
-    @pl.when(pl.program_id(0) == 0)
-    def _():
-        first_ref[...] = piece[:REACH]
-
-    @pl.when(pl.program_id(0) == pl.num_programs(0) - 1)
-    def _():
-        last_ref[...] = piece[piece.shape[0] - REACH :]
-
-
-def turned(images, index):
-    _, channels, rows, segment = images.shape
-    step = 2 * RG
-    edge = jax.ShapeDtypeStruct((REACH, channels, segment), jnp.bfloat16)
-    return pl.pallas_call(
-        turn_kernel,
-        out_shape=(jax.ShapeDtypeStruct((rows, channels, segment), jnp.bfloat16), edge, edge),
-        grid=(rows // step,),
-        in_specs=[pl.BlockSpec((None, channels, step, segment), lambda i: (index, 0, i, 0))],
-        out_specs=(
-            pl.BlockSpec((step, channels, segment), lambda i: (i, 0, 0)),
-            whole(edge),
-            whole(edge),
-        ),
-        compiler_params=pltpu.CompilerParams(vmem_limit_bytes=VMEM_LIMIT),
-        cost_estimate=cost(2),
-    )(images)
-
-
 def edge_steps(rows, segment):
     spacing = (rows + 2 * SECOND_DILATION) // (segment // SLOT)
     return spacing, spacing + 2 * FIRST_DILATION
@@ -78,47 +46,58 @@
     return jnp.where(inside, piece, jnp.zeros_like(piece))
 
 
-def pack_kernel(place_ref, *refs, chunks, last_row):
-    mid_ref, edge_ref = refs[0], refs[-1]
-    rows, channels, segment = mid_ref.shape
-    slot_of = lane_iota((channels, segment)) // SLOT
-
-    def row_at(row):
-        if row < 0:
-            return kept(refs[1][row + REACH], place_ref[0] > 0)
-        if row >= rows:
-            return kept(refs[2][row - rows], place_ref[0] < last_row)
-        return mid_ref[row]
-
+def pack_kernel(place_ref, *refs, images, last_row):
+    edge_ref = refs[-1]
+    per_image = (len(refs) - 1) // len(images)
     base = 0
-    for count, first in chunks:
-        spacing, steps = edge_steps(count, segment)
-        for q in range(steps):
-            packed = None
-            for g in range(segment // SLOT):
-                shift = (SLOT * g + SLOT // 2) % segment
-                moved = pltpu.roll(row_at(first - REACH + g * spacing + q), shift, 1)
-                packed = moved if packed is None else jnp.where(slot_of == g, moved, packed)
-            edge_ref[base + q] = packed
-        base += steps
+    for n, chunks in enumerate(images):
+        mid_ref = refs[n * per_image]
+        around = refs[n * per_image + 1 : (n + 1) * per_image]
+        rows, channels, segment = mid_ref.shape
+        slot_of = lane_iota((channels, segment)) // SLOT
+
+        def row_at(row):
+            if row < 0:
+                return kept(around[0][row + REACH], place_ref[0] > 0)
+            if row >= rows:
+                return kept(around[1][row - rows], place_ref[0] < last_row)
+            return mid_ref[row]
+
+        for count, first in chunks:
+            spacing, steps = edge_steps(count, segment)
+            for q in range(steps):
+                packed = None
+                for g in range(segment // SLOT):
+                    shift = (SLOT * g + SLOT // 2) % segment
+                    moved = pltpu.roll(row_at(first - REACH + g * spacing + q), shift, 1)
+                    packed = moved if packed is None else jnp.where(slot_of == g, moved, packed)
+                edge_ref[base + q] = packed
+            base += steps
 
 
 def whole(a):
     return pl.BlockSpec(a.shape, lambda i: (0,) * a.ndim)
 
 
-def pack_edges(place, pieces, chunks, row_count):
-    _, channels, segment = pieces[0].shape
-    total = sum(edge_steps(count, segment)[1] for count, _ in chunks)
+def image_of(a, index):
+    return pl.BlockSpec((None,) + a.shape[1:], lambda i: (index, 0, 0, 0))
+
+
+def pack_edges(place, pieces, images, row_count):
+    channels, segment = pieces[0].shape[2:]
+    total = sum(edge_steps(count, segment)[1] for _, chunks in images for count, _ in chunks)
     return pl.pallas_call(
-        functools.partial(pack_kernel, chunks=chunks, last_row=row_count - 1),
+        functools.partial(
+            pack_kernel, images=tuple(chunks for _, chunks in images), last_row=row_count - 1
+        ),
         out_shape=jax.ShapeDtypeStruct((total, channels, segment), jnp.bfloat16),
         grid=(1,),
-        in_specs=[pl.BlockSpec(memory_space=pltpu.SMEM)] + [whole(a) for a in pieces],
+        in_specs=[pl.BlockSpec(memory_space=pltpu.SMEM)]
+        + [image_of(a, index) for index, _ in images for a in pieces],
         out_specs=pl.BlockSpec((total, channels, segment), lambda i: (0, 0, 0)),
         compiler_params=pltpu.CompilerParams(vmem_limit_bytes=VMEM_LIMIT),
         cost_estimate=cost(2),
-    )(place, *pieces)
+    )(place, *(list(pieces) * len(images)))
 
 
 def feature_kernel(place_ref, *refs, spacing, offset, mesh_shape):
@@ -285,8 +264,8 @@
     lax.fori_loop(0, rows // 8, finish, 0)
 
 
-def unit_features(place, pieces, parts, rows, offset, edges, w1, w2, mesh_shape):
-    _, channels, segment = pieces[0].shape
+def unit_features(place, pieces, index, parts, rows, offset, edges, base, w1, w2, mesh_shape):
+    channels, segment = pieces[0].shape[2:]
     all_rows = rows + 2 * REACH
     hidden_rows = rows + 2 * SECOND_DILATION
     spacing, steps = edge_steps(rows, segment)
@@ -302,8 +281,14 @@
         out_shape=jax.ShapeDtypeStruct((parts * rows, channels, segment), jnp.bfloat16),
         grid=(parts,),
         in_specs=[pl.BlockSpec(memory_space=pltpu.SMEM)]
-        + [whole(a) for a in pieces]
-        + [pl.BlockSpec((steps, channels, segment), lambda i: (i, 0, 0)) for _ in edges]
+        + [image_of(a, index) for a in pieces]
+        + [
+            pl.BlockSpec(
+                (pl.Element(steps), pl.Element(channels), pl.Element(segment)),
+                lambda i: (base + i * steps, 0, 0),
+            )
+            for _ in edges
+        ]
         + [whole(w1), whole(w2)],
         out_specs=pl.BlockSpec((rows, channels, segment), lambda i: (i, 0, 0)),
         scratch_shapes=[
@@ -489,7 +474,7 @@
     row_count = lax.axis_size("rows")
     col_count = lax.axis_size("cols")
     col = lax.axis_index("cols")
-    _, rows, _ = images.shape[1:]
+    _, rows, segment = images.shape[1:]
     place = jnp.stack([lax.axis_index("rows"), col]).astype(jnp.int32)
     ranges = search_ranges.reshape(2, rows // RG)
 
@@ -505,28 +490,23 @@
         partner = lax.ppermute(own, "cols", swap)
         return own, partner, cross
 
-    def features(pieces, parts, count, offset, edges):
+    def features(pieces, index, parts, count, offset, edges, base):
         return unit_features(
-            place, pieces, parts, count, offset, edges, first_weight, second_weight,
-            (row_count, col_count),
+            place, pieces, index, parts, count, offset, edges, base,
+            first_weight, second_weight, (row_count, col_count),
         )
 
-    def rows_of(index):
-        mid, first, last = turned(images, index)
-        above = lax.ppermute(last, "rows", down)
-        below = lax.ppermute(first, "rows", up)
-        return mid, above, below
+    mid = images.transpose(0, 2, 1, 3)
+    above = lax.ppermute(mid[:, rows - REACH :], "rows", down)
+    below = lax.ppermute(mid[:, :REACH], "rows", up)
 
     inner = rows - 2 * RG
-    right_rows = rows_of(1)
-    edges_a = exchanged(right_rows[:1], ((inner, RG),))
-    edges_b = exchanged(right_rows, ((RG, 0), (RG, rows - RG)))
-    right_a = features(right_rows[:1], 1, inner, RG - REACH, edges_a)
-    right_b = features(right_rows, 2, RG, 0, edges_b)
-
-    left_rows = rows_of(0)
-    edges_l = exchanged(left_rows, ((rows, 0),))
-    left = features(left_rows, 1, rows, 0, edges_l)
+    around = (mid, above, below)
+    edges_a = exchanged((mid,), ((1, ((inner, RG),)),))
+    edges_r = exchanged(around, ((1, ((RG, 0), (RG, rows - RG))), (0, ((rows, 0),))))
+    right_a = features((mid,), 1, 1, inner, RG - REACH, edges_a, 0)
+    right_b = features(around, 1, 2, RG, 0, edges_r, 0)
+    left = features(around, 0, 1, rows, 0, edges_r, 2 * edge_steps(RG, segment)[1])
 
     steps = min(col_count // 2 - 1, HOPS // 2)
 

time: 133 us -> 138 us (1.038)
  the two profiles are of different devices: /device:TPU:4 before, /device:TPU:1 now
where the time goes in v6:
time: 138 us; the launch traced here: 137 us
  Pallas kernels  61.7 us (45%)
  waiting for transfers between devices  44.8 us (32%)
  starting transfers between devices  21.9 us (16%)
  local copies, waits for them, and re-layouts  7.12 us (5%)
    pallas_call x3, Pallas kernels, unit_features(): pl.pallas_call(functools.partial(feature_kernel, spacing=spacing, offset=...  27.7 us
    ppermute x3, waiting for transfers between devices, chain(): part = lax.ppermute(part, 'cols', hop)  27.5 us
    pallas_call x4, Pallas kernels, correlate(): pl.pallas_call(functools.partial(gather_kernel, inner=inner, groups=group...  18.6 us
    ppermute x4, waiting for transfers between devices, chain(): mine = lax.ppermute(mine, 'cols', hop)  15.6 us
    pallas_call x3, Pallas kernels, finish(): pl.pallas_call(functools.partial(finish_kernel, first=first, inner=inner,...  9.82 us
    ppermute x2, starting transfers between devices, exchanged(): cross = lax.ppermute(own, 'cols', across)  6.64 us
    pallas_call x2, Pallas kernels, pack_edges(): pl.pallas_call(functools.partial(pack_kernel, images=tuple((chunks for _,...  5.65 us
    ppermute x9, starting transfers between devices, pair(): return (mine, lax.ppermute(mine, 'cols', swap))  5.53 us
  transfers between devices with their start and end apart: 22, of which 5 were waited for; matrix products, arithmetic and copies ran while one was open for 2% of the time, Pallas kernels for 43%

profile of v6, /device:TPU:1, one launch (start us, length us, event | category | flops | bytes accessed | tf_op | source)
XLA Modules:
  0.0 136.9 jit_solution(14328577096345215063)
XLA Ops:
  0.6 2.9 %copy.14 = bf16[2,64,64,128]{3,1,2,0:T(8,128)(2,1)S(1)} copy(bf16[2,64,64,128]{3,2,1,0:T(8,128)(2,1)} %param.4) | data formatting | bytes 4194304 | tf_op args[0]
  3.6 1.3 copy-done
  4.9 0.8 fusion
  5.7 2.0 %collective-permute-start = (bf16[2,6,64,128]{3,2,1,0:T(8,128)(2,1)}, bf16[2,6,64,128]{3,2,1,0:T(8,128)(2,1)}, u32[]{:S(2)}, u32[]{:S(2)}) collective-permute-start(bf16[2,6,64,128]{3,2,1,0:T(8,128)(2,1)} %get-tuple-element.11), channel_id=1, source_target_pairs={{0,8},{8,16},{16,24},{24,0},{1,9},{9,17},{17,25},{25,1},{2,10},{10... | collective-permute-start | bytes 589832 | tf_op jit(solution)/shard_map/ppermute | solution.py:500
  7.7 1.0 collective-permute-start.1
  8.7 0.6 pad_add_fusion.place_ref
  9.3 2.3 %shard_map.64.refs_1_ = bf16[11,64,128]{2,1,0:T(8,128)(2,1)} custom-call(s32[2]{0:T(128)} %pad_add_fusion.place_ref, bf16[2,64,64,128]{3,2,1,0:T(8,128)(2,1)} %bitcast.7), custom_call_target="tpu_custom_call" | custom-call | flops 2000000000 | bytes 6000000 | tf_op jit(solution)/shard_map/pallas_call | solution.py:89
  11.7 1.0 collective-permute-start.11
  12.6 3.6 %collective-permute-start.12 = (bf16[11,64,128]{2,1,0:T(8,128)(2,1)}, bf16[11,64,128]{2,1,0:T(8,128)(2,1)}, u32[]{:S(2)}, u32[]{:S(2)}) collective-permute-start(bf16[11,64,128]{2,1,0:T(8,128)(2,1)} %shard_map.64.refs_1_), channel_id=1, source_target_pairs={{1,2},{3,4},{5,6},{2,1},{4,3},{6,5},{9,10},{11,12},{13,14},{10,9},... | collective-permute-start | bytes 540680 | tf_op jit(solution)/shard_map/ppermute | solution.py:489
  16.2 0.0 collective-permute-done.refs_1_.refs_4_
  16.2 1.6 %collective-permute-done.1.refs_2_.refs_5_ = bf16[2,6,64,128]{3,2,1,0:T(8,128)(2,1)} collective-permute-done((bf16[2,6,64,128]{3,2,1,0:T(8,128)(2,1)}, bf16[2,6,64,128]{3,2,1,0:T(8,128)(2,1)}, u32[]{:S(2)}, u32[]{:S(2)}) %collective-permute-start.1) | collective-permute-done | bytes 196640 | tf_op jit(solution)/shard_map/ppermute | solution.py:501
  17.8 3.3 %shard_map.59.refs_3_ = bf16[25,64,128]{2,1,0:T(8,128)(2,1)} custom-call(s32[2]{0:T(128)} %pad_add_fusion.place_ref, bf16[2,64,64,128]{3,2,1,0:T(8,128)(2,1)} %bitcast.8, bf16[2,6,64,128]{3,2,1,0:T(8,128)(2,1)} %collective-permute-done.refs_1_.refs_4_, bf16[2,6,64,128]{3,2,1,0:T(8,128)(2,1)} %collective-permute-done.1.refs_2_.refs_5_, ...), custom_call_target="tpu_custom_call" | custom-call | flops 2000000000 | bytes 6000000 | tf_op jit(solution)/shard_map/pallas_call | solution.py:89
  21.1 1.5 %collective-permute-start.2 = (bf16[25,64,128]{2,1,0:T(8,128)(2,1)}, bf16[25,64,128]{2,1,0:T(8,128)(2,1)}, u32[]{:S(2)}, u32[]{:S(2)}) collective-permute-start(bf16[25,64,128]{2,1,0:T(8,128)(2,1)} %shard_map.59.refs_3_), channel_id=1, source_target_pairs={{0,1},{1,0},{2,3},{3,2},{4,5},{5,4},{6,7},{7,6},{8,9},{9,8},{10,11... | collective-permute-start | bytes 1228808 | tf_op jit(solution)/shard_map/ppermute | solution.py:490
  22.6 3.1 %collective-permute-start.3 = (bf16[25,64,128]{2,1,0:T(8,128)(2,1)}, bf16[25,64,128]{2,1,0:T(8,128)(2,1)}, u32[]{:S(2)}, u32[]{:S(2)}) collective-permute-start(bf16[25,64,128]{2,1,0:T(8,128)(2,1)} %shard_map.59.refs_3_), channel_id=1, source_target_pairs={{1,2},{3,4},{5,6},{2,1},{4,3},{6,5},{9,10},{11,12},{13,14},{10,9},... | collective-permute-start | bytes 1228808 | tf_op jit(solution)/shard_map/ppermute | solution.py:489
  25.7 0.0 collective-permute-done.11.refs_2_
  25.7 9.0 %shard_map.65.refs_0_ = bf16[48,64,128]{2,1,0:T(8,128)(2,1)} custom-call(s32[2]{0:T(128)} %pad_add_fusion.place_ref, bf16[2,64,64,128]{3,2,1,0:T(8,128)(2,1)} %bitcast.10, bf16[11,64,128]{2,1,0:T(8,128)(2,1)} %shard_map.64.refs_1_, bf16[11,64,128]{2,1,0:T(8,128)(2,1)} %collective-permute-done.11.refs_2_, ...), custom_call_target="tpu_custom_call" | custom-call | flops 9600000000 | bytes 28800000 | tf_op jit(solution)/shard_map/pallas_call | solution.py:279
  34.7 1.3 collective-permute-start.13
  36.0 0.0 collective-permute-done.2.refs_4_
  36.0 7.9 %shard_map.61.refs_0_ = bf16[16,64,128]{2,1,0:T(8,128)(2,1)} custom-call(s32[2]{0:T(128)} %pad_add_fusion.place_ref, bf16[2,64,64,128]{3,2,1,0:T(8,128)(2,1)} %bitcast.11, bf16[2,6,64,128]{3,2,1,0:T(8,128)(2,1)} %collective-permute-done.refs_1_.refs_4_, bf16[2,6,64,128]{3,2,1,0:T(8,128)(2,1)} %collective-permute-done.1.refs_2_.refs_5_, ...), custom_call_target="tpu_custom_call" | custom-call | flops 3200000000 | bytes 9600000 | tf_op jit(solution)/shard_map/pallas_call | solution.py:279
  43.9 1.3 collective-permute-start.4
  45.2 0.0 collective-permute-start.18
  45.2 0.5 collective-permute-start.9
  45.7 15.6 %collective-permute-done.4.refs_2_ = bf16[16,64,128]{2,1,0:T(8,128)(2,1)} collective-permute-done((bf16[16,64,128]{2,1,0:T(8,128)(2,1)}, bf16[16,64,128]{2,1,0:T(8,128)(2,1)}, u32[]{:S(2)}, u32[]{:S(2)}) %collective-permute-start.4) | collective-permute-done | bytes 262176 | tf_op jit(solution)/shard_map/ppermute | solution.py:519
  61.3 0.5 collective-permute-start.10
  61.9 1.3 collective-permute-start.14
  63.2 10.8 %shard_map.60.left_ref = bf16[64,64,128]{2,1,0:T(8,128)(2,1)} custom-call(s32[2]{0:T(128)} %pad_add_fusion.place_ref, bf16[2,64,64,128]{3,2,1,0:T(8,128)(2,1)} %bitcast.12, bf16[2,6,64,128]{3,2,1,0:T(8,128)(2,1)} %collective-permute-done.refs_1_.refs_4_, bf16[2,6,64,128]{3,2,1,0:T(8,128)(2,1)} %collective-permute-done.1.refs_2_.refs_5_, ...), custom_call_target="tpu_custom_call" | custom-call | flops 12800000000 | bytes 38400000 | tf_op jit(solution)/shard_map/pallas_call | solution.py:279
  74.0 0.3 collective-permute-start.19
  74.3 0.3 collective-permute-start.6
  74.6 0.5 collective-permute-start.8
  75.1 3.2 %shard_map.62.refs_2_ = f32[16,128,128]{2,1,0:T(8,128)} custom-call(s32[2]{0:T(128)} %pad_add_fusion.place_ref, s32[2,8]{1,0:T(2,128)} %bitcast.13, bf16[64,64,128]{2,1,0:T(8,128)(2,1)} %shard_map.60.left_ref, bf16[16,64,128]{2,1,0:T(8,128)(2,1)} %shard_map.61.refs_0_, bf16[16,64,128]{2,1,0:T(8,128)(2,1)} %collective-permute-done.9.refs_1_, ...), custom_call_target="tpu_custom_call" | custom-call | flops 3000000000 | bytes 9000000 | tf_op jit(solution)/shard_map/pallas_call | solution.py:411
  78.3 15.2 %collective-permute-done.6.mine_ref = bf16[16,64,128]{2,1,0:T(8,128)(2,1)} collective-permute-done((bf16[16,64,128]{2,1,0:T(8,128)(2,1)}, bf16[16,64,128]{2,1,0:T(8,128)(2,1)}, u32[]{:S(2)}, u32[]{:S(2)}) %collective-permute-start.6) | collective-permute-done | bytes 262176 | tf_op jit(solution)/shard_map/ppermute | solution.py:525
  93.5 1.2 collective-permute-start.7
  94.6 0.0 collective-permute-done.8.refs_1_
  94.6 2.4 %shard_map.63.acc_in_ref = f32[16,128,128]{2,1,0:T(8,128)} custom-call(s32[2]{0:T(128)} %pad_add_fusion.place_ref, s32[2,8]{1,0:T(2,128)} %bitcast.14, bf16[64,64,128]{2,1,0:T(8,128)(2,1)} %shard_map.60.left_ref, bf16[16,64,128]{2,1,0:T(8,128)(2,1)} %collective-permute-done.5.refs_0_, ...), custom_call_target="tpu_custom_call", output_to_operand_aliasing={{}: (5, {})} | custom-call | flops 3000000000 | bytes 9000000 | tf_op jit(solution)/shard_map/pallas_call | solution.py:411
  97.0 2.1 %fusion.1 = (bf16[24,64,128]{2,1,0:T(8,128)(2,1)}, bf16[24,64,128]{2,1,0:T(8,128)(2,1)}) fusion(bf16[48,64,128]{2,1,0:T(8,128)(2,1)} %collective-permute-done.14.refs_0_), kind=kLoop, calls=%fused_computation.3 | loop fusion | bytes 1572864 | tf_op jit(solution)/shard_map/slice | solution.py:524
  99.1 0.0 collective-permute-start.15
  99.1 0.0 collective-permute-done.18.refs_1_
  99.1 0.4 collective-permute-start.17
  99.5 0.0 collective-permute-done.19.refs_3_
  99.5 7.1 %shard_map.66.refs_2_ = f32[48,128,128]{2,1,0:T(8,128)} custom-call(s32[2]{0:T(128)} %pad_add_fusion.place_ref, s32[2,8]{1,0:T(2,128)} %bitcast.15, bf16[64,64,128]{2,1,0:T(8,128)(2,1)} %shard_map.60.left_ref, bf16[48,64,128]{2,1,0:T(8,128)(2,1)} %shard_map.65.refs_0_, bf16[48,64,128]{2,1,0:T(8,128)(2,1)} %collective-permute-done.18.refs_1_, ...), custom_call_target="tpu_custom_call" | custom-call | flops 8999999488 | bytes 27000000 | tf_op jit(solution)/shard_map/pallas_call | solution.py:411
  106.6 5.3 %collective-permute-done.15.mine_ref = bf16[24,64,128]{2,1,0:T(8,128)(2,1)} collective-permute-done((bf16[24,64,128]{2,1,0:T(8,128)(2,1)}, bf16[24,64,128]{2,1,0:T(8,128)(2,1)}, u32[]{:S(2)}, u32[]{:S(2)}) %collective-permute-start.15) | collective-permute-done | bytes 393248 | tf_op jit(solution)/shard_map/ppermute | solution.py:525
  111.9 1.3 collective-permute-start.16
  113.2 7.1 %collective-permute-done.20.mine_ref = bf16[24,64,128]{2,1,0:T(8,128)(2,1)} collective-permute-done((bf16[24,64,128]{2,1,0:T(8,128)(2,1)}, bf16[24,64,128]{2,1,0:T(8,128)(2,1)}, u32[]{:S(2)}, u32[]{:S(2)}) %collective-permute-start.20) | collective-permute-done | bytes 393248 | tf_op jit(solution)/shard_map/ppermute | solution.py:525
  120.3 0.9 collective-permute-start.21
  121.2 5.8 %shard_map.67.acc_in_ref = f32[48,128,128]{2,1,0:T(8,128)} custom-call(s32[2]{0:T(128)} %pad_add_fusion.place_ref, s32[2,8]{1,0:T(2,128)} %bitcast.16, bf16[64,64,128]{2,1,0:T(8,128)(2,1)} %shard_map.60.left_ref, bf16[48,64,128]{2,1,0:T(8,128)(2,1)} %collective-permute-done.14.refs_0_, ...), custom_call_target="tpu_custom_call", output_to_operand_aliasing={{}: (5, {})} | custom-call | flops 8999999488 | bytes 27000000 | tf_op jit(solution)/shard_map/pallas_call | solution.py:411
  127.0 3.7 %shard_map.68 = (bf16[64,64,128]{2,1,0:T(8,128)(2,1)}, f32[64,128]{1,0:T(8,128)}) custom-call(s32[2]{0:T(128)} %pad_add_fusion.place_ref, s32[2,8]{1,0:T(2,128)} %bitcast.17, bf16[64,64,128]{2,1,0:T(8,128)(2,1)} %shard_map.60.left_ref, bf16[24,64,128]{2,1,0:T(8,128)(2,1)} %collective-permute-done.20.mine_ref, ...), custom_call_target="tpu_custom_call" | custom-call | flops 3000000000 | bytes 9000000 | tf_op jit(solution)/shard_map/pallas_call | solution.py:438
  130.7 3.7 %shard_map.69 = (bf16[64,64,128]{2,1,0:T(8,128)(2,1)}, f32[64,128]{1,0:T(8,128)}) custom-call(s32[2]{0:T(128)} %pad_add_fusion.place_ref, s32[2,8]{1,0:T(2,128)} %bitcast.18, bf16[64,64,128]{2,1,0:T(8,128)(2,1)} %shard_map.60.left_ref, bf16[24,64,128]{2,1,0:T(8,128)(2,1)} %collective-permute-done.15.mine_ref, ...), custom_call_target="tpu_custom_call", output_to_operand_aliasing={{0}: (6, {}), {1}: (7, {})} | custom-call | flops 3000000000 | bytes 9000000 | tf_op jit(solution)/shard_map/pallas_call | solution.py:438
  134.4 2.5 %shard_map.70 = (bf16[64,64,128]{2,1,0:T(8,128)(2,1)}, f32[64,128]{1,0:T(8,128)}) custom-call(s32[2]{0:T(128)} %pad_add_fusion.place_ref, s32[2,8]{1,0:T(2,128)} %bitcast.19, bf16[64,64,128]{2,1,0:T(8,128)(2,1)} %shard_map.60.left_ref, bf16[16,64,128]{2,1,0:T(8,128)(2,1)} %collective-permute-done.6.mine_ref, ...), custom_call_target="tpu_custom_call", output_to_operand_aliasing={{0}: (6, {}), {1}: (7, {})} | custom-call | flops 2000000000 | bytes 6000000 | tf_op jit(solution)/shard_map/pallas_call | solution.py:438
  (14 shorter events, 0.0 us)
Async XLA Ops:
  3.6 1.3 copy-start
  5.7 10.5 %collective-permute-start = (bf16[2,6,64,128]{3,2,1,0:T(8,128)(2,1)}, bf16[2,6,64,128]{3,2,1,0:T(8,128)(2,1)}, u32[]{:S(2)}, u32[]{:S(2)}) collective-permute-start(bf16[2,6,64,128]{3,2,1,0:T(8,128)(2,1)} %get-tuple-element.11), channel_id=1, source_target_pairs={{0,8},{8,16},{16,24},{24,0},{1,9},{9,17},{17,25},{25,1},{2,10},{10... | collective-permute-start | bytes 589832 | tf_op jit(solution)/shard_map/ppermute | solution.py:500
  7.7 10.1 %collective-permute-start.1 = (bf16[2,6,64,128]{3,2,1,0:T(8,128)(2,1)}, bf16[2,6,64,128]{3,2,1,0:T(8,128)(2,1)}, u32[]{:S(2)}, u32[]{:S(2)}) collective-permute-start(bf16[2,6,64,128]{3,2,1,0:T(8,128)(2,1)} %get-tuple-element.10), channel_id=1, source_target_pairs={{8,0},{16,8},{24,16},{0,24},{9,1},{17,9},{25,17},{1,25},{10,2},{18... | collective-permute-start | bytes 589832 | tf_op jit(solution)/shard_map/ppermute | solution.py:501
  11.7 14.1 %collective-permute-start.11 = (bf16[11,64,128]{2,1,0:T(8,128)(2,1)}, bf16[11,64,128]{2,1,0:T(8,128)(2,1)}, u32[]{:S(2)}, u32[]{:S(2)}) collective-permute-start(bf16[11,64,128]{2,1,0:T(8,128)(2,1)} %shard_map.64.refs_1_), channel_id=1, source_target_pairs={{0,1},{1,0},{2,3},{3,2},{4,5},{5,4},{6,7},{7,6},{8,9},{9,8},{10,11... | collective-permute-start | bytes 540680 | tf_op jit(solution)/shard_map/ppermute | solution.py:490
  12.6 13.1 %collective-permute-start.12 = (bf16[11,64,128]{2,1,0:T(8,128)(2,1)}, bf16[11,64,128]{2,1,0:T(8,128)(2,1)}, u32[]{:S(2)}, u32[]{:S(2)}) collective-permute-start(bf16[11,64,128]{2,1,0:T(8,128)(2,1)} %shard_map.64.refs_1_), channel_id=1, source_target_pairs={{1,2},{3,4},{5,6},{2,1},{4,3},{6,5},{9,10},{11,12},{13,14},{10,9},... | collective-permute-start | bytes 540680 | tf_op jit(solution)/shard_map/ppermute | solution.py:489
  21.1 14.9 %collective-permute-start.2 = (bf16[25,64,128]{2,1,0:T(8,128)(2,1)}, bf16[25,64,128]{2,1,0:T(8,128)(2,1)}, u32[]{:S(2)}, u32[]{:S(2)}) collective-permute-start(bf16[25,64,128]{2,1,0:T(8,128)(2,1)} %shard_map.59.refs_3_), channel_id=1, source_target_pairs={{0,1},{1,0},{2,3},{3,2},{4,5},{5,4},{6,7},{7,6},{8,9},{9,8},{10,11... | collective-permute-start | bytes 1228808 | tf_op jit(solution)/shard_map/ppermute | solution.py:490
  22.6 13.4 %collective-permute-start.3 = (bf16[25,64,128]{2,1,0:T(8,128)(2,1)}, bf16[25,64,128]{2,1,0:T(8,128)(2,1)}, u32[]{:S(2)}, u32[]{:S(2)}) collective-permute-start(bf16[25,64,128]{2,1,0:T(8,128)(2,1)} %shard_map.59.refs_3_), channel_id=1, source_target_pairs={{1,2},{3,4},{5,6},{2,1},{4,3},{6,5},{9,10},{11,12},{13,14},{10,9},... | collective-permute-start | bytes 1228808 | tf_op jit(solution)/shard_map/ppermute | solution.py:489
  34.7 27.1 %collective-permute-start.13 = (bf16[48,64,128]{2,1,0:T(8,128)(2,1)}, bf16[48,64,128]{2,1,0:T(8,128)(2,1)}, u32[]{:S(2)}, u32[]{:S(2)}) collective-permute-start(bf16[48,64,128]{2,1,0:T(8,128)(2,1)} %shard_map.65.refs_0_), channel_id=1, source_target_pairs={{0,2},{1,3},{2,4},{3,5},{4,6},{5,7},{6,0},{7,1},{8,10},{9,11},{10,... | collective-permute-start | bytes 2359304 | tf_op jit(solution)/shard_map/ppermute | solution.py:519
  43.9 17.4 %collective-permute-start.4 = (bf16[16,64,128]{2,1,0:T(8,128)(2,1)}, bf16[16,64,128]{2,1,0:T(8,128)(2,1)}, u32[]{:S(2)}, u32[]{:S(2)}) collective-permute-start(bf16[16,64,128]{2,1,0:T(8,128)(2,1)} %shard_map.61.refs_0_), channel_id=1, source_target_pairs={{0,2},{1,3},{2,4},{3,5},{4,6},{5,7},{6,0},{7,1},{8,10},{9,11},{10,... | collective-permute-start | bytes 786440 | tf_op jit(solution)/shard_map/ppermute | solution.py:519
  45.2 53.9 %collective-permute-start.18 = (bf16[48,64,128]{2,1,0:T(8,128)(2,1)}, bf16[48,64,128]{2,1,0:T(8,128)(2,1)}, u32[]{:S(2)}, u32[]{:S(2)}) collective-permute-start(bf16[48,64,128]{2,1,0:T(8,128)(2,1)} %shard_map.65.refs_0_), channel_id=1, source_target_pairs={{0,1},{1,0},{2,3},{3,2},{4,5},{5,4},{6,7},{7,6},{8,9},{9,8},{10,11... | collective-permute-start | bytes 2359304 | tf_op jit(solution)/shard_map/ppermute | solution.py:514
  45.2 28.7 %collective-permute-start.9 = (bf16[16,64,128]{2,1,0:T(8,128)(2,1)}, bf16[16,64,128]{2,1,0:T(8,128)(2,1)}, u32[]{:S(2)}, u32[]{:S(2)}) collective-permute-start(bf16[16,64,128]{2,1,0:T(8,128)(2,1)} %shard_map.61.refs_0_), channel_id=1, source_target_pairs={{0,1},{1,0},{2,3},{3,2},{4,5},{5,4},{6,7},{7,6},{8,9},{9,8},{10,11... | collective-permute-start | bytes 786440 | tf_op jit(solution)/shard_map/ppermute | solution.py:514
  61.3 12.9 %collective-permute-start.5 = (bf16[16,64,128]{2,1,0:T(8,128)(2,1)}, bf16[16,64,128]{2,1,0:T(8,128)(2,1)}, u32[]{:S(2)}, u32[]{:S(2)}) collective-permute-start(bf16[16,64,128]{2,1,0:T(8,128)(2,1)} %collective-permute-done.4.refs_2_), channel_id=1, source_target_pairs={{0,2},{1,3},{2,4},{3,5},{4,6},{5,7},{6,0},{7,1},{8,10},{9,11},{10,... | collective-permute-start | bytes 786440 | tf_op jit(solution)/shard_map/ppermute | solution.py:519
  61.3 13.2 %collective-permute-start.10 = (bf16[16,64,128]{2,1,0:T(8,128)(2,1)}, bf16[16,64,128]{2,1,0:T(8,128)(2,1)}, u32[]{:S(2)}, u32[]{:S(2)}) collective-permute-start(bf16[16,64,128]{2,1,0:T(8,128)(2,1)} %collective-permute-done.4.refs_2_), channel_id=1, source_target_pairs={{0,1},{1,0},{2,3},{3,2},{4,5},{5,4},{6,7},{7,6},{8,9},{9,8},{10,11... | collective-permute-start | bytes 786440 | tf_op jit(solution)/shard_map/ppermute | solution.py:514
  61.9 35.2 %collective-permute-start.14 = (bf16[48,64,128]{2,1,0:T(8,128)(2,1)}, bf16[48,64,128]{2,1,0:T(8,128)(2,1)}, u32[]{:S(2)}, u32[]{:S(2)}) collective-permute-start(bf16[48,64,128]{2,1,0:T(8,128)(2,1)} %collective-permute-done.13.refs_2_), channel_id=1, source_target_pairs={{0,2},{1,3},{2,4},{3,5},{4,6},{5,7},{6,0},{7,1},{8,10},{9,11},{10,... | collective-permute-start | bytes 2359304 | tf_op jit(solution)/shard_map/ppermute | solution.py:519
  74.0 25.5 %collective-permute-start.19 = (bf16[48,64,128]{2,1,0:T(8,128)(2,1)}, bf16[48,64,128]{2,1,0:T(8,128)(2,1)}, u32[]{:S(2)}, u32[]{:S(2)}) collective-permute-start(bf16[48,64,128]{2,1,0:T(8,128)(2,1)} %collective-permute-done.13.refs_2_), channel_id=1, source_target_pairs={{0,1},{1,0},{2,3},{3,2},{4,5},{5,4},{6,7},{7,6},{8,9},{9,8},{10,11... | collective-permute-start | bytes 2359304 | tf_op jit(solution)/shard_map/ppermute | solution.py:514
  74.3 19.2 %collective-permute-start.6 = (bf16[16,64,128]{2,1,0:T(8,128)(2,1)}, bf16[16,64,128]{2,1,0:T(8,128)(2,1)}, u32[]{:S(2)}, u32[]{:S(2)}) collective-permute-start(bf16[16,64,128]{2,1,0:T(8,128)(2,1)} %collective-permute-done.5.refs_0_), channel_id=1, source_target_pairs={{0,2},{1,3},{2,4},{3,5},{4,6},{5,7},{6,0},{7,1},{8,10},{9,11},{10,... | collective-permute-start | bytes 786440 | tf_op jit(solution)/shard_map/ppermute | solution.py:525
  74.6 20.1 %collective-permute-start.8 = (bf16[16,64,128]{2,1,0:T(8,128)(2,1)}, bf16[16,64,128]{2,1,0:T(8,128)(2,1)}, u32[]{:S(2)}, u32[]{:S(2)}) collective-permute-start(bf16[16,64,128]{2,1,0:T(8,128)(2,1)} %collective-permute-done.5.refs_0_), channel_id=1, source_target_pairs={{0,1},{1,0},{2,3},{3,2},{4,5},{5,4},{6,7},{7,6},{8,9},{9,8},{10,11... | collective-permute-start | bytes 786440 | tf_op jit(solution)/shard_map/ppermute | solution.py:514
  93.5 40.9 %collective-permute-start.7 = (bf16[16,64,128]{2,1,0:T(8,128)(2,1)}, bf16[16,64,128]{2,1,0:T(8,128)(2,1)}, u32[]{:S(2)}, u32[]{:S(2)}) collective-permute-start(bf16[16,64,128]{2,1,0:T(8,128)(2,1)} %collective-permute-done.6.mine_ref), channel_id=1, source_target_pairs={{0,1},{1,0},{2,3},{3,2},{4,5},{5,4},{6,7},{7,6},{8,9},{9,8},{10,11... | collective-permute-start | bytes 786440 | tf_op jit(solution)/shard_map/ppermute | solution.py:514
  99.1 12.8 %collective-permute-start.15 = (bf16[24,64,128]{2,1,0:T(8,128)(2,1)}, bf16[24,64,128]{2,1,0:T(8,128)(2,1)}, u32[]{:S(2)}, u32[]{:S(2)}) collective-permute-start(bf16[24,64,128]{2,1,0:T(8,128)(2,1)} %get-tuple-element.13), channel_id=1, source_target_pairs={{0,2},{1,3},{2,4},{3,5},{4,6},{5,7},{6,0},{7,1},{8,10},{9,11},{10,... | collective-permute-start | bytes 1179656 | tf_op jit(solution)/shard_map/ppermute | solution.py:525
  99.1 21.2 %collective-permute-start.20 = (bf16[24,64,128]{2,1,0:T(8,128)(2,1)}, bf16[24,64,128]{2,1,0:T(8,128)(2,1)}, u32[]{:S(2)}, u32[]{:S(2)}) collective-permute-start(bf16[24,64,128]{2,1,0:T(8,128)(2,1)} %get-tuple-element.12), channel_id=1, source_target_pairs={{0,2},{1,3},{2,4},{3,5},{4,6},{5,7},{6,0},{7,1},{8,10},{9,11},{10,... | collective-permute-start | bytes 1179656 | tf_op jit(solution)/shard_map/ppermute | solution.py:525
  99.1 22.1 %collective-permute-start.17 = (bf16[48,64,128]{2,1,0:T(8,128)(2,1)}, bf16[48,64,128]{2,1,0:T(8,128)(2,1)}, u32[]{:S(2)}, u32[]{:S(2)}) collective-permute-start(bf16[48,64,128]{2,1,0:T(8,128)(2,1)} %collective-permute-done.14.refs_0_), channel_id=1, source_target_pairs={{0,1},{1,0},{2,3},{3,2},{4,5},{5,4},{6,7},{7,6},{8,9},{9,8},{10,11... | collective-permute-start | bytes 2359304 | tf_op jit(solution)/shard_map/ppermute | solution.py:514
  111.9 18.8 %collective-permute-start.16 = (bf16[24,64,128]{2,1,0:T(8,128)(2,1)}, bf16[24,64,128]{2,1,0:T(8,128)(2,1)}, u32[]{:S(2)}, u32[]{:S(2)}) collective-permute-start(bf16[24,64,128]{2,1,0:T(8,128)(2,1)} %collective-permute-done.15.mine_ref), channel_id=1, source_target_pairs={{0,1},{1,0},{2,3},{3,2},{4,5},{5,4},{6,7},{7,6},{8,9},{9,8},{10,11... | collective-permute-start | bytes 1179656 | tf_op jit(solution)/shard_map/ppermute | solution.py:514
  120.3 6.7 %collective-permute-start.21 = (bf16[24,64,128]{2,1,0:T(8,128)(2,1)}, bf16[24,64,128]{2,1,0:T(8,128)(2,1)}, u32[]{:S(2)}, u32[]{:S(2)}) collective-permute-start(bf16[24,64,128]{2,1,0:T(8,128)(2,1)} %collective-permute-done.20.mine_ref), channel_id=1, source_target_pairs={{0,1},{1,0},{2,3},{3,2},{4,5},{5,4},{6,7},{7,6},{8,9},{9,8},{10,11... | collective-permute-start | bytes 1179656 | tf_op jit(solution)/shard_map/ppermute | solution.py:514

commit v7 on v6

--- a/solution.py
+++ b/solution.py
@@ -15,6 +15,8 @@
 REACH = FIRST_DILATION + SECOND_DILATION
 SLOT = 16
 
+EXTRA = 16
+
 sharpness_divisor = 10.0
 epsilon = 1e-05
 VMEM_LIMIT = 64 << 20
@@ -46,9 +48,12 @@
     return jnp.where(inside, piece, jnp.zeros_like(piece))
 
 
-def pack_kernel(place_ref, *refs, images, last_row):
+def pack_kernel(*refs, images, last_row):
     edge_ref = refs[-1]
-    per_image = (len(refs) - 1) // len(images)
+    alone = len(refs) == 2
+    place_ref = None if alone else refs[0]
+    refs = refs[:-1] if alone else refs[1:-1]
+    per_image = len(refs) // len(images)
     base = 0
     for n, chunks in enumerate(images):
         mid_ref = refs[n * per_image]
@@ -86,18 +91,19 @@
 def pack_edges(place, pieces, images, row_count):
     channels, segment = pieces[0].shape[2:]
     total = sum(edge_steps(count, segment)[1] for _, chunks in images for count, _ in chunks)
+    given = () if len(pieces) == 1 else (place,)
+    scalars = [pl.BlockSpec(memory_space=pltpu.SMEM)] * len(given)
     return pl.pallas_call(
         functools.partial(
             pack_kernel, images=tuple(chunks for _, chunks in images), last_row=row_count - 1
         ),
         out_shape=jax.ShapeDtypeStruct((total, channels, segment), jnp.bfloat16),
         grid=(1,),
-        in_specs=[pl.BlockSpec(memory_space=pltpu.SMEM)]
-        + [image_of(a, index) for index, _ in images for a in pieces],
+        in_specs=scalars + [image_of(a, index) for index, _ in images for a in pieces],
         out_specs=pl.BlockSpec((total, channels, segment), lambda i: (0, 0, 0)),
         compiler_params=pltpu.CompilerParams(vmem_limit_bytes=VMEM_LIMIT),
         cost_estimate=cost(2),
-    )(place, *(list(pieces) * len(images)))
+    )(*given, *(list(pieces) * len(images)))
 
 
 def feature_kernel(place_ref, *refs, spacing, offset, mesh_shape):
@@ -163,29 +169,31 @@
         target[channels : 2 * channels, lo : lo + segment] = main
         target[2 * channels :, lo : lo + segment] = after
 
-    def multiply(source, product_ref, base):
-        product = jnp.dot(w_ref[...], source[...], preferred_element_type=jnp.float32)
-        for j in range(width):
-            product_ref[base + j] = product[:, j * segment : (j + 1) * segment]
-
-    def conv(source_ref, skip, sides_ref, product_ref, total, amount):
-        def build(t, target):
-            for j in range(width):
-                row = jnp.minimum(t * width + j, total - 1)
-                slot = jnp.minimum(row // spacing, groups - 1)
-                main = source_ref[row + skip]
-                put(target, j, main, *shifted(main, sides_ref[row - slot * spacing], slot, amount))
+    def conv(source_ref, skip, sides_ref, product_ref, amount):
+        def build(q, target):
+            q = jnp.minimum(q, spacing - 1)
+            side = sides_ref[q]
+            for slot in range(groups):
+                main = source_ref[slot * spacing + q + skip]
+                put(target, slot, main, *shifted(main, side, slot, amount))
+
+        def multiply_rows(q, source):
+            product = jnp.dot(w_ref[...], source[...], preferred_element_type=jnp.float32)
+            for slot in range(groups):
+                product_ref[slot * spacing + q] = product[:, slot * segment : (slot + 1) * segment]
 
         build(0, rhs0_ref)
 
         def body(u, _):
             build(2 * u + 1, rhs1_ref)
-            multiply(rhs0_ref, product_ref, 2 * u * width)
+            multiply_rows(2 * u, rhs0_ref)
             build(2 * u + 2, rhs0_ref)
-            multiply(rhs1_ref, product_ref, (2 * u + 1) * width)
+            multiply_rows(2 * u + 1, rhs1_ref)
             return 0
 
-        lax.fori_loop(0, pl.cdiv(total, 2 * width), body, 0)
+        lax.fori_loop(0, spacing // 2, body, 0)
+        if spacing % 2:
+            multiply_rows(spacing - 1, rhs0_ref)
 
     if ends:
         top = kept(refs[1][...], ~first_row)
@@ -210,14 +218,27 @@
         x_ref = mid_ref
 
     stack(w1_ref)
-    conv(x_ref, offset, side_ref, p1_ref, all_rows, d1)
-
-    for t in range(pl.cdiv(steps, width)):
+    conv(x_ref, offset, side_ref, p1_ref, d1)
+
+    pending = [
+        (p1_ref, row, x_ref[row + offset], groups - 1, row - (groups - 1) * spacing)
+        for row in range(groups * spacing, all_rows)
+    ]
+    pending += [(p1e_ref, q, edge_ref[q], None, None) for q in range(steps)]
+    for t in range(pl.cdiv(len(pending), width)):
         target = rhs[t % 2]
-        for j in range(width):
-            main = edge_ref[min(t * width + j, steps - 1)]
-            put(target, j, main, pltpu.roll(main, d1, 1), pltpu.roll(main, segment - d1, 1))
-        multiply(target, p1e_ref, t * width)
+        batch = pending[t * width : (t + 1) * width]
+        for j, (_, _, main, slot, q) in enumerate(batch):
+            if slot is None:
+                moved = pltpu.roll(main, d1, 1), pltpu.roll(main, segment - d1, 1)
+            else:
+                moved = shifted(main, side_ref[q], slot, d1)
+            put(target, j, main, *moved)
+        product = jnp.dot(
+            w_ref[...], target[:, : len(batch) * segment], preferred_element_type=jnp.float32
+        )
+        for j, (product_ref, row, _, _, _) in enumerate(batch):
+            product_ref[row] = product[:, j * segment : (j + 1) * segment]
 
     def three(product_ref, row, apart):
         return (
@@ -250,7 +271,7 @@
         hide_ref[q] = jnp.where(in_slot < REACH, value, pltpu.roll(value, segment - gap, 1))
 
     stack(w2_ref)
-    conv(hid_ref, 0, hide_ref, p2_ref, hidden_rows, d2)
+    conv(hid_ref, 0, hide_ref, p2_ref, d2)
 
     def finish(t, _):
         for j in range(8):
@@ -269,11 +290,7 @@
     all_rows = rows + 2 * REACH
     hidden_rows = rows + 2 * SECOND_DILATION
     spacing, steps = edge_steps(rows, segment)
-    width = 8
-
-    def up_to(n, m):
-        return pl.cdiv(n, m) * m
-
+    width = segment // SLOT
     products = (3 * channels, segment)
     assembled = all_rows if len(pieces) == 3 else 1
     return pl.pallas_call(
@@ -295,11 +312,11 @@
             pltpu.VMEM((3 * channels, 3 * channels), jnp.bfloat16),
             pltpu.VMEM((steps, channels, segment), jnp.bfloat16),
             pltpu.VMEM((steps, channels, segment), jnp.bfloat16),
-            pltpu.VMEM((up_to(all_rows, 2 * width),) + products, jnp.float32),
-            pltpu.VMEM((up_to(steps, width),) + products, jnp.float32),
+            pltpu.VMEM((all_rows,) + products, jnp.float32),
+            pltpu.VMEM((steps,) + products, jnp.float32),
             pltpu.VMEM((hidden_rows, channels, segment), jnp.bfloat16),
             pltpu.VMEM((spacing, channels, segment), jnp.bfloat16),
-            pltpu.VMEM((up_to(hidden_rows, 2 * width),) + products, jnp.float32),
+            pltpu.VMEM((hidden_rows,) + products, jnp.float32),
             pltpu.VMEM((3 * channels, width * segment), jnp.bfloat16),
             pltpu.VMEM((3 * channels, width * segment), jnp.bfloat16),
             pltpu.VMEM((assembled, channels, segment), jnp.bfloat16),
@@ -309,7 +326,7 @@
     )(place, *pieces, *edges, w1, w2)
 
 
-def add_step(place_ref, range_ref, group, step, left_ref, mine_ref, theirs_ref, acc_ref, bias_ref):
+def add_step(place_ref, range_ref, group, step, left_ref, mine_ref, theirs_ref, acc_ref, bias_ref, scores_ref):
     _, channels, segment = left_ref.shape
     block = place_ref[1]
     low = segment * range_ref[0, group]
@@ -330,27 +347,27 @@
         offsets = base + lax.broadcasted_iota(jnp.int32, wide, 0) - key_column(wide)
         inside = (offsets >= low) & (offsets < high)
         bias_ref[...] = jnp.where(inside, 0.0, -1e30)
-        kind = lax.broadcasted_iota(jnp.int32, (16, 2 * segment), 0)
-        column = key_column((16, 2 * segment))
+        kind = lax.broadcasted_iota(jnp.int32, (EXTRA, 2 * segment), 0)
+        column = key_column((EXTRA, 2 * segment))
         extra = jnp.where(kind == 0, 1, jnp.where(kind == 1, column, jnp.where(kind == 2, step, 0)))
         extra = extra.astype(jnp.float32).astype(jnp.bfloat16)
+        rows = left_ref.shape[0]
 
         def score(r):
             keys = jnp.concatenate([mine_ref[r], theirs_ref[r]], axis=1)
-            return keys, lax.dot_general(
+            scores_ref[r % 2] = lax.dot_general(
                 left_ref[r], keys, (((0,), (0,)), ((), ())), preferred_element_type=jnp.float32
             )
 
-        rows = left_ref.shape[0]
-        upcoming = score(0)
+        score(0)
         for r in range(rows):
-            keys, scores = upcoming
             if r + 1 < rows:
-                upcoming = score(r + 1)
-            weights = jnp.exp2(scores * scale + bias_ref[...]).astype(jnp.bfloat16)
+                score(r + 1)
+            weights = jnp.exp2(scores_ref[r % 2] * scale + bias_ref[...]).astype(jnp.bfloat16)
+            keys = jnp.concatenate([mine_ref[r], theirs_ref[r]], axis=1)
             extended = jnp.concatenate([keys, extra], axis=0)
-            acc_ref[r, :, 0 : channels + 16] += lax.dot_general(
-                weights, extended, (((1,), (1,)), ((), ())), preferred_element_type=jnp.float32
+            acc_ref[r] += lax.dot_general(
+                extended, weights, (((1,), (1,)), ((), ())), preferred_element_type=jnp.float32
             )
 
 
@@ -359,25 +376,25 @@
 
 
 def gather_kernel(place_ref, range_ref, left_ref, *refs, inner, groups, start, count):
-    keys, (acc_ref, bias_ref) = refs[: 2 * count], refs[-2:]
+    keys, (acc_ref, bias_ref, scores_ref) = refs[: 2 * count], refs[-3:]
     group = group_of(pl.program_id(0), inner, groups)
     acc_ref[...] = refs[2 * count][...] if start else jnp.zeros_like(acc_ref)
     for index in range(count):
         add_step(
             place_ref, range_ref, group, start + index, left_ref, keys[2 * index], keys[2 * index + 1],
-            acc_ref, bias_ref,
+            acc_ref, bias_ref, scores_ref,
         )
 
 
 def finish_kernel(
     place_ref, range_ref, left_ref, mine_ref, theirs_ref, acc_in_ref, *refs, first, inner, groups, step
 ):
-    matched_ref, disparity_ref, acc_ref, bias_ref, rows_ref = refs[-5:]
+    matched_ref, disparity_ref, acc_ref, bias_ref, scores_ref, rows_ref = refs[-6:]
     group = group_of(first + pl.program_id(0), inner, groups)
     rows, channels, segment = left_ref.shape
     acc_ref[...] = acc_in_ref[...]
     add_step(
-        place_ref, range_ref, group, step, left_ref, mine_ref, theirs_ref, acc_ref, bias_ref
+        place_ref, range_ref, group, step, left_ref, mine_ref, theirs_ref, acc_ref, bias_ref, scores_ref
     )
     block = place_ref[1]
     low = segment * range_ref[0, group]
@@ -389,7 +406,7 @@
     beyond_sum = ((start + high - 1) * beyond).astype(jnp.float32) * 0.5
     beyond = beyond.astype(jnp.float32)
     for r in range(rows):
-        turned = acc_ref[r].T
+        turned = acc_ref[r]
         near = turned[channels : channels + 1]
         column = turned[channels + 1 : channels + 2]
         passed = turned[channels + 2 : channels + 3]
@@ -406,17 +423,21 @@
     own_groups = keys[0][0].shape[0] // RG
     block = (RG, channels, segment)
     smem = pl.BlockSpec(memory_space=pltpu.SMEM)
-    acc_spec = pl.BlockSpec((RG, segment, 128), lambda i: (i, 0, 0))
+    held = channels + EXTRA
+    acc_spec = pl.BlockSpec((RG, held, segment), lambda i: (i, 0, 0))
     given = (acc,) if start else ()
     return pl.pallas_call(
         functools.partial(gather_kernel, inner=inner, groups=groups, start=start, count=len(keys)),
-        out_shape=jax.ShapeDtypeStruct((own_groups * RG, segment, 128), jnp.float32),
+        out_shape=jax.ShapeDtypeStruct((own_groups * RG, held, segment), jnp.float32),
         grid=(own_groups,),
         in_specs=[smem, smem, pl.BlockSpec(block, lambda i: (group_of(i, inner, groups), 0, 0))]
         + [pl.BlockSpec(block, lambda i: (i, 0, 0))] * (2 * len(keys))
         + [acc_spec] * len(given),
         out_specs=acc_spec,
-        scratch_shapes=[pltpu.VMEM((segment, 2 * segment), jnp.float32)],
+        scratch_shapes=[
+            pltpu.VMEM((segment, 2 * segment), jnp.float32),
+            pltpu.VMEM((2, segment, 2 * segment), jnp.float32),
+        ],
         input_output_aliases={3 + 2 * len(keys): 0} if given else {},
         compiler_params=pltpu.CompilerParams(vmem_limit_bytes=VMEM_LIMIT),
         cost_estimate=cost(1.5 * own_groups),
@@ -448,7 +469,7 @@
             pl.BlockSpec(block, lambda i: (group(i), 0, 0)),
             pl.BlockSpec(block, lambda i: (i, 0, 0)),
             pl.BlockSpec(block, lambda i: (i, 0, 0)),
-            pl.BlockSpec((RG, segment, 128), lambda i: (first + i, 0, 0)),
+            pl.BlockSpec((RG, channels + EXTRA, segment), lambda i: (first + i, 0, 0)),
         ]
         + [pl.BlockSpec(memory_space=pl.ANY)] * len(given),
         out_specs=(
@@ -456,8 +477,9 @@
             pl.BlockSpec((RG, segment), lambda i: (group(i), 0)),
         ),
         scratch_shapes=[
-            pltpu.VMEM((RG, segment, 128), jnp.float32),
+            pltpu.VMEM((RG, channels + EXTRA, segment), jnp.float32),
             pltpu.VMEM((segment, 2 * segment), jnp.float32),
+            pltpu.VMEM((2, segment, 2 * segment), jnp.float32),
             pltpu.VMEM((RG, channels, segment), jnp.float32),
         ],
         input_output_aliases={6: 0, 7: 1} if given else {},

time: 138 us -> 136 us (0.986)
  Pallas kernels: 61.7 us -> 56.5 us
  waiting for transfers between devices: 44.8 us -> 48.6 us
    pallas_call x3, Pallas kernels: 27.7 us -> 24.5 us  [unit_features(): pl.pallas_call(functools.partial(feature_kernel, spacing=spacing, offset=...]
    ppermute x3, waiting for transfers between devices: 27.5 us -> 30.4 us  [chain(): part = lax.ppermute(part, 'cols', hop)]
    ppermute x2, starting transfers between devices: 2.49 us -> 0.14 us  [exchanged(): partner = lax.ppermute(own, 'cols', swap)]
    ppermute x1, waiting for transfers between devices: 0.01 us -> 2.04 us  [program(): above = lax.ppermute(mid[:, rows - REACH:], 'rows', down)]
    ppermute x1, starting transfers between devices: 2.03 us -> 0.01 us  [program(): above = lax.ppermute(mid[:, rows - REACH:], 'rows', down)]
    ppermute x1, starting transfers between devices: 0.96 us -> 2.98 us  [program(): below = lax.ppermute(mid[:, :REACH], 'rows', up)]
    ppermute x2, starting transfers between devices: 6.64 us -> 8.64 us  [exchanged(): cross = lax.ppermute(own, 'cols', across)]
    ppermute x1, waiting for transfers between devices: 1.59 us -> 0.01 us  [program(): below = lax.ppermute(mid[:, :REACH], 'rows', up)]
  transfers between devices with their start and end apart: 22 -> 22, of which waited for: 5 -> 5; matrix products, arithmetic and copies ran while one was open for 2% -> 2% of each run, Pallas kernels for 43% -> 40%
where the time goes in v7:
time: 136 us; the launch traced here: 135 us
  Pallas kernels  56.5 us (42%)
  waiting for transfers between devices  48.6 us (36%)
  starting transfers between devices  21.6 us (16%)
  local copies, waits for them, and re-layouts  7.13 us (5%)
    ppermute x3, waiting for transfers between devices, chain(): part = lax.ppermute(part, 'cols', hop)  30.4 us
    pallas_call x3, Pallas kernels, unit_features(): pl.pallas_call(functools.partial(feature_kernel, spacing=spacing, offset=...  24.5 us
    pallas_call x4, Pallas kernels, correlate(): pl.pallas_call(functools.partial(gather_kernel, inner=inner, groups=group...  17.6 us
    ppermute x4, waiting for transfers between devices, chain(): mine = lax.ppermute(mine, 'cols', hop)  16.1 us
    ppermute x2, starting transfers between devices, exchanged(): cross = lax.ppermute(own, 'cols', across)  8.64 us
    pallas_call x3, Pallas kernels, finish(): pl.pallas_call(functools.partial(finish_kernel, first=first, inner=inner,...  8.64 us
    ppermute x9, starting transfers between devices, pair(): return (mine, lax.ppermute(mine, 'cols', swap))  6.14 us
    pallas_call x2, Pallas kernels, pack_edges(): pl.pallas_call(functools.partial(pack_kernel, images=tuple((chunks for _,...  5.66 us
  transfers between devices with their start and end apart: 22, of which 5 were waited for; matrix products, arithmetic and copies ran while one was open for 2% of the time, Pallas kernels for 40%

profile of v7, /device:TPU:1, one launch (start us, length us, event | category | flops | bytes accessed | tf_op | source)
XLA Modules:
  0.0 135.1 jit_solution(15037540816545325764)
XLA Ops:
  0.6 2.9 %copy.14 = bf16[2,64,64,128]{3,1,2,0:T(8,128)(2,1)S(1)} copy(bf16[2,64,64,128]{3,2,1,0:T(8,128)(2,1)} %param.4) | data formatting | bytes 4194304 | tf_op args[0]
  3.6 1.4 %copy-done = bf16[2,64,64,128]{3,1,2,0:T(8,128)(2,1)} copy-done((bf16[2,64,64,128]{3,1,2,0:T(8,128)(2,1)}, bf16[2,64,64,128]{3,1,2,0:T(8,128)(2,1)S(1)}, u32[]{:S(2)}) %copy-start) | copy-done | bytes 2097176
  4.9 0.8 fusion
  5.7 3.0 %collective-permute-start.1 = (bf16[2,6,64,128]{3,2,1,0:T(8,128)(2,1)}, bf16[2,6,64,128]{3,2,1,0:T(8,128)(2,1)}, u32[]{:S(2)}, u32[]{:S(2)}) collective-permute-start(bf16[2,6,64,128]{3,2,1,0:T(8,128)(2,1)} %get-tuple-element.10), channel_id=1, source_target_pairs={{8,0},{16,8},{24,16},{0,24},{9,1},{17,9},{25,17},{1,25},{10,2},{18... | collective-permute-start | bytes 589832 | tf_op jit(solution)/shard_map/ppermute | solution.py:523
  8.7 2.3 %shard_map.64.refs_1_ = bf16[11,64,128]{2,1,0:T(8,128)(2,1)} custom-call(bf16[2,64,64,128]{3,2,1,0:T(8,128)(2,1)} %bitcast.7), custom_call_target="tpu_custom_call" | custom-call | flops 2000000000 | bytes 6000000 | tf_op jit(solution)/shard_map/pallas_call | solution.py:96
  11.0 4.0 %collective-permute-start.12 = (bf16[11,64,128]{2,1,0:T(8,128)(2,1)}, bf16[11,64,128]{2,1,0:T(8,128)(2,1)}, u32[]{:S(2)}, u32[]{:S(2)}) collective-permute-start(bf16[11,64,128]{2,1,0:T(8,128)(2,1)} %shard_map.64.refs_1_), channel_id=1, source_target_pairs={{1,2},{3,4},{5,6},{2,1},{4,3},{6,5},{9,10},{11,12},{13,14},{10,9},... | collective-permute-start | bytes 540680 | tf_op jit(solution)/shard_map/ppermute | solution.py:511
  15.1 0.1 collective-permute-start.11
  15.2 0.6 pad_add_fusion.refs_0_.place_ref
  15.8 2.0 %collective-permute-done.refs_2_.refs_5_.refs_1_ = bf16[2,6,64,128]{3,2,1,0:T(8,128)(2,1)} collective-permute-done((bf16[2,6,64,128]{3,2,1,0:T(8,128)(2,1)}, bf16[2,6,64,128]{3,2,1,0:T(8,128)(2,1)}, u32[]{:S(2)}, u32[]{:S(2)}) %collective-permute-start) | collective-permute-done | bytes 196640 | tf_op jit(solution)/shard_map/ppermute | solution.py:522
  17.8 3.3 %shard_map.59.refs_3_ = bf16[25,64,128]{2,1,0:T(8,128)(2,1)} custom-call(s32[2]{0:T(128)} %pad_add_fusion.refs_0_.place_ref, bf16[2,64,64,128]{3,2,1,0:T(8,128)(2,1)} %bitcast.8, bf16[2,6,64,128]{3,2,1,0:T(8,128)(2,1)} %collective-permute-done.refs_2_.refs_5_.refs_1_, bf16[2,6,64,128]{3,2,1,0:T(8,128)(2,1)} %collective-permute-done.1.refs_3_.refs_6_.refs_2_, ...), custom_call_target="tpu_custom_call" | custom-call | flops 2000000000 | bytes 6000000 | tf_op jit(solution)/shard_map/pallas_call | solution.py:96
  21.1 4.6 %collective-permute-start.3 = (bf16[25,64,128]{2,1,0:T(8,128)(2,1)}, bf16[25,64,128]{2,1,0:T(8,128)(2,1)}, u32[]{:S(2)}, u32[]{:S(2)}) collective-permute-start(bf16[25,64,128]{2,1,0:T(8,128)(2,1)} %shard_map.59.refs_3_), channel_id=1, source_target_pairs={{1,2},{3,4},{5,6},{2,1},{4,3},{6,5},{9,10},{11,12},{13,14},{10,9},... | collective-permute-start | bytes 1228808 | tf_op jit(solution)/shard_map/ppermute | solution.py:511
  25.8 0.1 collective-permute-start.2
  25.8 0.0 collective-permute-done.11.refs_2_
  25.9 8.0 %shard_map.65.refs_0_ = bf16[48,64,128]{2,1,0:T(8,128)(2,1)} custom-call(s32[2]{0:T(128)} %pad_add_fusion.refs_0_.place_ref, bf16[2,64,64,128]{3,2,1,0:T(8,128)(2,1)} %bitcast.10, bf16[11,64,128]{2,1,0:T(8,128)(2,1)} %shard_map.64.refs_1_, bf16[11,64,128]{2,1,0:T(8,128)(2,1)} %collective-permute-done.11.refs_2_, ...), custom_call_target="tpu_custom_call" | custom-call | flops 9600000000 | bytes 28800000 | tf_op jit(solution)/shard_map/pallas_call | solution.py:296
  33.9 1.3 collective-permute-start.13
  35.2 0.0 collective-permute-done.2.refs_4_
  35.2 6.6 %shard_map.61.refs_0_ = bf16[16,64,128]{2,1,0:T(8,128)(2,1)} custom-call(s32[2]{0:T(128)} %pad_add_fusion.refs_0_.place_ref, bf16[2,64,64,128]{3,2,1,0:T(8,128)(2,1)} %bitcast.11, bf16[2,6,64,128]{3,2,1,0:T(8,128)(2,1)} %collective-permute-done.refs_2_.refs_5_.refs_1_, bf16[2,6,64,128]{3,2,1,0:T(8,128)(2,1)} %collective-permute-done.1.refs_3_.refs_6_.refs_2_, ...), custom_call_target="tpu_custom_call" | custom-call | flops 3200000000 | bytes 9600000 | tf_op jit(solution)/shard_map/pallas_call | solution.py:296
  41.8 1.3 collective-permute-start.4
  43.1 1.0 collective-permute-start.18
  44.2 16.1 %collective-permute-done.4.refs_2_ = bf16[16,64,128]{2,1,0:T(8,128)(2,1)} collective-permute-done((bf16[16,64,128]{2,1,0:T(8,128)(2,1)}, bf16[16,64,128]{2,1,0:T(8,128)(2,1)}, u32[]{:S(2)}, u32[]{:S(2)}) %collective-permute-start.4) | collective-permute-done | bytes 262176 | tf_op jit(solution)/shard_map/ppermute | solution.py:541
  60.2 1.3 collective-permute-start.10
  61.6 0.0 collective-permute-start.5
  61.6 0.0 collective-permute-done.13.refs_2_
  61.6 0.8 collective-permute-start.14
  62.4 9.9 %shard_map.60.left_ref = bf16[64,64,128]{2,1,0:T(8,128)(2,1)} custom-call(s32[2]{0:T(128)} %pad_add_fusion.refs_0_.place_ref, bf16[2,64,64,128]{3,2,1,0:T(8,128)(2,1)} %bitcast.12, bf16[2,6,64,128]{3,2,1,0:T(8,128)(2,1)} %collective-permute-done.refs_2_.refs_5_.refs_1_, bf16[2,6,64,128]{3,2,1,0:T(8,128)(2,1)} %collective-permute-done.1.refs_3_.refs_6_.refs_2_, ...), custom_call_target="tpu_custom_call" | custom-call | flops 12800000000 | bytes 38400000 | tf_op jit(solution)/shard_map/pallas_call | solution.py:296
  72.2 0.0 collective-permute-done.9.refs_1_
  72.2 0.6 collective-permute-start.19
  72.8 0.1 collective-permute-start.8
  72.9 0.2 collective-permute-start.6
  73.2 3.2 %shard_map.62.refs_2_ = f32[16,80,128]{2,1,0:T(8,128)} custom-call(s32[2]{0:T(128)} %pad_add_fusion.refs_0_.place_ref, s32[2,8]{1,0:T(2,128)} %bitcast.13, bf16[64,64,128]{2,1,0:T(8,128)(2,1)} %shard_map.60.left_ref, bf16[16,64,128]{2,1,0:T(8,128)(2,1)} %shard_map.61.refs_0_, bf16[16,64,128]{2,1,0:T(8,128)(2,1)} %collective-permute-done.9.refs_1_, ...), custom_call_target="tpu_custom_call" | custom-call | flops 3000000000 | bytes 9000000 | tf_op jit(solution)/shard_map/pallas_call | solution.py:429
  76.4 17.7 %collective-permute-done.6.mine_ref = bf16[16,64,128]{2,1,0:T(8,128)(2,1)} collective-permute-done((bf16[16,64,128]{2,1,0:T(8,128)(2,1)}, bf16[16,64,128]{2,1,0:T(8,128)(2,1)}, u32[]{:S(2)}, u32[]{:S(2)}) %collective-permute-start.6) | collective-permute-done | bytes 262176 | tf_op jit(solution)/shard_map/ppermute | solution.py:547
  94.0 0.9 collective-permute-start.7
  94.9 0.0 collective-permute-done.8.refs_1_
  94.9 2.2 %shard_map.63.acc_in_ref = f32[16,80,128]{2,1,0:T(8,128)} custom-call(s32[2]{0:T(128)} %pad_add_fusion.refs_0_.place_ref, s32[2,8]{1,0:T(2,128)} %bitcast.14, bf16[64,64,128]{2,1,0:T(8,128)(2,1)} %shard_map.60.left_ref, bf16[16,64,128]{2,1,0:T(8,128)(2,1)} %collective-permute-done.5.refs_0_, ...), custom_call_target="tpu_custom_call", output_to_operand_aliasing={{}: (5, {})} | custom-call | flops 3000000000 | bytes 9000000 | tf_op jit(solution)/shard_map/pallas_call | solution.py:429
  97.1 2.0 %fusion.1 = (bf16[24,64,128]{2,1,0:T(8,128)(2,1)}, bf16[24,64,128]{2,1,0:T(8,128)(2,1)}) fusion(bf16[48,64,128]{2,1,0:T(8,128)(2,1)} %collective-permute-done.14.refs_0_), kind=kLoop, calls=%fused_computation.3 | loop fusion | bytes 1572864 | tf_op jit(solution)/shard_map/slice | solution.py:546
  99.1 0.0 collective-permute-start.20
  99.1 0.0 collective-permute-start.15
  99.1 0.1 collective-permute-start.17
  99.2 0.0 collective-permute-done.19.refs_3_
  99.2 7.0 %shard_map.66.refs_2_ = f32[48,80,128]{2,1,0:T(8,128)} custom-call(s32[2]{0:T(128)} %pad_add_fusion.refs_0_.place_ref, s32[2,8]{1,0:T(2,128)} %bitcast.15, bf16[64,64,128]{2,1,0:T(8,128)(2,1)} %shard_map.60.left_ref, bf16[48,64,128]{2,1,0:T(8,128)(2,1)} %shard_map.65.refs_0_, bf16[48,64,128]{2,1,0:T(8,128)(2,1)} %collective-permute-done.18.refs_1_, ...), custom_call_target="tpu_custom_call" | custom-call | flops 8999999488 | bytes 27000000 | tf_op jit(solution)/shard_map/pallas_call | solution.py:429
  106.3 5.6 %collective-permute-done.20.mine_ref = bf16[24,64,128]{2,1,0:T(8,128)(2,1)} collective-permute-done((bf16[24,64,128]{2,1,0:T(8,128)(2,1)}, bf16[24,64,128]{2,1,0:T(8,128)(2,1)}, u32[]{:S(2)}, u32[]{:S(2)}) %collective-permute-start.20) | collective-permute-done | bytes 393248 | tf_op jit(solution)/shard_map/ppermute | solution.py:547
  111.9 1.3 collective-permute-start.21
  113.2 7.1 %collective-permute-done.15.mine_ref = bf16[24,64,128]{2,1,0:T(8,128)(2,1)} collective-permute-done((bf16[24,64,128]{2,1,0:T(8,128)(2,1)}, bf16[24,64,128]{2,1,0:T(8,128)(2,1)}, u32[]{:S(2)}, u32[]{:S(2)}) %collective-permute-start.15) | collective-permute-done | bytes 393248 | tf_op jit(solution)/shard_map/ppermute | solution.py:547
  120.3 0.9 collective-permute-start.16
  121.2 5.2 %shard_map.67.acc_in_ref = f32[48,80,128]{2,1,0:T(8,128)} custom-call(s32[2]{0:T(128)} %pad_add_fusion.refs_0_.place_ref, s32[2,8]{1,0:T(2,128)} %bitcast.16, bf16[64,64,128]{2,1,0:T(8,128)(2,1)} %shard_map.60.left_ref, bf16[48,64,128]{2,1,0:T(8,128)(2,1)} %collective-permute-done.14.refs_0_, ...), custom_call_target="tpu_custom_call", output_to_operand_aliasing={{}: (5, {})} | custom-call | flops 8999999488 | bytes 27000000 | tf_op jit(solution)/shard_map/pallas_call | solution.py:429
  126.4 3.2 %shard_map.68 = (bf16[64,64,128]{2,1,0:T(8,128)(2,1)}, f32[64,128]{1,0:T(8,128)}) custom-call(s32[2]{0:T(128)} %pad_add_fusion.refs_0_.place_ref, s32[2,8]{1,0:T(2,128)} %bitcast.17, bf16[64,64,128]{2,1,0:T(8,128)(2,1)} %shard_map.60.left_ref, bf16[24,64,128]{2,1,0:T(8,128)(2,1)} %collective-permute-done.20.mine_ref, ...), custom_call_target="tpu_custom_call" | custom-call | flops 3000000000 | bytes 9000000 | tf_op jit(solution)/shard_map/pallas_call | solution.py:459
  129.7 3.2 %shard_map.69 = (bf16[64,64,128]{2,1,0:T(8,128)(2,1)}, f32[64,128]{1,0:T(8,128)}) custom-call(s32[2]{0:T(128)} %pad_add_fusion.refs_0_.place_ref, s32[2,8]{1,0:T(2,128)} %bitcast.18, bf16[64,64,128]{2,1,0:T(8,128)(2,1)} %shard_map.60.left_ref, bf16[24,64,128]{2,1,0:T(8,128)(2,1)} %collective-permute-done.15.mine_ref, ...), custom_call_target="tpu_custom_call", output_to_operand_aliasing={{0}: (6, {}), {1}: (7, {})} | custom-call | flops 3000000000 | bytes 9000000 | tf_op jit(solution)/shard_map/pallas_call | solution.py:459
  132.9 2.1 %shard_map.70 = (bf16[64,64,128]{2,1,0:T(8,128)(2,1)}, f32[64,128]{1,0:T(8,128)}) custom-call(s32[2]{0:T(128)} %pad_add_fusion.refs_0_.place_ref, s32[2,8]{1,0:T(2,128)} %bitcast.19, bf16[64,64,128]{2,1,0:T(8,128)(2,1)} %shard_map.60.left_ref, bf16[16,64,128]{2,1,0:T(8,128)(2,1)} %collective-permute-done.6.mine_ref, ...), custom_call_target="tpu_custom_call", output_to_operand_aliasing={{0}: (6, {}), {1}: (7, {})} | custom-call | flops 2000000000 | bytes 6000000 | tf_op jit(solution)/shard_map/pallas_call | solution.py:459
  (14 shorter events, 0.0 us)
Async XLA Ops:
  3.6 1.4 %copy-start = (bf16[2,64,64,128]{3,1,2,0:T(8,128)(2,1)}, bf16[2,64,64,128]{3,1,2,0:T(8,128)(2,1)S(1)}, u32[]{:S(2)}) copy-start(bf16[2,64,64,128]{3,1,2,0:T(8,128)(2,1)S(1)} %copy.14) | copy-start | bytes 6291460
  5.7 10.0 %collective-permute-start.1 = (bf16[2,6,64,128]{3,2,1,0:T(8,128)(2,1)}, bf16[2,6,64,128]{3,2,1,0:T(8,128)(2,1)}, u32[]{:S(2)}, u32[]{:S(2)}) collective-permute-start(bf16[2,6,64,128]{3,2,1,0:T(8,128)(2,1)} %get-tuple-element.10), channel_id=1, source_target_pairs={{8,0},{16,8},{24,16},{0,24},{9,1},{17,9},{25,17},{1,25},{10,2},{18... | collective-permute-start | bytes 589832 | tf_op jit(solution)/shard_map/ppermute | solution.py:523
  8.7 9.1 %collective-permute-start = (bf16[2,6,64,128]{3,2,1,0:T(8,128)(2,1)}, bf16[2,6,64,128]{3,2,1,0:T(8,128)(2,1)}, u32[]{:S(2)}, u32[]{:S(2)}) collective-permute-start(bf16[2,6,64,128]{3,2,1,0:T(8,128)(2,1)} %get-tuple-element.11), channel_id=1, source_target_pairs={{0,8},{8,16},{16,24},{24,0},{1,9},{9,17},{17,25},{25,1},{2,10},{10... | collective-permute-start | bytes 589832 | tf_op jit(solution)/shard_map/ppermute | solution.py:522
  11.0 14.8 %collective-permute-start.12 = (bf16[11,64,128]{2,1,0:T(8,128)(2,1)}, bf16[11,64,128]{2,1,0:T(8,128)(2,1)}, u32[]{:S(2)}, u32[]{:S(2)}) collective-permute-start(bf16[11,64,128]{2,1,0:T(8,128)(2,1)} %shard_map.64.refs_1_), channel_id=1, source_target_pairs={{1,2},{3,4},{5,6},{2,1},{4,3},{6,5},{9,10},{11,12},{13,14},{10,9},... | collective-permute-start | bytes 540680 | tf_op jit(solution)/shard_map/ppermute | solution.py:511
  15.1 10.8 %collective-permute-start.11 = (bf16[11,64,128]{2,1,0:T(8,128)(2,1)}, bf16[11,64,128]{2,1,0:T(8,128)(2,1)}, u32[]{:S(2)}, u32[]{:S(2)}) collective-permute-start(bf16[11,64,128]{2,1,0:T(8,128)(2,1)} %shard_map.64.refs_1_), channel_id=1, source_target_pairs={{0,1},{1,0},{2,3},{3,2},{4,5},{5,4},{6,7},{7,6},{8,9},{9,8},{10,11... | collective-permute-start | bytes 540680 | tf_op jit(solution)/shard_map/ppermute | solution.py:512
  21.1 14.1 %collective-permute-start.3 = (bf16[25,64,128]{2,1,0:T(8,128)(2,1)}, bf16[25,64,128]{2,1,0:T(8,128)(2,1)}, u32[]{:S(2)}, u32[]{:S(2)}) collective-permute-start(bf16[25,64,128]{2,1,0:T(8,128)(2,1)} %shard_map.59.refs_3_), channel_id=1, source_target_pairs={{1,2},{3,4},{5,6},{2,1},{4,3},{6,5},{9,10},{11,12},{13,14},{10,9},... | collective-permute-start | bytes 1228808 | tf_op jit(solution)/shard_map/ppermute | solution.py:511
  25.8 9.5 %collective-permute-start.2 = (bf16[25,64,128]{2,1,0:T(8,128)(2,1)}, bf16[25,64,128]{2,1,0:T(8,128)(2,1)}, u32[]{:S(2)}, u32[]{:S(2)}) collective-permute-start(bf16[25,64,128]{2,1,0:T(8,128)(2,1)} %shard_map.59.refs_3_), channel_id=1, source_target_pairs={{0,1},{1,0},{2,3},{3,2},{4,5},{5,4},{6,7},{7,6},{8,9},{9,8},{10,11... | collective-permute-start | bytes 1228808 | tf_op jit(solution)/shard_map/ppermute | solution.py:512
  33.9 27.7 %collective-permute-start.13 = (bf16[48,64,128]{2,1,0:T(8,128)(2,1)}, bf16[48,64,128]{2,1,0:T(8,128)(2,1)}, u32[]{:S(2)}, u32[]{:S(2)}) collective-permute-start(bf16[48,64,128]{2,1,0:T(8,128)(2,1)} %shard_map.65.refs_0_), channel_id=1, source_target_pairs={{0,2},{1,3},{2,4},{3,5},{4,6},{5,7},{6,0},{7,1},{8,10},{9,11},{10,... | collective-permute-start | bytes 2359304 | tf_op jit(solution)/shard_map/ppermute | solution.py:541
  41.8 18.4 %collective-permute-start.4 = (bf16[16,64,128]{2,1,0:T(8,128)(2,1)}, bf16[16,64,128]{2,1,0:T(8,128)(2,1)}, u32[]{:S(2)}, u32[]{:S(2)}) collective-permute-start(bf16[16,64,128]{2,1,0:T(8,128)(2,1)} %shard_map.61.refs_0_), channel_id=1, source_target_pairs={{0,2},{1,3},{2,4},{3,5},{4,6},{5,7},{6,0},{7,1},{8,10},{9,11},{10,... | collective-permute-start | bytes 786440 | tf_op jit(solution)/shard_map/ppermute | solution.py:541
  43.1 56.0 %collective-permute-start.18 = (bf16[48,64,128]{2,1,0:T(8,128)(2,1)}, bf16[48,64,128]{2,1,0:T(8,128)(2,1)}, u32[]{:S(2)}, u32[]{:S(2)}) collective-permute-start(bf16[48,64,128]{2,1,0:T(8,128)(2,1)} %shard_map.65.refs_0_), channel_id=1, source_target_pairs={{0,1},{1,0},{2,3},{3,2},{4,5},{5,4},{6,7},{7,6},{8,9},{9,8},{10,11... | collective-permute-start | bytes 2359304 | tf_op jit(solution)/shard_map/ppermute | solution.py:536
  44.1 28.1 %collective-permute-start.9 = (bf16[16,64,128]{2,1,0:T(8,128)(2,1)}, bf16[16,64,128]{2,1,0:T(8,128)(2,1)}, u32[]{:S(2)}, u32[]{:S(2)}) collective-permute-start(bf16[16,64,128]{2,1,0:T(8,128)(2,1)} %shard_map.61.refs_0_), channel_id=1, source_target_pairs={{0,1},{1,0},{2,3},{3,2},{4,5},{5,4},{6,7},{7,6},{8,9},{9,8},{10,11... | collective-permute-start | bytes 786440 | tf_op jit(solution)/shard_map/ppermute | solution.py:536
  60.2 12.7 %collective-permute-start.10 = (bf16[16,64,128]{2,1,0:T(8,128)(2,1)}, bf16[16,64,128]{2,1,0:T(8,128)(2,1)}, u32[]{:S(2)}, u32[]{:S(2)}) collective-permute-start(bf16[16,64,128]{2,1,0:T(8,128)(2,1)} %collective-permute-done.4.refs_2_), channel_id=1, source_target_pairs={{0,1},{1,0},{2,3},{3,2},{4,5},{5,4},{6,7},{7,6},{8,9},{9,8},{10,11... | collective-permute-start | bytes 786440 | tf_op jit(solution)/shard_map/ppermute | solution.py:536
  61.6 11.2 %collective-permute-start.5 = (bf16[16,64,128]{2,1,0:T(8,128)(2,1)}, bf16[16,64,128]{2,1,0:T(8,128)(2,1)}, u32[]{:S(2)}, u32[]{:S(2)}) collective-permute-start(bf16[16,64,128]{2,1,0:T(8,128)(2,1)} %collective-permute-done.4.refs_2_), channel_id=1, source_target_pairs={{0,2},{1,3},{2,4},{3,5},{4,6},{5,7},{6,0},{7,1},{8,10},{9,11},{10,... | collective-permute-start | bytes 786440 | tf_op jit(solution)/shard_map/ppermute | solution.py:541
  61.6 35.5 %collective-permute-start.14 = (bf16[48,64,128]{2,1,0:T(8,128)(2,1)}, bf16[48,64,128]{2,1,0:T(8,128)(2,1)}, u32[]{:S(2)}, u32[]{:S(2)}) collective-permute-start(bf16[48,64,128]{2,1,0:T(8,128)(2,1)} %collective-permute-done.13.refs_2_), channel_id=1, source_target_pairs={{0,2},{1,3},{2,4},{3,5},{4,6},{5,7},{6,0},{7,1},{8,10},{9,11},{10,... | collective-permute-start | bytes 2359304 | tf_op jit(solution)/shard_map/ppermute | solution.py:541
  72.2 27.0 %collective-permute-start.19 = (bf16[48,64,128]{2,1,0:T(8,128)(2,1)}, bf16[48,64,128]{2,1,0:T(8,128)(2,1)}, u32[]{:S(2)}, u32[]{:S(2)}) collective-permute-start(bf16[48,64,128]{2,1,0:T(8,128)(2,1)} %collective-permute-done.13.refs_2_), channel_id=1, source_target_pairs={{0,1},{1,0},{2,3},{3,2},{4,5},{5,4},{6,7},{7,6},{8,9},{9,8},{10,11... | collective-permute-start | bytes 2359304 | tf_op jit(solution)/shard_map/ppermute | solution.py:536
  72.8 22.1 %collective-permute-start.8 = (bf16[16,64,128]{2,1,0:T(8,128)(2,1)}, bf16[16,64,128]{2,1,0:T(8,128)(2,1)}, u32[]{:S(2)}, u32[]{:S(2)}) collective-permute-start(bf16[16,64,128]{2,1,0:T(8,128)(2,1)} %collective-permute-done.5.refs_0_), channel_id=1, source_target_pairs={{0,1},{1,0},{2,3},{3,2},{4,5},{5,4},{6,7},{7,6},{8,9},{9,8},{10,11... | collective-permute-start | bytes 786440 | tf_op jit(solution)/shard_map/ppermute | solution.py:536
  72.9 21.1 %collective-permute-start.6 = (bf16[16,64,128]{2,1,0:T(8,128)(2,1)}, bf16[16,64,128]{2,1,0:T(8,128)(2,1)}, u32[]{:S(2)}, u32[]{:S(2)}) collective-permute-start(bf16[16,64,128]{2,1,0:T(8,128)(2,1)} %collective-permute-done.5.refs_0_), channel_id=1, source_target_pairs={{0,2},{1,3},{2,4},{3,5},{4,6},{5,7},{6,0},{7,1},{8,10},{9,11},{10,... | collective-permute-start | bytes 786440 | tf_op jit(solution)/shard_map/ppermute | solution.py:547
  94.0 38.9 %collective-permute-start.7 = (bf16[16,64,128]{2,1,0:T(8,128)(2,1)}, bf16[16,64,128]{2,1,0:T(8,128)(2,1)}, u32[]{:S(2)}, u32[]{:S(2)}) collective-permute-start(bf16[16,64,128]{2,1,0:T(8,128)(2,1)} %collective-permute-done.6.mine_ref), channel_id=1, source_target_pairs={{0,1},{1,0},{2,3},{3,2},{4,5},{5,4},{6,7},{7,6},{8,9},{9,8},{10,11... | collective-permute-start | bytes 786440 | tf_op jit(solution)/shard_map/ppermute | solution.py:536
  99.1 12.8 %collective-permute-start.20 = (bf16[24,64,128]{2,1,0:T(8,128)(2,1)}, bf16[24,64,128]{2,1,0:T(8,128)(2,1)}, u32[]{:S(2)}, u32[]{:S(2)}) collective-permute-start(bf16[24,64,128]{2,1,0:T(8,128)(2,1)} %get-tuple-element.12), channel_id=1, source_target_pairs={{0,2},{1,3},{2,4},{3,5},{4,6},{5,7},{6,0},{7,1},{8,10},{9,11},{10,... | collective-permute-start | bytes 1179656 | tf_op jit(solution)/shard_map/ppermute | solution.py:547
  99.1 21.2 %collective-permute-start.15 = (bf16[24,64,128]{2,1,0:T(8,128)(2,1)}, bf16[24,64,128]{2,1,0:T(8,128)(2,1)}, u32[]{:S(2)}, u32[]{:S(2)}) collective-permute-start(bf16[24,64,128]{2,1,0:T(8,128)(2,1)} %get-tuple-element.13), channel_id=1, source_target_pairs={{0,2},{1,3},{2,4},{3,5},{4,6},{5,7},{6,0},{7,1},{8,10},{9,11},{10,... | collective-permute-start | bytes 1179656 | tf_op jit(solution)/shard_map/ppermute | solution.py:547
  99.1 22.1 %collective-permute-start.17 = (bf16[48,64,128]{2,1,0:T(8,128)(2,1)}, bf16[48,64,128]{2,1,0:T(8,128)(2,1)}, u32[]{:S(2)}, u32[]{:S(2)}) collective-permute-start(bf16[48,64,128]{2,1,0:T(8,128)(2,1)} %collective-permute-done.14.refs_0_), channel_id=1, source_target_pairs={{0,1},{1,0},{2,3},{3,2},{4,5},{5,4},{6,7},{7,6},{8,9},{9,8},{10,11... | collective-permute-start | bytes 2359304 | tf_op jit(solution)/shard_map/ppermute | solution.py:536
  111.9 14.5 %collective-permute-start.21 = (bf16[24,64,128]{2,1,0:T(8,128)(2,1)}, bf16[24,64,128]{2,1,0:T(8,128)(2,1)}, u32[]{:S(2)}, u32[]{:S(2)}) collective-permute-start(bf16[24,64,128]{2,1,0:T(8,128)(2,1)} %collective-permute-done.20.mine_ref), channel_id=1, source_target_pairs={{0,1},{1,0},{2,3},{3,2},{4,5},{5,4},{6,7},{7,6},{8,9},{9,8},{10,11... | collective-permute-start | bytes 1179656 | tf_op jit(solution)/shard_map/ppermute | solution.py:536
  120.3 9.3 %collective-permute-start.16 = (bf16[24,64,128]{2,1,0:T(8,128)(2,1)}, bf16[24,64,128]{2,1,0:T(8,128)(2,1)}, u32[]{:S(2)}, u32[]{:S(2)}) collective-permute-start(bf16[24,64,128]{2,1,0:T(8,128)(2,1)} %collective-permute-done.15.mine_ref), channel_id=1, source_target_pairs={{0,1},{1,0},{2,3},{3,2},{4,5},{5,4},{6,7},{7,6},{8,9},{9,8},{10,11... | collective-permute-start | bytes 1179656 | tf_op jit(solution)/shard_map/ppermute | solution.py:536

commit v8 on v7

--- a/solution.py
+++ b/solution.py
@@ -372,7 +372,8 @@
 
 
 def group_of(i, inner, groups):
-    return i + 1 if inner else i * (groups - 1)
+    quarter = groups // 4
+    return i + quarter if inner else jnp.where(i < quarter, i, i + 2 * quarter)
 
 
 def gather_kernel(place_ref, range_ref, left_ref, *refs, inner, groups, start, count):
@@ -387,10 +388,10 @@
 
 
 def finish_kernel(
-    place_ref, range_ref, left_ref, mine_ref, theirs_ref, acc_in_ref, *refs, first, inner, groups, step
+    place_ref, range_ref, left_ref, mine_ref, theirs_ref, acc_in_ref, *refs, inner, groups, step
 ):
     matched_ref, disparity_ref, acc_ref, bias_ref, scores_ref, rows_ref = refs[-6:]
-    group = group_of(first + pl.program_id(0), inner, groups)
+    group = group_of(pl.program_id(0), inner, groups)
     rows, channels, segment = left_ref.shape
     acc_ref[...] = acc_in_ref[...]
     add_step(
@@ -444,20 +445,19 @@
     )(place, ranges, left, *[a for pair in keys for a in pair], *given)
 
 
-def finish(place, ranges, left, pair, acc, piece, outs, inner, step):
+def finish(place, ranges, left, pair, acc, outs, inner, step):
     rows, channels, segment = left.shape
     groups = rows // RG
     own_groups = pair[0].shape[0] // RG
-    first = piece * own_groups
     block = (RG, channels, segment)
     smem = pl.BlockSpec(memory_space=pltpu.SMEM)
 
     def group(i):
-        return group_of(first + i, inner, groups)
+        return group_of(i, inner, groups)
 
     given = () if outs is None else tuple(outs)
     return pl.pallas_call(
-        functools.partial(finish_kernel, first=first, inner=inner, groups=groups, step=step),
+        functools.partial(finish_kernel, inner=inner, groups=groups, step=step),
         out_shape=(
             jax.ShapeDtypeStruct((channels, rows, segment), jnp.bfloat16),
             jax.ShapeDtypeStruct((rows, segment), jnp.float32),
@@ -469,7 +469,7 @@
             pl.BlockSpec(block, lambda i: (group(i), 0, 0)),
             pl.BlockSpec(block, lambda i: (i, 0, 0)),
             pl.BlockSpec(block, lambda i: (i, 0, 0)),
-            pl.BlockSpec((RG, channels + EXTRA, segment), lambda i: (first + i, 0, 0)),
+            pl.BlockSpec((RG, channels + EXTRA, segment), lambda i: (i, 0, 0)),
         ]
         + [pl.BlockSpec(memory_space=pl.ANY)] * len(given),
         out_specs=(
@@ -522,47 +522,36 @@
     above = lax.ppermute(mid[:, rows - REACH :], "rows", down)
     below = lax.ppermute(mid[:, :REACH], "rows", up)
 
-    inner = rows - 2 * RG
+    strip = rows // 4
+    inner = rows - 2 * strip
     around = (mid, above, below)
-    edges_a = exchanged((mid,), ((1, ((inner, RG),)),))
-    edges_r = exchanged(around, ((1, ((RG, 0), (RG, rows - RG))), (0, ((rows, 0),))))
-    right_a = features((mid,), 1, 1, inner, RG - REACH, edges_a, 0)
-    right_b = features(around, 1, 2, RG, 0, edges_r, 0)
-    left = features(around, 0, 1, rows, 0, edges_r, 2 * edge_steps(RG, segment)[1])
+    edges_a = exchanged((mid,), ((1, ((inner, strip),)),))
+    edges_r = exchanged(around, ((1, ((strip, 0), (strip, rows - strip))), (0, ((rows, 0),))))
+    right_a = features((mid,), 1, 1, inner, strip - REACH, edges_a, 0)
+    right_b = features(around, 1, 2, strip, 0, edges_r, 0)
+    left = features(around, 0, 1, rows, 0, edges_r, 2 * edge_steps(strip, segment)[1])
 
     steps = min(col_count // 2 - 1, HOPS // 2)
-
-    def pair(mine):
-        return mine, lax.ppermute(mine, "cols", swap)
-
-    def chain(mine, pieces):
-        pairs = [pair(mine)]
-        for _ in range(1, steps):
-            mine = lax.ppermute(mine, "cols", hop)
-            pairs.append(pair(mine))
-        last = []
-        for piece in range(pieces):
-            extent = mine.shape[0] // pieces
-            part = lax.slice_in_dim(mine, piece * extent, (piece + 1) * extent)
-            part = lax.ppermute(part, "cols", hop)
-            last.append(pair(part))
-        return pairs, last
-
-    keys_a, last_a = chain(right_a, 2)
-    keys_b, last_b = chain(right_b, 1)
     early = max(steps - 1, 1)
+
+    def chain(mine):
+        pairs = []
+        for step in range(steps + 1):
+            if step:
+                mine = lax.ppermute(mine, "cols", hop)
+            pairs.append((mine, lax.ppermute(mine, "cols", swap)))
+        return pairs
 
     def totals(keys, inside):
         acc = correlate(place, ranges, left, keys[:early], None, 0, inside)
         if early == steps:
             return acc
-        return correlate(place, ranges, left, keys[early:], acc, early, inside)
-
+        return correlate(place, ranges, left, keys[early:steps], acc, early, inside)
+
+    keys_a, keys_b = chain(right_a), chain(right_b)
     acc_a, acc_b = totals(keys_a, True), totals(keys_b, False)
-    outs = None
-    for piece, keys in enumerate(last_a):
-        outs = finish(place, ranges, left, keys, acc_a, piece, outs, True, steps)
-    return finish(place, ranges, left, last_b[0], acc_b, 0, outs, False, steps)
+    outs = finish(place, ranges, left, keys_a[steps], acc_a, None, True, steps)
+    return finish(place, ranges, left, keys_b[steps], acc_b, outs, False, steps)
 
 
 def solution(mesh):

time: 136 us -> 118 us (0.87)
  waiting for transfers between devices: 48.6 us -> 32.1 us
  local copies, waits for them, and re-layouts: 7.13 us -> 5.03 us
    ppermute x12 -> x8, waiting for transfers between devices: 30.4 us -> 0.02 us  [chain(): pairs.append((mine, lax.ppermute(mine, 'cols', swap)))]
    ppermute x4 -> x6, waiting for transfers between devices: 16.1 us -> 29.9 us  [chain(): mine = lax.ppermute(mine, 'cols', hop)]
    ppermute x12 -> x8, starting transfers between devices: 6.39 us -> 8.56 us  [chain(): pairs.append((mine, lax.ppermute(mine, 'cols', swap)))]
    slice x1 -> x0, local copies, waits for them, and re-layouts: 2.04 us -> none  [chain(): part = lax.slice_in_dim(mine, piece * extent, (piece + 1) * extent)]
    pallas_call x3 -> x2, Pallas kernels: 8.64 us -> 7.58 us  [finish(): pl.pallas_call(functools.partial(finish_kernel, inner=inner, groups=group...]
    ppermute x4 -> x6, starting transfers between devices: 3.39 us -> 2.61 us  [chain(): mine = lax.ppermute(mine, 'cols', hop)]
  transfers between devices with their start and end apart: 22 -> 20, of which waited for: 5 -> 6; matrix products, arithmetic and copies ran while one was open for 2% -> 1% of each run, Pallas kernels for 40% -> 44%
where the time goes in v8:
time: 118 us; the launch traced here: 117 us
  Pallas kernels  55.5 us (47%)
  waiting for transfers between devices  32.1 us (27%)
  starting transfers between devices  22.9 us (19%)
  local copies, waits for them, and re-layouts  5.03 us (4%)
    ppermute x6, waiting for transfers between devices, chain(): mine = lax.ppermute(mine, 'cols', hop)  29.9 us
    pallas_call x3, Pallas kernels, unit_features(): pl.pallas_call(functools.partial(feature_kernel, spacing=spacing, offset=...  24.3 us
    pallas_call x4, Pallas kernels, correlate(): pl.pallas_call(functools.partial(gather_kernel, inner=inner, groups=group...  18 us
    ppermute x2, starting transfers between devices, exchanged(): cross = lax.ppermute(own, 'cols', across)  8.64 us
    ppermute x8, starting transfers between devices, chain(): pairs.append((mine, lax.ppermute(mine, 'cols', swap)))  8.56 us
    pallas_call x2, Pallas kernels, finish(): pl.pallas_call(functools.partial(finish_kernel, inner=inner, groups=group...  7.58 us
    pallas_call x2, Pallas kernels, pack_edges(): pl.pallas_call(functools.partial(pack_kernel, images=tuple((chunks for _,...  5.65 us
    unnamed x3, local copies, waits for them, and re-layouts  4.27 us
  transfers between devices with their start and end apart: 20, of which 6 were waited for; matrix products, arithmetic and copies ran while one was open for 1% of the time, Pallas kernels for 44%

profile of v8, /device:TPU:1, one launch (start us, length us, event | category | flops | bytes accessed | tf_op | source)
XLA Modules:
  0.0 116.9 jit_solution(15761246558511563591)
XLA Ops:
  0.6 2.9 %copy.12 = bf16[2,64,64,128]{3,1,2,0:T(8,128)(2,1)S(1)} copy(bf16[2,64,64,128]{3,2,1,0:T(8,128)(2,1)} %param.4) | data formatting | bytes 4194304 | tf_op args[0]
  3.6 1.3 %copy-done = bf16[2,64,64,128]{3,1,2,0:T(8,128)(2,1)} copy-done((bf16[2,64,64,128]{3,1,2,0:T(8,128)(2,1)}, bf16[2,64,64,128]{3,1,2,0:T(8,128)(2,1)S(1)}, u32[]{:S(2)}) %copy-start) | copy-done | bytes 2097176
  4.9 0.8 fusion
  5.7 3.0 %collective-permute-start.1 = (bf16[2,6,64,128]{3,2,1,0:T(8,128)(2,1)}, bf16[2,6,64,128]{3,2,1,0:T(8,128)(2,1)}, u32[]{:S(2)}, u32[]{:S(2)}) collective-permute-start(bf16[2,6,64,128]{3,2,1,0:T(8,128)(2,1)} %get-tuple-element.6), channel_id=1, source_target_pairs={{8,0},{16,8},{24,16},{0,24},{9,1},{17,9},{25,17},{1,25},{10,2},{18... | collective-permute-start | bytes 589832 | tf_op jit(solution)/shard_map/ppermute | solution.py:523
  8.7 0.0 collective-permute-start
  8.7 2.2 %shard_map.64.refs_1_ = bf16[9,64,128]{2,1,0:T(8,128)(2,1)} custom-call(bf16[2,64,64,128]{3,2,1,0:T(8,128)(2,1)} %bitcast.7), custom_call_target="tpu_custom_call" | custom-call | flops 2000000000 | bytes 6000000 | tf_op jit(solution)/shard_map/pallas_call | solution.py:96
  10.9 4.0 %collective-permute-start.12 = (bf16[9,64,128]{2,1,0:T(8,128)(2,1)}, bf16[9,64,128]{2,1,0:T(8,128)(2,1)}, u32[]{:S(2)}, u32[]{:S(2)}) collective-permute-start(bf16[9,64,128]{2,1,0:T(8,128)(2,1)} %shard_map.64.refs_1_), channel_id=1, source_target_pairs={{1,2},{3,4},{5,6},{2,1},{4,3},{6,5},{9,10},{11,12},{13,14},{10,9},... | collective-permute-start | bytes 442376 | tf_op jit(solution)/shard_map/ppermute | solution.py:511
  14.9 0.1 collective-permute-start.11
  15.0 0.6 pad_add_fusion.refs_0_.place_ref
  15.6 0.0 collective-permute-done.1.refs_3_.refs_6_.refs_2_
  15.7 2.1 %collective-permute-done.refs_2_.refs_5_.refs_1_ = bf16[2,6,64,128]{3,2,1,0:T(8,128)(2,1)} collective-permute-done((bf16[2,6,64,128]{3,2,1,0:T(8,128)(2,1)}, bf16[2,6,64,128]{3,2,1,0:T(8,128)(2,1)}, u32[]{:S(2)}, u32[]{:S(2)}) %collective-permute-start) | collective-permute-done | bytes 196640 | tf_op jit(solution)/shard_map/ppermute | solution.py:522
  17.8 3.4 %shard_map.59.refs_3_ = bf16[27,64,128]{2,1,0:T(8,128)(2,1)} custom-call(s32[2]{0:T(128)} %pad_add_fusion.refs_0_.place_ref, bf16[2,64,64,128]{3,2,1,0:T(8,128)(2,1)} %bitcast.8, bf16[2,6,64,128]{3,2,1,0:T(8,128)(2,1)} %collective-permute-done.refs_2_.refs_5_.refs_1_, bf16[2,6,64,128]{3,2,1,0:T(8,128)(2,1)} %collective-permute-done.1.refs_3_.refs_6_.refs_2_, ...), custom_call_target="tpu_custom_call" | custom-call | flops 2000000000 | bytes 6000000 | tf_op jit(solution)/shard_map/pallas_call | solution.py:96
  21.2 4.6 %collective-permute-start.3 = (bf16[27,64,128]{2,1,0:T(8,128)(2,1)}, bf16[27,64,128]{2,1,0:T(8,128)(2,1)}, u32[]{:S(2)}, u32[]{:S(2)}) collective-permute-start(bf16[27,64,128]{2,1,0:T(8,128)(2,1)} %shard_map.59.refs_3_), channel_id=1, source_target_pairs={{1,2},{3,4},{5,6},{2,1},{4,3},{6,5},{9,10},{11,12},{13,14},{10,9},... | collective-permute-start | bytes 1327112 | tf_op jit(solution)/shard_map/ppermute | solution.py:511
  25.8 0.1 collective-permute-start.2
  25.9 0.0 collective-permute-done.12.refs_3_
  25.9 0.0 collective-permute-done.11.refs_2_
  25.9 6.5 %shard_map.65.refs_0_ = bf16[32,64,128]{2,1,0:T(8,128)(2,1)} custom-call(s32[2]{0:T(128)} %pad_add_fusion.refs_0_.place_ref, bf16[2,64,64,128]{3,2,1,0:T(8,128)(2,1)} %bitcast.10, bf16[9,64,128]{2,1,0:T(8,128)(2,1)} %shard_map.64.refs_1_, bf16[9,64,128]{2,1,0:T(8,128)(2,1)} %collective-permute-done.11.refs_2_, ...), custom_call_target="tpu_custom_call" | custom-call | flops 6400000000 | bytes 19200000 | tf_op jit(solution)/shard_map/pallas_call | solution.py:296
  32.3 0.5 collective-permute-start.18
  32.8 1.3 %collective-permute-start.13 = (bf16[32,64,128]{2,1,0:T(8,128)(2,1)}, bf16[32,64,128]{2,1,0:T(8,128)(2,1)}, u32[]{:S(2)}, u32[]{:S(2)}) collective-permute-start(bf16[32,64,128]{2,1,0:T(8,128)(2,1)} %shard_map.65.refs_0_), channel_id=1, source_target_pairs={{0,2},{1,3},{2,4},{3,5},{4,6},{5,7},{6,0},{7,1},{8,10},{9,11},{10,... | collective-permute-start | bytes 1572872 | tf_op jit(solution)/shard_map/ppermute | solution.py:541
  34.1 0.0 collective-permute-done.3.refs_5_
  34.1 8.0 %shard_map.61.refs_0_ = bf16[32,64,128]{2,1,0:T(8,128)(2,1)} custom-call(s32[2]{0:T(128)} %pad_add_fusion.refs_0_.place_ref, bf16[2,64,64,128]{3,2,1,0:T(8,128)(2,1)} %bitcast.11, bf16[2,6,64,128]{3,2,1,0:T(8,128)(2,1)} %collective-permute-done.refs_2_.refs_5_.refs_1_, bf16[2,6,64,128]{3,2,1,0:T(8,128)(2,1)} %collective-permute-done.1.refs_3_.refs_6_.refs_2_, ...), custom_call_target="tpu_custom_call" | custom-call | flops 6400000000 | bytes 19200000 | tf_op jit(solution)/shard_map/pallas_call | solution.py:296
  42.2 0.3 collective-permute-start.9
  42.5 1.3 %collective-permute-start.4 = (bf16[32,64,128]{2,1,0:T(8,128)(2,1)}, bf16[32,64,128]{2,1,0:T(8,128)(2,1)}, u32[]{:S(2)}, u32[]{:S(2)}) collective-permute-start(bf16[32,64,128]{2,1,0:T(8,128)(2,1)} %shard_map.61.refs_0_), channel_id=1, source_target_pairs={{0,2},{1,3},{2,4},{3,5},{4,6},{5,7},{6,0},{7,1},{8,10},{9,11},{10,... | collective-permute-start | bytes 1572872 | tf_op jit(solution)/shard_map/ppermute | solution.py:541
  43.8 4.6 %collective-permute-done.13.refs_2_ = bf16[32,64,128]{2,1,0:T(8,128)(2,1)} collective-permute-done((bf16[32,64,128]{2,1,0:T(8,128)(2,1)}, bf16[32,64,128]{2,1,0:T(8,128)(2,1)}, u32[]{:S(2)}, u32[]{:S(2)}) %collective-permute-start.13) | collective-permute-done | bytes 524320 | tf_op jit(solution)/shard_map/ppermute | solution.py:541
  48.4 1.4 %collective-permute-start.19 = (bf16[32,64,128]{2,1,0:T(8,128)(2,1)}, bf16[32,64,128]{2,1,0:T(8,128)(2,1)}, u32[]{:S(2)}, u32[]{:S(2)}) collective-permute-start(bf16[32,64,128]{2,1,0:T(8,128)(2,1)} %collective-permute-done.13.refs_2_), channel_id=1, source_target_pairs={{0,1},{1,0},{2,3},{3,2},{4,5},{5,4},{6,7},{7,6},{8,9},{9,8},{10,11... | collective-permute-start | bytes 1572872 | tf_op jit(solution)/shard_map/ppermute | solution.py:542
  49.8 0.0 collective-permute-start.14
  49.8 9.8 %shard_map.60.left_ref = bf16[64,64,128]{2,1,0:T(8,128)(2,1)} custom-call(s32[2]{0:T(128)} %pad_add_fusion.refs_0_.place_ref, bf16[2,64,64,128]{3,2,1,0:T(8,128)(2,1)} %bitcast.12, bf16[2,6,64,128]{3,2,1,0:T(8,128)(2,1)} %collective-permute-done.refs_2_.refs_5_.refs_1_, bf16[2,6,64,128]{3,2,1,0:T(8,128)(2,1)} %collective-permute-done.1.refs_3_.refs_6_.refs_2_, ...), custom_call_target="tpu_custom_call" | custom-call | flops 12800000000 | bytes 38400000 | tf_op jit(solution)/shard_map/pallas_call | solution.py:296
  59.6 0.0 collective-permute-done.4.refs_2_
  59.6 1.4 %collective-permute-start.10 = (bf16[32,64,128]{2,1,0:T(8,128)(2,1)}, bf16[32,64,128]{2,1,0:T(8,128)(2,1)}, u32[]{:S(2)}, u32[]{:S(2)}) collective-permute-start(bf16[32,64,128]{2,1,0:T(8,128)(2,1)} %collective-permute-done.4.refs_2_), channel_id=1, source_target_pairs={{0,1},{1,0},{2,3},{3,2},{4,5},{5,4},{6,7},{7,6},{8,9},{9,8},{10,11... | collective-permute-start | bytes 1572872 | tf_op jit(solution)/shard_map/ppermute | solution.py:542
  61.0 9.9 %collective-permute-done.14.refs_0_ = bf16[32,64,128]{2,1,0:T(8,128)(2,1)} collective-permute-done((bf16[32,64,128]{2,1,0:T(8,128)(2,1)}, bf16[32,64,128]{2,1,0:T(8,128)(2,1)}, u32[]{:S(2)}, u32[]{:S(2)}) %collective-permute-start.14) | collective-permute-done | bytes 524320 | tf_op jit(solution)/shard_map/ppermute | solution.py:541
  70.9 1.4 %collective-permute-start.17 = (bf16[32,64,128]{2,1,0:T(8,128)(2,1)}, bf16[32,64,128]{2,1,0:T(8,128)(2,1)}, u32[]{:S(2)}, u32[]{:S(2)}) collective-permute-start(bf16[32,64,128]{2,1,0:T(8,128)(2,1)} %collective-permute-done.14.refs_0_), channel_id=1, source_target_pairs={{0,1},{1,0},{2,3},{3,2},{4,5},{5,4},{6,7},{7,6},{8,9},{9,8},{10,11... | collective-permute-start | bytes 1572872 | tf_op jit(solution)/shard_map/ppermute | solution.py:542
  72.2 5.1 %shard_map.66.refs_2_ = f32[32,80,128]{2,1,0:T(8,128)} custom-call(s32[2]{0:T(128)} %pad_add_fusion.refs_0_.place_ref, s32[2,8]{1,0:T(2,128)} %bitcast.13, bf16[64,64,128]{2,1,0:T(8,128)(2,1)} %shard_map.60.left_ref, bf16[32,64,128]{2,1,0:T(8,128)(2,1)} %shard_map.65.refs_0_, bf16[32,64,128]{2,1,0:T(8,128)(2,1)} %collective-permute-done.18.refs_1_, ...), custom_call_target="tpu_custom_call" | custom-call | flops 6000000000 | bytes 18000000 | tf_op jit(solution)/shard_map/pallas_call | solution.py:430
  77.4 4.7 %collective-permute-done.5.refs_0_ = bf16[32,64,128]{2,1,0:T(8,128)(2,1)} collective-permute-done((bf16[32,64,128]{2,1,0:T(8,128)(2,1)}, bf16[32,64,128]{2,1,0:T(8,128)(2,1)}, u32[]{:S(2)}, u32[]{:S(2)}) %collective-permute-start.5) | collective-permute-done | bytes 524320 | tf_op jit(solution)/shard_map/ppermute | solution.py:541
  82.1 1.4 %collective-permute-start.8 = (bf16[32,64,128]{2,1,0:T(8,128)(2,1)}, bf16[32,64,128]{2,1,0:T(8,128)(2,1)}, u32[]{:S(2)}, u32[]{:S(2)}) collective-permute-start(bf16[32,64,128]{2,1,0:T(8,128)(2,1)} %collective-permute-done.5.refs_0_), channel_id=1, source_target_pairs={{0,1},{1,0},{2,3},{3,2},{4,5},{5,4},{6,7},{7,6},{8,9},{9,8},{10,11... | collective-permute-start | bytes 1572872 | tf_op jit(solution)/shard_map/ppermute | solution.py:542
  83.5 0.0 collective-permute-done.9.refs_1_
  83.5 0.0 collective-permute-start.6
  83.5 0.0 collective-permute-done.10.refs_3_
  83.5 5.1 %shard_map.62.refs_2_ = f32[32,80,128]{2,1,0:T(8,128)} custom-call(s32[2]{0:T(128)} %pad_add_fusion.refs_0_.place_ref, s32[2,8]{1,0:T(2,128)} %bitcast.14, bf16[64,64,128]{2,1,0:T(8,128)(2,1)} %shard_map.60.left_ref, bf16[32,64,128]{2,1,0:T(8,128)(2,1)} %shard_map.61.refs_0_, bf16[32,64,128]{2,1,0:T(8,128)(2,1)} %collective-permute-done.9.refs_1_, ...), custom_call_target="tpu_custom_call" | custom-call | flops 6000000000 | bytes 18000000 | tf_op jit(solution)/shard_map/pallas_call | solution.py:430
  88.6 4.7 %collective-permute-done.15.mine_ref = bf16[32,64,128]{2,1,0:T(8,128)(2,1)} collective-permute-done((bf16[32,64,128]{2,1,0:T(8,128)(2,1)}, bf16[32,64,128]{2,1,0:T(8,128)(2,1)}, u32[]{:S(2)}, u32[]{:S(2)}) %collective-permute-start.15) | collective-permute-done | bytes 524320 | tf_op jit(solution)/shard_map/ppermute | solution.py:541
  93.3 1.4 %collective-permute-start.16 = (bf16[32,64,128]{2,1,0:T(8,128)(2,1)}, bf16[32,64,128]{2,1,0:T(8,128)(2,1)}, u32[]{:S(2)}, u32[]{:S(2)}) collective-permute-start(bf16[32,64,128]{2,1,0:T(8,128)(2,1)} %collective-permute-done.15.mine_ref), channel_id=1, source_target_pairs={{0,1},{1,0},{2,3},{3,2},{4,5},{5,4},{6,7},{7,6},{8,9},{9,8},{10,11... | collective-permute-start | bytes 1572872 | tf_op jit(solution)/shard_map/ppermute | solution.py:542
  94.7 0.0 collective-permute-done.17.refs_1_
  94.7 3.8 %shard_map.67.acc_in_ref = f32[32,80,128]{2,1,0:T(8,128)} custom-call(s32[2]{0:T(128)} %pad_add_fusion.refs_0_.place_ref, s32[2,8]{1,0:T(2,128)} %bitcast.15, bf16[64,64,128]{2,1,0:T(8,128)(2,1)} %shard_map.60.left_ref, bf16[32,64,128]{2,1,0:T(8,128)(2,1)} %collective-permute-done.14.refs_0_, ...), custom_call_target="tpu_custom_call", output_to_operand_aliasing={{}: (5, {})} | custom-call | flops 6000000000 | bytes 18000000 | tf_op jit(solution)/shard_map/pallas_call | solution.py:430
  98.6 6.0 %collective-permute-done.6.mine_ref = bf16[32,64,128]{2,1,0:T(8,128)(2,1)} collective-permute-done((bf16[32,64,128]{2,1,0:T(8,128)(2,1)}, bf16[32,64,128]{2,1,0:T(8,128)(2,1)}, u32[]{:S(2)}, u32[]{:S(2)}) %collective-permute-start.6) | collective-permute-done | bytes 524320 | tf_op jit(solution)/shard_map/ppermute | solution.py:541
  104.6 0.9 collective-permute-start.7
  105.5 3.8 %shard_map.63.acc_in_ref = f32[32,80,128]{2,1,0:T(8,128)} custom-call(s32[2]{0:T(128)} %pad_add_fusion.refs_0_.place_ref, s32[2,8]{1,0:T(2,128)} %bitcast.16, bf16[64,64,128]{2,1,0:T(8,128)(2,1)} %shard_map.60.left_ref, bf16[32,64,128]{2,1,0:T(8,128)(2,1)} %collective-permute-done.5.refs_0_, ...), custom_call_target="tpu_custom_call", output_to_operand_aliasing={{}: (5, {})} | custom-call | flops 6000000000 | bytes 18000000 | tf_op jit(solution)/shard_map/pallas_call | solution.py:430
  109.3 3.8 %shard_map.68 = (bf16[64,64,128]{2,1,0:T(8,128)(2,1)}, f32[64,128]{1,0:T(8,128)}) custom-call(s32[2]{0:T(128)} %pad_add_fusion.refs_0_.place_ref, s32[2,8]{1,0:T(2,128)} %bitcast.17, bf16[64,64,128]{2,1,0:T(8,128)(2,1)} %shard_map.60.left_ref, bf16[32,64,128]{2,1,0:T(8,128)(2,1)} %collective-permute-done.15.mine_ref, ...), custom_call_target="tpu_custom_call" | custom-call | flops 4000000000 | bytes 12000000 | tf_op jit(solution)/shard_map/pallas_call | solution.py:459
  113.1 0.0 collective-permute-done.7.theirs_ref
  113.1 3.8 %shard_map.69 = (bf16[64,64,128]{2,1,0:T(8,128)(2,1)}, f32[64,128]{1,0:T(8,128)}) custom-call(s32[2]{0:T(128)} %pad_add_fusion.refs_0_.place_ref, s32[2,8]{1,0:T(2,128)} %bitcast.18, bf16[64,64,128]{2,1,0:T(8,128)(2,1)} %shard_map.60.left_ref, bf16[32,64,128]{2,1,0:T(8,128)(2,1)} %collective-permute-done.6.mine_ref, ...), custom_call_target="tpu_custom_call", output_to_operand_aliasing={{0}: (6, {}), {1}: (7, {})} | custom-call | flops 4000000000 | bytes 12000000 | tf_op jit(solution)/shard_map/pallas_call | solution.py:459
  (8 shorter events, 0.0 us)
Async XLA Ops:
  3.6 1.3 %copy-start = (bf16[2,64,64,128]{3,1,2,0:T(8,128)(2,1)}, bf16[2,64,64,128]{3,1,2,0:T(8,128)(2,1)S(1)}, u32[]{:S(2)}) copy-start(bf16[2,64,64,128]{3,1,2,0:T(8,128)(2,1)S(1)} %copy.12) | copy-start | bytes 6291460
  5.7 10.0 %collective-permute-start.1 = (bf16[2,6,64,128]{3,2,1,0:T(8,128)(2,1)}, bf16[2,6,64,128]{3,2,1,0:T(8,128)(2,1)}, u32[]{:S(2)}, u32[]{:S(2)}) collective-permute-start(bf16[2,6,64,128]{3,2,1,0:T(8,128)(2,1)} %get-tuple-element.6), channel_id=1, source_target_pairs={{8,0},{16,8},{24,16},{0,24},{9,1},{17,9},{25,17},{1,25},{10,2},{18... | collective-permute-start | bytes 589832 | tf_op jit(solution)/shard_map/ppermute | solution.py:523
  8.7 9.1 %collective-permute-start = (bf16[2,6,64,128]{3,2,1,0:T(8,128)(2,1)}, bf16[2,6,64,128]{3,2,1,0:T(8,128)(2,1)}, u32[]{:S(2)}, u32[]{:S(2)}) collective-permute-start(bf16[2,6,64,128]{3,2,1,0:T(8,128)(2,1)} %get-tuple-element.7), channel_id=1, source_target_pairs={{0,8},{8,16},{16,24},{24,0},{1,9},{9,17},{17,25},{25,1},{2,10},{10... | collective-permute-start | bytes 589832 | tf_op jit(solution)/shard_map/ppermute | solution.py:522
  10.9 15.0 %collective-permute-start.12 = (bf16[9,64,128]{2,1,0:T(8,128)(2,1)}, bf16[9,64,128]{2,1,0:T(8,128)(2,1)}, u32[]{:S(2)}, u32[]{:S(2)}) collective-permute-start(bf16[9,64,128]{2,1,0:T(8,128)(2,1)} %shard_map.64.refs_1_), channel_id=1, source_target_pairs={{1,2},{3,4},{5,6},{2,1},{4,3},{6,5},{9,10},{11,12},{13,14},{10,9},... | collective-permute-start | bytes 442376 | tf_op jit(solution)/shard_map/ppermute | solution.py:511
  14.9 10.9 %collective-permute-start.11 = (bf16[9,64,128]{2,1,0:T(8,128)(2,1)}, bf16[9,64,128]{2,1,0:T(8,128)(2,1)}, u32[]{:S(2)}, u32[]{:S(2)}) collective-permute-start(bf16[9,64,128]{2,1,0:T(8,128)(2,1)} %shard_map.64.refs_1_), channel_id=1, source_target_pairs={{0,1},{1,0},{2,3},{3,2},{4,5},{5,4},{6,7},{7,6},{8,9},{9,8},{10,11... | collective-permute-start | bytes 442376 | tf_op jit(solution)/shard_map/ppermute | solution.py:512
  21.2 13.0 %collective-permute-start.3 = (bf16[27,64,128]{2,1,0:T(8,128)(2,1)}, bf16[27,64,128]{2,1,0:T(8,128)(2,1)}, u32[]{:S(2)}, u32[]{:S(2)}) collective-permute-start(bf16[27,64,128]{2,1,0:T(8,128)(2,1)} %shard_map.59.refs_3_), channel_id=1, source_target_pairs={{1,2},{3,4},{5,6},{2,1},{4,3},{6,5},{9,10},{11,12},{13,14},{10,9},... | collective-permute-start | bytes 1327112 | tf_op jit(solution)/shard_map/ppermute | solution.py:511
  25.8 8.3 %collective-permute-start.2 = (bf16[27,64,128]{2,1,0:T(8,128)(2,1)}, bf16[27,64,128]{2,1,0:T(8,128)(2,1)}, u32[]{:S(2)}, u32[]{:S(2)}) collective-permute-start(bf16[27,64,128]{2,1,0:T(8,128)(2,1)} %shard_map.59.refs_3_), channel_id=1, source_target_pairs={{0,1},{1,0},{2,3},{3,2},{4,5},{5,4},{6,7},{7,6},{8,9},{9,8},{10,11... | collective-permute-start | bytes 1327112 | tf_op jit(solution)/shard_map/ppermute | solution.py:512
  32.3 28.7 %collective-permute-start.18 = (bf16[32,64,128]{2,1,0:T(8,128)(2,1)}, bf16[32,64,128]{2,1,0:T(8,128)(2,1)}, u32[]{:S(2)}, u32[]{:S(2)}) collective-permute-start(bf16[32,64,128]{2,1,0:T(8,128)(2,1)} %shard_map.65.refs_0_), channel_id=1, source_target_pairs={{0,1},{1,0},{2,3},{3,2},{4,5},{5,4},{6,7},{7,6},{8,9},{9,8},{10,11... | collective-permute-start | bytes 1572872 | tf_op jit(solution)/shard_map/ppermute | solution.py:542
  32.8 15.6 %collective-permute-start.13 = (bf16[32,64,128]{2,1,0:T(8,128)(2,1)}, bf16[32,64,128]{2,1,0:T(8,128)(2,1)}, u32[]{:S(2)}, u32[]{:S(2)}) collective-permute-start(bf16[32,64,128]{2,1,0:T(8,128)(2,1)} %shard_map.65.refs_0_), channel_id=1, source_target_pairs={{0,2},{1,3},{2,4},{3,5},{4,6},{5,7},{6,0},{7,1},{8,10},{9,11},{10,... | collective-permute-start | bytes 1572872 | tf_op jit(solution)/shard_map/ppermute | solution.py:541
  42.2 41.3 %collective-permute-start.9 = (bf16[32,64,128]{2,1,0:T(8,128)(2,1)}, bf16[32,64,128]{2,1,0:T(8,128)(2,1)}, u32[]{:S(2)}, u32[]{:S(2)}) collective-permute-start(bf16[32,64,128]{2,1,0:T(8,128)(2,1)} %shard_map.61.refs_0_), channel_id=1, source_target_pairs={{0,1},{1,0},{2,3},{3,2},{4,5},{5,4},{6,7},{7,6},{8,9},{9,8},{10,11... | collective-permute-start | bytes 1572872 | tf_op jit(solution)/shard_map/ppermute | solution.py:542
  42.5 17.1 %collective-permute-start.4 = (bf16[32,64,128]{2,1,0:T(8,128)(2,1)}, bf16[32,64,128]{2,1,0:T(8,128)(2,1)}, u32[]{:S(2)}, u32[]{:S(2)}) collective-permute-start(bf16[32,64,128]{2,1,0:T(8,128)(2,1)} %shard_map.61.refs_0_), channel_id=1, source_target_pairs={{0,2},{1,3},{2,4},{3,5},{4,6},{5,7},{6,0},{7,1},{8,10},{9,11},{10,... | collective-permute-start | bytes 1572872 | tf_op jit(solution)/shard_map/ppermute | solution.py:541
  48.4 23.9 %collective-permute-start.19 = (bf16[32,64,128]{2,1,0:T(8,128)(2,1)}, bf16[32,64,128]{2,1,0:T(8,128)(2,1)}, u32[]{:S(2)}, u32[]{:S(2)}) collective-permute-start(bf16[32,64,128]{2,1,0:T(8,128)(2,1)} %collective-permute-done.13.refs_2_), channel_id=1, source_target_pairs={{0,1},{1,0},{2,3},{3,2},{4,5},{5,4},{6,7},{7,6},{8,9},{9,8},{10,11... | collective-permute-start | bytes 1572872 | tf_op jit(solution)/shard_map/ppermute | solution.py:542
  49.8 21.1 %collective-permute-start.14 = (bf16[32,64,128]{2,1,0:T(8,128)(2,1)}, bf16[32,64,128]{2,1,0:T(8,128)(2,1)}, u32[]{:S(2)}, u32[]{:S(2)}) collective-permute-start(bf16[32,64,128]{2,1,0:T(8,128)(2,1)} %collective-permute-done.13.refs_2_), channel_id=1, source_target_pairs={{0,2},{1,3},{2,4},{3,5},{4,6},{5,7},{6,0},{7,1},{8,10},{9,11},{10,... | collective-permute-start | bytes 1572872 | tf_op jit(solution)/shard_map/ppermute | solution.py:541
  59.6 23.9 %collective-permute-start.10 = (bf16[32,64,128]{2,1,0:T(8,128)(2,1)}, bf16[32,64,128]{2,1,0:T(8,128)(2,1)}, u32[]{:S(2)}, u32[]{:S(2)}) collective-permute-start(bf16[32,64,128]{2,1,0:T(8,128)(2,1)} %collective-permute-done.4.refs_2_), channel_id=1, source_target_pairs={{0,1},{1,0},{2,3},{3,2},{4,5},{5,4},{6,7},{7,6},{8,9},{9,8},{10,11... | collective-permute-start | bytes 1572872 | tf_op jit(solution)/shard_map/ppermute | solution.py:542
  61.0 21.1 %collective-permute-start.5 = (bf16[32,64,128]{2,1,0:T(8,128)(2,1)}, bf16[32,64,128]{2,1,0:T(8,128)(2,1)}, u32[]{:S(2)}, u32[]{:S(2)}) collective-permute-start(bf16[32,64,128]{2,1,0:T(8,128)(2,1)} %collective-permute-done.4.refs_2_), channel_id=1, source_target_pairs={{0,2},{1,3},{2,4},{3,5},{4,6},{5,7},{6,0},{7,1},{8,10},{9,11},{10,... | collective-permute-start | bytes 1572872 | tf_op jit(solution)/shard_map/ppermute | solution.py:541
  70.9 23.9 %collective-permute-start.17 = (bf16[32,64,128]{2,1,0:T(8,128)(2,1)}, bf16[32,64,128]{2,1,0:T(8,128)(2,1)}, u32[]{:S(2)}, u32[]{:S(2)}) collective-permute-start(bf16[32,64,128]{2,1,0:T(8,128)(2,1)} %collective-permute-done.14.refs_0_), channel_id=1, source_target_pairs={{0,1},{1,0},{2,3},{3,2},{4,5},{5,4},{6,7},{7,6},{8,9},{9,8},{10,11... | collective-permute-start | bytes 1572872 | tf_op jit(solution)/shard_map/ppermute | solution.py:542
  72.2 21.1 %collective-permute-start.15 = (bf16[32,64,128]{2,1,0:T(8,128)(2,1)}, bf16[32,64,128]{2,1,0:T(8,128)(2,1)}, u32[]{:S(2)}, u32[]{:S(2)}) collective-permute-start(bf16[32,64,128]{2,1,0:T(8,128)(2,1)} %collective-permute-done.14.refs_0_), channel_id=1, source_target_pairs={{0,2},{1,3},{2,4},{3,5},{4,6},{5,7},{6,0},{7,1},{8,10},{9,11},{10,... | collective-permute-start | bytes 1572872 | tf_op jit(solution)/shard_map/ppermute | solution.py:541
  82.1 23.4 %collective-permute-start.8 = (bf16[32,64,128]{2,1,0:T(8,128)(2,1)}, bf16[32,64,128]{2,1,0:T(8,128)(2,1)}, u32[]{:S(2)}, u32[]{:S(2)}) collective-permute-start(bf16[32,64,128]{2,1,0:T(8,128)(2,1)} %collective-permute-done.5.refs_0_), channel_id=1, source_target_pairs={{0,1},{1,0},{2,3},{3,2},{4,5},{5,4},{6,7},{7,6},{8,9},{9,8},{10,11... | collective-permute-start | bytes 1572872 | tf_op jit(solution)/shard_map/ppermute | solution.py:542
  83.5 21.1 %collective-permute-start.6 = (bf16[32,64,128]{2,1,0:T(8,128)(2,1)}, bf16[32,64,128]{2,1,0:T(8,128)(2,1)}, u32[]{:S(2)}, u32[]{:S(2)}) collective-permute-start(bf16[32,64,128]{2,1,0:T(8,128)(2,1)} %collective-permute-done.5.refs_0_), channel_id=1, source_target_pairs={{0,2},{1,3},{2,4},{3,5},{4,6},{5,7},{6,0},{7,1},{8,10},{9,11},{10,... | collective-permute-start | bytes 1572872 | tf_op jit(solution)/shard_map/ppermute | solution.py:541
  93.3 16.0 %collective-permute-start.16 = (bf16[32,64,128]{2,1,0:T(8,128)(2,1)}, bf16[32,64,128]{2,1,0:T(8,128)(2,1)}, u32[]{:S(2)}, u32[]{:S(2)}) collective-permute-start(bf16[32,64,128]{2,1,0:T(8,128)(2,1)} %collective-permute-done.15.mine_ref), channel_id=1, source_target_pairs={{0,1},{1,0},{2,3},{3,2},{4,5},{5,4},{6,7},{7,6},{8,9},{9,8},{10,11... | collective-permute-start | bytes 1572872 | tf_op jit(solution)/shard_map/ppermute | solution.py:542
  104.6 8.5 %collective-permute-start.7 = (bf16[32,64,128]{2,1,0:T(8,128)(2,1)}, bf16[32,64,128]{2,1,0:T(8,128)(2,1)}, u32[]{:S(2)}, u32[]{:S(2)}) collective-permute-start(bf16[32,64,128]{2,1,0:T(8,128)(2,1)} %collective-permute-done.6.mine_ref), channel_id=1, source_target_pairs={{0,1},{1,0},{2,3},{3,2},{4,5},{5,4},{6,7},{7,6},{8,9},{9,8},{10,11... | collective-permute-start | bytes 1572872 | tf_op jit(solution)/shard_map/ppermute | solution.py:542

commit v9 on v8

--- a/solution.py
+++ b/solution.py
@@ -46,6 +46,11 @@
 
 def kept(piece, inside):
     return jnp.where(inside, piece, jnp.zeros_like(piece))
+
+
+def either_side(place_ref, near, far):
+    odd = place_ref[0] % 2 == 1
+    return jnp.where(odd, near, far), jnp.where(odd, far, near)
 
 
 def pack_kernel(*refs, images, last_row):
@@ -62,11 +67,11 @@
         slot_of = lane_iota((channels, segment)) // SLOT
 
         def row_at(row):
-            if row < 0:
-                return kept(around[0][row + REACH], place_ref[0] > 0)
-            if row >= rows:
-                return kept(around[1][row - rows], place_ref[0] < last_row)
-            return mid_ref[row]
+            if 0 <= row < rows:
+                return mid_ref[row]
+            at = row + REACH if row < 0 else row - rows
+            above, below = either_side(place_ref, around[0][at], around[1][at])
+            return kept(above, place_ref[0] > 0) if row < 0 else kept(below, place_ref[0] < last_row)
 
         for count, first in chunks:
             spacing, steps = edge_steps(count, segment)
@@ -140,7 +145,7 @@
     for q in range(steps):
         own = own_ref[q]
         partner = partner_ref[q]
-        cross = cross_ref[q]
+        cross = kept(cross_ref[q], ~(first_col | last_col))
         left = jnp.where(odd, partner, cross)
         right = jnp.where(odd, cross, partner)
         shift = half - REACH
@@ -196,8 +201,8 @@
             multiply_rows(spacing - 1, rhs0_ref)
 
     if ends:
-        top = kept(refs[1][...], ~first_row)
-        bottom = kept(refs[2][...], ~last_row)
+        top, bottom = either_side(place_ref, refs[1][...], refs[2][...])
+        top, bottom = kept(top, ~first_row), kept(bottom, ~last_row)
         if rows == held:
             x_ref[0:REACH] = top
             x_ref[REACH : REACH + rows] = mid_ref[...]
@@ -501,10 +506,10 @@
     ranges = search_ranges.reshape(2, rows // RG)
 
     swap = [(i, i ^ 1) for i in range(col_count)]
-    across = both_ways([(i, i + 1) for i in range(1, col_count - 1, 2)])
+    across = both_ways([(i, (i + 1) % col_count) for i in range(1, col_count, 2)])
     hop = [(i, (i + 2) % col_count) for i in range(col_count)]
-    down = [(i, (i + 1) % row_count) for i in range(row_count)]
-    up = [(b, a) for a, b in down]
+    near_pairs = both_ways([(i, i + 1) for i in range(0, row_count, 2)])
+    far_pairs = both_ways([(i, (i + 1) % row_count) for i in range(1, row_count, 2)])
 
     def exchanged(pieces, chunks):
         own = pack_edges(place, pieces, chunks, row_count)
@@ -519,12 +524,14 @@
         )
 
     mid = images.transpose(0, 2, 1, 3)
-    above = lax.ppermute(mid[:, rows - REACH :], "rows", down)
-    below = lax.ppermute(mid[:, :REACH], "rows", up)
+    odd_row = lax.axis_index("rows") % 2 == 1
+    first_rows, last_rows = mid[:, :REACH], mid[:, rows - REACH :]
+    near = lax.ppermute(jnp.where(odd_row, first_rows, last_rows), "rows", near_pairs)
+    far = lax.ppermute(jnp.where(odd_row, last_rows, first_rows), "rows", far_pairs)
 
     strip = rows // 4
     inner = rows - 2 * strip
-    around = (mid, above, below)
+    around = (mid, near, far)
     edges_a = exchanged((mid,), ((1, ((inner, strip),)),))
     edges_r = exchanged(around, ((1, ((strip, 0), (strip, rows - strip))), (0, ((rows, 0),))))
     right_a = features((mid,), 1, 1, inner, strip - REACH, edges_a, 0)

time: 118 us -> 119 us (level)
  waiting for transfers between devices: 32.1 us -> 34.1 us
    ppermute x2, starting transfers between devices: 8.64 us -> 5.13 us  [exchanged(): cross = lax.ppermute(own, 'cols', across)]
    ppermute x2, starting transfers between devices: 0.14 us -> 2.3 us  [exchanged(): partner = lax.ppermute(own, 'cols', swap)]
    ppermute x8, starting transfers between devices: 8.56 us -> 10.4 us  [chain(): pairs.append((mine, lax.ppermute(mine, 'cols', swap)))]
    ppermute x6, starting transfers between devices: 2.61 us -> 0.81 us  [chain(): mine = lax.ppermute(mine, 'cols', hop)]
    ppermute x2, waiting for transfers between devices: 0.01 us -> 1.74 us  [exchanged(): cross = lax.ppermute(own, 'cols', across)]
  transfers between devices with their start and end apart: 20 -> 20, of which waited for: 6 -> 8; matrix products, arithmetic and copies ran while one was open for 1% -> 1% of each run, Pallas kernels for 44% -> 44%
where the time goes in v9:
time: 119 us; the launch traced here: 118 us
  Pallas kernels  55.6 us (47%)
  waiting for transfers between devices  34.1 us (29%)
  starting transfers between devices  21.9 us (18%)
  local copies, waits for them, and re-layouts  4.27 us (4%)
  other arithmetic  1.38 us (1%)
    ppermute x6, waiting for transfers between devices, chain(): mine = lax.ppermute(mine, 'cols', hop)  30.1 us
    pallas_call x3, Pallas kernels, unit_features(): pl.pallas_call(functools.partial(feature_kernel, spacing=spacing, offset=...  24.4 us
    pallas_call x4, Pallas kernels, correlate(): pl.pallas_call(functools.partial(gather_kernel, inner=inner, groups=group...  18 us
    ppermute x8, starting transfers between devices, chain(): pairs.append((mine, lax.ppermute(mine, 'cols', swap)))  10.4 us
    pallas_call x2, Pallas kernels, finish(): pl.pallas_call(functools.partial(finish_kernel, inner=inner, groups=group...  7.58 us
    pallas_call x2, Pallas kernels, pack_edges(): pl.pallas_call(functools.partial(pack_kernel, images=tuple((chunks for _,...  5.65 us
    ppermute x2, starting transfers between devices, exchanged(): cross = lax.ppermute(own, 'cols', across)  5.13 us
    unnamed x3, local copies, waits for them, and re-layouts  4.27 us
  transfers between devices with their start and end apart: 20, of which 8 were waited for; matrix products, arithmetic and copies ran while one was open for 1% of the time, Pallas kernels for 44%

profile of v9, /device:TPU:1, one launch (start us, length us, event | category | flops | bytes accessed | tf_op | source)
XLA Modules:
  0.0 117.9 jit_solution(17946032886842724364)
XLA Ops:
  0.6 2.9 %copy.12 = bf16[2,64,64,128]{3,1,2,0:T(8,128)(2,1)S(1)} copy(bf16[2,64,64,128]{3,2,1,0:T(8,128)(2,1)} %param.4) | data formatting | bytes 4194304 | tf_op args[0]
  3.6 1.3 %copy-done = bf16[2,64,64,128]{3,1,2,0:T(8,128)(2,1)} copy-done((bf16[2,64,64,128]{3,1,2,0:T(8,128)(2,1)}, bf16[2,64,64,128]{3,1,2,0:T(8,128)(2,1)S(1)}, u32[]{:S(2)}) %copy-start) | copy-done | bytes 2097176
  4.9 0.8 broadcast_select_fusion
  5.7 3.0 %collective-permute-start.1 = (bf16[2,6,64,128]{3,2,1,0:T(8,128)(2,1)}, bf16[2,6,64,128]{3,2,1,0:T(8,128)(2,1)}, u32[]{:S(2)}, u32[]{:S(2)}) collective-permute-start(bf16[2,6,64,128]{3,2,1,0:T(8,128)(2,1)} %get-tuple-element.6), channel_id=1, source_target_pairs={{8,16},{24,0},{16,8},{0,24},{9,17},{25,1},{17,9},{1,25},{10,18},{2... | collective-permute-start | bytes 589832 | tf_op jit(solution)/shard_map/ppermute | solution.py:530
  8.7 0.3 collective-permute-start
  8.9 2.2 %shard_map.64.refs_1_ = bf16[9,64,128]{2,1,0:T(8,128)(2,1)} custom-call(bf16[2,64,64,128]{3,2,1,0:T(8,128)(2,1)} %bitcast.7), custom_call_target="tpu_custom_call" | custom-call | flops 2000000000 | bytes 6000000 | tf_op jit(solution)/shard_map/pallas_call | solution.py:101
  11.2 2.4 %collective-permute-start.12 = (bf16[9,64,128]{2,1,0:T(8,128)(2,1)}, bf16[9,64,128]{2,1,0:T(8,128)(2,1)}, u32[]{:S(2)}, u32[]{:S(2)}) collective-permute-start(bf16[9,64,128]{2,1,0:T(8,128)(2,1)} %shard_map.64.refs_1_), channel_id=1, source_target_pairs={{1,2},{3,4},{5,6},{7,0},{2,1},{4,3},{6,5},{0,7},{9,10},{11,12},{13... | collective-permute-start | bytes 442376 | tf_op jit(solution)/shard_map/ppermute | solution.py:516
  13.6 1.3 %collective-permute-start.11 = (bf16[9,64,128]{2,1,0:T(8,128)(2,1)}, bf16[9,64,128]{2,1,0:T(8,128)(2,1)}, u32[]{:S(2)}, u32[]{:S(2)}) collective-permute-start(bf16[9,64,128]{2,1,0:T(8,128)(2,1)} %shard_map.64.refs_1_), channel_id=1, source_target_pairs={{0,1},{1,0},{2,3},{3,2},{4,5},{5,4},{6,7},{7,6},{8,9},{9,8},{10,11... | collective-permute-start | bytes 442376 | tf_op jit(solution)/shard_map/ppermute | solution.py:517
  14.9 0.6 pad_add_fusion.refs_0_.place_ref
  15.5 2.3 %collective-permute-done.refs_2_.refs_5_.refs_1_ = bf16[2,6,64,128]{3,2,1,0:T(8,128)(2,1)} collective-permute-done((bf16[2,6,64,128]{3,2,1,0:T(8,128)(2,1)}, bf16[2,6,64,128]{3,2,1,0:T(8,128)(2,1)}, u32[]{:S(2)}, u32[]{:S(2)}) %collective-permute-start) | collective-permute-done | bytes 196640 | tf_op jit(solution)/shard_map/ppermute | solution.py:529
  17.8 3.4 %shard_map.59.refs_3_ = bf16[27,64,128]{2,1,0:T(8,128)(2,1)} custom-call(s32[2]{0:T(128)} %pad_add_fusion.refs_0_.place_ref, bf16[2,64,64,128]{3,2,1,0:T(8,128)(2,1)} %bitcast.8, bf16[2,6,64,128]{3,2,1,0:T(8,128)(2,1)} %collective-permute-done.refs_2_.refs_5_.refs_1_, bf16[2,6,64,128]{3,2,1,0:T(8,128)(2,1)} %collective-permute-done.1.refs_3_.refs_6_.refs_2_, ...), custom_call_target="tpu_custom_call" | custom-call | flops 2000000000 | bytes 6000000 | tf_op jit(solution)/shard_map/pallas_call | solution.py:101
  21.2 2.7 %collective-permute-start.3 = (bf16[27,64,128]{2,1,0:T(8,128)(2,1)}, bf16[27,64,128]{2,1,0:T(8,128)(2,1)}, u32[]{:S(2)}, u32[]{:S(2)}) collective-permute-start(bf16[27,64,128]{2,1,0:T(8,128)(2,1)} %shard_map.59.refs_3_), channel_id=1, source_target_pairs={{1,2},{3,4},{5,6},{7,0},{2,1},{4,3},{6,5},{0,7},{9,10},{11,12},{13... | collective-permute-start | bytes 1327112 | tf_op jit(solution)/shard_map/ppermute | solution.py:516
  23.9 1.0 collective-permute-start.2
  24.9 0.0 collective-permute-done.12.refs_3_
  24.9 0.0 collective-permute-done.11.refs_2_
  24.9 6.5 %shard_map.65.refs_0_ = bf16[32,64,128]{2,1,0:T(8,128)(2,1)} custom-call(s32[2]{0:T(128)} %pad_add_fusion.refs_0_.place_ref, bf16[2,64,64,128]{3,2,1,0:T(8,128)(2,1)} %bitcast.10, bf16[9,64,128]{2,1,0:T(8,128)(2,1)} %shard_map.64.refs_1_, bf16[9,64,128]{2,1,0:T(8,128)(2,1)} %collective-permute-done.11.refs_2_, ...), custom_call_target="tpu_custom_call" | custom-call | flops 6400000000 | bytes 19200000 | tf_op jit(solution)/shard_map/pallas_call | solution.py:301
  31.4 0.0 collective-permute-start.18
  31.4 0.8 collective-permute-start.13
  32.2 1.7 %collective-permute-done.3.refs_5_ = bf16[27,64,128]{2,1,0:T(8,128)(2,1)} collective-permute-done((bf16[27,64,128]{2,1,0:T(8,128)(2,1)}, bf16[27,64,128]{2,1,0:T(8,128)(2,1)}, u32[]{:S(2)}, u32[]{:S(2)}) %collective-permute-start.3) | collective-permute-done | bytes 442400 | tf_op jit(solution)/shard_map/ppermute | solution.py:516
  33.9 0.0 collective-permute-done.2.refs_4_
  33.9 8.1 %shard_map.61.refs_0_ = bf16[32,64,128]{2,1,0:T(8,128)(2,1)} custom-call(s32[2]{0:T(128)} %pad_add_fusion.refs_0_.place_ref, bf16[2,64,64,128]{3,2,1,0:T(8,128)(2,1)} %bitcast.11, bf16[2,6,64,128]{3,2,1,0:T(8,128)(2,1)} %collective-permute-done.refs_2_.refs_5_.refs_1_, bf16[2,6,64,128]{3,2,1,0:T(8,128)(2,1)} %collective-permute-done.1.refs_3_.refs_6_.refs_2_, ...), custom_call_target="tpu_custom_call" | custom-call | flops 6400000000 | bytes 19200000 | tf_op jit(solution)/shard_map/pallas_call | solution.py:301
  42.0 3.0 %collective-permute-start.9 = (bf16[32,64,128]{2,1,0:T(8,128)(2,1)}, bf16[32,64,128]{2,1,0:T(8,128)(2,1)}, u32[]{:S(2)}, u32[]{:S(2)}) collective-permute-start(bf16[32,64,128]{2,1,0:T(8,128)(2,1)} %shard_map.61.refs_0_), channel_id=1, source_target_pairs={{0,1},{1,0},{2,3},{3,2},{4,5},{5,4},{6,7},{7,6},{8,9},{9,8},{10,11... | collective-permute-start | bytes 1572872 | tf_op jit(solution)/shard_map/ppermute | solution.py:549
  45.0 0.0 collective-permute-start.4
  45.0 2.7 %collective-permute-done.13.refs_2_ = bf16[32,64,128]{2,1,0:T(8,128)(2,1)} collective-permute-done((bf16[32,64,128]{2,1,0:T(8,128)(2,1)}, bf16[32,64,128]{2,1,0:T(8,128)(2,1)}, u32[]{:S(2)}, u32[]{:S(2)}) %collective-permute-start.13) | collective-permute-done | bytes 524320 | tf_op jit(solution)/shard_map/ppermute | solution.py:548
  47.8 0.8 collective-permute-start.19
  48.5 0.0 collective-permute-start.14
  48.5 9.8 %shard_map.60.left_ref = bf16[64,64,128]{2,1,0:T(8,128)(2,1)} custom-call(s32[2]{0:T(128)} %pad_add_fusion.refs_0_.place_ref, bf16[2,64,64,128]{3,2,1,0:T(8,128)(2,1)} %bitcast.12, bf16[2,6,64,128]{3,2,1,0:T(8,128)(2,1)} %collective-permute-done.refs_2_.refs_5_.refs_1_, bf16[2,6,64,128]{3,2,1,0:T(8,128)(2,1)} %collective-permute-done.1.refs_3_.refs_6_.refs_2_, ...), custom_call_target="tpu_custom_call" | custom-call | flops 12800000000 | bytes 38400000 | tf_op jit(solution)/shard_map/pallas_call | solution.py:301
  58.4 2.2 %collective-permute-done.4.refs_2_ = bf16[32,64,128]{2,1,0:T(8,128)(2,1)} collective-permute-done((bf16[32,64,128]{2,1,0:T(8,128)(2,1)}, bf16[32,64,128]{2,1,0:T(8,128)(2,1)}, u32[]{:S(2)}, u32[]{:S(2)}) %collective-permute-start.4) | collective-permute-done | bytes 524320 | tf_op jit(solution)/shard_map/ppermute | solution.py:548
  60.6 1.4 %collective-permute-start.10 = (bf16[32,64,128]{2,1,0:T(8,128)(2,1)}, bf16[32,64,128]{2,1,0:T(8,128)(2,1)}, u32[]{:S(2)}, u32[]{:S(2)}) collective-permute-start(bf16[32,64,128]{2,1,0:T(8,128)(2,1)} %collective-permute-done.4.refs_2_), channel_id=1, source_target_pairs={{0,1},{1,0},{2,3},{3,2},{4,5},{5,4},{6,7},{7,6},{8,9},{9,8},{10,11... | collective-permute-start | bytes 1572872 | tf_op jit(solution)/shard_map/ppermute | solution.py:549
  62.0 9.8 %collective-permute-done.14.refs_0_ = bf16[32,64,128]{2,1,0:T(8,128)(2,1)} collective-permute-done((bf16[32,64,128]{2,1,0:T(8,128)(2,1)}, bf16[32,64,128]{2,1,0:T(8,128)(2,1)}, u32[]{:S(2)}, u32[]{:S(2)}) %collective-permute-start.14) | collective-permute-done | bytes 524320 | tf_op jit(solution)/shard_map/ppermute | solution.py:548
  71.8 1.4 %collective-permute-start.17 = (bf16[32,64,128]{2,1,0:T(8,128)(2,1)}, bf16[32,64,128]{2,1,0:T(8,128)(2,1)}, u32[]{:S(2)}, u32[]{:S(2)}) collective-permute-start(bf16[32,64,128]{2,1,0:T(8,128)(2,1)} %collective-permute-done.14.refs_0_), channel_id=1, source_target_pairs={{0,1},{1,0},{2,3},{3,2},{4,5},{5,4},{6,7},{7,6},{8,9},{9,8},{10,11... | collective-permute-start | bytes 1572872 | tf_op jit(solution)/shard_map/ppermute | solution.py:549
  73.2 5.1 %shard_map.66.refs_2_ = f32[32,80,128]{2,1,0:T(8,128)} custom-call(s32[2]{0:T(128)} %pad_add_fusion.refs_0_.place_ref, s32[2,8]{1,0:T(2,128)} %bitcast.13, bf16[64,64,128]{2,1,0:T(8,128)(2,1)} %shard_map.60.left_ref, bf16[32,64,128]{2,1,0:T(8,128)(2,1)} %shard_map.65.refs_0_, bf16[32,64,128]{2,1,0:T(8,128)(2,1)} %collective-permute-done.18.refs_1_, ...), custom_call_target="tpu_custom_call" | custom-call | flops 6000000000 | bytes 18000000 | tf_op jit(solution)/shard_map/pallas_call | solution.py:435
  78.4 4.7 %collective-permute-done.5.refs_0_ = bf16[32,64,128]{2,1,0:T(8,128)(2,1)} collective-permute-done((bf16[32,64,128]{2,1,0:T(8,128)(2,1)}, bf16[32,64,128]{2,1,0:T(8,128)(2,1)}, u32[]{:S(2)}, u32[]{:S(2)}) %collective-permute-start.5) | collective-permute-done | bytes 524320 | tf_op jit(solution)/shard_map/ppermute | solution.py:548
  83.0 1.4 %collective-permute-start.8 = (bf16[32,64,128]{2,1,0:T(8,128)(2,1)}, bf16[32,64,128]{2,1,0:T(8,128)(2,1)}, u32[]{:S(2)}, u32[]{:S(2)}) collective-permute-start(bf16[32,64,128]{2,1,0:T(8,128)(2,1)} %collective-permute-done.5.refs_0_), channel_id=1, source_target_pairs={{0,1},{1,0},{2,3},{3,2},{4,5},{5,4},{6,7},{7,6},{8,9},{9,8},{10,11... | collective-permute-start | bytes 1572872 | tf_op jit(solution)/shard_map/ppermute | solution.py:549
  84.5 0.0 collective-permute-done.9.refs_1_
  84.5 0.0 collective-permute-start.6
  84.5 0.0 collective-permute-done.10.refs_3_
  84.5 5.1 %shard_map.62.refs_2_ = f32[32,80,128]{2,1,0:T(8,128)} custom-call(s32[2]{0:T(128)} %pad_add_fusion.refs_0_.place_ref, s32[2,8]{1,0:T(2,128)} %bitcast.14, bf16[64,64,128]{2,1,0:T(8,128)(2,1)} %shard_map.60.left_ref, bf16[32,64,128]{2,1,0:T(8,128)(2,1)} %shard_map.61.refs_0_, bf16[32,64,128]{2,1,0:T(8,128)(2,1)} %collective-permute-done.9.refs_1_, ...), custom_call_target="tpu_custom_call" | custom-call | flops 6000000000 | bytes 18000000 | tf_op jit(solution)/shard_map/pallas_call | solution.py:435
  89.6 4.7 %collective-permute-done.15.mine_ref = bf16[32,64,128]{2,1,0:T(8,128)(2,1)} collective-permute-done((bf16[32,64,128]{2,1,0:T(8,128)(2,1)}, bf16[32,64,128]{2,1,0:T(8,128)(2,1)}, u32[]{:S(2)}, u32[]{:S(2)}) %collective-permute-start.15) | collective-permute-done | bytes 524320 | tf_op jit(solution)/shard_map/ppermute | solution.py:548
  94.3 1.4 %collective-permute-start.16 = (bf16[32,64,128]{2,1,0:T(8,128)(2,1)}, bf16[32,64,128]{2,1,0:T(8,128)(2,1)}, u32[]{:S(2)}, u32[]{:S(2)}) collective-permute-start(bf16[32,64,128]{2,1,0:T(8,128)(2,1)} %collective-permute-done.15.mine_ref), channel_id=1, source_target_pairs={{0,1},{1,0},{2,3},{3,2},{4,5},{5,4},{6,7},{7,6},{8,9},{9,8},{10,11... | collective-permute-start | bytes 1572872 | tf_op jit(solution)/shard_map/ppermute | solution.py:549
  95.7 0.0 collective-permute-done.17.refs_1_
  95.7 3.8 %shard_map.67.acc_in_ref = f32[32,80,128]{2,1,0:T(8,128)} custom-call(s32[2]{0:T(128)} %pad_add_fusion.refs_0_.place_ref, s32[2,8]{1,0:T(2,128)} %bitcast.15, bf16[64,64,128]{2,1,0:T(8,128)(2,1)} %shard_map.60.left_ref, bf16[32,64,128]{2,1,0:T(8,128)(2,1)} %collective-permute-done.14.refs_0_, ...), custom_call_target="tpu_custom_call", output_to_operand_aliasing={{}: (5, {})} | custom-call | flops 6000000000 | bytes 18000000 | tf_op jit(solution)/shard_map/pallas_call | solution.py:435
  99.5 6.0 %collective-permute-done.6.mine_ref = bf16[32,64,128]{2,1,0:T(8,128)(2,1)} collective-permute-done((bf16[32,64,128]{2,1,0:T(8,128)(2,1)}, bf16[32,64,128]{2,1,0:T(8,128)(2,1)}, u32[]{:S(2)}, u32[]{:S(2)}) %collective-permute-start.6) | collective-permute-done | bytes 524320 | tf_op jit(solution)/shard_map/ppermute | solution.py:548
  105.5 0.9 collective-permute-start.7
  106.4 3.8 %shard_map.63.acc_in_ref = f32[32,80,128]{2,1,0:T(8,128)} custom-call(s32[2]{0:T(128)} %pad_add_fusion.refs_0_.place_ref, s32[2,8]{1,0:T(2,128)} %bitcast.16, bf16[64,64,128]{2,1,0:T(8,128)(2,1)} %shard_map.60.left_ref, bf16[32,64,128]{2,1,0:T(8,128)(2,1)} %collective-permute-done.5.refs_0_, ...), custom_call_target="tpu_custom_call", output_to_operand_aliasing={{}: (5, {})} | custom-call | flops 6000000000 | bytes 18000000 | tf_op jit(solution)/shard_map/pallas_call | solution.py:435
  110.3 0.0 collective-permute-done.16.theirs_ref
  110.3 3.8 %shard_map.68 = (bf16[64,64,128]{2,1,0:T(8,128)(2,1)}, f32[64,128]{1,0:T(8,128)}) custom-call(s32[2]{0:T(128)} %pad_add_fusion.refs_0_.place_ref, s32[2,8]{1,0:T(2,128)} %bitcast.17, bf16[64,64,128]{2,1,0:T(8,128)(2,1)} %shard_map.60.left_ref, bf16[32,64,128]{2,1,0:T(8,128)(2,1)} %collective-permute-done.15.mine_ref, ...), custom_call_target="tpu_custom_call" | custom-call | flops 4000000000 | bytes 12000000 | tf_op jit(solution)/shard_map/pallas_call | solution.py:464
  114.1 3.8 %shard_map.69 = (bf16[64,64,128]{2,1,0:T(8,128)(2,1)}, f32[64,128]{1,0:T(8,128)}) custom-call(s32[2]{0:T(128)} %pad_add_fusion.refs_0_.place_ref, s32[2,8]{1,0:T(2,128)} %bitcast.18, bf16[64,64,128]{2,1,0:T(8,128)(2,1)} %shard_map.60.left_ref, bf16[32,64,128]{2,1,0:T(8,128)(2,1)} %collective-permute-done.6.mine_ref, ...), custom_call_target="tpu_custom_call", output_to_operand_aliasing={{0}: (6, {}), {1}: (7, {})} | custom-call | flops 4000000000 | bytes 12000000 | tf_op jit(solution)/shard_map/pallas_call | solution.py:464
  (8 shorter events, 0.0 us)
Async XLA Ops:
  3.6 1.3 %copy-start = (bf16[2,64,64,128]{3,1,2,0:T(8,128)(2,1)}, bf16[2,64,64,128]{3,1,2,0:T(8,128)(2,1)S(1)}, u32[]{:S(2)}) copy-start(bf16[2,64,64,128]{3,1,2,0:T(8,128)(2,1)S(1)} %copy.12) | copy-start | bytes 6291460
  5.7 9.8 %collective-permute-start.1 = (bf16[2,6,64,128]{3,2,1,0:T(8,128)(2,1)}, bf16[2,6,64,128]{3,2,1,0:T(8,128)(2,1)}, u32[]{:S(2)}, u32[]{:S(2)}) collective-permute-start(bf16[2,6,64,128]{3,2,1,0:T(8,128)(2,1)} %get-tuple-element.6), channel_id=1, source_target_pairs={{8,16},{24,0},{16,8},{0,24},{9,17},{25,1},{17,9},{1,25},{10,18},{2... | collective-permute-start | bytes 589832 | tf_op jit(solution)/shard_map/ppermute | solution.py:530
  8.7 9.1 %collective-permute-start = (bf16[2,6,64,128]{3,2,1,0:T(8,128)(2,1)}, bf16[2,6,64,128]{3,2,1,0:T(8,128)(2,1)}, u32[]{:S(2)}, u32[]{:S(2)}) collective-permute-start(bf16[2,6,64,128]{3,2,1,0:T(8,128)(2,1)} %get-tuple-element.7), channel_id=1, source_target_pairs={{0,8},{16,24},{8,0},{24,16},{1,9},{17,25},{9,1},{25,17},{2,10},{18... | collective-permute-start | bytes 589832 | tf_op jit(solution)/shard_map/ppermute | solution.py:529
  11.2 13.7 %collective-permute-start.12 = (bf16[9,64,128]{2,1,0:T(8,128)(2,1)}, bf16[9,64,128]{2,1,0:T(8,128)(2,1)}, u32[]{:S(2)}, u32[]{:S(2)}) collective-permute-start(bf16[9,64,128]{2,1,0:T(8,128)(2,1)} %shard_map.64.refs_1_), channel_id=1, source_target_pairs={{1,2},{3,4},{5,6},{7,0},{2,1},{4,3},{6,5},{0,7},{9,10},{11,12},{13... | collective-permute-start | bytes 442376 | tf_op jit(solution)/shard_map/ppermute | solution.py:516
  13.6 11.3 %collective-permute-start.11 = (bf16[9,64,128]{2,1,0:T(8,128)(2,1)}, bf16[9,64,128]{2,1,0:T(8,128)(2,1)}, u32[]{:S(2)}, u32[]{:S(2)}) collective-permute-start(bf16[9,64,128]{2,1,0:T(8,128)(2,1)} %shard_map.64.refs_1_), channel_id=1, source_target_pairs={{0,1},{1,0},{2,3},{3,2},{4,5},{5,4},{6,7},{7,6},{8,9},{9,8},{10,11... | collective-permute-start | bytes 442376 | tf_op jit(solution)/shard_map/ppermute | solution.py:517
  21.2 12.7 %collective-permute-start.3 = (bf16[27,64,128]{2,1,0:T(8,128)(2,1)}, bf16[27,64,128]{2,1,0:T(8,128)(2,1)}, u32[]{:S(2)}, u32[]{:S(2)}) collective-permute-start(bf16[27,64,128]{2,1,0:T(8,128)(2,1)} %shard_map.59.refs_3_), channel_id=1, source_target_pairs={{1,2},{3,4},{5,6},{7,0},{2,1},{4,3},{6,5},{0,7},{9,10},{11,12},{13... | collective-permute-start | bytes 1327112 | tf_op jit(solution)/shard_map/ppermute | solution.py:516
  23.9 10.0 %collective-permute-start.2 = (bf16[27,64,128]{2,1,0:T(8,128)(2,1)}, bf16[27,64,128]{2,1,0:T(8,128)(2,1)}, u32[]{:S(2)}, u32[]{:S(2)}) collective-permute-start(bf16[27,64,128]{2,1,0:T(8,128)(2,1)} %shard_map.59.refs_3_), channel_id=1, source_target_pairs={{0,1},{1,0},{2,3},{3,2},{4,5},{5,4},{6,7},{7,6},{8,9},{9,8},{10,11... | collective-permute-start | bytes 1327112 | tf_op jit(solution)/shard_map/ppermute | solution.py:517
  31.4 30.6 %collective-permute-start.18 = (bf16[32,64,128]{2,1,0:T(8,128)(2,1)}, bf16[32,64,128]{2,1,0:T(8,128)(2,1)}, u32[]{:S(2)}, u32[]{:S(2)}) collective-permute-start(bf16[32,64,128]{2,1,0:T(8,128)(2,1)} %shard_map.65.refs_0_), channel_id=1, source_target_pairs={{0,1},{1,0},{2,3},{3,2},{4,5},{5,4},{6,7},{7,6},{8,9},{9,8},{10,11... | collective-permute-start | bytes 1572872 | tf_op jit(solution)/shard_map/ppermute | solution.py:549
  31.4 16.4 %collective-permute-start.13 = (bf16[32,64,128]{2,1,0:T(8,128)(2,1)}, bf16[32,64,128]{2,1,0:T(8,128)(2,1)}, u32[]{:S(2)}, u32[]{:S(2)}) collective-permute-start(bf16[32,64,128]{2,1,0:T(8,128)(2,1)} %shard_map.65.refs_0_), channel_id=1, source_target_pairs={{0,2},{1,3},{2,4},{3,5},{4,6},{5,7},{6,0},{7,1},{8,10},{9,11},{10,... | collective-permute-start | bytes 1572872 | tf_op jit(solution)/shard_map/ppermute | solution.py:548
  42.0 42.5 %collective-permute-start.9 = (bf16[32,64,128]{2,1,0:T(8,128)(2,1)}, bf16[32,64,128]{2,1,0:T(8,128)(2,1)}, u32[]{:S(2)}, u32[]{:S(2)}) collective-permute-start(bf16[32,64,128]{2,1,0:T(8,128)(2,1)} %shard_map.61.refs_0_), channel_id=1, source_target_pairs={{0,1},{1,0},{2,3},{3,2},{4,5},{5,4},{6,7},{7,6},{8,9},{9,8},{10,11... | collective-permute-start | bytes 1572872 | tf_op jit(solution)/shard_map/ppermute | solution.py:549
  45.0 15.5 %collective-permute-start.4 = (bf16[32,64,128]{2,1,0:T(8,128)(2,1)}, bf16[32,64,128]{2,1,0:T(8,128)(2,1)}, u32[]{:S(2)}, u32[]{:S(2)}) collective-permute-start(bf16[32,64,128]{2,1,0:T(8,128)(2,1)} %shard_map.61.refs_0_), channel_id=1, source_target_pairs={{0,2},{1,3},{2,4},{3,5},{4,6},{5,7},{6,0},{7,1},{8,10},{9,11},{10,... | collective-permute-start | bytes 1572872 | tf_op jit(solution)/shard_map/ppermute | solution.py:548
  47.8 25.5 %collective-permute-start.19 = (bf16[32,64,128]{2,1,0:T(8,128)(2,1)}, bf16[32,64,128]{2,1,0:T(8,128)(2,1)}, u32[]{:S(2)}, u32[]{:S(2)}) collective-permute-start(bf16[32,64,128]{2,1,0:T(8,128)(2,1)} %collective-permute-done.13.refs_2_), channel_id=1, source_target_pairs={{0,1},{1,0},{2,3},{3,2},{4,5},{5,4},{6,7},{7,6},{8,9},{9,8},{10,11... | collective-permute-start | bytes 1572872 | tf_op jit(solution)/shard_map/ppermute | solution.py:549
  48.5 23.3 %collective-permute-start.14 = (bf16[32,64,128]{2,1,0:T(8,128)(2,1)}, bf16[32,64,128]{2,1,0:T(8,128)(2,1)}, u32[]{:S(2)}, u32[]{:S(2)}) collective-permute-start(bf16[32,64,128]{2,1,0:T(8,128)(2,1)} %collective-permute-done.13.refs_2_), channel_id=1, source_target_pairs={{0,2},{1,3},{2,4},{3,5},{4,6},{5,7},{6,0},{7,1},{8,10},{9,11},{10,... | collective-permute-start | bytes 1572872 | tf_op jit(solution)/shard_map/ppermute | solution.py:548
  60.6 23.9 %collective-permute-start.10 = (bf16[32,64,128]{2,1,0:T(8,128)(2,1)}, bf16[32,64,128]{2,1,0:T(8,128)(2,1)}, u32[]{:S(2)}, u32[]{:S(2)}) collective-permute-start(bf16[32,64,128]{2,1,0:T(8,128)(2,1)} %collective-permute-done.4.refs_2_), channel_id=1, source_target_pairs={{0,1},{1,0},{2,3},{3,2},{4,5},{5,4},{6,7},{7,6},{8,9},{9,8},{10,11... | collective-permute-start | bytes 1572872 | tf_op jit(solution)/shard_map/ppermute | solution.py:549
  62.0 21.0 %collective-permute-start.5 = (bf16[32,64,128]{2,1,0:T(8,128)(2,1)}, bf16[32,64,128]{2,1,0:T(8,128)(2,1)}, u32[]{:S(2)}, u32[]{:S(2)}) collective-permute-start(bf16[32,64,128]{2,1,0:T(8,128)(2,1)} %collective-permute-done.4.refs_2_), channel_id=1, source_target_pairs={{0,2},{1,3},{2,4},{3,5},{4,6},{5,7},{6,0},{7,1},{8,10},{9,11},{10,... | collective-permute-start | bytes 1572872 | tf_op jit(solution)/shard_map/ppermute | solution.py:548
  71.8 23.9 %collective-permute-start.17 = (bf16[32,64,128]{2,1,0:T(8,128)(2,1)}, bf16[32,64,128]{2,1,0:T(8,128)(2,1)}, u32[]{:S(2)}, u32[]{:S(2)}) collective-permute-start(bf16[32,64,128]{2,1,0:T(8,128)(2,1)} %collective-permute-done.14.refs_0_), channel_id=1, source_target_pairs={{0,1},{1,0},{2,3},{3,2},{4,5},{5,4},{6,7},{7,6},{8,9},{9,8},{10,11... | collective-permute-start | bytes 1572872 | tf_op jit(solution)/shard_map/ppermute | solution.py:549
  73.2 21.0 %collective-permute-start.15 = (bf16[32,64,128]{2,1,0:T(8,128)(2,1)}, bf16[32,64,128]{2,1,0:T(8,128)(2,1)}, u32[]{:S(2)}, u32[]{:S(2)}) collective-permute-start(bf16[32,64,128]{2,1,0:T(8,128)(2,1)} %collective-permute-done.14.refs_0_), channel_id=1, source_target_pairs={{0,2},{1,3},{2,4},{3,5},{4,6},{5,7},{6,0},{7,1},{8,10},{9,11},{10,... | collective-permute-start | bytes 1572872 | tf_op jit(solution)/shard_map/ppermute | solution.py:548
  83.0 23.4 %collective-permute-start.8 = (bf16[32,64,128]{2,1,0:T(8,128)(2,1)}, bf16[32,64,128]{2,1,0:T(8,128)(2,1)}, u32[]{:S(2)}, u32[]{:S(2)}) collective-permute-start(bf16[32,64,128]{2,1,0:T(8,128)(2,1)} %collective-permute-done.5.refs_0_), channel_id=1, source_target_pairs={{0,1},{1,0},{2,3},{3,2},{4,5},{5,4},{6,7},{7,6},{8,9},{9,8},{10,11... | collective-permute-start | bytes 1572872 | tf_op jit(solution)/shard_map/ppermute | solution.py:549
  84.5 21.0 %collective-permute-start.6 = (bf16[32,64,128]{2,1,0:T(8,128)(2,1)}, bf16[32,64,128]{2,1,0:T(8,128)(2,1)}, u32[]{:S(2)}, u32[]{:S(2)}) collective-permute-start(bf16[32,64,128]{2,1,0:T(8,128)(2,1)} %collective-permute-done.5.refs_0_), channel_id=1, source_target_pairs={{0,2},{1,3},{2,4},{3,5},{4,6},{5,7},{6,0},{7,1},{8,10},{9,11},{10,... | collective-permute-start | bytes 1572872 | tf_op jit(solution)/shard_map/ppermute | solution.py:548
  94.3 16.0 %collective-permute-start.16 = (bf16[32,64,128]{2,1,0:T(8,128)(2,1)}, bf16[32,64,128]{2,1,0:T(8,128)(2,1)}, u32[]{:S(2)}, u32[]{:S(2)}) collective-permute-start(bf16[32,64,128]{2,1,0:T(8,128)(2,1)} %collective-permute-done.15.mine_ref), channel_id=1, source_target_pairs={{0,1},{1,0},{2,3},{3,2},{4,5},{5,4},{6,7},{7,6},{8,9},{9,8},{10,11... | collective-permute-start | bytes 1572872 | tf_op jit(solution)/shard_map/ppermute | solution.py:549
  105.5 8.6 %collective-permute-start.7 = (bf16[32,64,128]{2,1,0:T(8,128)(2,1)}, bf16[32,64,128]{2,1,0:T(8,128)(2,1)}, u32[]{:S(2)}, u32[]{:S(2)}) collective-permute-start(bf16[32,64,128]{2,1,0:T(8,128)(2,1)} %collective-permute-done.6.mine_ref), channel_id=1, source_target_pairs={{0,1},{1,0},{2,3},{3,2},{4,5},{5,4},{6,7},{7,6},{8,9},{9,8},{10,11... | collective-permute-start | bytes 1572872 | tf_op jit(solution)/shard_map/ppermute | solution.py:549

commit v10 on v9

--- a/solution.py
+++ b/solution.py
@@ -506,14 +506,15 @@
     ranges = search_ranges.reshape(2, rows // RG)
 
     swap = [(i, i ^ 1) for i in range(col_count)]
-    across = both_ways([(i, (i + 1) % col_count) for i in range(1, col_count, 2)])
+    across = both_ways([(i, i + 1) for i in range(1, col_count - 1, 2)])
+    around_across = across + both_ways([(0, col_count - 1)])
     hop = [(i, (i + 2) % col_count) for i in range(col_count)]
     near_pairs = both_ways([(i, i + 1) for i in range(0, row_count, 2)])
     far_pairs = both_ways([(i, (i + 1) % row_count) for i in range(1, row_count, 2)])
 
-    def exchanged(pieces, chunks):
+    def exchanged(pieces, chunks, pairs):
         own = pack_edges(place, pieces, chunks, row_count)
-        cross = lax.ppermute(own, "cols", across)
+        cross = lax.ppermute(own, "cols", pairs)
         partner = lax.ppermute(own, "cols", swap)
         return own, partner, cross
 
@@ -532,8 +533,9 @@
     strip = rows // 4
     inner = rows - 2 * strip
     around = (mid, near, far)
-    edges_a = exchanged((mid,), ((1, ((inner, strip),)),))
-    edges_r = exchanged(around, ((1, ((strip, 0), (strip, rows - strip))), (0, ((rows, 0),))))
+    edges_a = exchanged((mid,), ((1, ((inner, strip),)),), around_across)
+    chunks_r = (1, ((strip, 0), (strip, rows - strip))), (0, ((rows, 0),))
+    edges_r = exchanged(around, chunks_r, across)
     right_a = features((mid,), 1, 1, inner, strip - REACH, edges_a, 0)
     right_b = features(around, 1, 2, strip, 0, edges_r, 0)
     left = features(around, 0, 1, rows, 0, edges_r, 2 * edge_steps(strip, segment)[1])

time: 119 us -> 118 us (level)
  waiting for transfers between devices: 34.1 us -> 32.2 us
    ppermute x2, starting transfers between devices: 5.13 us -> 7.03 us  [exchanged(): cross = lax.ppermute(own, 'cols', pairs)]
    ppermute x8, starting transfers between devices: 10.4 us -> 8.57 us  [chain(): pairs.append((mine, lax.ppermute(mine, 'cols', swap)))]
    ppermute x6, starting transfers between devices: 0.81 us -> 2.59 us  [chain(): mine = lax.ppermute(mine, 'cols', hop)]
    ppermute x2, waiting for transfers between devices: 1.74 us -> 0.01 us  [exchanged(): cross = lax.ppermute(own, 'cols', pairs)]
  transfers between devices with their start and end apart: 20 -> 20, of which waited for: 8 -> 6; matrix products, arithmetic and copies ran while one was open for 1% -> 1% of each run, Pallas kernels for 44% -> 44%
where the time goes in v10:
time: 118 us; the launch traced here: 117 us
  Pallas kernels  55.6 us (47%)
  waiting for transfers between devices  32.2 us (27%)
  starting transfers between devices  22.8 us (19%)
  local copies, waits for them, and re-layouts  4.27 us (4%)
  other arithmetic  1.38 us (1%)
    ppermute x6, waiting for transfers between devices, chain(): mine = lax.ppermute(mine, 'cols', hop)  29.9 us
    pallas_call x3, Pallas kernels, unit_features(): pl.pallas_call(functools.partial(feature_kernel, spacing=spacing, offset=...  24.4 us
    pallas_call x4, Pallas kernels, correlate(): pl.pallas_call(functools.partial(gather_kernel, inner=inner, groups=group...  18 us
    ppermute x8, starting transfers between devices, chain(): pairs.append((mine, lax.ppermute(mine, 'cols', swap)))  8.57 us
    pallas_call x2, Pallas kernels, finish(): pl.pallas_call(functools.partial(finish_kernel, inner=inner, groups=group...  7.58 us
    ppermute x2, starting transfers between devices, exchanged(): cross = lax.ppermute(own, 'cols', pairs)  7.03 us
    pallas_call x2, Pallas kernels, pack_edges(): pl.pallas_call(functools.partial(pack_kernel, images=tuple((chunks for _,...  5.65 us
    unnamed x3, local copies, waits for them, and re-layouts  4.27 us
  transfers between devices with their start and end apart: 20, of which 6 were waited for; matrix products, arithmetic and copies ran while one was open for 1% of the time, Pallas kernels for 44%

profile of v10, /device:TPU:1, one launch (start us, length us, event | category | flops | bytes accessed | tf_op | source)
XLA Modules:
  0.0 116.9 jit_solution(12536424628184768748)
XLA Ops:
  0.6 2.9 %copy.12 = bf16[2,64,64,128]{3,1,2,0:T(8,128)(2,1)S(1)} copy(bf16[2,64,64,128]{3,2,1,0:T(8,128)(2,1)} %param.4) | data formatting | bytes 4194304 | tf_op args[0]
  3.6 1.3 %copy-done = bf16[2,64,64,128]{3,1,2,0:T(8,128)(2,1)} copy-done((bf16[2,64,64,128]{3,1,2,0:T(8,128)(2,1)}, bf16[2,64,64,128]{3,1,2,0:T(8,128)(2,1)S(1)}, u32[]{:S(2)}) %copy-start) | copy-done | bytes 2097176
  4.9 0.8 broadcast_select_fusion
  5.7 3.0 %collective-permute-start.1 = (bf16[2,6,64,128]{3,2,1,0:T(8,128)(2,1)}, bf16[2,6,64,128]{3,2,1,0:T(8,128)(2,1)}, u32[]{:S(2)}, u32[]{:S(2)}) collective-permute-start(bf16[2,6,64,128]{3,2,1,0:T(8,128)(2,1)} %get-tuple-element.6), channel_id=1, source_target_pairs={{8,16},{24,0},{16,8},{0,24},{9,17},{25,1},{17,9},{1,25},{10,18},{2... | collective-permute-start | bytes 589832 | tf_op jit(solution)/shard_map/ppermute | solution.py:531
  8.7 0.3 collective-permute-start
  8.9 2.2 %shard_map.64.refs_1_ = bf16[9,64,128]{2,1,0:T(8,128)(2,1)} custom-call(bf16[2,64,64,128]{3,2,1,0:T(8,128)(2,1)} %bitcast.7), custom_call_target="tpu_custom_call" | custom-call | flops 2000000000 | bytes 6000000 | tf_op jit(solution)/shard_map/pallas_call | solution.py:101
  11.2 2.4 %collective-permute-start.12 = (bf16[9,64,128]{2,1,0:T(8,128)(2,1)}, bf16[9,64,128]{2,1,0:T(8,128)(2,1)}, u32[]{:S(2)}, u32[]{:S(2)}) collective-permute-start(bf16[9,64,128]{2,1,0:T(8,128)(2,1)} %shard_map.64.refs_1_), channel_id=1, source_target_pairs={{1,2},{3,4},{5,6},{2,1},{4,3},{6,5},{0,7},{7,0},{9,10},{11,12},{13... | collective-permute-start | bytes 442376 | tf_op jit(solution)/shard_map/ppermute | solution.py:517
  13.6 1.3 %collective-permute-start.11 = (bf16[9,64,128]{2,1,0:T(8,128)(2,1)}, bf16[9,64,128]{2,1,0:T(8,128)(2,1)}, u32[]{:S(2)}, u32[]{:S(2)}) collective-permute-start(bf16[9,64,128]{2,1,0:T(8,128)(2,1)} %shard_map.64.refs_1_), channel_id=1, source_target_pairs={{0,1},{1,0},{2,3},{3,2},{4,5},{5,4},{6,7},{7,6},{8,9},{9,8},{10,11... | collective-permute-start | bytes 442376 | tf_op jit(solution)/shard_map/ppermute | solution.py:518
  14.9 0.6 pad_add_fusion.refs_0_.place_ref
  15.5 2.3 %collective-permute-done.refs_2_.refs_5_.refs_1_ = bf16[2,6,64,128]{3,2,1,0:T(8,128)(2,1)} collective-permute-done((bf16[2,6,64,128]{3,2,1,0:T(8,128)(2,1)}, bf16[2,6,64,128]{3,2,1,0:T(8,128)(2,1)}, u32[]{:S(2)}, u32[]{:S(2)}) %collective-permute-start) | collective-permute-done | bytes 196640 | tf_op jit(solution)/shard_map/ppermute | solution.py:530
  17.8 3.4 %shard_map.59.refs_3_ = bf16[27,64,128]{2,1,0:T(8,128)(2,1)} custom-call(s32[2]{0:T(128)} %pad_add_fusion.refs_0_.place_ref, bf16[2,64,64,128]{3,2,1,0:T(8,128)(2,1)} %bitcast.8, bf16[2,6,64,128]{3,2,1,0:T(8,128)(2,1)} %collective-permute-done.refs_2_.refs_5_.refs_1_, bf16[2,6,64,128]{3,2,1,0:T(8,128)(2,1)} %collective-permute-done.1.refs_3_.refs_6_.refs_2_, ...), custom_call_target="tpu_custom_call" | custom-call | flops 2000000000 | bytes 6000000 | tf_op jit(solution)/shard_map/pallas_call | solution.py:101
  21.2 4.6 %collective-permute-start.3 = (bf16[27,64,128]{2,1,0:T(8,128)(2,1)}, bf16[27,64,128]{2,1,0:T(8,128)(2,1)}, u32[]{:S(2)}, u32[]{:S(2)}) collective-permute-start(bf16[27,64,128]{2,1,0:T(8,128)(2,1)} %shard_map.59.refs_3_), channel_id=1, source_target_pairs={{1,2},{3,4},{5,6},{2,1},{4,3},{6,5},{9,10},{11,12},{13,14},{10,9},... | collective-permute-start | bytes 1327112 | tf_op jit(solution)/shard_map/ppermute | solution.py:517
  25.8 0.1 collective-permute-start.2
  25.9 0.0 collective-permute-done.12.refs_3_
  25.9 0.0 collective-permute-done.11.refs_2_
  25.9 6.5 %shard_map.65.refs_0_ = bf16[32,64,128]{2,1,0:T(8,128)(2,1)} custom-call(s32[2]{0:T(128)} %pad_add_fusion.refs_0_.place_ref, bf16[2,64,64,128]{3,2,1,0:T(8,128)(2,1)} %bitcast.10, bf16[9,64,128]{2,1,0:T(8,128)(2,1)} %shard_map.64.refs_1_, bf16[9,64,128]{2,1,0:T(8,128)(2,1)} %collective-permute-done.11.refs_2_, ...), custom_call_target="tpu_custom_call" | custom-call | flops 6400000000 | bytes 19200000 | tf_op jit(solution)/shard_map/pallas_call | solution.py:301
  32.4 0.5 collective-permute-start.18
  32.8 1.3 %collective-permute-start.13 = (bf16[32,64,128]{2,1,0:T(8,128)(2,1)}, bf16[32,64,128]{2,1,0:T(8,128)(2,1)}, u32[]{:S(2)}, u32[]{:S(2)}) collective-permute-start(bf16[32,64,128]{2,1,0:T(8,128)(2,1)} %shard_map.65.refs_0_), channel_id=1, source_target_pairs={{0,2},{1,3},{2,4},{3,5},{4,6},{5,7},{6,0},{7,1},{8,10},{9,11},{10,... | collective-permute-start | bytes 1572872 | tf_op jit(solution)/shard_map/ppermute | solution.py:550
  34.1 0.0 collective-permute-done.3.refs_5_
  34.1 0.0 collective-permute-done.2.refs_4_
  34.1 8.1 %shard_map.61.refs_0_ = bf16[32,64,128]{2,1,0:T(8,128)(2,1)} custom-call(s32[2]{0:T(128)} %pad_add_fusion.refs_0_.place_ref, bf16[2,64,64,128]{3,2,1,0:T(8,128)(2,1)} %bitcast.11, bf16[2,6,64,128]{3,2,1,0:T(8,128)(2,1)} %collective-permute-done.refs_2_.refs_5_.refs_1_, bf16[2,6,64,128]{3,2,1,0:T(8,128)(2,1)} %collective-permute-done.1.refs_3_.refs_6_.refs_2_, ...), custom_call_target="tpu_custom_call" | custom-call | flops 6400000000 | bytes 19200000 | tf_op jit(solution)/shard_map/pallas_call | solution.py:301
  42.2 0.3 collective-permute-start.9
  42.6 1.3 %collective-permute-start.4 = (bf16[32,64,128]{2,1,0:T(8,128)(2,1)}, bf16[32,64,128]{2,1,0:T(8,128)(2,1)}, u32[]{:S(2)}, u32[]{:S(2)}) collective-permute-start(bf16[32,64,128]{2,1,0:T(8,128)(2,1)} %shard_map.61.refs_0_), channel_id=1, source_target_pairs={{0,2},{1,3},{2,4},{3,5},{4,6},{5,7},{6,0},{7,1},{8,10},{9,11},{10,... | collective-permute-start | bytes 1572872 | tf_op jit(solution)/shard_map/ppermute | solution.py:550
  43.8 4.6 %collective-permute-done.13.refs_2_ = bf16[32,64,128]{2,1,0:T(8,128)(2,1)} collective-permute-done((bf16[32,64,128]{2,1,0:T(8,128)(2,1)}, bf16[32,64,128]{2,1,0:T(8,128)(2,1)}, u32[]{:S(2)}, u32[]{:S(2)}) %collective-permute-start.13) | collective-permute-done | bytes 524320 | tf_op jit(solution)/shard_map/ppermute | solution.py:550
  48.4 1.4 %collective-permute-start.19 = (bf16[32,64,128]{2,1,0:T(8,128)(2,1)}, bf16[32,64,128]{2,1,0:T(8,128)(2,1)}, u32[]{:S(2)}, u32[]{:S(2)}) collective-permute-start(bf16[32,64,128]{2,1,0:T(8,128)(2,1)} %collective-permute-done.13.refs_2_), channel_id=1, source_target_pairs={{0,1},{1,0},{2,3},{3,2},{4,5},{5,4},{6,7},{7,6},{8,9},{9,8},{10,11... | collective-permute-start | bytes 1572872 | tf_op jit(solution)/shard_map/ppermute | solution.py:551
  49.8 0.0 collective-permute-start.14
  49.8 9.8 %shard_map.60.left_ref = bf16[64,64,128]{2,1,0:T(8,128)(2,1)} custom-call(s32[2]{0:T(128)} %pad_add_fusion.refs_0_.place_ref, bf16[2,64,64,128]{3,2,1,0:T(8,128)(2,1)} %bitcast.12, bf16[2,6,64,128]{3,2,1,0:T(8,128)(2,1)} %collective-permute-done.refs_2_.refs_5_.refs_1_, bf16[2,6,64,128]{3,2,1,0:T(8,128)(2,1)} %collective-permute-done.1.refs_3_.refs_6_.refs_2_, ...), custom_call_target="tpu_custom_call" | custom-call | flops 12800000000 | bytes 38400000 | tf_op jit(solution)/shard_map/pallas_call | solution.py:301
  59.6 0.0 collective-permute-done.4.refs_2_
  59.6 1.4 %collective-permute-start.10 = (bf16[32,64,128]{2,1,0:T(8,128)(2,1)}, bf16[32,64,128]{2,1,0:T(8,128)(2,1)}, u32[]{:S(2)}, u32[]{:S(2)}) collective-permute-start(bf16[32,64,128]{2,1,0:T(8,128)(2,1)} %collective-permute-done.4.refs_2_), channel_id=1, source_target_pairs={{0,1},{1,0},{2,3},{3,2},{4,5},{5,4},{6,7},{7,6},{8,9},{9,8},{10,11... | collective-permute-start | bytes 1572872 | tf_op jit(solution)/shard_map/ppermute | solution.py:551
  61.0 9.9 %collective-permute-done.14.refs_0_ = bf16[32,64,128]{2,1,0:T(8,128)(2,1)} collective-permute-done((bf16[32,64,128]{2,1,0:T(8,128)(2,1)}, bf16[32,64,128]{2,1,0:T(8,128)(2,1)}, u32[]{:S(2)}, u32[]{:S(2)}) %collective-permute-start.14) | collective-permute-done | bytes 524320 | tf_op jit(solution)/shard_map/ppermute | solution.py:550
  70.9 1.4 %collective-permute-start.17 = (bf16[32,64,128]{2,1,0:T(8,128)(2,1)}, bf16[32,64,128]{2,1,0:T(8,128)(2,1)}, u32[]{:S(2)}, u32[]{:S(2)}) collective-permute-start(bf16[32,64,128]{2,1,0:T(8,128)(2,1)} %collective-permute-done.14.refs_0_), channel_id=1, source_target_pairs={{0,1},{1,0},{2,3},{3,2},{4,5},{5,4},{6,7},{7,6},{8,9},{9,8},{10,11... | collective-permute-start | bytes 1572872 | tf_op jit(solution)/shard_map/ppermute | solution.py:551
  72.3 0.0 collective-permute-done.19.refs_3_
  72.3 5.1 %shard_map.66.refs_2_ = f32[32,80,128]{2,1,0:T(8,128)} custom-call(s32[2]{0:T(128)} %pad_add_fusion.refs_0_.place_ref, s32[2,8]{1,0:T(2,128)} %bitcast.13, bf16[64,64,128]{2,1,0:T(8,128)(2,1)} %shard_map.60.left_ref, bf16[32,64,128]{2,1,0:T(8,128)(2,1)} %shard_map.65.refs_0_, bf16[32,64,128]{2,1,0:T(8,128)(2,1)} %collective-permute-done.18.refs_1_, ...), custom_call_target="tpu_custom_call" | custom-call | flops 6000000000 | bytes 18000000 | tf_op jit(solution)/shard_map/pallas_call | solution.py:435
  77.4 4.7 %collective-permute-done.5.refs_0_ = bf16[32,64,128]{2,1,0:T(8,128)(2,1)} collective-permute-done((bf16[32,64,128]{2,1,0:T(8,128)(2,1)}, bf16[32,64,128]{2,1,0:T(8,128)(2,1)}, u32[]{:S(2)}, u32[]{:S(2)}) %collective-permute-start.5) | collective-permute-done | bytes 524320 | tf_op jit(solution)/shard_map/ppermute | solution.py:550
  82.1 1.4 %collective-permute-start.8 = (bf16[32,64,128]{2,1,0:T(8,128)(2,1)}, bf16[32,64,128]{2,1,0:T(8,128)(2,1)}, u32[]{:S(2)}, u32[]{:S(2)}) collective-permute-start(bf16[32,64,128]{2,1,0:T(8,128)(2,1)} %collective-permute-done.5.refs_0_), channel_id=1, source_target_pairs={{0,1},{1,0},{2,3},{3,2},{4,5},{5,4},{6,7},{7,6},{8,9},{9,8},{10,11... | collective-permute-start | bytes 1572872 | tf_op jit(solution)/shard_map/ppermute | solution.py:551
  83.5 0.0 collective-permute-done.9.refs_1_
  83.5 0.0 collective-permute-start.6
  83.5 0.0 collective-permute-done.10.refs_3_
  83.5 5.1 %shard_map.62.refs_2_ = f32[32,80,128]{2,1,0:T(8,128)} custom-call(s32[2]{0:T(128)} %pad_add_fusion.refs_0_.place_ref, s32[2,8]{1,0:T(2,128)} %bitcast.14, bf16[64,64,128]{2,1,0:T(8,128)(2,1)} %shard_map.60.left_ref, bf16[32,64,128]{2,1,0:T(8,128)(2,1)} %shard_map.61.refs_0_, bf16[32,64,128]{2,1,0:T(8,128)(2,1)} %collective-permute-done.9.refs_1_, ...), custom_call_target="tpu_custom_call" | custom-call | flops 6000000000 | bytes 18000000 | tf_op jit(solution)/shard_map/pallas_call | solution.py:435
  88.6 4.7 %collective-permute-done.15.mine_ref = bf16[32,64,128]{2,1,0:T(8,128)(2,1)} collective-permute-done((bf16[32,64,128]{2,1,0:T(8,128)(2,1)}, bf16[32,64,128]{2,1,0:T(8,128)(2,1)}, u32[]{:S(2)}, u32[]{:S(2)}) %collective-permute-start.15) | collective-permute-done | bytes 524320 | tf_op jit(solution)/shard_map/ppermute | solution.py:550
  93.3 1.4 %collective-permute-start.16 = (bf16[32,64,128]{2,1,0:T(8,128)(2,1)}, bf16[32,64,128]{2,1,0:T(8,128)(2,1)}, u32[]{:S(2)}, u32[]{:S(2)}) collective-permute-start(bf16[32,64,128]{2,1,0:T(8,128)(2,1)} %collective-permute-done.15.mine_ref), channel_id=1, source_target_pairs={{0,1},{1,0},{2,3},{3,2},{4,5},{5,4},{6,7},{7,6},{8,9},{9,8},{10,11... | collective-permute-start | bytes 1572872 | tf_op jit(solution)/shard_map/ppermute | solution.py:551
  94.7 0.0 collective-permute-done.17.refs_1_
  94.7 3.8 %shard_map.67.acc_in_ref = f32[32,80,128]{2,1,0:T(8,128)} custom-call(s32[2]{0:T(128)} %pad_add_fusion.refs_0_.place_ref, s32[2,8]{1,0:T(2,128)} %bitcast.15, bf16[64,64,128]{2,1,0:T(8,128)(2,1)} %shard_map.60.left_ref, bf16[32,64,128]{2,1,0:T(8,128)(2,1)} %collective-permute-done.14.refs_0_, ...), custom_call_target="tpu_custom_call", output_to_operand_aliasing={{}: (5, {})} | custom-call | flops 6000000000 | bytes 18000000 | tf_op jit(solution)/shard_map/pallas_call | solution.py:435
  98.6 6.0 %collective-permute-done.6.mine_ref = bf16[32,64,128]{2,1,0:T(8,128)(2,1)} collective-permute-done((bf16[32,64,128]{2,1,0:T(8,128)(2,1)}, bf16[32,64,128]{2,1,0:T(8,128)(2,1)}, u32[]{:S(2)}, u32[]{:S(2)}) %collective-permute-start.6) | collective-permute-done | bytes 524320 | tf_op jit(solution)/shard_map/ppermute | solution.py:550
  104.6 0.9 collective-permute-start.7
  105.5 3.8 %shard_map.63.acc_in_ref = f32[32,80,128]{2,1,0:T(8,128)} custom-call(s32[2]{0:T(128)} %pad_add_fusion.refs_0_.place_ref, s32[2,8]{1,0:T(2,128)} %bitcast.16, bf16[64,64,128]{2,1,0:T(8,128)(2,1)} %shard_map.60.left_ref, bf16[32,64,128]{2,1,0:T(8,128)(2,1)} %collective-permute-done.5.refs_0_, ...), custom_call_target="tpu_custom_call", output_to_operand_aliasing={{}: (5, {})} | custom-call | flops 6000000000 | bytes 18000000 | tf_op jit(solution)/shard_map/pallas_call | solution.py:435
  109.3 3.8 %shard_map.68 = (bf16[64,64,128]{2,1,0:T(8,128)(2,1)}, f32[64,128]{1,0:T(8,128)}) custom-call(s32[2]{0:T(128)} %pad_add_fusion.refs_0_.place_ref, s32[2,8]{1,0:T(2,128)} %bitcast.17, bf16[64,64,128]{2,1,0:T(8,128)(2,1)} %shard_map.60.left_ref, bf16[32,64,128]{2,1,0:T(8,128)(2,1)} %collective-permute-done.15.mine_ref, ...), custom_call_target="tpu_custom_call" | custom-call | flops 4000000000 | bytes 12000000 | tf_op jit(solution)/shard_map/pallas_call | solution.py:464
  113.1 3.8 %shard_map.69 = (bf16[64,64,128]{2,1,0:T(8,128)(2,1)}, f32[64,128]{1,0:T(8,128)}) custom-call(s32[2]{0:T(128)} %pad_add_fusion.refs_0_.place_ref, s32[2,8]{1,0:T(2,128)} %bitcast.18, bf16[64,64,128]{2,1,0:T(8,128)(2,1)} %shard_map.60.left_ref, bf16[32,64,128]{2,1,0:T(8,128)(2,1)} %collective-permute-done.6.mine_ref, ...), custom_call_target="tpu_custom_call", output_to_operand_aliasing={{0}: (6, {}), {1}: (7, {})} | custom-call | flops 4000000000 | bytes 12000000 | tf_op jit(solution)/shard_map/pallas_call | solution.py:464
  (8 shorter events, 0.0 us)
Async XLA Ops:
  3.6 1.3 %copy-start = (bf16[2,64,64,128]{3,1,2,0:T(8,128)(2,1)}, bf16[2,64,64,128]{3,1,2,0:T(8,128)(2,1)S(1)}, u32[]{:S(2)}) copy-start(bf16[2,64,64,128]{3,1,2,0:T(8,128)(2,1)S(1)} %copy.12) | copy-start | bytes 6291460
  5.7 9.8 %collective-permute-start.1 = (bf16[2,6,64,128]{3,2,1,0:T(8,128)(2,1)}, bf16[2,6,64,128]{3,2,1,0:T(8,128)(2,1)}, u32[]{:S(2)}, u32[]{:S(2)}) collective-permute-start(bf16[2,6,64,128]{3,2,1,0:T(8,128)(2,1)} %get-tuple-element.6), channel_id=1, source_target_pairs={{8,16},{24,0},{16,8},{0,24},{9,17},{25,1},{17,9},{1,25},{10,18},{2... | collective-permute-start | bytes 589832 | tf_op jit(solution)/shard_map/ppermute | solution.py:531
  8.7 9.1 %collective-permute-start = (bf16[2,6,64,128]{3,2,1,0:T(8,128)(2,1)}, bf16[2,6,64,128]{3,2,1,0:T(8,128)(2,1)}, u32[]{:S(2)}, u32[]{:S(2)}) collective-permute-start(bf16[2,6,64,128]{3,2,1,0:T(8,128)(2,1)} %get-tuple-element.7), channel_id=1, source_target_pairs={{0,8},{16,24},{8,0},{24,16},{1,9},{17,25},{9,1},{25,17},{2,10},{18... | collective-permute-start | bytes 589832 | tf_op jit(solution)/shard_map/ppermute | solution.py:530
  11.2 14.7 %collective-permute-start.12 = (bf16[9,64,128]{2,1,0:T(8,128)(2,1)}, bf16[9,64,128]{2,1,0:T(8,128)(2,1)}, u32[]{:S(2)}, u32[]{:S(2)}) collective-permute-start(bf16[9,64,128]{2,1,0:T(8,128)(2,1)} %shard_map.64.refs_1_), channel_id=1, source_target_pairs={{1,2},{3,4},{5,6},{2,1},{4,3},{6,5},{0,7},{7,0},{9,10},{11,12},{13... | collective-permute-start | bytes 442376 | tf_op jit(solution)/shard_map/ppermute | solution.py:517
  13.6 12.3 %collective-permute-start.11 = (bf16[9,64,128]{2,1,0:T(8,128)(2,1)}, bf16[9,64,128]{2,1,0:T(8,128)(2,1)}, u32[]{:S(2)}, u32[]{:S(2)}) collective-permute-start(bf16[9,64,128]{2,1,0:T(8,128)(2,1)} %shard_map.64.refs_1_), channel_id=1, source_target_pairs={{0,1},{1,0},{2,3},{3,2},{4,5},{5,4},{6,7},{7,6},{8,9},{9,8},{10,11... | collective-permute-start | bytes 442376 | tf_op jit(solution)/shard_map/ppermute | solution.py:518
  21.2 13.0 %collective-permute-start.3 = (bf16[27,64,128]{2,1,0:T(8,128)(2,1)}, bf16[27,64,128]{2,1,0:T(8,128)(2,1)}, u32[]{:S(2)}, u32[]{:S(2)}) collective-permute-start(bf16[27,64,128]{2,1,0:T(8,128)(2,1)} %shard_map.59.refs_3_), channel_id=1, source_target_pairs={{1,2},{3,4},{5,6},{2,1},{4,3},{6,5},{9,10},{11,12},{13,14},{10,9},... | collective-permute-start | bytes 1327112 | tf_op jit(solution)/shard_map/ppermute | solution.py:517
  25.8 8.3 %collective-permute-start.2 = (bf16[27,64,128]{2,1,0:T(8,128)(2,1)}, bf16[27,64,128]{2,1,0:T(8,128)(2,1)}, u32[]{:S(2)}, u32[]{:S(2)}) collective-permute-start(bf16[27,64,128]{2,1,0:T(8,128)(2,1)} %shard_map.59.refs_3_), channel_id=1, source_target_pairs={{0,1},{1,0},{2,3},{3,2},{4,5},{5,4},{6,7},{7,6},{8,9},{9,8},{10,11... | collective-permute-start | bytes 1327112 | tf_op jit(solution)/shard_map/ppermute | solution.py:518
  32.4 28.7 %collective-permute-start.18 = (bf16[32,64,128]{2,1,0:T(8,128)(2,1)}, bf16[32,64,128]{2,1,0:T(8,128)(2,1)}, u32[]{:S(2)}, u32[]{:S(2)}) collective-permute-start(bf16[32,64,128]{2,1,0:T(8,128)(2,1)} %shard_map.65.refs_0_), channel_id=1, source_target_pairs={{0,1},{1,0},{2,3},{3,2},{4,5},{5,4},{6,7},{7,6},{8,9},{9,8},{10,11... | collective-permute-start | bytes 1572872 | tf_op jit(solution)/shard_map/ppermute | solution.py:551
  32.8 15.6 %collective-permute-start.13 = (bf16[32,64,128]{2,1,0:T(8,128)(2,1)}, bf16[32,64,128]{2,1,0:T(8,128)(2,1)}, u32[]{:S(2)}, u32[]{:S(2)}) collective-permute-start(bf16[32,64,128]{2,1,0:T(8,128)(2,1)} %shard_map.65.refs_0_), channel_id=1, source_target_pairs={{0,2},{1,3},{2,4},{3,5},{4,6},{5,7},{6,0},{7,1},{8,10},{9,11},{10,... | collective-permute-start | bytes 1572872 | tf_op jit(solution)/shard_map/ppermute | solution.py:550
  42.2 41.3 %collective-permute-start.9 = (bf16[32,64,128]{2,1,0:T(8,128)(2,1)}, bf16[32,64,128]{2,1,0:T(8,128)(2,1)}, u32[]{:S(2)}, u32[]{:S(2)}) collective-permute-start(bf16[32,64,128]{2,1,0:T(8,128)(2,1)} %shard_map.61.refs_0_), channel_id=1, source_target_pairs={{0,1},{1,0},{2,3},{3,2},{4,5},{5,4},{6,7},{7,6},{8,9},{9,8},{10,11... | collective-permute-start | bytes 1572872 | tf_op jit(solution)/shard_map/ppermute | solution.py:551
  42.6 17.1 %collective-permute-start.4 = (bf16[32,64,128]{2,1,0:T(8,128)(2,1)}, bf16[32,64,128]{2,1,0:T(8,128)(2,1)}, u32[]{:S(2)}, u32[]{:S(2)}) collective-permute-start(bf16[32,64,128]{2,1,0:T(8,128)(2,1)} %shard_map.61.refs_0_), channel_id=1, source_target_pairs={{0,2},{1,3},{2,4},{3,5},{4,6},{5,7},{6,0},{7,1},{8,10},{9,11},{10,... | collective-permute-start | bytes 1572872 | tf_op jit(solution)/shard_map/ppermute | solution.py:550
  48.4 23.9 %collective-permute-start.19 = (bf16[32,64,128]{2,1,0:T(8,128)(2,1)}, bf16[32,64,128]{2,1,0:T(8,128)(2,1)}, u32[]{:S(2)}, u32[]{:S(2)}) collective-permute-start(bf16[32,64,128]{2,1,0:T(8,128)(2,1)} %collective-permute-done.13.refs_2_), channel_id=1, source_target_pairs={{0,1},{1,0},{2,3},{3,2},{4,5},{5,4},{6,7},{7,6},{8,9},{9,8},{10,11... | collective-permute-start | bytes 1572872 | tf_op jit(solution)/shard_map/ppermute | solution.py:551
  49.8 21.1 %collective-permute-start.14 = (bf16[32,64,128]{2,1,0:T(8,128)(2,1)}, bf16[32,64,128]{2,1,0:T(8,128)(2,1)}, u32[]{:S(2)}, u32[]{:S(2)}) collective-permute-start(bf16[32,64,128]{2,1,0:T(8,128)(2,1)} %collective-permute-done.13.refs_2_), channel_id=1, source_target_pairs={{0,2},{1,3},{2,4},{3,5},{4,6},{5,7},{6,0},{7,1},{8,10},{9,11},{10,... | collective-permute-start | bytes 1572872 | tf_op jit(solution)/shard_map/ppermute | solution.py:550
  59.6 23.9 %collective-permute-start.10 = (bf16[32,64,128]{2,1,0:T(8,128)(2,1)}, bf16[32,64,128]{2,1,0:T(8,128)(2,1)}, u32[]{:S(2)}, u32[]{:S(2)}) collective-permute-start(bf16[32,64,128]{2,1,0:T(8,128)(2,1)} %collective-permute-done.4.refs_2_), channel_id=1, source_target_pairs={{0,1},{1,0},{2,3},{3,2},{4,5},{5,4},{6,7},{7,6},{8,9},{9,8},{10,11... | collective-permute-start | bytes 1572872 | tf_op jit(solution)/shard_map/ppermute | solution.py:551
  61.0 21.1 %collective-permute-start.5 = (bf16[32,64,128]{2,1,0:T(8,128)(2,1)}, bf16[32,64,128]{2,1,0:T(8,128)(2,1)}, u32[]{:S(2)}, u32[]{:S(2)}) collective-permute-start(bf16[32,64,128]{2,1,0:T(8,128)(2,1)} %collective-permute-done.4.refs_2_), channel_id=1, source_target_pairs={{0,2},{1,3},{2,4},{3,5},{4,6},{5,7},{6,0},{7,1},{8,10},{9,11},{10,... | collective-permute-start | bytes 1572872 | tf_op jit(solution)/shard_map/ppermute | solution.py:550
  70.9 23.9 %collective-permute-start.17 = (bf16[32,64,128]{2,1,0:T(8,128)(2,1)}, bf16[32,64,128]{2,1,0:T(8,128)(2,1)}, u32[]{:S(2)}, u32[]{:S(2)}) collective-permute-start(bf16[32,64,128]{2,1,0:T(8,128)(2,1)} %collective-permute-done.14.refs_0_), channel_id=1, source_target_pairs={{0,1},{1,0},{2,3},{3,2},{4,5},{5,4},{6,7},{7,6},{8,9},{9,8},{10,11... | collective-permute-start | bytes 1572872 | tf_op jit(solution)/shard_map/ppermute | solution.py:551
  72.3 21.1 %collective-permute-start.15 = (bf16[32,64,128]{2,1,0:T(8,128)(2,1)}, bf16[32,64,128]{2,1,0:T(8,128)(2,1)}, u32[]{:S(2)}, u32[]{:S(2)}) collective-permute-start(bf16[32,64,128]{2,1,0:T(8,128)(2,1)} %collective-permute-done.14.refs_0_), channel_id=1, source_target_pairs={{0,2},{1,3},{2,4},{3,5},{4,6},{5,7},{6,0},{7,1},{8,10},{9,11},{10,... | collective-permute-start | bytes 1572872 | tf_op jit(solution)/shard_map/ppermute | solution.py:550
  82.1 23.4 %collective-permute-start.8 = (bf16[32,64,128]{2,1,0:T(8,128)(2,1)}, bf16[32,64,128]{2,1,0:T(8,128)(2,1)}, u32[]{:S(2)}, u32[]{:S(2)}) collective-permute-start(bf16[32,64,128]{2,1,0:T(8,128)(2,1)} %collective-permute-done.5.refs_0_), channel_id=1, source_target_pairs={{0,1},{1,0},{2,3},{3,2},{4,5},{5,4},{6,7},{7,6},{8,9},{9,8},{10,11... | collective-permute-start | bytes 1572872 | tf_op jit(solution)/shard_map/ppermute | solution.py:551
  83.5 21.1 %collective-permute-start.6 = (bf16[32,64,128]{2,1,0:T(8,128)(2,1)}, bf16[32,64,128]{2,1,0:T(8,128)(2,1)}, u32[]{:S(2)}, u32[]{:S(2)}) collective-permute-start(bf16[32,64,128]{2,1,0:T(8,128)(2,1)} %collective-permute-done.5.refs_0_), channel_id=1, source_target_pairs={{0,2},{1,3},{2,4},{3,5},{4,6},{5,7},{6,0},{7,1},{8,10},{9,11},{10,... | collective-permute-start | bytes 1572872 | tf_op jit(solution)/shard_map/ppermute | solution.py:550
  93.3 16.0 %collective-permute-start.16 = (bf16[32,64,128]{2,1,0:T(8,128)(2,1)}, bf16[32,64,128]{2,1,0:T(8,128)(2,1)}, u32[]{:S(2)}, u32[]{:S(2)}) collective-permute-start(bf16[32,64,128]{2,1,0:T(8,128)(2,1)} %collective-permute-done.15.mine_ref), channel_id=1, source_target_pairs={{0,1},{1,0},{2,3},{3,2},{4,5},{5,4},{6,7},{7,6},{8,9},{9,8},{10,11... | collective-permute-start | bytes 1572872 | tf_op jit(solution)/shard_map/ppermute | solution.py:551
  104.6 8.5 %collective-permute-start.7 = (bf16[32,64,128]{2,1,0:T(8,128)(2,1)}, bf16[32,64,128]{2,1,0:T(8,128)(2,1)}, u32[]{:S(2)}, u32[]{:S(2)}) collective-permute-start(bf16[32,64,128]{2,1,0:T(8,128)(2,1)} %collective-permute-done.6.mine_ref), channel_id=1, source_target_pairs={{0,1},{1,0},{2,3},{3,2},{4,5},{5,4},{6,7},{7,6},{8,9},{9,8},{10,11... | collective-permute-start | bytes 1572872 | tf_op jit(solution)/shard_map/ppermute | solution.py:551

commit v11 on v8

--- a/solution.py
+++ b/solution.py
@@ -37,6 +37,30 @@
     return pl.CostEstimate(
         flops=int(microseconds * 1e9), transcendentals=0, bytes_accessed=int(microseconds * 3e6)
     )
+
+
+def ends_kernel(low_ref, high_ref, first_ref, last_ref):
+    first_ref[...] = jnp.swapaxes(low_ref[...], 0, 1)[:REACH]
+    last_ref[...] = jnp.swapaxes(high_ref[...], 0, 1)[RG - REACH :]
+
+
+def end_rows(images):
+    count, channels, rows, segment = images.shape
+    tile = (None, channels, RG, segment)
+    ends = jax.ShapeDtypeStruct((count, REACH, channels, segment), jnp.bfloat16)
+    ends_spec = pl.BlockSpec((None, REACH, channels, segment), lambda n: (n, 0, 0, 0))
+    return pl.pallas_call(
+        ends_kernel,
+        out_shape=(ends, ends),
+        grid=(count,),
+        in_specs=[
+            pl.BlockSpec(tile, lambda n: (n, 0, 0, 0)),
+            pl.BlockSpec(tile, lambda n: (n, 0, rows // RG - 1, 0)),
+        ],
+        out_specs=(ends_spec, ends_spec),
+        compiler_params=pltpu.CompilerParams(vmem_limit_bytes=VMEM_LIMIT),
+        cost_estimate=cost(1),
+    )(images, images)
 
 
 def edge_steps(rows, segment):
@@ -500,9 +524,11 @@
     place = jnp.stack([lax.axis_index("rows"), col]).astype(jnp.int32)
     ranges = search_ranges.reshape(2, rows // RG)
 
+    steps = min(col_count // 2 - 1, HOPS // 2)
     swap = [(i, i ^ 1) for i in range(col_count)]
     across = both_ways([(i, i + 1) for i in range(1, col_count - 1, 2)])
     hop = [(i, (i + 2) % col_count) for i in range(col_count)]
+    last_hop = [(i, i + 2) for i in range(2 * (steps - 1), col_count - 2)]
     down = [(i, (i + 1) % row_count) for i in range(row_count)]
     up = [(b, a) for a, b in down]
 
@@ -518,9 +544,10 @@
             first_weight, second_weight, (row_count, col_count),
         )
 
+    first_rows, last_rows = end_rows(images)
+    above = lax.ppermute(last_rows, "rows", down)
+    below = lax.ppermute(first_rows, "rows", up)
     mid = images.transpose(0, 2, 1, 3)
-    above = lax.ppermute(mid[:, rows - REACH :], "rows", down)
-    below = lax.ppermute(mid[:, :REACH], "rows", up)
 
     strip = rows // 4
     inner = rows - 2 * strip
@@ -531,14 +558,13 @@
     right_b = features(around, 1, 2, strip, 0, edges_r, 0)
     left = features(around, 0, 1, rows, 0, edges_r, 2 * edge_steps(strip, segment)[1])
 
-    steps = min(col_count // 2 - 1, HOPS // 2)
     early = max(steps - 1, 1)
 
     def chain(mine):
         pairs = []
         for step in range(steps + 1):
             if step:
-                mine = lax.ppermute(mine, "cols", hop)
+                mine = lax.ppermute(mine, "cols", hop if step < steps else last_hop)
             pairs.append((mine, lax.ppermute(mine, "cols", swap)))
         return pairs
 

time: 118 us -> 114 us (0.966)
  the two profiles are of different devices: /device:TPU:1 before, /device:TPU:25 now
where the time goes in v11:
time: 114 us; the launch traced here: 113 us
  Pallas kernels  64.6 us (57%)
  starting transfers between devices  29.9 us (26%)
  waiting for transfers between devices  13.4 us (12%)
  local copies, waits for them, and re-layouts  4.25 us (4%)
    pallas_call x3, Pallas kernels, unit_features(): pl.pallas_call(functools.partial(feature_kernel, spacing=spacing, offset=...  24.4 us
    pallas_call x4, Pallas kernels, correlate(): pl.pallas_call(functools.partial(gather_kernel, inner=inner, groups=group...  23.6 us
    ppermute x6, waiting for transfers between devices, chain(): mine = lax.ppermute(mine, 'cols', hop if step < steps else last_hop)  13.4 us
    ppermute x8, starting transfers between devices, chain(): pairs.append((mine, lax.ppermute(mine, 'cols', swap)))  11 us
    ppermute x6, starting transfers between devices, chain(): mine = lax.ppermute(mine, 'cols', hop if step < steps else last_hop)  9.54 us
    pallas_call x2, Pallas kernels, finish(): pl.pallas_call(functools.partial(finish_kernel, inner=inner, groups=group...  9.08 us
    pallas_call x2, Pallas kernels, pack_edges(): pl.pallas_call(functools.partial(pack_kernel, images=tuple((chunks for _,...  5.64 us
    unnamed x1, local copies, waits for them, and re-layouts  4.25 us
  transfers between devices with their start and end apart: 20, of which 5 were waited for; matrix products, arithmetic and copies ran while one was open for 4% of the time, Pallas kernels for 52%

profile of v11, /device:TPU:25, one launch (start us, length us, event | category | flops | bytes accessed | tf_op | source)
XLA Modules:
  0.0 113.4 jit_solution(3435976512155821578)
XLA Ops:
  0.6 1.8 %shard_map.59 = (bf16[2,6,64,128]{3,2,1,0:T(8,128)(2,1)}, bf16[2,6,64,128]{3,2,1,0:T(8,128)(2,1)}) custom-call(bf16[2,64,64,128]{3,2,1,0:T(8,128)(2,1)} %high_ref.1, bf16[2,64,64,128]{3,2,1,0:T(8,128)(2,1)} %high_ref.1), custom_call_target="tpu_custom_call" | custom-call | flops 1000000000 | bytes 3000000 | tf_op jit(solution)/shard_map/pallas_call | solution.py:52
  2.5 1.2 %collective-permute-start = (bf16[2,6,64,128]{3,2,1,0:T(8,128)(2,1)}, bf16[2,6,64,128]{3,2,1,0:T(8,128)(2,1)}, u32[]{:S(2)}, u32[]{:S(2)}) collective-permute-start(bf16[2,6,64,128]{3,2,1,0:T(8,128)(2,1)} %get-tuple-element.6), channel_id=1, source_target_pairs={{0,8},{8,16},{16,24},{24,0},{1,9},{9,17},{17,25},{25,1},{2,10},{10... | collective-permute-start | bytes 589832 | tf_op jit(solution)/shard_map/ppermute | solution.py:548
  3.7 1.2 %collective-permute-start.1 = (bf16[2,6,64,128]{3,2,1,0:T(8,128)(2,1)}, bf16[2,6,64,128]{3,2,1,0:T(8,128)(2,1)}, u32[]{:S(2)}, u32[]{:S(2)}) collective-permute-start(bf16[2,6,64,128]{3,2,1,0:T(8,128)(2,1)} %get-tuple-element.7), channel_id=1, source_target_pairs={{8,0},{16,8},{24,16},{0,24},{9,1},{17,9},{25,17},{1,25},{10,2},{18... | collective-permute-start | bytes 589832 | tf_op jit(solution)/shard_map/ppermute | solution.py:549
  4.8 4.2 %copy.12 = bf16[2,64,64,128]{3,1,2,0:T(8,128)(2,1)} copy(bf16[2,64,64,128]{3,2,1,0:T(8,128)(2,1)} %high_ref.1) | data formatting | bytes 4194304 | tf_op args[0]
  9.1 2.3 %shard_map.65.refs_1_ = bf16[9,64,128]{2,1,0:T(8,128)(2,1)} custom-call(bf16[2,64,64,128]{3,2,1,0:T(8,128)(2,1)} %bitcast.6), custom_call_target="tpu_custom_call" | custom-call | flops 2000000000 | bytes 6000000 | tf_op jit(solution)/shard_map/pallas_call | solution.py:120
  11.3 1.3 %collective-permute-start.12 = (bf16[9,64,128]{2,1,0:T(8,128)(2,1)}, bf16[9,64,128]{2,1,0:T(8,128)(2,1)}, u32[]{:S(2)}, u32[]{:S(2)}) collective-permute-start(bf16[9,64,128]{2,1,0:T(8,128)(2,1)} %shard_map.65.refs_1_), channel_id=1, source_target_pairs={{1,2},{3,4},{5,6},{2,1},{4,3},{6,5},{9,10},{11,12},{13,14},{10,9},... | collective-permute-start | bytes 442376 | tf_op jit(solution)/shard_map/ppermute | solution.py:537
  12.7 1.9 %collective-permute-start.11 = (bf16[9,64,128]{2,1,0:T(8,128)(2,1)}, bf16[9,64,128]{2,1,0:T(8,128)(2,1)}, u32[]{:S(2)}, u32[]{:S(2)}) collective-permute-start(bf16[9,64,128]{2,1,0:T(8,128)(2,1)} %shard_map.65.refs_1_), channel_id=1, source_target_pairs={{0,1},{1,0},{2,3},{3,2},{4,5},{5,4},{6,7},{7,6},{8,9},{9,8},{10,11... | collective-permute-start | bytes 442376 | tf_op jit(solution)/shard_map/ppermute | solution.py:538
  14.6 0.6 pad_add_fusion.refs_0_.place_ref
  15.2 0.0 collective-permute-done.refs_2_.refs_5_.refs_1_
  15.2 0.0 collective-permute-done.1.refs_3_.refs_6_.refs_2_
  15.2 3.4 %shard_map.60.refs_3_ = bf16[27,64,128]{2,1,0:T(8,128)(2,1)} custom-call(s32[2]{0:T(128)} %pad_add_fusion.refs_0_.place_ref, bf16[2,64,64,128]{3,2,1,0:T(8,128)(2,1)} %bitcast.7, bf16[2,6,64,128]{3,2,1,0:T(8,128)(2,1)} %collective-permute-done.refs_2_.refs_5_.refs_1_, bf16[2,6,64,128]{3,2,1,0:T(8,128)(2,1)} %collective-permute-done.1.refs_3_.refs_6_.refs_2_, ...), custom_call_target="tpu_custom_call" | custom-call | flops 2000000000 | bytes 6000000 | tf_op jit(solution)/shard_map/pallas_call | solution.py:120
  18.6 1.5 %collective-permute-start.3 = (bf16[27,64,128]{2,1,0:T(8,128)(2,1)}, bf16[27,64,128]{2,1,0:T(8,128)(2,1)}, u32[]{:S(2)}, u32[]{:S(2)}) collective-permute-start(bf16[27,64,128]{2,1,0:T(8,128)(2,1)} %shard_map.60.refs_3_), channel_id=1, source_target_pairs={{1,2},{3,4},{5,6},{2,1},{4,3},{6,5},{9,10},{11,12},{13,14},{10,9},... | collective-permute-start | bytes 1327112 | tf_op jit(solution)/shard_map/ppermute | solution.py:537
  20.0 2.3 %collective-permute-start.2 = (bf16[27,64,128]{2,1,0:T(8,128)(2,1)}, bf16[27,64,128]{2,1,0:T(8,128)(2,1)}, u32[]{:S(2)}, u32[]{:S(2)}) collective-permute-start(bf16[27,64,128]{2,1,0:T(8,128)(2,1)} %shard_map.60.refs_3_), channel_id=1, source_target_pairs={{0,1},{1,0},{2,3},{3,2},{4,5},{5,4},{6,7},{7,6},{8,9},{9,8},{10,11... | collective-permute-start | bytes 1327112 | tf_op jit(solution)/shard_map/ppermute | solution.py:538
  22.3 0.0 collective-permute-done.12.refs_3_
  22.3 0.0 collective-permute-done.11.refs_2_
  22.3 6.5 %shard_map.66.refs_0_ = bf16[32,64,128]{2,1,0:T(8,128)(2,1)} custom-call(s32[2]{0:T(128)} %pad_add_fusion.refs_0_.place_ref, bf16[2,64,64,128]{3,2,1,0:T(8,128)(2,1)} %bitcast.9, bf16[9,64,128]{2,1,0:T(8,128)(2,1)} %shard_map.65.refs_1_, bf16[9,64,128]{2,1,0:T(8,128)(2,1)} %collective-permute-done.11.refs_2_, ...), custom_call_target="tpu_custom_call" | custom-call | flops 6400000000 | bytes 19200000 | tf_op jit(solution)/shard_map/pallas_call | solution.py:320
  28.8 0.0 collective-permute-start.18
  28.8 1.5 %collective-permute-start.13 = (bf16[32,64,128]{2,1,0:T(8,128)(2,1)}, bf16[32,64,128]{2,1,0:T(8,128)(2,1)}, u32[]{:S(2)}, u32[]{:S(2)}) collective-permute-start(bf16[32,64,128]{2,1,0:T(8,128)(2,1)} %shard_map.66.refs_0_), channel_id=1, source_target_pairs={{0,2},{1,3},{2,4},{3,5},{4,6},{5,7},{6,0},{7,1},{8,10},{9,11},{10,... | collective-permute-start | bytes 1572872 | tf_op jit(solution)/shard_map/ppermute | solution.py:567
  30.4 8.0 %shard_map.62.refs_0_ = bf16[32,64,128]{2,1,0:T(8,128)(2,1)} custom-call(s32[2]{0:T(128)} %pad_add_fusion.refs_0_.place_ref, bf16[2,64,64,128]{3,2,1,0:T(8,128)(2,1)} %bitcast.10, bf16[2,6,64,128]{3,2,1,0:T(8,128)(2,1)} %collective-permute-done.refs_2_.refs_5_.refs_1_, bf16[2,6,64,128]{3,2,1,0:T(8,128)(2,1)} %collective-permute-done.1.refs_3_.refs_6_.refs_2_, ...), custom_call_target="tpu_custom_call" | custom-call | flops 6400000000 | bytes 19200000 | tf_op jit(solution)/shard_map/pallas_call | solution.py:320
  38.4 0.3 collective-permute-start.9
  38.7 1.3 %collective-permute-start.4 = (bf16[32,64,128]{2,1,0:T(8,128)(2,1)}, bf16[32,64,128]{2,1,0:T(8,128)(2,1)}, u32[]{:S(2)}, u32[]{:S(2)}) collective-permute-start(bf16[32,64,128]{2,1,0:T(8,128)(2,1)} %shard_map.62.refs_0_), channel_id=1, source_target_pairs={{0,2},{1,3},{2,4},{3,5},{4,6},{5,7},{6,0},{7,1},{8,10},{9,11},{10,... | collective-permute-start | bytes 1572872 | tf_op jit(solution)/shard_map/ppermute | solution.py:567
  40.0 2.1 %collective-permute-done.13.refs_2_ = bf16[32,64,128]{2,1,0:T(8,128)(2,1)} collective-permute-done((bf16[32,64,128]{2,1,0:T(8,128)(2,1)}, bf16[32,64,128]{2,1,0:T(8,128)(2,1)}, u32[]{:S(2)}, u32[]{:S(2)}) %collective-permute-start.13) | collective-permute-done | bytes 524320 | tf_op jit(solution)/shard_map/ppermute | solution.py:567
  42.1 2.3 %collective-permute-start.19 = (bf16[32,64,128]{2,1,0:T(8,128)(2,1)}, bf16[32,64,128]{2,1,0:T(8,128)(2,1)}, u32[]{:S(2)}, u32[]{:S(2)}) collective-permute-start(bf16[32,64,128]{2,1,0:T(8,128)(2,1)} %collective-permute-done.13.refs_2_), channel_id=1, source_target_pairs={{0,1},{1,0},{2,3},{3,2},{4,5},{5,4},{6,7},{7,6},{8,9},{9,8},{10,11... | collective-permute-start | bytes 1572872 | tf_op jit(solution)/shard_map/ppermute | solution.py:568
  44.4 2.9 %collective-permute-start.14 = (bf16[32,64,128]{2,1,0:T(8,128)(2,1)}, bf16[32,64,128]{2,1,0:T(8,128)(2,1)}, u32[]{:S(2)}, u32[]{:S(2)}) collective-permute-start(bf16[32,64,128]{2,1,0:T(8,128)(2,1)} %collective-permute-done.13.refs_2_), channel_id=1, source_target_pairs={{0,2},{1,3},{2,4},{3,5},{4,6},{5,7},{6,0},{7,1},{8,10},{9,11},{10,... | collective-permute-start | bytes 1572872 | tf_op jit(solution)/shard_map/ppermute | solution.py:567
  47.3 9.8 %shard_map.61.left_ref = bf16[64,64,128]{2,1,0:T(8,128)(2,1)} custom-call(s32[2]{0:T(128)} %pad_add_fusion.refs_0_.place_ref, bf16[2,64,64,128]{3,2,1,0:T(8,128)(2,1)} %bitcast.11, bf16[2,6,64,128]{3,2,1,0:T(8,128)(2,1)} %collective-permute-done.refs_2_.refs_5_.refs_1_, bf16[2,6,64,128]{3,2,1,0:T(8,128)(2,1)} %collective-permute-done.1.refs_3_.refs_6_.refs_2_, ...), custom_call_target="tpu_custom_call" | custom-call | flops 12800000000 | bytes 38400000 | tf_op jit(solution)/shard_map/pallas_call | solution.py:320
  57.1 0.0 collective-permute-done.4.refs_2_
  57.1 0.3 collective-permute-start.10
  57.4 1.1 collective-permute-start.5
  58.5 6.1 %collective-permute-done.14.refs_0_ = bf16[32,64,128]{2,1,0:T(8,128)(2,1)} collective-permute-done((bf16[32,64,128]{2,1,0:T(8,128)(2,1)}, bf16[32,64,128]{2,1,0:T(8,128)(2,1)}, u32[]{:S(2)}, u32[]{:S(2)}) %collective-permute-start.14) | collective-permute-done | bytes 524320 | tf_op jit(solution)/shard_map/ppermute | solution.py:567
  64.6 2.3 %collective-permute-start.17 = (bf16[32,64,128]{2,1,0:T(8,128)(2,1)}, bf16[32,64,128]{2,1,0:T(8,128)(2,1)}, u32[]{:S(2)}, u32[]{:S(2)}) collective-permute-start(bf16[32,64,128]{2,1,0:T(8,128)(2,1)} %collective-permute-done.14.refs_0_), channel_id=1, source_target_pairs={{0,1},{1,0},{2,3},{3,2},{4,5},{5,4},{6,7},{7,6},{8,9},{9,8},{10,11... | collective-permute-start | bytes 1572872 | tf_op jit(solution)/shard_map/ppermute | solution.py:568
  66.9 0.0 collective-permute-done.19.refs_3_
  66.9 1.3 %collective-permute-start.15 = (bf16[32,64,128]{2,1,0:T(8,128)(2,1)}, bf16[32,64,128]{2,1,0:T(8,128)(2,1)}, u32[]{:S(2)}, u32[]{:S(2)}) collective-permute-start(bf16[32,64,128]{2,1,0:T(8,128)(2,1)} %collective-permute-done.14.refs_0_), channel_id=1, source_target_pairs={{4,6},{5,7},{12,14},{13,15},{20,22},{21,23},{28,30},{29,31}} | collective-permute-start | bytes 1572872 | tf_op jit(solution)/shard_map/ppermute | solution.py:567
  68.2 6.9 %shard_map.67.refs_2_ = f32[32,80,128]{2,1,0:T(8,128)} custom-call(s32[2]{0:T(128)} %pad_add_fusion.refs_0_.place_ref, s32[2,8]{1,0:T(2,128)} %bitcast.12, bf16[64,64,128]{2,1,0:T(8,128)(2,1)} %shard_map.61.left_ref, bf16[32,64,128]{2,1,0:T(8,128)(2,1)} %shard_map.66.refs_0_, bf16[32,64,128]{2,1,0:T(8,128)(2,1)} %collective-permute-done.18.refs_1_, ...), custom_call_target="tpu_custom_call" | custom-call | flops 6000000000 | bytes 18000000 | tf_op jit(solution)/shard_map/pallas_call | solution.py:454
  75.1 0.7 collective-permute-done.5.refs_0_
  75.9 2.3 %collective-permute-start.8 = (bf16[32,64,128]{2,1,0:T(8,128)(2,1)}, bf16[32,64,128]{2,1,0:T(8,128)(2,1)}, u32[]{:S(2)}, u32[]{:S(2)}) collective-permute-start(bf16[32,64,128]{2,1,0:T(8,128)(2,1)} %collective-permute-done.5.refs_0_), channel_id=1, source_target_pairs={{0,1},{1,0},{2,3},{3,2},{4,5},{5,4},{6,7},{7,6},{8,9},{9,8},{10,11... | collective-permute-start | bytes 1572872 | tf_op jit(solution)/shard_map/ppermute | solution.py:568
  78.1 0.0 collective-permute-done.9.refs_1_
  78.1 1.5 %collective-permute-start.6 = (bf16[32,64,128]{2,1,0:T(8,128)(2,1)}, bf16[32,64,128]{2,1,0:T(8,128)(2,1)}, u32[]{:S(2)}, u32[]{:S(2)}) collective-permute-start(bf16[32,64,128]{2,1,0:T(8,128)(2,1)} %collective-permute-done.5.refs_0_), channel_id=1, source_target_pairs={{4,6},{5,7},{12,14},{13,15},{20,22},{21,23},{28,30},{29,31}} | collective-permute-start | bytes 1572872 | tf_op jit(solution)/shard_map/ppermute | solution.py:567
  79.6 6.9 %shard_map.63.refs_2_ = f32[32,80,128]{2,1,0:T(8,128)} custom-call(s32[2]{0:T(128)} %pad_add_fusion.refs_0_.place_ref, s32[2,8]{1,0:T(2,128)} %bitcast.13, bf16[64,64,128]{2,1,0:T(8,128)(2,1)} %shard_map.61.left_ref, bf16[32,64,128]{2,1,0:T(8,128)(2,1)} %shard_map.62.refs_0_, bf16[32,64,128]{2,1,0:T(8,128)(2,1)} %collective-permute-done.9.refs_1_, ...), custom_call_target="tpu_custom_call" | custom-call | flops 6000000000 | bytes 18000000 | tf_op jit(solution)/shard_map/pallas_call | solution.py:454
  86.5 0.6 collective-permute-done.15.mine_ref
  87.1 2.3 %collective-permute-start.16 = (bf16[32,64,128]{2,1,0:T(8,128)(2,1)}, bf16[32,64,128]{2,1,0:T(8,128)(2,1)}, u32[]{:S(2)}, u32[]{:S(2)}) collective-permute-start(bf16[32,64,128]{2,1,0:T(8,128)(2,1)} %collective-permute-done.15.mine_ref), channel_id=1, source_target_pairs={{0,1},{1,0},{2,3},{3,2},{4,5},{5,4},{6,7},{7,6},{8,9},{9,8},{10,11... | collective-permute-start | bytes 1572872 | tf_op jit(solution)/shard_map/ppermute | solution.py:568
  89.4 5.1 %shard_map.68.acc_in_ref = f32[32,80,128]{2,1,0:T(8,128)} custom-call(s32[2]{0:T(128)} %pad_add_fusion.refs_0_.place_ref, s32[2,8]{1,0:T(2,128)} %bitcast.14, bf16[64,64,128]{2,1,0:T(8,128)(2,1)} %shard_map.61.left_ref, bf16[32,64,128]{2,1,0:T(8,128)(2,1)} %collective-permute-done.14.refs_0_, ...), custom_call_target="tpu_custom_call", output_to_operand_aliasing={{}: (5, {})} | custom-call | flops 6000000000 | bytes 18000000 | tf_op jit(solution)/shard_map/pallas_call | solution.py:454
  94.5 3.8 %collective-permute-done.6.mine_ref = bf16[32,64,128]{2,1,0:T(8,128)(2,1)} collective-permute-done((bf16[32,64,128]{2,1,0:T(8,128)(2,1)}, bf16[32,64,128]{2,1,0:T(8,128)(2,1)}, u32[]{:S(2)}, u32[]{:S(2)}) %collective-permute-start.6) | collective-permute-done | bytes 524320 | tf_op jit(solution)/shard_map/ppermute | solution.py:567
  98.3 1.3 %collective-permute-start.7 = (bf16[32,64,128]{2,1,0:T(8,128)(2,1)}, bf16[32,64,128]{2,1,0:T(8,128)(2,1)}, u32[]{:S(2)}, u32[]{:S(2)}) collective-permute-start(bf16[32,64,128]{2,1,0:T(8,128)(2,1)} %collective-permute-done.6.mine_ref), channel_id=1, source_target_pairs={{0,1},{1,0},{2,3},{3,2},{4,5},{5,4},{6,7},{7,6},{8,9},{9,8},{10,11... | collective-permute-start | bytes 1572872 | tf_op jit(solution)/shard_map/ppermute | solution.py:568
  99.7 0.0 collective-permute-done.8.refs_1_
  99.7 4.6 %shard_map.64.acc_in_ref = f32[32,80,128]{2,1,0:T(8,128)} custom-call(s32[2]{0:T(128)} %pad_add_fusion.refs_0_.place_ref, s32[2,8]{1,0:T(2,128)} %bitcast.15, bf16[64,64,128]{2,1,0:T(8,128)(2,1)} %shard_map.61.left_ref, bf16[32,64,128]{2,1,0:T(8,128)(2,1)} %collective-permute-done.5.refs_0_, ...), custom_call_target="tpu_custom_call", output_to_operand_aliasing={{}: (5, {})} | custom-call | flops 6000000000 | bytes 18000000 | tf_op jit(solution)/shard_map/pallas_call | solution.py:454
  104.3 0.0 collective-permute-done.16.theirs_ref
  104.3 5.1 %shard_map.69 = (bf16[64,64,128]{2,1,0:T(8,128)(2,1)}, f32[64,128]{1,0:T(8,128)}) custom-call(s32[2]{0:T(128)} %pad_add_fusion.refs_0_.place_ref, s32[2,8]{1,0:T(2,128)} %bitcast.16, bf16[64,64,128]{2,1,0:T(8,128)(2,1)} %shard_map.61.left_ref, bf16[32,64,128]{2,1,0:T(8,128)(2,1)} %collective-permute-done.15.mine_ref, ...), custom_call_target="tpu_custom_call" | custom-call | flops 4000000000 | bytes 12000000 | tf_op jit(solution)/shard_map/pallas_call | solution.py:483
  109.4 4.0 %shard_map.70 = (bf16[64,64,128]{2,1,0:T(8,128)(2,1)}, f32[64,128]{1,0:T(8,128)}) custom-call(s32[2]{0:T(128)} %pad_add_fusion.refs_0_.place_ref, s32[2,8]{1,0:T(2,128)} %bitcast.17, bf16[64,64,128]{2,1,0:T(8,128)(2,1)} %shard_map.61.left_ref, bf16[32,64,128]{2,1,0:T(8,128)(2,1)} %collective-permute-done.6.mine_ref, ...), custom_call_target="tpu_custom_call", output_to_operand_aliasing={{0}: (6, {}), {1}: (7, {})} | custom-call | flops 4000000000 | bytes 12000000 | tf_op jit(solution)/shard_map/pallas_call | solution.py:483
  (6 shorter events, 0.0 us)
Async XLA Ops:
  2.5 12.7 %collective-permute-start = (bf16[2,6,64,128]{3,2,1,0:T(8,128)(2,1)}, bf16[2,6,64,128]{3,2,1,0:T(8,128)(2,1)}, u32[]{:S(2)}, u32[]{:S(2)}) collective-permute-start(bf16[2,6,64,128]{3,2,1,0:T(8,128)(2,1)} %get-tuple-element.6), channel_id=1, source_target_pairs={{0,8},{8,16},{16,24},{24,0},{1,9},{9,17},{17,25},{25,1},{2,10},{10... | collective-permute-start | bytes 589832 | tf_op jit(solution)/shard_map/ppermute | solution.py:548
  3.7 11.5 %collective-permute-start.1 = (bf16[2,6,64,128]{3,2,1,0:T(8,128)(2,1)}, bf16[2,6,64,128]{3,2,1,0:T(8,128)(2,1)}, u32[]{:S(2)}, u32[]{:S(2)}) collective-permute-start(bf16[2,6,64,128]{3,2,1,0:T(8,128)(2,1)} %get-tuple-element.7), channel_id=1, source_target_pairs={{8,0},{16,8},{24,16},{0,24},{9,1},{17,9},{25,17},{1,25},{10,2},{18... | collective-permute-start | bytes 589832 | tf_op jit(solution)/shard_map/ppermute | solution.py:549
  11.3 10.9 %collective-permute-start.12 = (bf16[9,64,128]{2,1,0:T(8,128)(2,1)}, bf16[9,64,128]{2,1,0:T(8,128)(2,1)}, u32[]{:S(2)}, u32[]{:S(2)}) collective-permute-start(bf16[9,64,128]{2,1,0:T(8,128)(2,1)} %shard_map.65.refs_1_), channel_id=1, source_target_pairs={{1,2},{3,4},{5,6},{2,1},{4,3},{6,5},{9,10},{11,12},{13,14},{10,9},... | collective-permute-start | bytes 442376 | tf_op jit(solution)/shard_map/ppermute | solution.py:537
  12.7 9.6 %collective-permute-start.11 = (bf16[9,64,128]{2,1,0:T(8,128)(2,1)}, bf16[9,64,128]{2,1,0:T(8,128)(2,1)}, u32[]{:S(2)}, u32[]{:S(2)}) collective-permute-start(bf16[9,64,128]{2,1,0:T(8,128)(2,1)} %shard_map.65.refs_1_), channel_id=1, source_target_pairs={{0,1},{1,0},{2,3},{3,2},{4,5},{5,4},{6,7},{7,6},{8,9},{9,8},{10,11... | collective-permute-start | bytes 442376 | tf_op jit(solution)/shard_map/ppermute | solution.py:538
  18.6 11.8 %collective-permute-start.3 = (bf16[27,64,128]{2,1,0:T(8,128)(2,1)}, bf16[27,64,128]{2,1,0:T(8,128)(2,1)}, u32[]{:S(2)}, u32[]{:S(2)}) collective-permute-start(bf16[27,64,128]{2,1,0:T(8,128)(2,1)} %shard_map.60.refs_3_), channel_id=1, source_target_pairs={{1,2},{3,4},{5,6},{2,1},{4,3},{6,5},{9,10},{11,12},{13,14},{10,9},... | collective-permute-start | bytes 1327112 | tf_op jit(solution)/shard_map/ppermute | solution.py:537
  20.0 10.3 %collective-permute-start.2 = (bf16[27,64,128]{2,1,0:T(8,128)(2,1)}, bf16[27,64,128]{2,1,0:T(8,128)(2,1)}, u32[]{:S(2)}, u32[]{:S(2)}) collective-permute-start(bf16[27,64,128]{2,1,0:T(8,128)(2,1)} %shard_map.60.refs_3_), channel_id=1, source_target_pairs={{0,1},{1,0},{2,3},{3,2},{4,5},{5,4},{6,7},{7,6},{8,9},{9,8},{10,11... | collective-permute-start | bytes 1327112 | tf_op jit(solution)/shard_map/ppermute | solution.py:538
  28.8 28.6 %collective-permute-start.18 = (bf16[32,64,128]{2,1,0:T(8,128)(2,1)}, bf16[32,64,128]{2,1,0:T(8,128)(2,1)}, u32[]{:S(2)}, u32[]{:S(2)}) collective-permute-start(bf16[32,64,128]{2,1,0:T(8,128)(2,1)} %shard_map.66.refs_0_), channel_id=1, source_target_pairs={{0,1},{1,0},{2,3},{3,2},{4,5},{5,4},{6,7},{7,6},{8,9},{9,8},{10,11... | collective-permute-start | bytes 1572872 | tf_op jit(solution)/shard_map/ppermute | solution.py:568
  28.8 13.3 %collective-permute-start.13 = (bf16[32,64,128]{2,1,0:T(8,128)(2,1)}, bf16[32,64,128]{2,1,0:T(8,128)(2,1)}, u32[]{:S(2)}, u32[]{:S(2)}) collective-permute-start(bf16[32,64,128]{2,1,0:T(8,128)(2,1)} %shard_map.66.refs_0_), channel_id=1, source_target_pairs={{0,2},{1,3},{2,4},{3,5},{4,6},{5,7},{6,0},{7,1},{8,10},{9,11},{10,... | collective-permute-start | bytes 1572872 | tf_op jit(solution)/shard_map/ppermute | solution.py:567
  38.4 39.7 %collective-permute-start.9 = (bf16[32,64,128]{2,1,0:T(8,128)(2,1)}, bf16[32,64,128]{2,1,0:T(8,128)(2,1)}, u32[]{:S(2)}, u32[]{:S(2)}) collective-permute-start(bf16[32,64,128]{2,1,0:T(8,128)(2,1)} %shard_map.62.refs_0_), channel_id=1, source_target_pairs={{0,1},{1,0},{2,3},{3,2},{4,5},{5,4},{6,7},{7,6},{8,9},{9,8},{10,11... | collective-permute-start | bytes 1572872 | tf_op jit(solution)/shard_map/ppermute | solution.py:568
  38.7 18.4 %collective-permute-start.4 = (bf16[32,64,128]{2,1,0:T(8,128)(2,1)}, bf16[32,64,128]{2,1,0:T(8,128)(2,1)}, u32[]{:S(2)}, u32[]{:S(2)}) collective-permute-start(bf16[32,64,128]{2,1,0:T(8,128)(2,1)} %shard_map.62.refs_0_), channel_id=1, source_target_pairs={{0,2},{1,3},{2,4},{3,5},{4,6},{5,7},{6,0},{7,1},{8,10},{9,11},{10,... | collective-permute-start | bytes 1572872 | tf_op jit(solution)/shard_map/ppermute | solution.py:567
  42.1 24.7 %collective-permute-start.19 = (bf16[32,64,128]{2,1,0:T(8,128)(2,1)}, bf16[32,64,128]{2,1,0:T(8,128)(2,1)}, u32[]{:S(2)}, u32[]{:S(2)}) collective-permute-start(bf16[32,64,128]{2,1,0:T(8,128)(2,1)} %collective-permute-done.13.refs_2_), channel_id=1, source_target_pairs={{0,1},{1,0},{2,3},{3,2},{4,5},{5,4},{6,7},{7,6},{8,9},{9,8},{10,11... | collective-permute-start | bytes 1572872 | tf_op jit(solution)/shard_map/ppermute | solution.py:568
  44.4 20.2 %collective-permute-start.14 = (bf16[32,64,128]{2,1,0:T(8,128)(2,1)}, bf16[32,64,128]{2,1,0:T(8,128)(2,1)}, u32[]{:S(2)}, u32[]{:S(2)}) collective-permute-start(bf16[32,64,128]{2,1,0:T(8,128)(2,1)} %collective-permute-done.13.refs_2_), channel_id=1, source_target_pairs={{0,2},{1,3},{2,4},{3,5},{4,6},{5,7},{6,0},{7,1},{8,10},{9,11},{10,... | collective-permute-start | bytes 1572872 | tf_op jit(solution)/shard_map/ppermute | solution.py:567
  57.1 22.4 %collective-permute-start.10 = (bf16[32,64,128]{2,1,0:T(8,128)(2,1)}, bf16[32,64,128]{2,1,0:T(8,128)(2,1)}, u32[]{:S(2)}, u32[]{:S(2)}) collective-permute-start(bf16[32,64,128]{2,1,0:T(8,128)(2,1)} %collective-permute-done.4.refs_2_), channel_id=1, source_target_pairs={{0,1},{1,0},{2,3},{3,2},{4,5},{5,4},{6,7},{7,6},{8,9},{9,8},{10,11... | collective-permute-start | bytes 1572872 | tf_op jit(solution)/shard_map/ppermute | solution.py:568
  57.4 18.4 %collective-permute-start.5 = (bf16[32,64,128]{2,1,0:T(8,128)(2,1)}, bf16[32,64,128]{2,1,0:T(8,128)(2,1)}, u32[]{:S(2)}, u32[]{:S(2)}) collective-permute-start(bf16[32,64,128]{2,1,0:T(8,128)(2,1)} %collective-permute-done.4.refs_2_), channel_id=1, source_target_pairs={{0,2},{1,3},{2,4},{3,5},{4,6},{5,7},{6,0},{7,1},{8,10},{9,11},{10,... | collective-permute-start | bytes 1572872 | tf_op jit(solution)/shard_map/ppermute | solution.py:567
  64.6 24.7 %collective-permute-start.17 = (bf16[32,64,128]{2,1,0:T(8,128)(2,1)}, bf16[32,64,128]{2,1,0:T(8,128)(2,1)}, u32[]{:S(2)}, u32[]{:S(2)}) collective-permute-start(bf16[32,64,128]{2,1,0:T(8,128)(2,1)} %collective-permute-done.14.refs_0_), channel_id=1, source_target_pairs={{0,1},{1,0},{2,3},{3,2},{4,5},{5,4},{6,7},{7,6},{8,9},{9,8},{10,11... | collective-permute-start | bytes 1572872 | tf_op jit(solution)/shard_map/ppermute | solution.py:568
  66.9 20.2 %collective-permute-start.15 = (bf16[32,64,128]{2,1,0:T(8,128)(2,1)}, bf16[32,64,128]{2,1,0:T(8,128)(2,1)}, u32[]{:S(2)}, u32[]{:S(2)}) collective-permute-start(bf16[32,64,128]{2,1,0:T(8,128)(2,1)} %collective-permute-done.14.refs_0_), channel_id=1, source_target_pairs={{4,6},{5,7},{12,14},{13,15},{20,22},{21,23},{28,30},{29,31}} | collective-permute-start | bytes 1572872 | tf_op jit(solution)/shard_map/ppermute | solution.py:567
  75.9 23.8 %collective-permute-start.8 = (bf16[32,64,128]{2,1,0:T(8,128)(2,1)}, bf16[32,64,128]{2,1,0:T(8,128)(2,1)}, u32[]{:S(2)}, u32[]{:S(2)}) collective-permute-start(bf16[32,64,128]{2,1,0:T(8,128)(2,1)} %collective-permute-done.5.refs_0_), channel_id=1, source_target_pairs={{0,1},{1,0},{2,3},{3,2},{4,5},{5,4},{6,7},{7,6},{8,9},{9,8},{10,11... | collective-permute-start | bytes 1572872 | tf_op jit(solution)/shard_map/ppermute | solution.py:568
  78.1 20.2 %collective-permute-start.6 = (bf16[32,64,128]{2,1,0:T(8,128)(2,1)}, bf16[32,64,128]{2,1,0:T(8,128)(2,1)}, u32[]{:S(2)}, u32[]{:S(2)}) collective-permute-start(bf16[32,64,128]{2,1,0:T(8,128)(2,1)} %collective-permute-done.5.refs_0_), channel_id=1, source_target_pairs={{4,6},{5,7},{12,14},{13,15},{20,22},{21,23},{28,30},{29,31}} | collective-permute-start | bytes 1572872 | tf_op jit(solution)/shard_map/ppermute | solution.py:567
  87.1 17.2 %collective-permute-start.16 = (bf16[32,64,128]{2,1,0:T(8,128)(2,1)}, bf16[32,64,128]{2,1,0:T(8,128)(2,1)}, u32[]{:S(2)}, u32[]{:S(2)}) collective-permute-start(bf16[32,64,128]{2,1,0:T(8,128)(2,1)} %collective-permute-done.15.mine_ref), channel_id=1, source_target_pairs={{0,1},{1,0},{2,3},{3,2},{4,5},{5,4},{6,7},{7,6},{8,9},{9,8},{10,11... | collective-permute-start | bytes 1572872 | tf_op jit(solution)/shard_map/ppermute | solution.py:568
  98.3 11.1 %collective-permute-start.7 = (bf16[32,64,128]{2,1,0:T(8,128)(2,1)}, bf16[32,64,128]{2,1,0:T(8,128)(2,1)}, u32[]{:S(2)}, u32[]{:S(2)}) collective-permute-start(bf16[32,64,128]{2,1,0:T(8,128)(2,1)} %collective-permute-done.6.mine_ref), channel_id=1, source_target_pairs={{0,1},{1,0},{2,3},{3,2},{4,5},{5,4},{6,7},{7,6},{8,9},{9,8},{10,11... | collective-permute-start | bytes 1572872 | tf_op jit(solution)/shard_map/ppermute | solution.py:568

commit v12 on v11

--- a/solution.py
+++ b/solution.py
@@ -164,7 +164,7 @@
     for q in range(steps):
         own = own_ref[q]
         partner = partner_ref[q]
-        cross = cross_ref[q]
+        cross = kept(cross_ref[q], ~(first_col | last_col))
         left = jnp.where(odd, partner, cross)
         right = jnp.where(odd, cross, partner)
         shift = half - REACH
@@ -527,14 +527,15 @@
     steps = min(col_count // 2 - 1, HOPS // 2)
     swap = [(i, i ^ 1) for i in range(col_count)]
     across = both_ways([(i, i + 1) for i in range(1, col_count - 1, 2)])
+    around_across = across + both_ways([(0, col_count - 1)])
     hop = [(i, (i + 2) % col_count) for i in range(col_count)]
     last_hop = [(i, i + 2) for i in range(2 * (steps - 1), col_count - 2)]
     down = [(i, (i + 1) % row_count) for i in range(row_count)]
     up = [(b, a) for a, b in down]
 
-    def exchanged(pieces, chunks):
+    def exchanged(pieces, chunks, pairs):
         own = pack_edges(place, pieces, chunks, row_count)
-        cross = lax.ppermute(own, "cols", across)
+        cross = lax.ppermute(own, "cols", pairs)
         partner = lax.ppermute(own, "cols", swap)
         return own, partner, cross
 
@@ -552,8 +553,9 @@
     strip = rows // 4
     inner = rows - 2 * strip
     around = (mid, above, below)
-    edges_a = exchanged((mid,), ((1, ((inner, strip),)),))
-    edges_r = exchanged(around, ((1, ((strip, 0), (strip, rows - strip))), (0, ((rows, 0),))))
+    edges_a = exchanged((mid,), ((1, ((inner, strip),)),), around_across)
+    chunks_r = (1, ((strip, 0), (strip, rows - strip))), (0, ((rows, 0),))
+    edges_r = exchanged(around, chunks_r, across)
     right_a = features((mid,), 1, 1, inner, strip - REACH, edges_a, 0)
     right_b = features(around, 1, 2, strip, 0, edges_r, 0)
     left = features(around, 0, 1, rows, 0, edges_r, 2 * edge_steps(strip, segment)[1])

time: 114 us -> 113 us (level)
  starting transfers between devices: 29.9 us -> 24.7 us
  waiting for transfers between devices: 13.4 us -> 17.3 us
    ppermute x6, waiting for transfers between devices: 13.4 us -> 16.7 us  [chain(): mine = lax.ppermute(mine, 'cols', hop if step < steps else last_hop)]
    ppermute x8, starting transfers between devices: 11 us -> 7.91 us  [chain(): pairs.append((mine, lax.ppermute(mine, 'cols', swap)))]
    ppermute x2, starting transfers between devices: 4.15 us -> 2.67 us  [exchanged(): partner = lax.ppermute(own, 'cols', swap)]
  transfers between devices with their start and end apart: 20 -> 20, of which waited for: 5 -> 6; matrix products, arithmetic and copies ran while one was open for 4% -> 4% of each run, Pallas kernels for 52% -> 52%
where the time goes in v12:
time: 113 us; the launch traced here: 112 us
  Pallas kernels  64.6 us (57%)
  starting transfers between devices  24.7 us (22%)
  waiting for transfers between devices  17.3 us (15%)
  local copies, waits for them, and re-layouts  4.25 us (4%)
    pallas_call x3, Pallas kernels, unit_features(): pl.pallas_call(functools.partial(feature_kernel, spacing=spacing, offset=...  24.4 us
    pallas_call x4, Pallas kernels, correlate(): pl.pallas_call(functools.partial(gather_kernel, inner=inner, groups=group...  23.6 us
    ppermute x6, waiting for transfers between devices, chain(): mine = lax.ppermute(mine, 'cols', hop if step < steps else last_hop)  16.7 us
    ppermute x6, starting transfers between devices, chain(): mine = lax.ppermute(mine, 'cols', hop if step < steps else last_hop)  9.66 us
    pallas_call x2, Pallas kernels, finish(): pl.pallas_call(functools.partial(finish_kernel, inner=inner, groups=group...  9.08 us
    ppermute x8, starting transfers between devices, chain(): pairs.append((mine, lax.ppermute(mine, 'cols', swap)))  7.91 us
    pallas_call x2, Pallas kernels, pack_edges(): pl.pallas_call(functools.partial(pack_kernel, images=tuple((chunks for _,...  5.64 us
    unnamed x1, local copies, waits for them, and re-layouts  4.25 us
  transfers between devices with their start and end apart: 20, of which 6 were waited for; matrix products, arithmetic and copies ran while one was open for 4% of the time, Pallas kernels for 52%

profile of v12, /device:TPU:25, one launch (start us, length us, event | category | flops | bytes accessed | tf_op | source)
XLA Modules:
  0.0 112.1 jit_solution(452815642444957113)
XLA Ops:
  0.6 1.8 %shard_map.59 = (bf16[2,6,64,128]{3,2,1,0:T(8,128)(2,1)}, bf16[2,6,64,128]{3,2,1,0:T(8,128)(2,1)}) custom-call(bf16[2,64,64,128]{3,2,1,0:T(8,128)(2,1)} %high_ref.1, bf16[2,64,64,128]{3,2,1,0:T(8,128)(2,1)} %high_ref.1), custom_call_target="tpu_custom_call" | custom-call | flops 1000000000 | bytes 3000000 | tf_op jit(solution)/shard_map/pallas_call | solution.py:52
  2.5 1.2 %collective-permute-start = (bf16[2,6,64,128]{3,2,1,0:T(8,128)(2,1)}, bf16[2,6,64,128]{3,2,1,0:T(8,128)(2,1)}, u32[]{:S(2)}, u32[]{:S(2)}) collective-permute-start(bf16[2,6,64,128]{3,2,1,0:T(8,128)(2,1)} %get-tuple-element.6), channel_id=1, source_target_pairs={{0,8},{8,16},{16,24},{24,0},{1,9},{9,17},{17,25},{25,1},{2,10},{10... | collective-permute-start | bytes 589832 | tf_op jit(solution)/shard_map/ppermute | solution.py:549
  3.7 1.2 %collective-permute-start.1 = (bf16[2,6,64,128]{3,2,1,0:T(8,128)(2,1)}, bf16[2,6,64,128]{3,2,1,0:T(8,128)(2,1)}, u32[]{:S(2)}, u32[]{:S(2)}) collective-permute-start(bf16[2,6,64,128]{3,2,1,0:T(8,128)(2,1)} %get-tuple-element.7), channel_id=1, source_target_pairs={{8,0},{16,8},{24,16},{0,24},{9,1},{17,9},{25,17},{1,25},{10,2},{18... | collective-permute-start | bytes 589832 | tf_op jit(solution)/shard_map/ppermute | solution.py:550
  4.8 4.2 %copy.12 = bf16[2,64,64,128]{3,1,2,0:T(8,128)(2,1)} copy(bf16[2,64,64,128]{3,2,1,0:T(8,128)(2,1)} %high_ref.1) | data formatting | bytes 4194304 | tf_op args[0]
  9.1 2.3 %shard_map.65.refs_1_ = bf16[9,64,128]{2,1,0:T(8,128)(2,1)} custom-call(bf16[2,64,64,128]{3,2,1,0:T(8,128)(2,1)} %bitcast.6), custom_call_target="tpu_custom_call" | custom-call | flops 2000000000 | bytes 6000000 | tf_op jit(solution)/shard_map/pallas_call | solution.py:120
  11.3 0.6 collective-permute-start.12
  12.0 0.6 collective-permute-start.11
  12.6 0.6 pad_add_fusion.refs_0_.place_ref
  13.2 0.0 collective-permute-done.refs_2_.refs_5_.refs_1_
  13.2 0.6 collective-permute-done.1.refs_3_.refs_6_.refs_2_
  13.7 3.4 %shard_map.60.refs_3_ = bf16[27,64,128]{2,1,0:T(8,128)(2,1)} custom-call(s32[2]{0:T(128)} %pad_add_fusion.refs_0_.place_ref, bf16[2,64,64,128]{3,2,1,0:T(8,128)(2,1)} %bitcast.7, bf16[2,6,64,128]{3,2,1,0:T(8,128)(2,1)} %collective-permute-done.refs_2_.refs_5_.refs_1_, bf16[2,6,64,128]{3,2,1,0:T(8,128)(2,1)} %collective-permute-done.1.refs_3_.refs_6_.refs_2_, ...), custom_call_target="tpu_custom_call" | custom-call | flops 2000000000 | bytes 6000000 | tf_op jit(solution)/shard_map/pallas_call | solution.py:120
  17.1 1.5 %collective-permute-start.3 = (bf16[27,64,128]{2,1,0:T(8,128)(2,1)}, bf16[27,64,128]{2,1,0:T(8,128)(2,1)}, u32[]{:S(2)}, u32[]{:S(2)}) collective-permute-start(bf16[27,64,128]{2,1,0:T(8,128)(2,1)} %shard_map.60.refs_3_), channel_id=1, source_target_pairs={{1,2},{3,4},{5,6},{2,1},{4,3},{6,5},{9,10},{11,12},{13,14},{10,9},... | collective-permute-start | bytes 1327112 | tf_op jit(solution)/shard_map/ppermute | solution.py:538
  18.6 2.0 %collective-permute-start.2 = (bf16[27,64,128]{2,1,0:T(8,128)(2,1)}, bf16[27,64,128]{2,1,0:T(8,128)(2,1)}, u32[]{:S(2)}, u32[]{:S(2)}) collective-permute-start(bf16[27,64,128]{2,1,0:T(8,128)(2,1)} %shard_map.60.refs_3_), channel_id=1, source_target_pairs={{0,1},{1,0},{2,3},{3,2},{4,5},{5,4},{6,7},{7,6},{8,9},{9,8},{10,11... | collective-permute-start | bytes 1327112 | tf_op jit(solution)/shard_map/ppermute | solution.py:539
  20.7 6.5 %shard_map.66.refs_0_ = bf16[32,64,128]{2,1,0:T(8,128)(2,1)} custom-call(s32[2]{0:T(128)} %pad_add_fusion.refs_0_.place_ref, bf16[2,64,64,128]{3,2,1,0:T(8,128)(2,1)} %bitcast.9, bf16[9,64,128]{2,1,0:T(8,128)(2,1)} %shard_map.65.refs_1_, bf16[9,64,128]{2,1,0:T(8,128)(2,1)} %collective-permute-done.11.refs_2_, ...), custom_call_target="tpu_custom_call" | custom-call | flops 6400000000 | bytes 19200000 | tf_op jit(solution)/shard_map/pallas_call | solution.py:320
  27.2 0.0 collective-permute-start.18
  27.2 1.6 %collective-permute-start.13 = (bf16[32,64,128]{2,1,0:T(8,128)(2,1)}, bf16[32,64,128]{2,1,0:T(8,128)(2,1)}, u32[]{:S(2)}, u32[]{:S(2)}) collective-permute-start(bf16[32,64,128]{2,1,0:T(8,128)(2,1)} %shard_map.66.refs_0_), channel_id=1, source_target_pairs={{0,2},{1,3},{2,4},{3,5},{4,6},{5,7},{6,0},{7,1},{8,10},{9,11},{10,... | collective-permute-start | bytes 1572872 | tf_op jit(solution)/shard_map/ppermute | solution.py:569
  28.8 0.0 collective-permute-done.3.refs_5_
  28.8 0.0 collective-permute-done.2.refs_4_
  28.8 8.0 %shard_map.62.refs_0_ = bf16[32,64,128]{2,1,0:T(8,128)(2,1)} custom-call(s32[2]{0:T(128)} %pad_add_fusion.refs_0_.place_ref, bf16[2,64,64,128]{3,2,1,0:T(8,128)(2,1)} %bitcast.10, bf16[2,6,64,128]{3,2,1,0:T(8,128)(2,1)} %collective-permute-done.refs_2_.refs_5_.refs_1_, bf16[2,6,64,128]{3,2,1,0:T(8,128)(2,1)} %collective-permute-done.1.refs_3_.refs_6_.refs_2_, ...), custom_call_target="tpu_custom_call" | custom-call | flops 6400000000 | bytes 19200000 | tf_op jit(solution)/shard_map/pallas_call | solution.py:320
  36.8 0.3 collective-permute-start.9
  37.1 1.3 %collective-permute-start.4 = (bf16[32,64,128]{2,1,0:T(8,128)(2,1)}, bf16[32,64,128]{2,1,0:T(8,128)(2,1)}, u32[]{:S(2)}, u32[]{:S(2)}) collective-permute-start(bf16[32,64,128]{2,1,0:T(8,128)(2,1)} %shard_map.62.refs_0_), channel_id=1, source_target_pairs={{0,2},{1,3},{2,4},{3,5},{4,6},{5,7},{6,0},{7,1},{8,10},{9,11},{10,... | collective-permute-start | bytes 1572872 | tf_op jit(solution)/shard_map/ppermute | solution.py:569
  38.4 2.8 %collective-permute-done.13.refs_2_ = bf16[32,64,128]{2,1,0:T(8,128)(2,1)} collective-permute-done((bf16[32,64,128]{2,1,0:T(8,128)(2,1)}, bf16[32,64,128]{2,1,0:T(8,128)(2,1)}, u32[]{:S(2)}, u32[]{:S(2)}) %collective-permute-start.13) | collective-permute-done | bytes 524320 | tf_op jit(solution)/shard_map/ppermute | solution.py:569
  41.2 1.6 %collective-permute-start.19 = (bf16[32,64,128]{2,1,0:T(8,128)(2,1)}, bf16[32,64,128]{2,1,0:T(8,128)(2,1)}, u32[]{:S(2)}, u32[]{:S(2)}) collective-permute-start(bf16[32,64,128]{2,1,0:T(8,128)(2,1)} %collective-permute-done.13.refs_2_), channel_id=1, source_target_pairs={{0,1},{1,0},{2,3},{3,2},{4,5},{5,4},{6,7},{7,6},{8,9},{9,8},{10,11... | collective-permute-start | bytes 1572872 | tf_op jit(solution)/shard_map/ppermute | solution.py:570
  42.8 2.9 %collective-permute-start.14 = (bf16[32,64,128]{2,1,0:T(8,128)(2,1)}, bf16[32,64,128]{2,1,0:T(8,128)(2,1)}, u32[]{:S(2)}, u32[]{:S(2)}) collective-permute-start(bf16[32,64,128]{2,1,0:T(8,128)(2,1)} %collective-permute-done.13.refs_2_), channel_id=1, source_target_pairs={{0,2},{1,3},{2,4},{3,5},{4,6},{5,7},{6,0},{7,1},{8,10},{9,11},{10,... | collective-permute-start | bytes 1572872 | tf_op jit(solution)/shard_map/ppermute | solution.py:569
  45.7 9.9 %shard_map.61.left_ref = bf16[64,64,128]{2,1,0:T(8,128)(2,1)} custom-call(s32[2]{0:T(128)} %pad_add_fusion.refs_0_.place_ref, bf16[2,64,64,128]{3,2,1,0:T(8,128)(2,1)} %bitcast.11, bf16[2,6,64,128]{3,2,1,0:T(8,128)(2,1)} %collective-permute-done.refs_2_.refs_5_.refs_1_, bf16[2,6,64,128]{3,2,1,0:T(8,128)(2,1)} %collective-permute-done.1.refs_3_.refs_6_.refs_2_, ...), custom_call_target="tpu_custom_call" | custom-call | flops 12800000000 | bytes 38400000 | tf_op jit(solution)/shard_map/pallas_call | solution.py:320
  55.6 0.0 collective-permute-done.4.refs_2_
  55.6 0.3 collective-permute-start.10
  55.9 1.1 collective-permute-start.5
  57.0 6.7 %collective-permute-done.14.refs_0_ = bf16[32,64,128]{2,1,0:T(8,128)(2,1)} collective-permute-done((bf16[32,64,128]{2,1,0:T(8,128)(2,1)}, bf16[32,64,128]{2,1,0:T(8,128)(2,1)}, u32[]{:S(2)}, u32[]{:S(2)}) %collective-permute-start.14) | collective-permute-done | bytes 524320 | tf_op jit(solution)/shard_map/ppermute | solution.py:569
  63.7 1.6 %collective-permute-start.17 = (bf16[32,64,128]{2,1,0:T(8,128)(2,1)}, bf16[32,64,128]{2,1,0:T(8,128)(2,1)}, u32[]{:S(2)}, u32[]{:S(2)}) collective-permute-start(bf16[32,64,128]{2,1,0:T(8,128)(2,1)} %collective-permute-done.14.refs_0_), channel_id=1, source_target_pairs={{0,1},{1,0},{2,3},{3,2},{4,5},{5,4},{6,7},{7,6},{8,9},{9,8},{10,11... | collective-permute-start | bytes 1572872 | tf_op jit(solution)/shard_map/ppermute | solution.py:570
  65.3 0.0 collective-permute-done.19.refs_3_
  65.3 1.3 %collective-permute-start.15 = (bf16[32,64,128]{2,1,0:T(8,128)(2,1)}, bf16[32,64,128]{2,1,0:T(8,128)(2,1)}, u32[]{:S(2)}, u32[]{:S(2)}) collective-permute-start(bf16[32,64,128]{2,1,0:T(8,128)(2,1)} %collective-permute-done.14.refs_0_), channel_id=1, source_target_pairs={{4,6},{5,7},{12,14},{13,15},{20,22},{21,23},{28,30},{29,31}} | collective-permute-start | bytes 1572872 | tf_op jit(solution)/shard_map/ppermute | solution.py:569
  66.6 6.9 %shard_map.67.refs_2_ = f32[32,80,128]{2,1,0:T(8,128)} custom-call(s32[2]{0:T(128)} %pad_add_fusion.refs_0_.place_ref, s32[2,8]{1,0:T(2,128)} %bitcast.12, bf16[64,64,128]{2,1,0:T(8,128)(2,1)} %shard_map.61.left_ref, bf16[32,64,128]{2,1,0:T(8,128)(2,1)} %shard_map.66.refs_0_, bf16[32,64,128]{2,1,0:T(8,128)(2,1)} %collective-permute-done.18.refs_1_, ...), custom_call_target="tpu_custom_call" | custom-call | flops 6000000000 | bytes 18000000 | tf_op jit(solution)/shard_map/pallas_call | solution.py:454
  73.5 1.4 %collective-permute-done.5.refs_0_ = bf16[32,64,128]{2,1,0:T(8,128)(2,1)} collective-permute-done((bf16[32,64,128]{2,1,0:T(8,128)(2,1)}, bf16[32,64,128]{2,1,0:T(8,128)(2,1)}, u32[]{:S(2)}, u32[]{:S(2)}) %collective-permute-start.5) | collective-permute-done | bytes 524320 | tf_op jit(solution)/shard_map/ppermute | solution.py:569
  74.9 1.6 %collective-permute-start.8 = (bf16[32,64,128]{2,1,0:T(8,128)(2,1)}, bf16[32,64,128]{2,1,0:T(8,128)(2,1)}, u32[]{:S(2)}, u32[]{:S(2)}) collective-permute-start(bf16[32,64,128]{2,1,0:T(8,128)(2,1)} %collective-permute-done.5.refs_0_), channel_id=1, source_target_pairs={{0,1},{1,0},{2,3},{3,2},{4,5},{5,4},{6,7},{7,6},{8,9},{9,8},{10,11... | collective-permute-start | bytes 1572872 | tf_op jit(solution)/shard_map/ppermute | solution.py:570
  76.5 0.0 collective-permute-done.9.refs_1_
  76.5 1.5 %collective-permute-start.6 = (bf16[32,64,128]{2,1,0:T(8,128)(2,1)}, bf16[32,64,128]{2,1,0:T(8,128)(2,1)}, u32[]{:S(2)}, u32[]{:S(2)}) collective-permute-start(bf16[32,64,128]{2,1,0:T(8,128)(2,1)} %collective-permute-done.5.refs_0_), channel_id=1, source_target_pairs={{4,6},{5,7},{12,14},{13,15},{20,22},{21,23},{28,30},{29,31}} | collective-permute-start | bytes 1572872 | tf_op jit(solution)/shard_map/ppermute | solution.py:569
  78.0 0.0 collective-permute-done.10.refs_3_
  78.0 6.9 %shard_map.63.refs_2_ = f32[32,80,128]{2,1,0:T(8,128)} custom-call(s32[2]{0:T(128)} %pad_add_fusion.refs_0_.place_ref, s32[2,8]{1,0:T(2,128)} %bitcast.13, bf16[64,64,128]{2,1,0:T(8,128)(2,1)} %shard_map.61.left_ref, bf16[32,64,128]{2,1,0:T(8,128)(2,1)} %shard_map.62.refs_0_, bf16[32,64,128]{2,1,0:T(8,128)(2,1)} %collective-permute-done.9.refs_1_, ...), custom_call_target="tpu_custom_call" | custom-call | flops 6000000000 | bytes 18000000 | tf_op jit(solution)/shard_map/pallas_call | solution.py:454
  84.9 1.2 %collective-permute-done.15.mine_ref = bf16[32,64,128]{2,1,0:T(8,128)(2,1)} collective-permute-done((bf16[32,64,128]{2,1,0:T(8,128)(2,1)}, bf16[32,64,128]{2,1,0:T(8,128)(2,1)}, u32[]{:S(2)}, u32[]{:S(2)}) %collective-permute-start.15) | collective-permute-done | bytes 524320 | tf_op jit(solution)/shard_map/ppermute | solution.py:569
  86.2 1.6 %collective-permute-start.16 = (bf16[32,64,128]{2,1,0:T(8,128)(2,1)}, bf16[32,64,128]{2,1,0:T(8,128)(2,1)}, u32[]{:S(2)}, u32[]{:S(2)}) collective-permute-start(bf16[32,64,128]{2,1,0:T(8,128)(2,1)} %collective-permute-done.15.mine_ref), channel_id=1, source_target_pairs={{0,1},{1,0},{2,3},{3,2},{4,5},{5,4},{6,7},{7,6},{8,9},{9,8},{10,11... | collective-permute-start | bytes 1572872 | tf_op jit(solution)/shard_map/ppermute | solution.py:570
  87.7 5.1 %shard_map.68.acc_in_ref = f32[32,80,128]{2,1,0:T(8,128)} custom-call(s32[2]{0:T(128)} %pad_add_fusion.refs_0_.place_ref, s32[2,8]{1,0:T(2,128)} %bitcast.14, bf16[64,64,128]{2,1,0:T(8,128)(2,1)} %shard_map.61.left_ref, bf16[32,64,128]{2,1,0:T(8,128)(2,1)} %collective-permute-done.14.refs_0_, ...), custom_call_target="tpu_custom_call", output_to_operand_aliasing={{}: (5, {})} | custom-call | flops 6000000000 | bytes 18000000 | tf_op jit(solution)/shard_map/pallas_call | solution.py:454
  92.9 4.5 %collective-permute-done.6.mine_ref = bf16[32,64,128]{2,1,0:T(8,128)(2,1)} collective-permute-done((bf16[32,64,128]{2,1,0:T(8,128)(2,1)}, bf16[32,64,128]{2,1,0:T(8,128)(2,1)}, u32[]{:S(2)}, u32[]{:S(2)}) %collective-permute-start.6) | collective-permute-done | bytes 524320 | tf_op jit(solution)/shard_map/ppermute | solution.py:569
  97.4 1.0 collective-permute-start.7
  98.4 4.6 %shard_map.64.acc_in_ref = f32[32,80,128]{2,1,0:T(8,128)} custom-call(s32[2]{0:T(128)} %pad_add_fusion.refs_0_.place_ref, s32[2,8]{1,0:T(2,128)} %bitcast.15, bf16[64,64,128]{2,1,0:T(8,128)(2,1)} %shard_map.61.left_ref, bf16[32,64,128]{2,1,0:T(8,128)(2,1)} %collective-permute-done.5.refs_0_, ...), custom_call_target="tpu_custom_call", output_to_operand_aliasing={{}: (5, {})} | custom-call | flops 6000000000 | bytes 18000000 | tf_op jit(solution)/shard_map/pallas_call | solution.py:454
  103.0 0.0 collective-permute-done.16.theirs_ref
  103.0 5.1 %shard_map.69 = (bf16[64,64,128]{2,1,0:T(8,128)(2,1)}, f32[64,128]{1,0:T(8,128)}) custom-call(s32[2]{0:T(128)} %pad_add_fusion.refs_0_.place_ref, s32[2,8]{1,0:T(2,128)} %bitcast.16, bf16[64,64,128]{2,1,0:T(8,128)(2,1)} %shard_map.61.left_ref, bf16[32,64,128]{2,1,0:T(8,128)(2,1)} %collective-permute-done.15.mine_ref, ...), custom_call_target="tpu_custom_call" | custom-call | flops 4000000000 | bytes 12000000 | tf_op jit(solution)/shard_map/pallas_call | solution.py:483
  108.1 4.0 %shard_map.70 = (bf16[64,64,128]{2,1,0:T(8,128)(2,1)}, f32[64,128]{1,0:T(8,128)}) custom-call(s32[2]{0:T(128)} %pad_add_fusion.refs_0_.place_ref, s32[2,8]{1,0:T(2,128)} %bitcast.17, bf16[64,64,128]{2,1,0:T(8,128)(2,1)} %shard_map.61.left_ref, bf16[32,64,128]{2,1,0:T(8,128)(2,1)} %collective-permute-done.6.mine_ref, ...), custom_call_target="tpu_custom_call", output_to_operand_aliasing={{0}: (6, {}), {1}: (7, {})} | custom-call | flops 4000000000 | bytes 12000000 | tf_op jit(solution)/shard_map/pallas_call | solution.py:483
  (6 shorter events, 0.0 us)
Async XLA Ops:
  2.5 10.7 %collective-permute-start = (bf16[2,6,64,128]{3,2,1,0:T(8,128)(2,1)}, bf16[2,6,64,128]{3,2,1,0:T(8,128)(2,1)}, u32[]{:S(2)}, u32[]{:S(2)}) collective-permute-start(bf16[2,6,64,128]{3,2,1,0:T(8,128)(2,1)} %get-tuple-element.6), channel_id=1, source_target_pairs={{0,8},{8,16},{16,24},{24,0},{1,9},{9,17},{17,25},{25,1},{2,10},{10... | collective-permute-start | bytes 589832 | tf_op jit(solution)/shard_map/ppermute | solution.py:549
  3.7 10.1 %collective-permute-start.1 = (bf16[2,6,64,128]{3,2,1,0:T(8,128)(2,1)}, bf16[2,6,64,128]{3,2,1,0:T(8,128)(2,1)}, u32[]{:S(2)}, u32[]{:S(2)}) collective-permute-start(bf16[2,6,64,128]{3,2,1,0:T(8,128)(2,1)} %get-tuple-element.7), channel_id=1, source_target_pairs={{8,0},{16,8},{24,16},{0,24},{9,1},{17,9},{25,17},{1,25},{10,2},{18... | collective-permute-start | bytes 589832 | tf_op jit(solution)/shard_map/ppermute | solution.py:550
  11.3 9.3 %collective-permute-start.12 = (bf16[9,64,128]{2,1,0:T(8,128)(2,1)}, bf16[9,64,128]{2,1,0:T(8,128)(2,1)}, u32[]{:S(2)}, u32[]{:S(2)}) collective-permute-start(bf16[9,64,128]{2,1,0:T(8,128)(2,1)} %shard_map.65.refs_1_), channel_id=1, source_target_pairs={{1,2},{3,4},{5,6},{2,1},{4,3},{6,5},{0,7},{7,0},{9,10},{11,12},{13... | collective-permute-start | bytes 442376 | tf_op jit(solution)/shard_map/ppermute | solution.py:538
  12.0 8.7 %collective-permute-start.11 = (bf16[9,64,128]{2,1,0:T(8,128)(2,1)}, bf16[9,64,128]{2,1,0:T(8,128)(2,1)}, u32[]{:S(2)}, u32[]{:S(2)}) collective-permute-start(bf16[9,64,128]{2,1,0:T(8,128)(2,1)} %shard_map.65.refs_1_), channel_id=1, source_target_pairs={{0,1},{1,0},{2,3},{3,2},{4,5},{5,4},{6,7},{7,6},{8,9},{9,8},{10,11... | collective-permute-start | bytes 442376 | tf_op jit(solution)/shard_map/ppermute | solution.py:539
  17.1 11.7 %collective-permute-start.3 = (bf16[27,64,128]{2,1,0:T(8,128)(2,1)}, bf16[27,64,128]{2,1,0:T(8,128)(2,1)}, u32[]{:S(2)}, u32[]{:S(2)}) collective-permute-start(bf16[27,64,128]{2,1,0:T(8,128)(2,1)} %shard_map.60.refs_3_), channel_id=1, source_target_pairs={{1,2},{3,4},{5,6},{2,1},{4,3},{6,5},{9,10},{11,12},{13,14},{10,9},... | collective-permute-start | bytes 1327112 | tf_op jit(solution)/shard_map/ppermute | solution.py:538
  18.6 10.2 %collective-permute-start.2 = (bf16[27,64,128]{2,1,0:T(8,128)(2,1)}, bf16[27,64,128]{2,1,0:T(8,128)(2,1)}, u32[]{:S(2)}, u32[]{:S(2)}) collective-permute-start(bf16[27,64,128]{2,1,0:T(8,128)(2,1)} %shard_map.60.refs_3_), channel_id=1, source_target_pairs={{0,1},{1,0},{2,3},{3,2},{4,5},{5,4},{6,7},{7,6},{8,9},{9,8},{10,11... | collective-permute-start | bytes 1327112 | tf_op jit(solution)/shard_map/ppermute | solution.py:539
  27.2 28.7 %collective-permute-start.18 = (bf16[32,64,128]{2,1,0:T(8,128)(2,1)}, bf16[32,64,128]{2,1,0:T(8,128)(2,1)}, u32[]{:S(2)}, u32[]{:S(2)}) collective-permute-start(bf16[32,64,128]{2,1,0:T(8,128)(2,1)} %shard_map.66.refs_0_), channel_id=1, source_target_pairs={{0,1},{1,0},{2,3},{3,2},{4,5},{5,4},{6,7},{7,6},{8,9},{9,8},{10,11... | collective-permute-start | bytes 1572872 | tf_op jit(solution)/shard_map/ppermute | solution.py:570
  27.2 14.0 %collective-permute-start.13 = (bf16[32,64,128]{2,1,0:T(8,128)(2,1)}, bf16[32,64,128]{2,1,0:T(8,128)(2,1)}, u32[]{:S(2)}, u32[]{:S(2)}) collective-permute-start(bf16[32,64,128]{2,1,0:T(8,128)(2,1)} %shard_map.66.refs_0_), channel_id=1, source_target_pairs={{0,2},{1,3},{2,4},{3,5},{4,6},{5,7},{6,0},{7,1},{8,10},{9,11},{10,... | collective-permute-start | bytes 1572872 | tf_op jit(solution)/shard_map/ppermute | solution.py:569
  36.8 39.7 %collective-permute-start.9 = (bf16[32,64,128]{2,1,0:T(8,128)(2,1)}, bf16[32,64,128]{2,1,0:T(8,128)(2,1)}, u32[]{:S(2)}, u32[]{:S(2)}) collective-permute-start(bf16[32,64,128]{2,1,0:T(8,128)(2,1)} %shard_map.62.refs_0_), channel_id=1, source_target_pairs={{0,1},{1,0},{2,3},{3,2},{4,5},{5,4},{6,7},{7,6},{8,9},{9,8},{10,11... | collective-permute-start | bytes 1572872 | tf_op jit(solution)/shard_map/ppermute | solution.py:570
  37.1 18.4 %collective-permute-start.4 = (bf16[32,64,128]{2,1,0:T(8,128)(2,1)}, bf16[32,64,128]{2,1,0:T(8,128)(2,1)}, u32[]{:S(2)}, u32[]{:S(2)}) collective-permute-start(bf16[32,64,128]{2,1,0:T(8,128)(2,1)} %shard_map.62.refs_0_), channel_id=1, source_target_pairs={{0,2},{1,3},{2,4},{3,5},{4,6},{5,7},{6,0},{7,1},{8,10},{9,11},{10,... | collective-permute-start | bytes 1572872 | tf_op jit(solution)/shard_map/ppermute | solution.py:569
  41.2 24.0 %collective-permute-start.19 = (bf16[32,64,128]{2,1,0:T(8,128)(2,1)}, bf16[32,64,128]{2,1,0:T(8,128)(2,1)}, u32[]{:S(2)}, u32[]{:S(2)}) collective-permute-start(bf16[32,64,128]{2,1,0:T(8,128)(2,1)} %collective-permute-done.13.refs_2_), channel_id=1, source_target_pairs={{0,1},{1,0},{2,3},{3,2},{4,5},{5,4},{6,7},{7,6},{8,9},{9,8},{10,11... | collective-permute-start | bytes 1572872 | tf_op jit(solution)/shard_map/ppermute | solution.py:570
  42.8 20.9 %collective-permute-start.14 = (bf16[32,64,128]{2,1,0:T(8,128)(2,1)}, bf16[32,64,128]{2,1,0:T(8,128)(2,1)}, u32[]{:S(2)}, u32[]{:S(2)}) collective-permute-start(bf16[32,64,128]{2,1,0:T(8,128)(2,1)} %collective-permute-done.13.refs_2_), channel_id=1, source_target_pairs={{0,2},{1,3},{2,4},{3,5},{4,6},{5,7},{6,0},{7,1},{8,10},{9,11},{10,... | collective-permute-start | bytes 1572872 | tf_op jit(solution)/shard_map/ppermute | solution.py:569
  55.6 22.4 %collective-permute-start.10 = (bf16[32,64,128]{2,1,0:T(8,128)(2,1)}, bf16[32,64,128]{2,1,0:T(8,128)(2,1)}, u32[]{:S(2)}, u32[]{:S(2)}) collective-permute-start(bf16[32,64,128]{2,1,0:T(8,128)(2,1)} %collective-permute-done.4.refs_2_), channel_id=1, source_target_pairs={{0,1},{1,0},{2,3},{3,2},{4,5},{5,4},{6,7},{7,6},{8,9},{9,8},{10,11... | collective-permute-start | bytes 1572872 | tf_op jit(solution)/shard_map/ppermute | solution.py:570
  55.9 19.0 %collective-permute-start.5 = (bf16[32,64,128]{2,1,0:T(8,128)(2,1)}, bf16[32,64,128]{2,1,0:T(8,128)(2,1)}, u32[]{:S(2)}, u32[]{:S(2)}) collective-permute-start(bf16[32,64,128]{2,1,0:T(8,128)(2,1)} %collective-permute-done.4.refs_2_), channel_id=1, source_target_pairs={{0,2},{1,3},{2,4},{3,5},{4,6},{5,7},{6,0},{7,1},{8,10},{9,11},{10,... | collective-permute-start | bytes 1572872 | tf_op jit(solution)/shard_map/ppermute | solution.py:569
  63.7 24.0 %collective-permute-start.17 = (bf16[32,64,128]{2,1,0:T(8,128)(2,1)}, bf16[32,64,128]{2,1,0:T(8,128)(2,1)}, u32[]{:S(2)}, u32[]{:S(2)}) collective-permute-start(bf16[32,64,128]{2,1,0:T(8,128)(2,1)} %collective-permute-done.14.refs_0_), channel_id=1, source_target_pairs={{0,1},{1,0},{2,3},{3,2},{4,5},{5,4},{6,7},{7,6},{8,9},{9,8},{10,11... | collective-permute-start | bytes 1572872 | tf_op jit(solution)/shard_map/ppermute | solution.py:570
  65.3 20.9 %collective-permute-start.15 = (bf16[32,64,128]{2,1,0:T(8,128)(2,1)}, bf16[32,64,128]{2,1,0:T(8,128)(2,1)}, u32[]{:S(2)}, u32[]{:S(2)}) collective-permute-start(bf16[32,64,128]{2,1,0:T(8,128)(2,1)} %collective-permute-done.14.refs_0_), channel_id=1, source_target_pairs={{4,6},{5,7},{12,14},{13,15},{20,22},{21,23},{28,30},{29,31}} | collective-permute-start | bytes 1572872 | tf_op jit(solution)/shard_map/ppermute | solution.py:569
  74.9 23.5 %collective-permute-start.8 = (bf16[32,64,128]{2,1,0:T(8,128)(2,1)}, bf16[32,64,128]{2,1,0:T(8,128)(2,1)}, u32[]{:S(2)}, u32[]{:S(2)}) collective-permute-start(bf16[32,64,128]{2,1,0:T(8,128)(2,1)} %collective-permute-done.5.refs_0_), channel_id=1, source_target_pairs={{0,1},{1,0},{2,3},{3,2},{4,5},{5,4},{6,7},{7,6},{8,9},{9,8},{10,11... | collective-permute-start | bytes 1572872 | tf_op jit(solution)/shard_map/ppermute | solution.py:570
  76.5 20.9 %collective-permute-start.6 = (bf16[32,64,128]{2,1,0:T(8,128)(2,1)}, bf16[32,64,128]{2,1,0:T(8,128)(2,1)}, u32[]{:S(2)}, u32[]{:S(2)}) collective-permute-start(bf16[32,64,128]{2,1,0:T(8,128)(2,1)} %collective-permute-done.5.refs_0_), channel_id=1, source_target_pairs={{4,6},{5,7},{12,14},{13,15},{20,22},{21,23},{28,30},{29,31}} | collective-permute-start | bytes 1572872 | tf_op jit(solution)/shard_map/ppermute | solution.py:569
  86.2 16.8 %collective-permute-start.16 = (bf16[32,64,128]{2,1,0:T(8,128)(2,1)}, bf16[32,64,128]{2,1,0:T(8,128)(2,1)}, u32[]{:S(2)}, u32[]{:S(2)}) collective-permute-start(bf16[32,64,128]{2,1,0:T(8,128)(2,1)} %collective-permute-done.15.mine_ref), channel_id=1, source_target_pairs={{0,1},{1,0},{2,3},{3,2},{4,5},{5,4},{6,7},{7,6},{8,9},{9,8},{10,11... | collective-permute-start | bytes 1572872 | tf_op jit(solution)/shard_map/ppermute | solution.py:570
  97.4 10.7 %collective-permute-start.7 = (bf16[32,64,128]{2,1,0:T(8,128)(2,1)}, bf16[32,64,128]{2,1,0:T(8,128)(2,1)}, u32[]{:S(2)}, u32[]{:S(2)}) collective-permute-start(bf16[32,64,128]{2,1,0:T(8,128)(2,1)} %collective-permute-done.6.mine_ref), channel_id=1, source_target_pairs={{0,1},{1,0},{2,3},{3,2},{4,5},{5,4},{6,7},{7,6},{8,9},{9,8},{10,11... | collective-permute-start | bytes 1572872 | tf_op jit(solution)/shard_map/ppermute | solution.py:570

commit v13 on v12

--- a/solution.py
+++ b/solution.py
@@ -350,7 +350,7 @@
     )(place, *pieces, *edges, w1, w2)
 
 
-def add_step(place_ref, range_ref, group, step, left_ref, mine_ref, theirs_ref, acc_ref, bias_ref, scores_ref):
+def add_step(place_ref, range_ref, group, step, left_ref, key_refs, acc_ref, bias_ref, scores_ref, which=None):
     _, channels, segment = left_ref.shape
     block = place_ref[1]
     low = segment * range_ref[0, group]
@@ -362,24 +362,26 @@
 
     def key_column(shape):
         column = lane_iota(shape)
-        own = column < segment
+        own = column < segment if which is None else which == "mine"
         return column % segment + segment * jnp.where(own, odd, 1 - odd)
+
+    width = len(key_refs) * segment
 
     @pl.when(active)
     def _():
-        wide = (segment, 2 * segment)
+        wide = (segment, width)
         offsets = base + lax.broadcasted_iota(jnp.int32, wide, 0) - key_column(wide)
         inside = (offsets >= low) & (offsets < high)
-        bias_ref[...] = jnp.where(inside, 0.0, -1e30)
-        kind = lax.broadcasted_iota(jnp.int32, (EXTRA, 2 * segment), 0)
-        column = key_column((EXTRA, 2 * segment))
+        bias_ref[:, :width] = jnp.where(inside, 0.0, -1e30)
+        kind = lax.broadcasted_iota(jnp.int32, (EXTRA, width), 0)
+        column = key_column((EXTRA, width))
         extra = jnp.where(kind == 0, 1, jnp.where(kind == 1, column, jnp.where(kind == 2, step, 0)))
         extra = extra.astype(jnp.float32).astype(jnp.bfloat16)
         rows = left_ref.shape[0]
 
         def score(r):
-            keys = jnp.concatenate([mine_ref[r], theirs_ref[r]], axis=1)
-            scores_ref[r % 2] = lax.dot_general(
+            keys = jnp.concatenate([ref[r] for ref in key_refs], axis=1)
+            scores_ref[r % 2, :, :width] = lax.dot_general(
                 left_ref[r], keys, (((0,), (0,)), ((), ())), preferred_element_type=jnp.float32
             )
 
@@ -387,8 +389,8 @@
         for r in range(rows):
             if r + 1 < rows:
                 score(r + 1)
-            weights = jnp.exp2(scores_ref[r % 2] * scale + bias_ref[...]).astype(jnp.bfloat16)
-            keys = jnp.concatenate([mine_ref[r], theirs_ref[r]], axis=1)
+            weights = jnp.exp2(scores_ref[r % 2, :, :width] * scale + bias_ref[:, :width]).astype(jnp.bfloat16)
+            keys = jnp.concatenate([ref[r] for ref in key_refs], axis=1)
             extended = jnp.concatenate([keys, extra], axis=0)
             acc_ref[r] += lax.dot_general(
                 extended, weights, (((1,), (1,)), ((), ())), preferred_element_type=jnp.float32
@@ -400,26 +402,26 @@
     return i + quarter if inner else jnp.where(i < quarter, i, i + 2 * quarter)
 
 
-def gather_kernel(place_ref, range_ref, left_ref, *refs, inner, groups, start, count):
-    keys, (acc_ref, bias_ref, scores_ref) = refs[: 2 * count], refs[-3:]
+def gather_kernel(place_ref, range_ref, left_ref, *refs, inner, groups, start, per_step, which):
+    acc_ref, bias_ref, scores_ref = refs[-3:]
+    keys = refs[: -4 if start else -3]
     group = group_of(pl.program_id(0), inner, groups)
-    acc_ref[...] = refs[2 * count][...] if start else jnp.zeros_like(acc_ref)
-    for index in range(count):
+    acc_ref[...] = refs[-4][...] if start else jnp.zeros_like(acc_ref)
+    for index in range(len(keys) // per_step):
         add_step(
-            place_ref, range_ref, group, start + index, left_ref, keys[2 * index], keys[2 * index + 1],
-            acc_ref, bias_ref, scores_ref,
+            place_ref, range_ref, group, start + index, left_ref,
+            keys[per_step * index : per_step * (index + 1)], acc_ref, bias_ref, scores_ref, which,
         )
 
 
-def finish_kernel(
-    place_ref, range_ref, left_ref, mine_ref, theirs_ref, acc_in_ref, *refs, inner, groups, step
-):
+def finish_kernel(place_ref, range_ref, left_ref, *refs, inner, groups, step, per_step, which):
+    keys, acc_in_ref = refs[:per_step], refs[per_step]
     matched_ref, disparity_ref, acc_ref, bias_ref, scores_ref, rows_ref = refs[-6:]
     group = group_of(pl.program_id(0), inner, groups)
     rows, channels, segment = left_ref.shape
     acc_ref[...] = acc_in_ref[...]
     add_step(
-        place_ref, range_ref, group, step, left_ref, mine_ref, theirs_ref, acc_ref, bias_ref, scores_ref
+        place_ref, range_ref, group, step, left_ref, keys, acc_ref, bias_ref, scores_ref, which
     )
     block = place_ref[1]
     low = segment * range_ref[0, group]
@@ -442,7 +444,7 @@
     matched_ref[...] = jnp.swapaxes(rows_ref[...].astype(jnp.bfloat16), 0, 1)
 
 
-def correlate(place, ranges, left, keys, acc, start, inner):
+def correlate(place, ranges, left, keys, acc, start, inner, which=None):
     rows, channels, segment = left.shape
     groups = rows // RG
     own_groups = keys[0][0].shape[0] // RG
@@ -452,27 +454,29 @@
     acc_spec = pl.BlockSpec((RG, held, segment), lambda i: (i, 0, 0))
     given = (acc,) if start else ()
     return pl.pallas_call(
-        functools.partial(gather_kernel, inner=inner, groups=groups, start=start, count=len(keys)),
+        functools.partial(
+            gather_kernel, inner=inner, groups=groups, start=start, per_step=len(keys[0]), which=which
+        ),
         out_shape=jax.ShapeDtypeStruct((own_groups * RG, held, segment), jnp.float32),
         grid=(own_groups,),
         in_specs=[smem, smem, pl.BlockSpec(block, lambda i: (group_of(i, inner, groups), 0, 0))]
-        + [pl.BlockSpec(block, lambda i: (i, 0, 0))] * (2 * len(keys))
+        + [pl.BlockSpec(block, lambda i: (i, 0, 0))] * sum(map(len, keys))
         + [acc_spec] * len(given),
         out_specs=acc_spec,
         scratch_shapes=[
             pltpu.VMEM((segment, 2 * segment), jnp.float32),
             pltpu.VMEM((2, segment, 2 * segment), jnp.float32),
         ],
-        input_output_aliases={3 + 2 * len(keys): 0} if given else {},
+        input_output_aliases={3 + sum(map(len, keys)): 0} if given else {},
         compiler_params=pltpu.CompilerParams(vmem_limit_bytes=VMEM_LIMIT),
         cost_estimate=cost(1.5 * own_groups),
     )(place, ranges, left, *[a for pair in keys for a in pair], *given)
 
 
-def finish(place, ranges, left, pair, acc, outs, inner, step):
+def finish(place, ranges, left, keys, acc, outs, inner, step, which=None):
     rows, channels, segment = left.shape
     groups = rows // RG
-    own_groups = pair[0].shape[0] // RG
+    own_groups = keys[0].shape[0] // RG
     block = (RG, channels, segment)
     smem = pl.BlockSpec(memory_space=pltpu.SMEM)
 
@@ -481,7 +485,9 @@
 
     given = () if outs is None else tuple(outs)
     return pl.pallas_call(
-        functools.partial(finish_kernel, inner=inner, groups=groups, step=step),
+        functools.partial(
+            finish_kernel, inner=inner, groups=groups, step=step, per_step=len(keys), which=which
+        ),
         out_shape=(
             jax.ShapeDtypeStruct((channels, rows, segment), jnp.bfloat16),
             jax.ShapeDtypeStruct((rows, segment), jnp.float32),
@@ -491,8 +497,7 @@
             smem,
             smem,
             pl.BlockSpec(block, lambda i: (group(i), 0, 0)),
-            pl.BlockSpec(block, lambda i: (i, 0, 0)),
-            pl.BlockSpec(block, lambda i: (i, 0, 0)),
+            *[pl.BlockSpec(block, lambda i: (i, 0, 0)) for _ in keys],
             pl.BlockSpec((RG, channels + EXTRA, segment), lambda i: (i, 0, 0)),
         ]
         + [pl.BlockSpec(memory_space=pl.ANY)] * len(given),
@@ -506,10 +511,10 @@
             pltpu.VMEM((2, segment, 2 * segment), jnp.float32),
             pltpu.VMEM((RG, channels, segment), jnp.float32),
         ],
-        input_output_aliases={6: 0, 7: 1} if given else {},
+        input_output_aliases={4 + len(keys): 0, 5 + len(keys): 1} if given else {},
         compiler_params=pltpu.CompilerParams(vmem_limit_bytes=VMEM_LIMIT),
         cost_estimate=cost(own_groups),
-    )(place, ranges, left, *pair, acc, *given)
+    )(place, ranges, left, *keys, acc, *given)
 
 
 def both_ways(pairs):
@@ -579,7 +584,9 @@
     keys_a, keys_b = chain(right_a), chain(right_b)
     acc_a, acc_b = totals(keys_a, True), totals(keys_b, False)
     outs = finish(place, ranges, left, keys_a[steps], acc_a, None, True, steps)
-    return finish(place, ranges, left, keys_b[steps], acc_b, outs, False, steps)
+    mine, theirs = keys_b[steps]
+    acc_b = correlate(place, ranges, left, [(mine,)], acc_b, steps, False, "mine")
+    return finish(place, ranges, left, (theirs,), acc_b, outs, False, steps, "theirs")
 
 
 def solution(mesh):

time: 113 us -> 118 us (1.044)
  the two profiles are of different devices: /device:TPU:25 before, /device:TPU:30 now
where the time goes in v13:
time: 118 us; the launch traced here: 117 us
  Pallas kernels  69 us (58%)
  waiting for transfers between devices  27.1 us (23%)
  starting transfers between devices  15.4 us (13%)
  local copies, waits for them, and re-layouts  4.28 us (4%)
    pallas_call x5, Pallas kernels, correlate(): pl.pallas_call(functools.partial(gather_kernel, inner=inner, groups=group...  27.2 us
    ppermute x6, waiting for transfers between devices, chain(): mine = lax.ppermute(mine, 'cols', hop if step < steps else last_hop)  25.5 us
    pallas_call x3, Pallas kernels, unit_features(): pl.pallas_call(functools.partial(feature_kernel, spacing=spacing, offset=...  24.3 us
    ppermute x6, starting transfers between devices, chain(): mine = lax.ppermute(mine, 'cols', hop if step < steps else last_hop)  10.2 us
    pallas_call x2, Pallas kernels, finish(): pl.pallas_call(functools.partial(finish_kernel, inner=inner, groups=group...  9.97 us
    pallas_call x2, Pallas kernels, pack_edges(): pl.pallas_call(functools.partial(pack_kernel, images=tuple((chunks for _,...  5.66 us
    unnamed x1, local copies, waits for them, and re-layouts  4.28 us
  transfers between devices with their start and end apart: 20, of which 6 were waited for; matrix products, arithmetic and copies ran while one was open for 4% of the time, Pallas kernels for 53%

profile of v13, /device:TPU:30, one launch (start us, length us, event | category | flops | bytes accessed | tf_op | source)
XLA Modules:
  0.0 117.2 jit_solution(5069963546733579934)
XLA Ops:
  0.6 1.8 %shard_map.59 = (bf16[2,6,64,128]{3,2,1,0:T(8,128)(2,1)}, bf16[2,6,64,128]{3,2,1,0:T(8,128)(2,1)}) custom-call(bf16[2,64,64,128]{3,2,1,0:T(8,128)(2,1)} %high_ref.1, bf16[2,64,64,128]{3,2,1,0:T(8,128)(2,1)} %high_ref.1), custom_call_target="tpu_custom_call" | custom-call | flops 1000000000 | bytes 3000000 | tf_op jit(solution)/shard_map/pallas_call | solution.py:52
  2.5 0.5 collective-permute-start
  2.9 1.5 %collective-permute-start.1 = (bf16[2,6,64,128]{3,2,1,0:T(8,128)(2,1)}, bf16[2,6,64,128]{3,2,1,0:T(8,128)(2,1)}, u32[]{:S(2)}, u32[]{:S(2)}) collective-permute-start(bf16[2,6,64,128]{3,2,1,0:T(8,128)(2,1)} %get-tuple-element.7), channel_id=1, source_target_pairs={{8,0},{16,8},{24,16},{0,24},{9,1},{17,9},{25,17},{1,25},{10,2},{18... | collective-permute-start | bytes 589832 | tf_op jit(solution)/shard_map/ppermute | solution.py:555
  4.5 4.3 %copy.13 = bf16[2,64,64,128]{3,1,2,0:T(8,128)(2,1)} copy(bf16[2,64,64,128]{3,2,1,0:T(8,128)(2,1)} %high_ref.1) | data formatting | bytes 4194304 | tf_op args[0]
  8.8 2.3 %shard_map.66.refs_1_ = bf16[9,64,128]{2,1,0:T(8,128)(2,1)} custom-call(bf16[2,64,64,128]{3,2,1,0:T(8,128)(2,1)} %bitcast.6), custom_call_target="tpu_custom_call" | custom-call | flops 2000000000 | bytes 6000000 | tf_op jit(solution)/shard_map/pallas_call | solution.py:120
  11.0 0.0 collective-permute-start.12
  11.0 0.3 collective-permute-start.11
  11.4 0.7 pad_add_fusion.refs_0_.place_ref
  12.0 0.0 collective-permute-done.refs_2_.refs_5_.refs_1_
  12.0 1.6 %collective-permute-done.1.refs_3_.refs_6_.refs_2_ = bf16[2,6,64,128]{3,2,1,0:T(8,128)(2,1)} collective-permute-done((bf16[2,6,64,128]{3,2,1,0:T(8,128)(2,1)}, bf16[2,6,64,128]{3,2,1,0:T(8,128)(2,1)}, u32[]{:S(2)}, u32[]{:S(2)}) %collective-permute-start.1) | collective-permute-done | bytes 196640 | tf_op jit(solution)/shard_map/ppermute | solution.py:555
  13.6 3.4 %shard_map.60.refs_3_ = bf16[27,64,128]{2,1,0:T(8,128)(2,1)} custom-call(s32[2]{0:T(128)} %pad_add_fusion.refs_0_.place_ref, bf16[2,64,64,128]{3,2,1,0:T(8,128)(2,1)} %bitcast.7, bf16[2,6,64,128]{3,2,1,0:T(8,128)(2,1)} %collective-permute-done.refs_2_.refs_5_.refs_1_, bf16[2,6,64,128]{3,2,1,0:T(8,128)(2,1)} %collective-permute-done.1.refs_3_.refs_6_.refs_2_, ...), custom_call_target="tpu_custom_call" | custom-call | flops 2000000000 | bytes 6000000 | tf_op jit(solution)/shard_map/pallas_call | solution.py:120
  17.0 1.9 %collective-permute-start.3 = (bf16[27,64,128]{2,1,0:T(8,128)(2,1)}, bf16[27,64,128]{2,1,0:T(8,128)(2,1)}, u32[]{:S(2)}, u32[]{:S(2)}) collective-permute-start(bf16[27,64,128]{2,1,0:T(8,128)(2,1)} %shard_map.60.refs_3_), channel_id=1, source_target_pairs={{1,2},{3,4},{5,6},{2,1},{4,3},{6,5},{9,10},{11,12},{13,14},{10,9},... | collective-permute-start | bytes 1327112 | tf_op jit(solution)/shard_map/ppermute | solution.py:543
  18.9 0.1 collective-permute-start.2
  19.0 0.0 collective-permute-done.12.refs_3_
  19.0 0.0 collective-permute-done.11.refs_2_
  19.0 6.5 %shard_map.67.refs_0_ = bf16[32,64,128]{2,1,0:T(8,128)(2,1)} custom-call(s32[2]{0:T(128)} %pad_add_fusion.refs_0_.place_ref, bf16[2,64,64,128]{3,2,1,0:T(8,128)(2,1)} %bitcast.9, bf16[9,64,128]{2,1,0:T(8,128)(2,1)} %shard_map.66.refs_1_, bf16[9,64,128]{2,1,0:T(8,128)(2,1)} %collective-permute-done.11.refs_2_, ...), custom_call_target="tpu_custom_call" | custom-call | flops 6400000000 | bytes 19200000 | tf_op jit(solution)/shard_map/pallas_call | solution.py:320
  25.5 0.5 collective-permute-start.18
  25.9 1.4 %collective-permute-start.13 = (bf16[32,64,128]{2,1,0:T(8,128)(2,1)}, bf16[32,64,128]{2,1,0:T(8,128)(2,1)}, u32[]{:S(2)}, u32[]{:S(2)}) collective-permute-start(bf16[32,64,128]{2,1,0:T(8,128)(2,1)} %shard_map.67.refs_0_), channel_id=1, source_target_pairs={{0,2},{1,3},{2,4},{3,5},{4,6},{5,7},{6,0},{7,1},{8,10},{9,11},{10,... | collective-permute-start | bytes 1572872 | tf_op jit(solution)/shard_map/ppermute | solution.py:574
  27.4 8.0 %shard_map.62.refs_0_ = bf16[32,64,128]{2,1,0:T(8,128)(2,1)} custom-call(s32[2]{0:T(128)} %pad_add_fusion.refs_0_.place_ref, bf16[2,64,64,128]{3,2,1,0:T(8,128)(2,1)} %bitcast.10, bf16[2,6,64,128]{3,2,1,0:T(8,128)(2,1)} %collective-permute-done.refs_2_.refs_5_.refs_1_, bf16[2,6,64,128]{3,2,1,0:T(8,128)(2,1)} %collective-permute-done.1.refs_3_.refs_6_.refs_2_, ...), custom_call_target="tpu_custom_call" | custom-call | flops 6400000000 | bytes 19200000 | tf_op jit(solution)/shard_map/pallas_call | solution.py:320
  35.4 0.2 collective-permute-start.9
  35.6 1.6 %collective-permute-start.4 = (bf16[32,64,128]{2,1,0:T(8,128)(2,1)}, bf16[32,64,128]{2,1,0:T(8,128)(2,1)}, u32[]{:S(2)}, u32[]{:S(2)}) collective-permute-start(bf16[32,64,128]{2,1,0:T(8,128)(2,1)} %shard_map.62.refs_0_), channel_id=1, source_target_pairs={{0,2},{1,3},{2,4},{3,5},{4,6},{5,7},{6,0},{7,1},{8,10},{9,11},{10,... | collective-permute-start | bytes 1572872 | tf_op jit(solution)/shard_map/ppermute | solution.py:574
  37.2 3.9 %collective-permute-done.13.refs_2_ = bf16[32,64,128]{2,1,0:T(8,128)(2,1)} collective-permute-done((bf16[32,64,128]{2,1,0:T(8,128)(2,1)}, bf16[32,64,128]{2,1,0:T(8,128)(2,1)}, u32[]{:S(2)}, u32[]{:S(2)}) %collective-permute-start.13) | collective-permute-done | bytes 524320 | tf_op jit(solution)/shard_map/ppermute | solution.py:574
  41.1 3.2 %collective-permute-start.14 = (bf16[32,64,128]{2,1,0:T(8,128)(2,1)}, bf16[32,64,128]{2,1,0:T(8,128)(2,1)}, u32[]{:S(2)}, u32[]{:S(2)}) collective-permute-start(bf16[32,64,128]{2,1,0:T(8,128)(2,1)} %collective-permute-done.13.refs_2_), channel_id=1, source_target_pairs={{0,2},{1,3},{2,4},{3,5},{4,6},{5,7},{6,0},{7,1},{8,10},{9,11},{10,... | collective-permute-start | bytes 1572872 | tf_op jit(solution)/shard_map/ppermute | solution.py:574
  44.3 9.8 %shard_map.61.left_ref = bf16[64,64,128]{2,1,0:T(8,128)(2,1)} custom-call(s32[2]{0:T(128)} %pad_add_fusion.refs_0_.place_ref, bf16[2,64,64,128]{3,2,1,0:T(8,128)(2,1)} %bitcast.11, bf16[2,6,64,128]{3,2,1,0:T(8,128)(2,1)} %collective-permute-done.refs_2_.refs_5_.refs_1_, bf16[2,6,64,128]{3,2,1,0:T(8,128)(2,1)} %collective-permute-done.1.refs_3_.refs_6_.refs_2_, ...), custom_call_target="tpu_custom_call" | custom-call | flops 12800000000 | bytes 38400000 | tf_op jit(solution)/shard_map/pallas_call | solution.py:320
  54.1 0.0 collective-permute-done.4.refs_2_
  54.1 0.2 collective-permute-start.10
  54.3 1.2 %collective-permute-start.5 = (bf16[32,64,128]{2,1,0:T(8,128)(2,1)}, bf16[32,64,128]{2,1,0:T(8,128)(2,1)}, u32[]{:S(2)}, u32[]{:S(2)}) collective-permute-start(bf16[32,64,128]{2,1,0:T(8,128)(2,1)} %collective-permute-done.4.refs_2_), channel_id=1, source_target_pairs={{0,2},{1,3},{2,4},{3,5},{4,6},{5,7},{6,0},{7,1},{8,10},{9,11},{10,... | collective-permute-start | bytes 1572872 | tf_op jit(solution)/shard_map/ppermute | solution.py:574
  55.5 8.0 %collective-permute-done.14.refs_0_ = bf16[32,64,128]{2,1,0:T(8,128)(2,1)} collective-permute-done((bf16[32,64,128]{2,1,0:T(8,128)(2,1)}, bf16[32,64,128]{2,1,0:T(8,128)(2,1)}, u32[]{:S(2)}, u32[]{:S(2)}) %collective-permute-start.14) | collective-permute-done | bytes 524320 | tf_op jit(solution)/shard_map/ppermute | solution.py:574
  63.5 0.0 collective-permute-start.17
  63.5 0.0 collective-permute-done.19.refs_3_
  63.5 1.3 %collective-permute-start.15 = (bf16[32,64,128]{2,1,0:T(8,128)(2,1)}, bf16[32,64,128]{2,1,0:T(8,128)(2,1)}, u32[]{:S(2)}, u32[]{:S(2)}) collective-permute-start(bf16[32,64,128]{2,1,0:T(8,128)(2,1)} %collective-permute-done.14.refs_0_), channel_id=1, source_target_pairs={{4,6},{5,7},{12,14},{13,15},{20,22},{21,23},{28,30},{29,31}} | collective-permute-start | bytes 1572872 | tf_op jit(solution)/shard_map/ppermute | solution.py:574
  64.8 6.3 %shard_map.68.refs_2_ = f32[32,80,128]{2,1,0:T(8,128)} custom-call(s32[2]{0:T(128)} %pad_add_fusion.refs_0_.place_ref, s32[2,8]{1,0:T(2,128)} %bitcast.12, bf16[64,64,128]{2,1,0:T(8,128)(2,1)} %shard_map.61.left_ref, bf16[32,64,128]{2,1,0:T(8,128)(2,1)} %shard_map.67.refs_0_, bf16[32,64,128]{2,1,0:T(8,128)(2,1)} %collective-permute-done.18.refs_1_, ...), custom_call_target="tpu_custom_call" | custom-call | flops 6000000000 | bytes 18000000 | tf_op jit(solution)/shard_map/pallas_call | solution.py:456
  71.2 3.6 %collective-permute-done.5.refs_0_ = bf16[32,64,128]{2,1,0:T(8,128)(2,1)} collective-permute-done((bf16[32,64,128]{2,1,0:T(8,128)(2,1)}, bf16[32,64,128]{2,1,0:T(8,128)(2,1)}, u32[]{:S(2)}, u32[]{:S(2)}) %collective-permute-start.5) | collective-permute-done | bytes 524320 | tf_op jit(solution)/shard_map/ppermute | solution.py:574
  74.8 0.0 collective-permute-start.8
  74.8 0.0 collective-permute-done.9.refs_1_
  74.8 1.5 %collective-permute-start.6 = (bf16[32,64,128]{2,1,0:T(8,128)(2,1)}, bf16[32,64,128]{2,1,0:T(8,128)(2,1)}, u32[]{:S(2)}, u32[]{:S(2)}) collective-permute-start(bf16[32,64,128]{2,1,0:T(8,128)(2,1)} %collective-permute-done.5.refs_0_), channel_id=1, source_target_pairs={{4,6},{5,7},{12,14},{13,15},{20,22},{21,23},{28,30},{29,31}} | collective-permute-start | bytes 1572872 | tf_op jit(solution)/shard_map/ppermute | solution.py:574
  76.2 5.7 %shard_map.63.refs_2_ = f32[32,80,128]{2,1,0:T(8,128)} custom-call(s32[2]{0:T(128)} %pad_add_fusion.refs_0_.place_ref, s32[2,8]{1,0:T(2,128)} %bitcast.13, bf16[64,64,128]{2,1,0:T(8,128)(2,1)} %shard_map.61.left_ref, bf16[32,64,128]{2,1,0:T(8,128)(2,1)} %shard_map.62.refs_0_, bf16[32,64,128]{2,1,0:T(8,128)(2,1)} %collective-permute-done.9.refs_1_, ...), custom_call_target="tpu_custom_call" | custom-call | flops 6000000000 | bytes 18000000 | tf_op jit(solution)/shard_map/pallas_call | solution.py:456
  82.0 4.0 %collective-permute-done.15.refs_0_ = bf16[32,64,128]{2,1,0:T(8,128)(2,1)} collective-permute-done((bf16[32,64,128]{2,1,0:T(8,128)(2,1)}, bf16[32,64,128]{2,1,0:T(8,128)(2,1)}, u32[]{:S(2)}, u32[]{:S(2)}) %collective-permute-start.15) | collective-permute-done | bytes 524320 | tf_op jit(solution)/shard_map/ppermute | solution.py:574
  86.0 4.6 %shard_map.69.refs_2_ = f32[32,80,128]{2,1,0:T(8,128)} custom-call(s32[2]{0:T(128)} %pad_add_fusion.refs_0_.place_ref, s32[2,8]{1,0:T(2,128)} %bitcast.14, bf16[64,64,128]{2,1,0:T(8,128)(2,1)} %shard_map.61.left_ref, bf16[32,64,128]{2,1,0:T(8,128)(2,1)} %collective-permute-done.14.refs_0_, ...), custom_call_target="tpu_custom_call", output_to_operand_aliasing={{}: (5, {})} | custom-call | flops 6000000000 | bytes 18000000 | tf_op jit(solution)/shard_map/pallas_call | solution.py:456
  90.6 6.1 %collective-permute-done.6.refs_0_ = bf16[32,64,128]{2,1,0:T(8,128)(2,1)} collective-permute-done((bf16[32,64,128]{2,1,0:T(8,128)(2,1)}, bf16[32,64,128]{2,1,0:T(8,128)(2,1)}, u32[]{:S(2)}, u32[]{:S(2)}) %collective-permute-start.6) | collective-permute-done | bytes 524320 | tf_op jit(solution)/shard_map/ppermute | solution.py:574
  96.7 0.0 collective-permute-start.7
  96.7 0.0 collective-permute-done.8.refs_1_
  96.7 5.1 %shard_map.64.refs_1_ = f32[32,80,128]{2,1,0:T(8,128)} custom-call(s32[2]{0:T(128)} %pad_add_fusion.refs_0_.place_ref, s32[2,8]{1,0:T(2,128)} %bitcast.15, bf16[64,64,128]{2,1,0:T(8,128)(2,1)} %shard_map.61.left_ref, bf16[32,64,128]{2,1,0:T(8,128)(2,1)} %collective-permute-done.5.refs_0_, ...), custom_call_target="tpu_custom_call", output_to_operand_aliasing={{}: (5, {})} | custom-call | flops 6000000000 | bytes 18000000 | tf_op jit(solution)/shard_map/pallas_call | solution.py:456
  101.8 5.5 %shard_map.65.refs_1_ = f32[32,80,128]{2,1,0:T(8,128)} custom-call(s32[2]{0:T(128)} %pad_add_fusion.refs_0_.place_ref, s32[2,8]{1,0:T(2,128)} %bitcast.16, bf16[64,64,128]{2,1,0:T(8,128)(2,1)} %shard_map.61.left_ref, bf16[32,64,128]{2,1,0:T(8,128)(2,1)} %collective-permute-done.6.refs_0_, ...), custom_call_target="tpu_custom_call", output_to_operand_aliasing={{}: (4, {})} | custom-call | flops 6000000000 | bytes 18000000 | tf_op jit(solution)/shard_map/pallas_call | solution.py:456
  107.2 0.0 collective-permute-done.16.refs_1_
  107.3 4.5 %shard_map.70 = (bf16[64,64,128]{2,1,0:T(8,128)(2,1)}, f32[64,128]{1,0:T(8,128)}) custom-call(s32[2]{0:T(128)} %pad_add_fusion.refs_0_.place_ref, s32[2,8]{1,0:T(2,128)} %bitcast.17, bf16[64,64,128]{2,1,0:T(8,128)(2,1)} %shard_map.61.left_ref, bf16[32,64,128]{2,1,0:T(8,128)(2,1)} %collective-permute-done.15.refs_0_, ...), custom_call_target="tpu_custom_call" | custom-call | flops 4000000000 | bytes 12000000 | tf_op jit(solution)/shard_map/pallas_call | solution.py:487
  111.8 0.0 collective-permute-done.7.refs_0_
  111.8 5.5 %shard_map.71 = (bf16[64,64,128]{2,1,0:T(8,128)(2,1)}, f32[64,128]{1,0:T(8,128)}) custom-call(s32[2]{0:T(128)} %pad_add_fusion.refs_0_.place_ref, s32[2,8]{1,0:T(2,128)} %bitcast.18, bf16[64,64,128]{2,1,0:T(8,128)(2,1)} %shard_map.61.left_ref, bf16[32,64,128]{2,1,0:T(8,128)(2,1)} %collective-permute-done.7.refs_0_, ...), custom_call_target="tpu_custom_call", output_to_operand_aliasing={{0}: (5, {}), {1}: (6, {})} | custom-call | flops 4000000000 | bytes 12000000 | tf_op jit(solution)/shard_map/pallas_call | solution.py:487
  (7 shorter events, 0.0 us)
Async XLA Ops:
  2.5 9.6 %collective-permute-start = (bf16[2,6,64,128]{3,2,1,0:T(8,128)(2,1)}, bf16[2,6,64,128]{3,2,1,0:T(8,128)(2,1)}, u32[]{:S(2)}, u32[]{:S(2)}) collective-permute-start(bf16[2,6,64,128]{3,2,1,0:T(8,128)(2,1)} %get-tuple-element.6), channel_id=1, source_target_pairs={{0,8},{8,16},{16,24},{24,0},{1,9},{9,17},{17,25},{25,1},{2,10},{10... | collective-permute-start | bytes 589832 | tf_op jit(solution)/shard_map/ppermute | solution.py:554
  2.9 10.6 %collective-permute-start.1 = (bf16[2,6,64,128]{3,2,1,0:T(8,128)(2,1)}, bf16[2,6,64,128]{3,2,1,0:T(8,128)(2,1)}, u32[]{:S(2)}, u32[]{:S(2)}) collective-permute-start(bf16[2,6,64,128]{3,2,1,0:T(8,128)(2,1)} %get-tuple-element.7), channel_id=1, source_target_pairs={{8,0},{16,8},{24,16},{0,24},{9,1},{17,9},{25,17},{1,25},{10,2},{18... | collective-permute-start | bytes 589832 | tf_op jit(solution)/shard_map/ppermute | solution.py:555
  11.0 8.0 %collective-permute-start.12 = (bf16[9,64,128]{2,1,0:T(8,128)(2,1)}, bf16[9,64,128]{2,1,0:T(8,128)(2,1)}, u32[]{:S(2)}, u32[]{:S(2)}) collective-permute-start(bf16[9,64,128]{2,1,0:T(8,128)(2,1)} %shard_map.66.refs_1_), channel_id=1, source_target_pairs={{1,2},{3,4},{5,6},{2,1},{4,3},{6,5},{0,7},{7,0},{9,10},{11,12},{13... | collective-permute-start | bytes 442376 | tf_op jit(solution)/shard_map/ppermute | solution.py:543
  11.0 8.0 %collective-permute-start.11 = (bf16[9,64,128]{2,1,0:T(8,128)(2,1)}, bf16[9,64,128]{2,1,0:T(8,128)(2,1)}, u32[]{:S(2)}, u32[]{:S(2)}) collective-permute-start(bf16[9,64,128]{2,1,0:T(8,128)(2,1)} %shard_map.66.refs_1_), channel_id=1, source_target_pairs={{0,1},{1,0},{2,3},{3,2},{4,5},{5,4},{6,7},{7,6},{8,9},{9,8},{10,11... | collective-permute-start | bytes 442376 | tf_op jit(solution)/shard_map/ppermute | solution.py:544
  17.0 10.4 %collective-permute-start.3 = (bf16[27,64,128]{2,1,0:T(8,128)(2,1)}, bf16[27,64,128]{2,1,0:T(8,128)(2,1)}, u32[]{:S(2)}, u32[]{:S(2)}) collective-permute-start(bf16[27,64,128]{2,1,0:T(8,128)(2,1)} %shard_map.60.refs_3_), channel_id=1, source_target_pairs={{1,2},{3,4},{5,6},{2,1},{4,3},{6,5},{9,10},{11,12},{13,14},{10,9},... | collective-permute-start | bytes 1327112 | tf_op jit(solution)/shard_map/ppermute | solution.py:543
  18.9 8.5 %collective-permute-start.2 = (bf16[27,64,128]{2,1,0:T(8,128)(2,1)}, bf16[27,64,128]{2,1,0:T(8,128)(2,1)}, u32[]{:S(2)}, u32[]{:S(2)}) collective-permute-start(bf16[27,64,128]{2,1,0:T(8,128)(2,1)} %shard_map.60.refs_3_), channel_id=1, source_target_pairs={{0,1},{1,0},{2,3},{3,2},{4,5},{5,4},{6,7},{7,6},{8,9},{9,8},{10,11... | collective-permute-start | bytes 1327112 | tf_op jit(solution)/shard_map/ppermute | solution.py:544
  25.5 28.9 %collective-permute-start.18 = (bf16[32,64,128]{2,1,0:T(8,128)(2,1)}, bf16[32,64,128]{2,1,0:T(8,128)(2,1)}, u32[]{:S(2)}, u32[]{:S(2)}) collective-permute-start(bf16[32,64,128]{2,1,0:T(8,128)(2,1)} %shard_map.67.refs_0_), channel_id=1, source_target_pairs={{0,1},{1,0},{2,3},{3,2},{4,5},{5,4},{6,7},{7,6},{8,9},{9,8},{10,11... | collective-permute-start | bytes 1572872 | tf_op jit(solution)/shard_map/ppermute | solution.py:575
  25.9 15.1 %collective-permute-start.13 = (bf16[32,64,128]{2,1,0:T(8,128)(2,1)}, bf16[32,64,128]{2,1,0:T(8,128)(2,1)}, u32[]{:S(2)}, u32[]{:S(2)}) collective-permute-start(bf16[32,64,128]{2,1,0:T(8,128)(2,1)} %shard_map.67.refs_0_), channel_id=1, source_target_pairs={{0,2},{1,3},{2,4},{3,5},{4,6},{5,7},{6,0},{7,1},{8,10},{9,11},{10,... | collective-permute-start | bytes 1572872 | tf_op jit(solution)/shard_map/ppermute | solution.py:574
  35.4 39.4 %collective-permute-start.9 = (bf16[32,64,128]{2,1,0:T(8,128)(2,1)}, bf16[32,64,128]{2,1,0:T(8,128)(2,1)}, u32[]{:S(2)}, u32[]{:S(2)}) collective-permute-start(bf16[32,64,128]{2,1,0:T(8,128)(2,1)} %shard_map.62.refs_0_), channel_id=1, source_target_pairs={{0,1},{1,0},{2,3},{3,2},{4,5},{5,4},{6,7},{7,6},{8,9},{9,8},{10,11... | collective-permute-start | bytes 1572872 | tf_op jit(solution)/shard_map/ppermute | solution.py:575
  35.6 18.5 %collective-permute-start.4 = (bf16[32,64,128]{2,1,0:T(8,128)(2,1)}, bf16[32,64,128]{2,1,0:T(8,128)(2,1)}, u32[]{:S(2)}, u32[]{:S(2)}) collective-permute-start(bf16[32,64,128]{2,1,0:T(8,128)(2,1)} %shard_map.62.refs_0_), channel_id=1, source_target_pairs={{0,2},{1,3},{2,4},{3,5},{4,6},{5,7},{6,0},{7,1},{8,10},{9,11},{10,... | collective-permute-start | bytes 1572872 | tf_op jit(solution)/shard_map/ppermute | solution.py:574
  41.1 22.5 %collective-permute-start.19 = (bf16[32,64,128]{2,1,0:T(8,128)(2,1)}, bf16[32,64,128]{2,1,0:T(8,128)(2,1)}, u32[]{:S(2)}, u32[]{:S(2)}) collective-permute-start(bf16[32,64,128]{2,1,0:T(8,128)(2,1)} %collective-permute-done.13.refs_2_), channel_id=1, source_target_pairs={{0,1},{1,0},{2,3},{3,2},{4,5},{5,4},{6,7},{7,6},{8,9},{9,8},{10,11... | collective-permute-start | bytes 1572872 | tf_op jit(solution)/shard_map/ppermute | solution.py:575
  41.1 22.5 %collective-permute-start.14 = (bf16[32,64,128]{2,1,0:T(8,128)(2,1)}, bf16[32,64,128]{2,1,0:T(8,128)(2,1)}, u32[]{:S(2)}, u32[]{:S(2)}) collective-permute-start(bf16[32,64,128]{2,1,0:T(8,128)(2,1)} %collective-permute-done.13.refs_2_), channel_id=1, source_target_pairs={{0,2},{1,3},{2,4},{3,5},{4,6},{5,7},{6,0},{7,1},{8,10},{9,11},{10,... | collective-permute-start | bytes 1572872 | tf_op jit(solution)/shard_map/ppermute | solution.py:574
  54.1 22.1 %collective-permute-start.10 = (bf16[32,64,128]{2,1,0:T(8,128)(2,1)}, bf16[32,64,128]{2,1,0:T(8,128)(2,1)}, u32[]{:S(2)}, u32[]{:S(2)}) collective-permute-start(bf16[32,64,128]{2,1,0:T(8,128)(2,1)} %collective-permute-done.4.refs_2_), channel_id=1, source_target_pairs={{0,1},{1,0},{2,3},{3,2},{4,5},{5,4},{6,7},{7,6},{8,9},{9,8},{10,11... | collective-permute-start | bytes 1572872 | tf_op jit(solution)/shard_map/ppermute | solution.py:575
  54.3 20.4 %collective-permute-start.5 = (bf16[32,64,128]{2,1,0:T(8,128)(2,1)}, bf16[32,64,128]{2,1,0:T(8,128)(2,1)}, u32[]{:S(2)}, u32[]{:S(2)}) collective-permute-start(bf16[32,64,128]{2,1,0:T(8,128)(2,1)} %collective-permute-done.4.refs_2_), channel_id=1, source_target_pairs={{0,2},{1,3},{2,4},{3,5},{4,6},{5,7},{6,0},{7,1},{8,10},{9,11},{10,... | collective-permute-start | bytes 1572872 | tf_op jit(solution)/shard_map/ppermute | solution.py:574
  63.5 22.5 %collective-permute-start.17 = (bf16[32,64,128]{2,1,0:T(8,128)(2,1)}, bf16[32,64,128]{2,1,0:T(8,128)(2,1)}, u32[]{:S(2)}, u32[]{:S(2)}) collective-permute-start(bf16[32,64,128]{2,1,0:T(8,128)(2,1)} %collective-permute-done.14.refs_0_), channel_id=1, source_target_pairs={{0,1},{1,0},{2,3},{3,2},{4,5},{5,4},{6,7},{7,6},{8,9},{9,8},{10,11... | collective-permute-start | bytes 1572872 | tf_op jit(solution)/shard_map/ppermute | solution.py:575
  63.5 22.5 %collective-permute-start.15 = (bf16[32,64,128]{2,1,0:T(8,128)(2,1)}, bf16[32,64,128]{2,1,0:T(8,128)(2,1)}, u32[]{:S(2)}, u32[]{:S(2)}) collective-permute-start(bf16[32,64,128]{2,1,0:T(8,128)(2,1)} %collective-permute-done.14.refs_0_), channel_id=1, source_target_pairs={{4,6},{5,7},{12,14},{13,15},{20,22},{21,23},{28,30},{29,31}} | collective-permute-start | bytes 1572872 | tf_op jit(solution)/shard_map/ppermute | solution.py:574
  74.8 21.9 %collective-permute-start.8 = (bf16[32,64,128]{2,1,0:T(8,128)(2,1)}, bf16[32,64,128]{2,1,0:T(8,128)(2,1)}, u32[]{:S(2)}, u32[]{:S(2)}) collective-permute-start(bf16[32,64,128]{2,1,0:T(8,128)(2,1)} %collective-permute-done.5.refs_0_), channel_id=1, source_target_pairs={{0,1},{1,0},{2,3},{3,2},{4,5},{5,4},{6,7},{7,6},{8,9},{9,8},{10,11... | collective-permute-start | bytes 1572872 | tf_op jit(solution)/shard_map/ppermute | solution.py:575
  74.8 21.9 %collective-permute-start.6 = (bf16[32,64,128]{2,1,0:T(8,128)(2,1)}, bf16[32,64,128]{2,1,0:T(8,128)(2,1)}, u32[]{:S(2)}, u32[]{:S(2)}) collective-permute-start(bf16[32,64,128]{2,1,0:T(8,128)(2,1)} %collective-permute-done.5.refs_0_), channel_id=1, source_target_pairs={{4,6},{5,7},{12,14},{13,15},{20,22},{21,23},{28,30},{29,31}} | collective-permute-start | bytes 1572872 | tf_op jit(solution)/shard_map/ppermute | solution.py:574
  86.0 21.3 %collective-permute-start.16 = (bf16[32,64,128]{2,1,0:T(8,128)(2,1)}, bf16[32,64,128]{2,1,0:T(8,128)(2,1)}, u32[]{:S(2)}, u32[]{:S(2)}) collective-permute-start(bf16[32,64,128]{2,1,0:T(8,128)(2,1)} %collective-permute-done.15.refs_0_), channel_id=1, source_target_pairs={{0,1},{1,0},{2,3},{3,2},{4,5},{5,4},{6,7},{7,6},{8,9},{9,8},{10,11... | collective-permute-start | bytes 1572872 | tf_op jit(solution)/shard_map/ppermute | solution.py:575
  96.7 15.1 %collective-permute-start.7 = (bf16[32,64,128]{2,1,0:T(8,128)(2,1)}, bf16[32,64,128]{2,1,0:T(8,128)(2,1)}, u32[]{:S(2)}, u32[]{:S(2)}) collective-permute-start(bf16[32,64,128]{2,1,0:T(8,128)(2,1)} %collective-permute-done.6.refs_0_), channel_id=1, source_target_pairs={{0,1},{1,0},{2,3},{3,2},{4,5},{5,4},{6,7},{7,6},{8,9},{9,8},{10,11... | collective-permute-start | bytes 1572872 | tf_op jit(solution)/shard_map/ppermute | solution.py:575
